TPU v7x, 32 devices: a whole 2x2x4 slice. The times are simulated.
32 devices in a mesh: depth: 2 (over core), height: 4 (over y, x), dp: 4 (over z).
Axes of the slice: x: 2, y: 2, z: 4, core: 2. Of those that a mesh axis runs over, the one named last changes fastest.
Arguments:
- inputs: bfloat16 [4, 32, 16, 16, 128], P('dp', None, 'depth', 'height'), may hold values from -6 to 6
- weight: bfloat16 [64, 32, 3, 3, 3], replicated, may hold values from -0.21875 to 0.21875
- bias: float32 [64], replicated, may hold values from -3 to 3
- cotangent: bfloat16 [4, 64, 16, 16, 128], P('dp', None, 'depth', 'height'), may hold values from -6 to 6
Outputs:
- grad_input: bfloat16 [4, 32, 16, 16, 128], P('dp', None, 'depth', 'height')
- grad_weight: float32 [64, 32, 3, 3, 3], replicated
- grad_bias: float32 [64], replicated
All inputs are finite; a program needn't handle non-finite values.
Results may differ from a plain program's by a relative error of at most 0.0065.
Values may be sent and summed in bfloat16 or wider, within the bound.
No kernel may reach another device: no remote copies, remote signals or barrier semaphores. Data moves between devices by JAX's collectives and lax.ppermute only.
A program may use at most 64 MiB of HBM per device.

v0:
```python
import jax
import jax.numpy as jnp
from jax import lax
from jax.experimental import pallas as pl
from jax.experimental.pallas import tpu as pltpu
from jax.sharding import PartitionSpec as P

F32 = jnp.float32
BF16 = jnp.bfloat16
AXES = ("depth", "height", "dp")


def exchange(low_edge, high_edge, axis):
    count = lax.axis_size(axis)
    if count == 1:
        return jnp.zeros_like(high_edge), jnp.zeros_like(low_edge)
    if count == 2:
        first = lax.axis_index(axis) == 0
        got = lax.ppermute(jnp.where(first, high_edge, low_edge), axis, [(0, 1), (1, 0)])
        none = jnp.zeros_like(got)
        return jnp.where(first, none, got), jnp.where(first, got, none)
    up = [(i, i + 1) for i in range(count - 1)]
    down = [(i + 1, i) for i in range(count - 1)]
    return lax.ppermute(high_edge, axis, up), lax.ppermute(low_edge, axis, down)


def halo(field):
    below, above = exchange(field[0], field[-1], "depth")

    def column(at):
        return jnp.concatenate([below[at][None], field[:, at], above[at][None]], axis=0)

    left, right = exchange(column(0), column(-1), "height")
    return below, above, left, right


def swap(array, axis, bit):
    return lax.ppermute(array, axis, [(i, i ^ bit) for i in range(lax.axis_size(axis))])


def padded_row(core, below, above, left, right, d, h):
    depth, height = core.shape[0], core.shape[1]
    if h == 0:
        return left[d]
    if h == height + 1:
        return right[d]
    if d == 0:
        return below[h - 1]
    if d == depth + 1:
        return above[h - 1]
    return core[d - 1, h - 1]


def fill_patches(refs, patches):
    depth, height, chans, width = refs[0].shape
    for d in range(depth + 2):
        for row in range(height + 2):
            value = padded_row(*refs, d, row)
            for b in range(3):
                h = row - b
                if 0 <= h < height:
                    patches[pl.ds((d * 3 + b) * chans, chans), pl.ds(h * width, width)] = value


def shifted(value, step):
    if step == 0:
        return value
    width = value.shape[1]
    lane = lax.broadcasted_iota(jnp.int32, value.shape, 1)
    edge = width - 1 if step == 1 else 0
    return jnp.where(lane == edge, 0.0, pltpu.roll(value, (-step) % width, 1))


def forward_kernel(x, below, above, left, right, w1, bias, cot, delta, payload, patches, grad):
    depth, height, ci, width = x.shape
    co = cot.shape[2]
    fill_patches((x, below, above, left, right), patches)
    shift_bias = jnp.broadcast_to(bias[...], (co, width))
    bias_acc = jnp.zeros((co, width), F32)
    for d in range(depth):
        window = pl.ds(d * 3 * ci, 9 * ci)
        taps = jnp.dot(w1[...], patches[window, :], preferred_element_type=F32)
        blocks = [[], [], []]
        for h in range(height):
            lanes = slice(h * width, (h + 1) * width)
            linear = taps[co : 2 * co, lanes] + shift_bias
            linear = linear + shifted(taps[:co, lanes], -1) + shifted(taps[2 * co :, lanes], 1)
            sigma = 1.0 / (1.0 + jnp.exp(-linear))
            slope = cot[d, h].astype(F32) * sigma * (1.0 + linear * (1.0 - sigma))
            rounded = slope.astype(BF16)
            delta[d, h] = rounded
            wide = rounded.astype(F32)
            bias_acc = bias_acc + wide
            blocks[0].append(shifted(wide, 1).astype(BF16))
            blocks[1].append(rounded)
            blocks[2].append(shifted(wide, -1).astype(BF16))
        slopes = jnp.concatenate([jnp.concatenate(part, axis=1) for part in blocks], axis=0)
        term = lax.dot_general(
            patches[window, :], slopes, (((1,), (1,)), ((), ())), preferred_element_type=F32
        )
        if d == 0:
            grad[...] = term
        else:
            grad[...] += term
    rows = 9 * ci
    payload[0:rows, :] = grad[:, : 2 * co]
    payload[rows : rows + rows // 2, :co] = grad[: rows // 2, 2 * co :]
    payload[rows : rows + rows // 2, co:] = grad[rows // 2 :, 2 * co :]
    tail = rows + rows // 2
    total = jnp.sum(bias_acc.T, axis=0, keepdims=True)
    left_over = payload.shape[0] - tail
    row_at = lax.broadcasted_iota(jnp.int32, (left_over, co), 0)
    payload[tail:, :co] = jnp.where(row_at == 0, jnp.broadcast_to(total, (left_over, co)), 0.0)
    payload[tail:, co:] = jnp.zeros((left_over, payload.shape[1] - co), F32)


def input_kernel(delta, below, above, left, right, w2, out, patches):
    depth, height, co, width = delta.shape
    ci = out.shape[2]
    fill_patches((delta, below, above, left, right), patches)
    for d in range(depth):
        taps = jnp.dot(w2[...], patches[pl.ds(d * 3 * co, 9 * co), :], preferred_element_type=F32)
        for h in range(height):
            lanes = slice(h * width, (h + 1) * width)
            total = taps[ci : 2 * ci, lanes]
            total = total + shifted(taps[:ci, lanes], 1) + shifted(taps[2 * ci :, lanes], -1)
            out[d, h] = total.astype(BF16)


def unpack_kernel(scale, low, high, weight_out, bias_out, full):
    half = low.shape[0]
    co = bias_out.shape[1]
    full[:half, :] = low[...] * scale
    full[half:, :] = high[...] * scale
    rows = weight_out.shape[0] // 3
    ci = rows // 9
    step = ci // 2
    for j in range(9):
        for part in range(2):
            source = j * ci + part * step
            to = 3 * j * ci + part * step
            weight_out[pl.ds(to, step), :] = full[pl.ds(source, step), :co]
            weight_out[pl.ds(to + ci, step), :] = full[pl.ds(source, step), co:]
            at = rows + source % (rows // 2)
            lanes = slice(0, co) if source < rows // 2 else slice(co, 2 * co)
            weight_out[pl.ds(to + 2 * ci, step), :] = full[pl.ds(at, step), lanes]
    bias_out[...] = full[rows + rows // 2 : rows + rows // 2 + 1, :co]


def call(kernel, outs, scratch, flops, *args):
    size = sum(a.size * a.dtype.itemsize for a in args) + sum(o.size * o.dtype.itemsize for o in outs)
    return pl.pallas_call(
        kernel,
        out_shape=outs,
        scratch_shapes=scratch,
        compiler_params=pltpu.CompilerParams(vmem_limit_bytes=40 << 20),
        cost_estimate=pl.CostEstimate(flops=flops, bytes_accessed=size, transcendentals=0),
    )(*args)


def summed(total):
    stages = []
    for axis in AXES:
        count = lax.axis_size(axis)
        assert count & (count - 1) == 0
        stages += [(axis, 1 << bit) for bit in range(count.bit_length() - 1)]
    half = total.shape[0] // 2
    low, high = total[:half], total[half:]
    scattered = bool(stages) and stages[0] == ("depth", 1)
    if scattered:
        first = lax.axis_index("depth") % 2 == 0
        got = swap(jnp.where(first, high, low), "depth", 1)
        part = jnp.where(first, low, high) + got
        stages = stages[1:]
    else:
        part = total
    for axis, bit in stages:
        own = lax.reduce_precision(part, 8, 7)
        part = own + swap(own.astype(BF16), axis, bit).astype(F32)
    if not scattered:
        return part[:half], part[half:]
    other = swap(part, "depth", 1)
    return jnp.where(first, part, other), jnp.where(first, other, part)


def local(inputs, weight, bias, cotangent):
    cubes, ci, depth, height, width = inputs.shape
    co = cotangent.shape[1]
    taps = weight.transpose(2, 3, 4, 1, 0)
    w1 = taps.transpose(2, 4, 0, 1, 3).reshape(3 * co, 9 * ci)
    w2 = jnp.flip(taps, (0, 1)).transpose(2, 3, 0, 1, 4).reshape(3 * ci, 9 * co)
    payload_rows = 9 * ci + 9 * ci // 2 + 16
    voxels = cubes * depth * height * width
    total = None
    grads = []
    for cube in range(cubes):
        x = inputs[cube].transpose(1, 2, 0, 3)
        cot = cotangent[cube].transpose(1, 2, 0, 3)
        flops = 2 * depth * height * width * 27 * ci * co
        delta, payload = call(
            forward_kernel,
            (
                jax.ShapeDtypeStruct((depth, height, co, width), BF16),
                jax.ShapeDtypeStruct((payload_rows, 2 * co), F32),
            ),
            [
                pltpu.VMEM(((depth + 2) * 3 * ci, height * width), BF16),
                pltpu.VMEM((9 * ci, 3 * co), F32),
            ],
            2 * flops,
            x,
            *halo(x),
            w1,
            bias[:, None],
            cot,
        )
        total = payload if total is None else total + payload
        (grad,) = call(
            input_kernel,
            (jax.ShapeDtypeStruct((depth, height, ci, width), BF16),),
            [pltpu.VMEM(((depth + 2) * 3 * co, height * width), BF16)],
            flops,
            delta,
            *halo(delta),
            w2,
        )
        grads.append(grad.transpose(2, 0, 1, 3))
    for axis in AXES:
        voxels *= lax.axis_size(axis)
    scale = float(voxels) ** -0.5
    low, high = summed(total)
    grad_taps, grad_bias = call(
        lambda *refs: unpack_kernel(scale, *refs),
        (jax.ShapeDtypeStruct((27 * ci, co), F32), jax.ShapeDtypeStruct((1, co), F32)),
        [pltpu.VMEM((payload_rows, 2 * co), F32)],
        payload_rows * 2 * co,
        low,
        high,
    )
    grad_weight = grad_taps.reshape(3, 3, 3, ci, co).transpose(4, 3, 0, 1, 2)
    return jnp.stack(grads), grad_weight, grad_bias.reshape(co)


def solution(mesh):
    voxels = P("dp", None, "depth", "height", None)
    return jax.shard_map(
        local,
        mesh=mesh,
        in_specs=(voxels, P(), P(), voxels),
        out_specs=(voxels, P(), P()),
        check_vma=False,
    )
```

profile of v0, /device:TPU:4, one launch (start us, length us, event | category | flops | bytes accessed | tf_op | source)
XLA Modules:
  0.0 46.7 jit_solution(10205002221561172886)
XLA Ops:
  0.6 1.1 %copy.29 = bf16[1,32,8,4,128]{4,1,3,2,0:T(8,128)(2,1)S(1)} copy(bf16[1,32,8,4,128]{4,3,2,1,0:T(4,128)(2,1)} %param.4) | data formatting | bytes 524288 | tf_op args[0]
  1.8 1.2 %collective-permute-done = bf16[4,32,128]{2,1,0:T(8,128)(2,1)S(1)} collective-permute-done((bf16[4,32,128]{2,1,0:T(8,128)(2,1)S(1)}, bf16[4,32,128]{2,1,0:T(8,128)(2,1)S(1)}, u32[]{:S(2)}, u32[]{:S(2)}) %collective-permute-start) | collective-permute-done | bytes 32800 | tf_op jit(solution)/shard_map/ppermute | solution.py:19
  3.0 3.5 %collective-permute-start.2 = (bf16[10,32,128]{2,1,0:T(8,128)(2,1)S(1)}, bf16[10,32,128]{2,1,0:T(8,128)(2,1)S(1)}, u32[]{:S(2)}, u32[]{:S(2)}) collective-permute-start(bf16[10,32,128]{2,1,0:T(8,128)(2,1)S(1)} %pad_maximum_fusion.3), channel_id=1, source_target_pairs={{4,0},{8,4},{12,8},{5,1},{9,5},{13,9},{6,2},{10,6},{14,10},{7,3},{... | collective-permute-start | bytes 245768 | tf_op jit(solution)/shard_map/ppermute | solution.py:24
  6.5 2.5 %collective-permute-start.1 = (bf16[10,32,128]{2,1,0:T(8,128)(2,1)S(1)}, bf16[10,32,128]{2,1,0:T(8,128)(2,1)S(1)}, u32[]{:S(2)}, u32[]{:S(2)}) collective-permute-start(bf16[10,32,128]{2,1,0:T(8,128)(2,1)S(1)} %pad_maximum_fusion.2), channel_id=1, source_target_pairs={{0,4},{4,8},{8,12},{1,5},{5,9},{9,13},{2,6},{6,10},{10,14},{3,7},{... | collective-permute-start | bytes 245768 | tf_op jit(solution)/shard_map/ppermute | solution.py:24
  9.2 0.2 reshape.22
  9.6 0.5 %copy-done.1 = bf16[1,64,8,4,128]{4,3,2,1,0:T(4,128)(2,1)S(1)} copy-done((bf16[1,64,8,4,128]{4,3,2,1,0:T(4,128)(2,1)S(1)}, bf16[1,64,8,4,128]{4,3,2,1,0:T(4,128)(2,1)}, u32[]{:S(2)}) %copy-start.1) | copy-done | bytes 524312
  10.3 0.6 %copy-done.2 = f32[64]{0:T(128)S(1)} copy-done((f32[64]{0:T(128)S(1)}, f32[64]{0:T(128)}, u32[]{:S(2)}) %copy-start.2) | copy-done | bytes 280
  11.1 2.7 %collective-permute-done.1.left = bf16[10,32,128]{2,1,0:T(8,128)(2,1)S(1)} collective-permute-done((bf16[10,32,128]{2,1,0:T(8,128)(2,1)S(1)}, bf16[10,32,128]{2,1,0:T(8,128)(2,1)S(1)}, u32[]{:S(2)}, u32[]{:S(2)}) %collective-permute-start.1) | collective-permute-done | bytes 81952 | tf_op jit(solution)/shard_map/ppermute | solution.py:24
  13.8 4.1 %shard_map.67 = (bf16[8,4,64,128]{3,2,1,0:T(8,128)(2,1)S(1)}, f32[448,128]{1,0:T(8,128)S(1)}) custom-call(bf16[8,4,32,128]{3,2,1,0:T(8,128)(2,1)S(1)} %bitcast.38, bf16[4,32,128]{2,1,0:T(8,128)(2,1)S(1)} %get-tuple-element.36.below, bf16[4,32,128]{2,1,0:T(8,128)(2,1)S(1)} %get-tuple-element.35.above, bf16[10,32,128]{2,1,0:T(8,128)(2,1)S(1)} %collective-permute-done.1.left, ...), custom_call_target="tpu_custom_call" | custom-call | flops 905969664 | bytes 1880320 | tf_op jit(solution)/shard_map/pallas_call | solution.py:152
  18.1 0.6 %collective-permute-start.6 = (f32[224,128]{1,0:T(8,128)S(1)}, f32[224,128]{1,0:T(8,128)S(1)}, u32[]{:S(2)}, u32[]{:S(2)}) collective-permute-start(f32[224,128]{1,0:T(8,128)S(1)} %slice_select_fusion), channel_id=1, source_target_pairs={{0,16},{16,0},{1,17},{17,1},{2,18},{18,2},{3,19},{19,3},{4,20},{20... | collective-permute-start | bytes 344072 | tf_op jit(solution)/shard_map/ppermute | solution.py:38
  18.6 0.7 %collective-permute-done.3 = bf16[4,64,128]{2,1,0:T(8,128)(2,1)S(1)} collective-permute-done((bf16[4,64,128]{2,1,0:T(8,128)(2,1)S(1)}, bf16[4,64,128]{2,1,0:T(8,128)(2,1)S(1)}, u32[]{:S(2)}, u32[]{:S(2)}) %collective-permute-start.3) | collective-permute-done | bytes 65568 | tf_op jit(solution)/shard_map/ppermute | solution.py:19
  19.3 0.3 collective-permute-done.6
  19.7 4.2 %collective-permute-done.7 = bf16[224,128]{1,0:T(8,128)(2,1)S(1)} collective-permute-done((bf16[224,128]{1,0:T(8,128)(2,1)S(1)}, bf16[224,128]{1,0:T(8,128)(2,1)S(1)}, u32[]{:S(2)}, u32[]{:S(2)}) %collective-permute-start.7) | collective-permute-done | bytes 57376 | tf_op jit(solution)/shard_map/ppermute | solution.py:38
  24.0 4.2 %collective-permute-done.8 = bf16[224,128]{1,0:T(8,128)(2,1)S(1)} collective-permute-done((bf16[224,128]{1,0:T(8,128)(2,1)S(1)}, bf16[224,128]{1,0:T(8,128)(2,1)S(1)}, u32[]{:S(2)}, u32[]{:S(2)}) %collective-permute-start.8) | collective-permute-done | bytes 57376 | tf_op jit(solution)/shard_map/ppermute | solution.py:38
  28.2 1.6 %collective-permute-start.9 = (bf16[224,128]{1,0:T(8,128)(2,1)S(1)}, bf16[224,128]{1,0:T(8,128)(2,1)S(1)}, u32[]{:S(2)}, u32[]{:S(2)}) collective-permute-start(bf16[224,128]{1,0:T(8,128)(2,1)S(1)} %fusion.3), channel_id=1, source_target_pairs={{0,1},{1,0},{2,3},{3,2},{4,5},{5,4},{6,7},{7,6},{8,9},{9,8},{10,11... | collective-permute-start | bytes 172040 | tf_op jit(solution)/shard_map/ppermute | solution.py:38
  29.8 1.9 %collective-permute-start.5 = (bf16[10,64,128]{2,1,0:T(8,128)(2,1)S(1)}, bf16[10,64,128]{2,1,0:T(8,128)(2,1)S(1)}, u32[]{:S(2)}, u32[]{:S(2)}) collective-permute-start(bf16[10,64,128]{2,1,0:T(8,128)(2,1)S(1)} %pad_maximum_fusion.1), channel_id=1, source_target_pairs={{4,0},{8,4},{12,8},{5,1},{9,5},{13,9},{6,2},{10,6},{14,10},{7,3},{... | collective-permute-start | bytes 491528 | tf_op jit(solution)/shard_map/ppermute | solution.py:24
  31.8 0.6 %collective-permute-done.9 = bf16[224,128]{1,0:T(8,128)(2,1)S(1)} collective-permute-done((bf16[224,128]{1,0:T(8,128)(2,1)S(1)}, bf16[224,128]{1,0:T(8,128)(2,1)S(1)}, u32[]{:S(2)}, u32[]{:S(2)}) %collective-permute-start.9) | collective-permute-done | bytes 57376 | tf_op jit(solution)/shard_map/ppermute | solution.py:38
  32.5 3.2 %collective-permute-start.10 = (bf16[224,128]{1,0:T(8,128)(2,1)S(1)}, bf16[224,128]{1,0:T(8,128)(2,1)S(1)}, u32[]{:S(2)}, u32[]{:S(2)}) collective-permute-start(bf16[224,128]{1,0:T(8,128)(2,1)S(1)} %fusion.1), channel_id=1, source_target_pairs={{0,2},{1,3},{2,0},{3,1},{4,6},{5,7},{6,4},{7,5},{8,10},{9,11},{10,... | collective-permute-start | bytes 172040 | tf_op jit(solution)/shard_map/ppermute | solution.py:38
  35.6 2.8 %collective-permute-start.4 = (bf16[10,64,128]{2,1,0:T(8,128)(2,1)S(1)}, bf16[10,64,128]{2,1,0:T(8,128)(2,1)S(1)}, u32[]{:S(2)}, u32[]{:S(2)}) collective-permute-start(bf16[10,64,128]{2,1,0:T(8,128)(2,1)S(1)} %pad_maximum_fusion), channel_id=1, source_target_pairs={{0,4},{4,8},{8,12},{1,5},{5,9},{9,13},{2,6},{6,10},{10,14},{3,7},{... | collective-permute-start | bytes 491528 | tf_op jit(solution)/shard_map/ppermute | solution.py:24
  38.8 0.2 reshape.23.w2
  39.0 4.8 %collective-permute-done.4.left = bf16[10,64,128]{2,1,0:T(8,128)(2,1)S(1)} collective-permute-done((bf16[10,64,128]{2,1,0:T(8,128)(2,1)S(1)}, bf16[10,64,128]{2,1,0:T(8,128)(2,1)S(1)}, u32[]{:S(2)}, u32[]{:S(2)}) %collective-permute-start.4) | collective-permute-done | bytes 163872 | tf_op jit(solution)/shard_map/ppermute | solution.py:24
  43.8 1.2 %shard_map.68 = bf16[8,4,32,128]{3,2,1,0:T(8,128)(2,1)S(1)} custom-call(bf16[8,4,64,128]{3,2,1,0:T(8,128)(2,1)S(1)} %get-tuple-element.7.delta, bf16[4,64,128]{2,1,0:T(8,128)(2,1)S(1)} %get-tuple-element.30.below, bf16[4,64,128]{2,1,0:T(8,128)(2,1)S(1)} %get-tuple-element.29.above, bf16[10,64,128]{2,1,0:T(8,128)(2,1)S(1)} %collective-permute-done.4.left, ...), custom_call_target="tpu_custom_call" | custom-call | flops 452984832 | bytes 1355776 | tf_op jit(solution)/shard_map/pallas_call | solution.py:152
  44.9 0.8 %copy.23 = bf16[1,32,8,4,128]{4,3,2,1,0:T(4,128)(2,1)} copy(bf16[1,32,8,4,128]{4,1,3,2,0:T(8,128)(2,1)S(1)} %bitcast.40) | data formatting | bytes 524288
  45.8 0.9 %shard_map.69 = (f32[864,64]{1,0:T(8,128)}, f32[1,64]{1,0:T(1,128)}) custom-call(f32[224,128]{1,0:T(8,128)S(1)} %get-tuple-element.24.refs_0_, f32[224,128]{1,0:T(8,128)S(1)} %get-tuple-element.23.refs_1_), custom_call_target="tpu_custom_call" | custom-call | flops 57344 | bytes 450816 | tf_op jit(solution)/shard_map/pallas_call | solution.py:152
  (39 shorter events, 1.5 us)
Async XLA Ops:
  1.7 1.3 %collective-permute-start = (bf16[4,32,128]{2,1,0:T(8,128)(2,1)S(1)}, bf16[4,32,128]{2,1,0:T(8,128)(2,1)S(1)}, u32[]{:S(2)}, u32[]{:S(2)}) collective-permute-start(bf16[4,32,128]{2,1,0:T(8,128)(2,1)S(1)} %fusion.2), channel_id=1, source_target_pairs={{0,16},{16,0},{1,17},{17,1},{2,18},{18,2},{3,19},{19,3},{4,20},{20... | collective-permute-start | bytes 98312 | tf_op jit(solution)/shard_map/ppermute | solution.py:19
  3.0 6.1 %copy-start = (bf16[64,32,3,3,3]{0,1,4,3,2:T(8,128)(2,1)S(1)}, bf16[64,32,3,3,3]{0,1,4,3,2:T(8,128)(2,1)}, u32[]{:S(2)}) copy-start(bf16[64,32,3,3,3]{0,1,4,3,2:T(8,128)(2,1)} %param.5) | copy-start | bytes 331780
  3.0 8.0 %collective-permute-start.2 = (bf16[10,32,128]{2,1,0:T(8,128)(2,1)S(1)}, bf16[10,32,128]{2,1,0:T(8,128)(2,1)S(1)}, u32[]{:S(2)}, u32[]{:S(2)}) collective-permute-start(bf16[10,32,128]{2,1,0:T(8,128)(2,1)S(1)} %pad_maximum_fusion.3), channel_id=1, source_target_pairs={{4,0},{8,4},{12,8},{5,1},{9,5},{13,9},{6,2},{10,6},{14,10},{7,3},{... | collective-permute-start | bytes 245768 | tf_op jit(solution)/shard_map/ppermute | solution.py:24
  6.5 7.2 %collective-permute-start.1 = (bf16[10,32,128]{2,1,0:T(8,128)(2,1)S(1)}, bf16[10,32,128]{2,1,0:T(8,128)(2,1)S(1)}, u32[]{:S(2)}, u32[]{:S(2)}) collective-permute-start(bf16[10,32,128]{2,1,0:T(8,128)(2,1)S(1)} %pad_maximum_fusion.2), channel_id=1, source_target_pairs={{0,4},{4,8},{8,12},{1,5},{5,9},{9,13},{2,6},{6,10},{10,14},{3,7},{... | collective-permute-start | bytes 245768 | tf_op jit(solution)/shard_map/ppermute | solution.py:24
  9.1 1.0 %copy-start.1 = (bf16[1,64,8,4,128]{4,3,2,1,0:T(4,128)(2,1)S(1)}, bf16[1,64,8,4,128]{4,3,2,1,0:T(4,128)(2,1)}, u32[]{:S(2)}) copy-start(bf16[1,64,8,4,128]{4,3,2,1,0:T(4,128)(2,1)} %param.7) | copy-start | bytes 1572868
  10.3 0.7 %copy-start.2 = (f32[64]{0:T(128)S(1)}, f32[64]{0:T(128)}, u32[]{:S(2)}) copy-start(f32[64]{0:T(128)} %param.6) | copy-start | bytes 772
  18.0 1.3 %collective-permute-start.3 = (bf16[4,64,128]{2,1,0:T(8,128)(2,1)S(1)}, bf16[4,64,128]{2,1,0:T(8,128)(2,1)S(1)}, u32[]{:S(2)}, u32[]{:S(2)}) collective-permute-start(bf16[4,64,128]{2,1,0:T(8,128)(2,1)S(1)} %select_bitcast_fusion), channel_id=1, source_target_pairs={{0,16},{16,0},{1,17},{17,1},{2,18},{18,2},{3,19},{19,3},{4,20},{20... | collective-permute-start | bytes 196616 | tf_op jit(solution)/shard_map/ppermute | solution.py:19
  18.1 1.5 %collective-permute-start.6 = (f32[224,128]{1,0:T(8,128)S(1)}, f32[224,128]{1,0:T(8,128)S(1)}, u32[]{:S(2)}, u32[]{:S(2)}) collective-permute-start(f32[224,128]{1,0:T(8,128)S(1)} %slice_select_fusion), channel_id=1, source_target_pairs={{0,16},{16,0},{1,17},{17,1},{2,18},{18,2},{3,19},{19,3},{4,20},{20... | collective-permute-start | bytes 344072 | tf_op jit(solution)/shard_map/ppermute | solution.py:38
  19.6 4.3 %collective-permute-start.7 = (bf16[224,128]{1,0:T(8,128)(2,1)S(1)}, bf16[224,128]{1,0:T(8,128)(2,1)S(1)}, u32[]{:S(2)}, u32[]{:S(2)}) collective-permute-start(bf16[224,128]{1,0:T(8,128)(2,1)S(1)} %get-tuple-element.17), channel_id=1, source_target_pairs={{0,4},{4,0},{8,12},{12,8},{1,5},{5,1},{9,13},{13,9},{2,6},{6,2},{1... | collective-permute-start | bytes 172040 | tf_op jit(solution)/shard_map/ppermute | solution.py:38
  23.9 4.2 %collective-permute-start.8 = (bf16[224,128]{1,0:T(8,128)(2,1)S(1)}, bf16[224,128]{1,0:T(8,128)(2,1)S(1)}, u32[]{:S(2)}, u32[]{:S(2)}) collective-permute-start(bf16[224,128]{1,0:T(8,128)(2,1)S(1)} %fusion), channel_id=1, source_target_pairs={{0,8},{4,12},{8,0},{12,4},{1,9},{5,13},{9,1},{13,5},{2,10},{6,14},... | collective-permute-start | bytes 172040 | tf_op jit(solution)/shard_map/ppermute | solution.py:38
  28.2 4.2 %collective-permute-start.9 = (bf16[224,128]{1,0:T(8,128)(2,1)S(1)}, bf16[224,128]{1,0:T(8,128)(2,1)S(1)}, u32[]{:S(2)}, u32[]{:S(2)}) collective-permute-start(bf16[224,128]{1,0:T(8,128)(2,1)S(1)} %fusion.3), channel_id=1, source_target_pairs={{0,1},{1,0},{2,3},{3,2},{4,5},{5,4},{6,7},{7,6},{8,9},{9,8},{10,11... | collective-permute-start | bytes 172040 | tf_op jit(solution)/shard_map/ppermute | solution.py:38
  29.8 9.2 %collective-permute-start.5 = (bf16[10,64,128]{2,1,0:T(8,128)(2,1)S(1)}, bf16[10,64,128]{2,1,0:T(8,128)(2,1)S(1)}, u32[]{:S(2)}, u32[]{:S(2)}) collective-permute-start(bf16[10,64,128]{2,1,0:T(8,128)(2,1)S(1)} %pad_maximum_fusion.1), channel_id=1, source_target_pairs={{4,0},{8,4},{12,8},{5,1},{9,5},{13,9},{6,2},{10,6},{14,10},{7,3},{... | collective-permute-start | bytes 491528 | tf_op jit(solution)/shard_map/ppermute | solution.py:24
  32.5 6.0 %collective-permute-start.10 = (bf16[224,128]{1,0:T(8,128)(2,1)S(1)}, bf16[224,128]{1,0:T(8,128)(2,1)S(1)}, u32[]{:S(2)}, u32[]{:S(2)}) collective-permute-start(bf16[224,128]{1,0:T(8,128)(2,1)S(1)} %fusion.1), channel_id=1, source_target_pairs={{0,2},{1,3},{2,0},{3,1},{4,6},{5,7},{6,4},{7,5},{8,10},{9,11},{10,... | collective-permute-start | bytes 172040 | tf_op jit(solution)/shard_map/ppermute | solution.py:38
  35.6 8.1 %collective-permute-start.4 = (bf16[10,64,128]{2,1,0:T(8,128)(2,1)S(1)}, bf16[10,64,128]{2,1,0:T(8,128)(2,1)S(1)}, u32[]{:S(2)}, u32[]{:S(2)}) collective-permute-start(bf16[10,64,128]{2,1,0:T(8,128)(2,1)S(1)} %pad_maximum_fusion), channel_id=1, source_target_pairs={{0,4},{4,8},{8,12},{1,5},{5,9},{9,13},{2,6},{6,10},{10,14},{3,7},{... | collective-permute-start | bytes 491528 | tf_op jit(solution)/shard_map/ppermute | solution.py:24
  38.5 7.3 %collective-permute-start.11 = (f32[224,128]{1,0:T(8,128)S(1)}, f32[224,128]{1,0:T(8,128)S(1)}, u32[]{:S(2)}, u32[]{:S(2)}) collective-permute-start(f32[224,128]{1,0:T(8,128)S(1)} %convert_add_fusion), channel_id=1, source_target_pairs={{0,16},{16,0},{1,17},{17,1},{2,18},{18,2},{3,19},{19,3},{4,20},{20... | collective-permute-start | bytes 344072 | tf_op jit(solution)/shard_map/ppermute | solution.py:38
where the time goes:
time: 47 us; the launch traced here: 46.7 us
  waiting for transfers between devices  18.5 us (39%)
  starting transfers between devices  16.4 us (35%)
  Pallas kernels  6.18 us (13%)
  local copies, waits for them, and re-layouts  4.3 us (9%)
  between operations  0.93 us (2%)
    ppermute x6, waiting for transfers between devices, swap(): lax.ppermute(array, axis, [(i, i ^ bit) for i in range(lax.axis_size(axis...  9.25 us
    ppermute x2, waiting for transfers between devices, exchange(): lax.ppermute(high_edge, axis, up)  7.45 us
    pallas_call x3, Pallas kernels, call(): pl.pallas_call(kernel, out_shape=outs, scratch_shapes=scratch, compiler_p...  6.18 us
    ppermute x6, starting transfers between devices, swap(): lax.ppermute(array, axis, [(i, i ^ bit) for i in range(lax.axis_size(axis...  5.57 us
    ppermute x2, starting transfers between devices, exchange(): lax.ppermute(low_edge, axis, down)  5.39 us
    ppermute x2, starting transfers between devices, exchange(): lax.ppermute(high_edge, axis, up)  5.29 us
    unnamed x9, local copies, waits for them, and re-layouts  3.28 us
    ppermute x2, waiting for transfers between devices, exchange(): lax.ppermute(jnp.where(first, high_edge, low_edge), axis, [(0, 1), (1, 0)])  1.84 us
  transfers between devices with their start and end apart: 12, of which 8 were waited for; matrix products, arithmetic and copies ran while one was open for 5% of the time, Pallas kernels for 2%

commit v1 on v0

v1 whole, which is shorter than its diff:
```python
import jax
import jax.numpy as jnp
from jax import lax
from jax.experimental import pallas as pl
from jax.experimental.pallas import tpu as pltpu
from jax.sharding import PartitionSpec as P

F32 = jnp.float32
BF16 = jnp.bfloat16
AXES = ("depth", "height", "dp")


def exchange(low_edge, high_edge, axis):
    count = lax.axis_size(axis)
    none = jnp.zeros_like(low_edge)
    if count == 1:
        return none, none
    at = lax.axis_index(axis)
    if count % 2:
        up = [(i, i + 1) for i in range(count - 1)]
        down = [(i + 1, i) for i in range(count - 1)]
        return lax.ppermute(high_edge, axis, up), lax.ppermute(low_edge, axis, down)
    even = at % 2 == 0
    inner = [(i, i ^ 1) for i in range(count)]
    got = lax.ppermute(jnp.where(even, high_edge, low_edge), axis, inner)
    if count == 2:
        return jnp.where(even, none, got), jnp.where(even, got, none)
    outer = [(i, (i - 1 if i % 2 == 0 else i + 1) % count) for i in range(count)]
    other = lax.ppermute(jnp.where(even, low_edge, high_edge), axis, outer)
    below = jnp.where(at == 0, none, jnp.where(even, other, got))
    above = jnp.where(at == count - 1, none, jnp.where(even, got, other))
    return below, above


def height_halo(first_row, last_row, below, above):
    def column(rows, at):
        return jnp.concatenate([below[at][None], rows, above[at][None]], axis=0)

    return exchange(column(first_row, 0), column(last_row, -1), "height")


def swap(array, axis, mask):
    return lax.ppermute(array, axis, [(i, i ^ mask) for i in range(lax.axis_size(axis))])


def fill_patches(row_of, depth, rows, patches):
    chans, width = row_of(1, 1).shape
    for d in range(depth + 2):
        for at, h in enumerate(rows):
            for b in range(3):
                patches[pl.ds((d * 3 + b) * chans, chans), pl.ds(at * width, width)] = row_of(d, h + b)


def shifted(value, step):
    if step == 0:
        return value
    width = value.shape[1]
    lane = lax.broadcasted_iota(jnp.int32, value.shape, 1)
    edge = width - 1 if step == 1 else 0
    return jnp.where(lane == edge, 0.0, pltpu.roll(value, (-step) % width, 1))


def forward_rows(row_of, rows, w1, bias, cot, delta, before, payload, patches, grad):
    depth, co = cot.shape[0], cot.shape[2]
    width = cot.shape[3]
    ci = row_of(1, 1).shape[0]
    fill_patches(row_of, depth, rows, patches)
    shift_bias = jnp.broadcast_to(bias[...], (co, width))
    bias_acc = jnp.zeros((co, width), F32)
    for d in range(depth):
        window = pl.ds(d * 3 * ci, 9 * ci)
        taps = jnp.dot(w1[...], patches[window, :], preferred_element_type=F32)
        blocks = [[], [], []]
        for at, h in enumerate(rows):
            lanes = slice(at * width, (at + 1) * width)
            linear = taps[co : 2 * co, lanes] + shift_bias
            linear = linear + shifted(taps[:co, lanes], -1) + shifted(taps[2 * co :, lanes], 1)
            sigma = 1.0 / (1.0 + jnp.exp(-linear))
            slope = cot[d, h].astype(F32) * sigma * (1.0 + linear * (1.0 - sigma))
            rounded = slope.astype(BF16)
            delta[at, d] = rounded
            wide = rounded.astype(F32)
            bias_acc = bias_acc + wide
            blocks[0].append(shifted(wide, 1).astype(BF16))
            blocks[1].append(rounded)
            blocks[2].append(shifted(wide, -1).astype(BF16))
        slopes = jnp.concatenate([jnp.concatenate(part, axis=1) for part in blocks], axis=0)
        term = lax.dot_general(
            patches[window, :], slopes, (((1,), (1,)), ((), ())), preferred_element_type=F32
        )
        if d == 0:
            grad[...] = term
        else:
            grad[...] += term
    taps_rows = 9 * ci
    tail = taps_rows + taps_rows // 2
    total = jnp.sum(bias_acc.T, axis=0, keepdims=True)
    left_over = payload.shape[0] - tail
    row_at = lax.broadcasted_iota(jnp.int32, (left_over, co), 0)
    bias_rows = jnp.where(row_at == 0, jnp.broadcast_to(total, (left_over, co)), 0.0)
    zeros = jnp.zeros((left_over, payload.shape[1] - co), F32)
    for at, value in (
        (pl.ds(0, taps_rows), grad[:, : 2 * co]),
        (
            pl.ds(taps_rows, taps_rows // 2),
            jnp.concatenate(
                [grad[: taps_rows // 2, 2 * co :], grad[taps_rows // 2 :, 2 * co :]], axis=1
            ),
        ),
        (pl.ds(tail, left_over), jnp.concatenate([bias_rows, zeros], axis=1)),
    ):
        payload[at, :] = value if before is None else before[at, :] + value


def inner_kernel(x, below, above, w1, bias, cot, delta, payload, patches, grad):
    depth, height = x.shape[:2]

    def row_of(d, h):
        return below[h - 1] if d == 0 else above[h - 1] if d == depth + 1 else x[d - 1, h - 1]

    rows = range(1, height - 1)
    forward_rows(row_of, rows, w1, bias, cot, delta, None, payload, patches, grad)


def outer_kernel(x, below, above, left, right, w1, bias, cot, before, delta, payload, patches, grad):
    depth, height = x.shape[:2]

    def row_of(d, h):
        if h == 0:
            return left[d]
        if h == height + 1:
            return right[d]
        return below[h - 1] if d == 0 else above[h - 1] if d == depth + 1 else x[d - 1, h - 1]

    rows = (0, height - 1)
    forward_rows(row_of, rows, w1, bias, cot, delta, before, payload, patches, grad)


def input_kernel(inner, outer, below, above, left, right, w2, out, patches):
    co, width = inner.shape[2:]
    depth, height, ci = out.shape[:3]

    def row_of(d, h):
        if h == 0:
            return left[d]
        if h == height + 1:
            return right[d]
        if d == 0:
            return below[h - 1]
        if d == depth + 1:
            return above[h - 1]
        return outer[0, d - 1] if h == 1 else outer[1, d - 1] if h == height else inner[h - 2, d - 1]

    fill_patches(row_of, depth, range(height), patches)
    for d in range(depth):
        taps = jnp.dot(w2[...], patches[pl.ds(d * 3 * co, 9 * co), :], preferred_element_type=F32)
        for h in range(height):
            lanes = slice(h * width, (h + 1) * width)
            total = taps[ci : 2 * ci, lanes]
            total = total + shifted(taps[:ci, lanes], 1) + shifted(taps[2 * ci :, lanes], -1)
            out[d, h] = total.astype(BF16)


def unpack_kernel(scale, low, high, weight_out, bias_out, full):
    half = low.shape[0]
    co = bias_out.shape[1]
    full[:half, :] = low[...] * scale
    full[half:, :] = high[...] * scale
    rows = weight_out.shape[0] // 3
    ci = rows // 9
    step = ci // 2
    for j in range(9):
        for part in range(2):
            source = j * ci + part * step
            to = 3 * j * ci + part * step
            weight_out[pl.ds(to, step), :] = full[pl.ds(source, step), :co]
            weight_out[pl.ds(to + ci, step), :] = full[pl.ds(source, step), co:]
            at = rows + source % (rows // 2)
            lanes = slice(0, co) if source < rows // 2 else slice(co, 2 * co)
            weight_out[pl.ds(to + 2 * ci, step), :] = full[pl.ds(at, step), lanes]
    bias_out[...] = full[rows + rows // 2 : rows + rows // 2 + 1, :co]


def call(kernel, outs, scratch, flops, *args):
    size = sum(a.size * a.dtype.itemsize for a in args) + sum(o.size * o.dtype.itemsize for o in outs)
    return pl.pallas_call(
        kernel,
        out_shape=outs,
        scratch_shapes=scratch,
        compiler_params=pltpu.CompilerParams(vmem_limit_bytes=40 << 20),
        cost_estimate=pl.CostEstimate(flops=flops, bytes_accessed=size, transcendentals=0),
    )(*args)


def gathered_sum(part, axis, masks):
    own = lax.reduce_precision(part, 8, 7)
    sent = own.astype(BF16)
    terms = [own] + [swap(sent, axis, mask).astype(F32) for mask in masks]
    while len(terms) > 1:
        terms = [terms[i] + terms[i + 1] for i in range(0, len(terms), 2)]
    return terms[0]


def summed(total, meanwhile, work):
    half = total.shape[0] // 2
    low, high = total[:half], total[half:]
    first = lax.axis_index("depth") % 2 == 0
    got = swap(jnp.where(first, high, low), "depth", 1)
    part = jnp.where(first, low, high) + got
    for axis in AXES:
        count = lax.axis_size(axis)
        assert count & (count - 1) == 0
        if axis == AXES[-1]:
            part, meanwhile = lax.optimization_barrier((part, meanwhile))
        bit = 2 if axis == "depth" else 1
        while bit < count:
            masks = [bit, 2 * bit, 3 * bit] if 2 * bit < count else [bit]
            part = gathered_sum(part, axis, masks)
            bit *= len(masks) + 1
    part, done = lax.optimization_barrier((part, work(meanwhile)))
    other = swap(part, "depth", 1)
    return jnp.where(first, part, other), jnp.where(first, other, part), done


def local(inputs, weight, bias, cotangent):
    cubes, ci, depth, height, width = inputs.shape
    co = cotangent.shape[1]
    taps = weight.transpose(2, 3, 4, 1, 0)
    w1 = taps.transpose(2, 4, 0, 1, 3).reshape(3 * co, 9 * ci)
    w2 = jnp.flip(taps, (0, 1)).transpose(2, 3, 0, 1, 4).reshape(3 * ci, 9 * co)
    w1, w2 = lax.optimization_barrier((w1, w2))
    column = bias[:, None]
    payload_rows = 9 * ci + 9 * ci // 2 + 16
    payload_shape = jax.ShapeDtypeStruct((payload_rows, 2 * co), F32)
    flops = 2 * depth * width * 27 * ci * co
    total = None
    fields = []
    for cube in range(cubes):
        edges = exchange(inputs[cube][:, 0], inputs[cube][:, -1], "depth")
        below, above = (edge.transpose(1, 0, 2) for edge in edges)
        x = inputs[cube].transpose(1, 2, 0, 3)
        cot = cotangent[cube].transpose(1, 2, 0, 3)

        def forward(kernel, rows, *args):
            return call(
                kernel,
                (jax.ShapeDtypeStruct((rows, depth, co, width), BF16), payload_shape),
                [
                    pltpu.VMEM(((depth + 2) * 3 * ci, rows * width), BF16),
                    pltpu.VMEM((9 * ci, 3 * co), F32),
                ],
                2 * flops * rows,
                *args,
            )

        inner, part = forward(inner_kernel, height - 2, x, below, above, w1, column, cot)
        sides = height_halo(x[:, 0], x[:, -1], below, above)
        outer, part = forward(outer_kernel, 2, x, below, above, *sides, w1, column, cot, part)
        total = part if total is None else total + part

        def layer(at):
            return jnp.concatenate([outer[:1, at], inner[:, at], outer[1:, at]], axis=0)

        below, above = exchange(layer(0), layer(-1), "depth")
        sides = height_halo(outer[0], outer[1], below, above)
        fields.append((inner, outer, below, above, *sides))

    def input_gradients(fields):
        grads = []
        for field in fields:
            (grad,) = call(
                input_kernel,
                (jax.ShapeDtypeStruct((depth, height, ci, width), BF16),),
                [pltpu.VMEM(((depth + 2) * 3 * co, height * width), BF16)],
                flops * height,
                *field,
                w2,
            )
            grads.append(grad.transpose(2, 0, 1, 3))
        return jnp.stack(grads)

    low, high, grads = summed(total, fields, input_gradients)
    voxels = cubes * depth * height * width
    for axis in AXES:
        voxels *= lax.axis_size(axis)
    scale = float(voxels) ** -0.5
    grad_taps, grad_bias = call(
        lambda *refs: unpack_kernel(scale, *refs),
        (jax.ShapeDtypeStruct((27 * ci, co), F32), jax.ShapeDtypeStruct((1, co), F32)),
        [pltpu.VMEM((payload_rows, 2 * co), F32)],
        payload_rows * 2 * co,
        low,
        high,
    )
    grad_weight = grad_taps.reshape(3, 3, 3, ci, co).transpose(4, 3, 0, 1, 2)
    return grads, grad_weight, grad_bias.reshape(co)


def solution(mesh):
    voxels = P("dp", None, "depth", "height", None)
    return jax.shard_map(
        local,
        mesh=mesh,
        in_specs=(voxels, P(), P(), voxels),
        out_specs=(voxels, P(), P()),
        check_vma=False,
    )
```

time: 47 us -> 45.2 us (0.962)
  the two profiles are of different devices: /device:TPU:4 before, /device:TPU:0 now
where the time goes in v1:
time: 45.2 us; the launch traced here: 45 us
  starting transfers between devices  16.3 us (36%)
  waiting for transfers between devices  12.2 us (27%)
  Pallas kernels  10.5 us (23%)
  local copies, waits for them, and re-layouts  4.69 us (10%)
  between operations  0.91 us (2%)
    pallas_call x4, Pallas kernels, call(): pl.pallas_call(kernel, out_shape=outs, scratch_shapes=scratch, compiler_p...  10.5 us
    ppermute x8, starting transfers between devices, swap(): lax.ppermute(array, axis, [(i, i ^ mask) for i in range(lax.axis_size(axi...  8.65 us
    ppermute x8, waiting for transfers between devices, swap(): lax.ppermute(array, axis, [(i, i ^ mask) for i in range(lax.axis_size(axi...  5.5 us
    ppermute x4, starting transfers between devices, exchange(): got = lax.ppermute(jnp.where(even, high_edge, low_edge), axis, inner)  5.15 us
    ppermute x4, waiting for transfers between devices, exchange(): got = lax.ppermute(jnp.where(even, high_edge, low_edge), axis, inner)  4.14 us
    unnamed x9, local copies, waits for them, and re-layouts  3.65 us
    ppermute x2, waiting for transfers between devices, exchange(): other = lax.ppermute(jnp.where(even, low_edge, high_edge), axis, outer)  2.57 us
    ppermute x2, starting transfers between devices, exchange(): other = lax.ppermute(jnp.where(even, low_edge, high_edge), axis, outer)  2.53 us
  transfers between devices with their start and end apart: 14, of which 9 were waited for; matrix products, arithmetic and copies ran while one was open for 5% of the time, Pallas kernels for 12%

profile of v1, /device:TPU:0, one launch (start us, length us, event | category | flops | bytes accessed | tf_op | source)
XLA Modules:
  0.0 45.0 jit_solution(6043824256541204714)
XLA Ops:
  0.6 1.1 %copy.33 = bf16[1,32,8,4,128]{4,1,3,2,0:T(8,128)(2,1)S(1)} copy(bf16[1,32,8,4,128]{4,3,2,1,0:T(4,128)(2,1)} %param.4) | data formatting | bytes 524288 | tf_op args[0]
  1.7 0.5 %collective-permute-start = (bf16[32,4,128]{2,0,1:T(8,128)(2,1)S(1)}, bf16[32,4,128]{2,0,1:T(8,128)(2,1)S(1)}, u32[]{:S(2)}, u32[]{:S(2)}) collective-permute-start(bf16[32,4,128]{2,0,1:T(8,128)(2,1)S(1)} %fusion), channel_id=1, source_target_pairs={{0,16},{16,0},{1,17},{17,1},{2,18},{18,2},{3,19},{19,3},{4,20},{20... | collective-permute-start | bytes 98312 | tf_op jit(solution)/shard_map/ppermute | solution.py:25
  2.7 0.6 %copy-done.2 = f32[64]{0:T(128)S(1)} copy-done((f32[64]{0:T(128)S(1)}, f32[64]{0:T(128)}, u32[]{:S(2)}) %copy-start.2) | copy-done | bytes 280
  5.1 3.0 %collective-permute-start.2 = (bf16[10,32,128]{2,1,0:T(8,128)(2,1)S(1)}, bf16[10,32,128]{2,1,0:T(8,128)(2,1)S(1)}, u32[]{:S(2)}, u32[]{:S(2)}) collective-permute-start(bf16[10,32,128]{2,1,0:T(8,128)(2,1)S(1)} %get-tuple-element.65), channel_id=1, source_target_pairs={{0,4},{4,0},{8,12},{12,8},{1,5},{5,1},{9,13},{13,9},{2,6},{6,2},{1... | collective-permute-start | bytes 245768 | tf_op jit(solution)/shard_map/ppermute | solution.py:25
  8.1 1.5 %collective-permute-start.1 = (bf16[10,32,128]{2,1,0:T(8,128)(2,1)S(1)}, bf16[10,32,128]{2,1,0:T(8,128)(2,1)S(1)}, u32[]{:S(2)}, u32[]{:S(2)}) collective-permute-start(bf16[10,32,128]{2,1,0:T(8,128)(2,1)S(1)} %get-tuple-element.66), channel_id=1, source_target_pairs={{0,12},{4,8},{8,4},{12,0},{1,13},{5,9},{9,5},{13,1},{2,14},{6,10},... | collective-permute-start | bytes 245768 | tf_op jit(solution)/shard_map/ppermute | solution.py:29
  9.6 4.3 %shard_map.67 = (bf16[2,8,64,128]{3,2,1,0:T(8,128)(2,1)S(1)}, f32[448,128]{1,0:T(8,128)S(1)}) custom-call(bf16[8,4,32,128]{3,2,1,0:T(8,128)(2,1)S(1)} %bitcast.53, bf16[4,32,128]{2,1,0:T(8,128)(2,1)S(1)} %get-tuple-element.78.below, bf16[4,32,128]{2,1,0:T(8,128)(2,1)S(1)} %get-tuple-element.77.above, bf16[192,288]{1,0:T(8,128)(2,1)S(1)} %copy.22.w1, ...), custom_call_target="tpu_custom_call" | custom-call | flops 452984832 | bytes 1454336 | tf_op jit(solution)/shard_map/pallas_call | solution.py:186
  14.0 4.2 %shard_map.68 = (bf16[2,8,64,128]{3,2,1,0:T(8,128)(2,1)S(1)}, f32[448,128]{1,0:T(8,128)S(1)}) custom-call(bf16[8,4,32,128]{3,2,1,0:T(8,128)(2,1)S(1)} %bitcast.54, bf16[4,32,128]{2,1,0:T(8,128)(2,1)S(1)} %get-tuple-element.78.below, bf16[4,32,128]{2,1,0:T(8,128)(2,1)S(1)} %get-tuple-element.77.above, bf16[10,32,128]{2,1,0:T(8,128)(2,1)S(1)} %get-tuple-element.64.left, ...), custom_call_target="tpu_custom_call" | custom-call | flops 452984832 | bytes 1847552 | tf_op jit(solution)/shard_map/pallas_call | solution.py:186
  18.4 0.6 %collective-permute-start.3 = (f32[224,128]{1,0:T(8,128)S(1)}, f32[224,128]{1,0:T(8,128)S(1)}, u32[]{:S(2)}, u32[]{:S(2)}) collective-permute-start(f32[224,128]{1,0:T(8,128)S(1)} %slice_select_fusion), channel_id=1, source_target_pairs={{0,16},{16,0},{1,17},{17,1},{2,18},{18,2},{3,19},{19,3},{4,20},{20... | collective-permute-start | bytes 344072 | tf_op jit(solution)/shard_map/ppermute | solution.py:43
  18.9 0.7 %collective-permute-done.7 = bf16[4,64,128]{2,1,0:T(8,128)(2,1)S(1)} collective-permute-done((bf16[4,64,128]{2,1,0:T(8,128)(2,1)S(1)}, bf16[4,64,128]{2,1,0:T(8,128)(2,1)S(1)}, u32[]{:S(2)}, u32[]{:S(2)}) %collective-permute-start.7) | collective-permute-done | bytes 65568 | tf_op jit(solution)/shard_map/ppermute | solution.py:25
  19.9 1.5 %collective-permute-start.6 = (bf16[224,128]{1,0:T(8,128)(2,1)S(1)}, bf16[224,128]{1,0:T(8,128)(2,1)S(1)}, u32[]{:S(2)}, u32[]{:S(2)}) collective-permute-start(bf16[224,128]{1,0:T(8,128)(2,1)S(1)} %get-tuple-element.43), channel_id=1, source_target_pairs={{0,12},{4,8},{8,4},{12,0},{1,13},{5,9},{9,5},{13,1},{2,14},{6,10},... | collective-permute-start | bytes 172040 | tf_op jit(solution)/shard_map/ppermute | solution.py:43
  21.4 1.5 %collective-permute-start.5 = (bf16[224,128]{1,0:T(8,128)(2,1)S(1)}, bf16[224,128]{1,0:T(8,128)(2,1)S(1)}, u32[]{:S(2)}, u32[]{:S(2)}) collective-permute-start(bf16[224,128]{1,0:T(8,128)(2,1)S(1)} %get-tuple-element.43), channel_id=1, source_target_pairs={{0,8},{4,12},{8,0},{12,4},{1,9},{5,13},{9,1},{13,5},{2,10},{6,14},... | collective-permute-start | bytes 172040 | tf_op jit(solution)/shard_map/ppermute | solution.py:43
  22.9 0.5 %collective-permute-start.4 = (bf16[224,128]{1,0:T(8,128)(2,1)S(1)}, bf16[224,128]{1,0:T(8,128)(2,1)S(1)}, u32[]{:S(2)}, u32[]{:S(2)}) collective-permute-start(bf16[224,128]{1,0:T(8,128)(2,1)S(1)} %get-tuple-element.43), channel_id=1, source_target_pairs={{0,4},{4,0},{8,12},{12,8},{1,5},{5,1},{9,13},{13,9},{2,6},{6,2},{1... | collective-permute-start | bytes 172040 | tf_op jit(solution)/shard_map/ppermute | solution.py:43
  23.5 1.6 %collective-permute-start.9 = (bf16[10,64,128]{2,1,0:T(8,128)(2,1)S(1)}, bf16[10,64,128]{2,1,0:T(8,128)(2,1)S(1)}, u32[]{:S(2)}, u32[]{:S(2)}) collective-permute-start(bf16[10,64,128]{2,1,0:T(8,128)(2,1)S(1)} %get-tuple-element.47), channel_id=1, source_target_pairs={{0,4},{4,0},{8,12},{12,8},{1,5},{5,1},{9,13},{13,9},{2,6},{6,2},{1... | collective-permute-start | bytes 491528 | tf_op jit(solution)/shard_map/ppermute | solution.py:25
  25.1 1.0 %collective-permute-start.8 = (bf16[10,64,128]{2,1,0:T(8,128)(2,1)S(1)}, bf16[10,64,128]{2,1,0:T(8,128)(2,1)S(1)}, u32[]{:S(2)}, u32[]{:S(2)}) collective-permute-start(bf16[10,64,128]{2,1,0:T(8,128)(2,1)S(1)} %get-tuple-element.48), channel_id=1, source_target_pairs={{0,12},{4,8},{8,4},{12,0},{1,13},{5,9},{9,5},{13,1},{2,14},{6,10},... | collective-permute-start | bytes 491528 | tf_op jit(solution)/shard_map/ppermute | solution.py:29
  26.3 1.5 %collective-permute-done.4 = bf16[224,128]{1,0:T(8,128)(2,1)S(1)} collective-permute-done((bf16[224,128]{1,0:T(8,128)(2,1)S(1)}, bf16[224,128]{1,0:T(8,128)(2,1)S(1)}, u32[]{:S(2)}, u32[]{:S(2)}) %collective-permute-start.4) | collective-permute-done | bytes 57376 | tf_op jit(solution)/shard_map/ppermute | solution.py:43
  27.8 3.5 %collective-permute-done.9 = bf16[10,64,128]{2,1,0:T(8,128)(2,1)S(1)} collective-permute-done((bf16[10,64,128]{2,1,0:T(8,128)(2,1)S(1)}, bf16[10,64,128]{2,1,0:T(8,128)(2,1)S(1)}, u32[]{:S(2)}, u32[]{:S(2)}) %collective-permute-start.9) | collective-permute-done | bytes 163872 | tf_op jit(solution)/shard_map/ppermute | solution.py:25
  31.3 2.6 %collective-permute-done.8 = bf16[10,64,128]{2,1,0:T(8,128)(2,1)S(1)} collective-permute-done((bf16[10,64,128]{2,1,0:T(8,128)(2,1)S(1)}, bf16[10,64,128]{2,1,0:T(8,128)(2,1)S(1)}, u32[]{:S(2)}, u32[]{:S(2)}) %collective-permute-start.8) | collective-permute-done | bytes 163872 | tf_op jit(solution)/shard_map/ppermute | solution.py:29
  33.9 3.7 %collective-permute-start.12 = (bf16[224,128]{1,0:T(8,128)(2,1)S(1)}, bf16[224,128]{1,0:T(8,128)(2,1)S(1)}, u32[]{:S(2)}, u32[]{:S(2)}) collective-permute-start(bf16[224,128]{1,0:T(8,128)(2,1)S(1)} %reduce-precision_convert_fusion), channel_id=1, source_target_pairs={{0,3},{1,2},{2,1},{3,0},{4,7},{5,6},{6,5},{7,4},{8,11},{9,10},{10,... | collective-permute-start | bytes 172040 | tf_op jit(solution)/shard_map/ppermute | solution.py:43
  37.6 0.8 %collective-permute-start.10 = (bf16[224,128]{1,0:T(8,128)(2,1)S(1)}, bf16[224,128]{1,0:T(8,128)(2,1)S(1)}, u32[]{:S(2)}, u32[]{:S(2)}) collective-permute-start(bf16[224,128]{1,0:T(8,128)(2,1)S(1)} %reduce-precision_convert_fusion), channel_id=1, source_target_pairs={{0,1},{1,0},{2,3},{3,2},{4,5},{5,4},{6,7},{7,6},{8,9},{9,8},{10,11... | collective-permute-start | bytes 172040 | tf_op jit(solution)/shard_map/ppermute | solution.py:43
  38.3 1.2 %shard_map.69 = bf16[8,4,32,128]{3,2,1,0:T(8,128)(2,1)S(1)} custom-call(bf16[2,8,64,128]{3,2,1,0:T(8,128)(2,1)S(1)} %get-tuple-element.26.inner, bf16[2,8,64,128]{3,2,1,0:T(8,128)(2,1)S(1)} %get-tuple-element.27.outer, bf16[4,64,128]{2,1,0:T(8,128)(2,1)S(1)} %get-tuple-element.28.below, bf16[4,64,128]{2,1,0:T(8,128)(2,1)S(1)} %get-tuple-element.29.above, ...), custom_call_target="tpu_custom_call" | custom-call | flops 452984832 | bytes 1355776 | tf_op jit(solution)/shard_map/pallas_call | solution.py:186
  39.5 0.8 %collective-permute-done.12 = bf16[224,128]{1,0:T(8,128)(2,1)S(1)} collective-permute-done((bf16[224,128]{1,0:T(8,128)(2,1)S(1)}, bf16[224,128]{1,0:T(8,128)(2,1)S(1)}, u32[]{:S(2)}, u32[]{:S(2)}) %collective-permute-start.12) | collective-permute-done | bytes 57376 | tf_op jit(solution)/shard_map/ppermute | solution.py:43
  40.3 2.3 %collective-permute-done.11 = bf16[224,128]{1,0:T(8,128)(2,1)S(1)} collective-permute-done((bf16[224,128]{1,0:T(8,128)(2,1)S(1)}, bf16[224,128]{1,0:T(8,128)(2,1)S(1)}, u32[]{:S(2)}, u32[]{:S(2)}) %collective-permute-start.11) | collective-permute-done | bytes 57376 | tf_op jit(solution)/shard_map/ppermute | solution.py:43
  42.8 0.8 %copy.26 = bf16[1,32,8,4,128]{4,3,2,1,0:T(4,128)(2,1)} copy(bf16[1,32,8,4,128]{4,1,3,2,0:T(8,128)(2,1)S(1)} %bitcast.57) | data formatting | bytes 524288
  44.1 0.9 %shard_map.70 = (f32[864,64]{1,0:T(8,128)}, f32[1,64]{1,0:T(1,128)}) custom-call(f32[224,128]{1,0:T(8,128)S(1)} %get-tuple-element.62.refs_0_, f32[224,128]{1,0:T(8,128)S(1)} %get-tuple-element.61.refs_1_), custom_call_target="tpu_custom_call" | custom-call | flops 57344 | bytes 450816 | tf_op jit(solution)/shard_map/pallas_call | solution.py:186
  (45 shorter events, 3.5 us)
Async XLA Ops:
  1.7 0.9 %copy-start = (bf16[64,32,3,3,3]{0,1,4,3,2:T(8,128)(2,1)S(1)}, bf16[64,32,3,3,3]{0,1,4,3,2:T(8,128)(2,1)}, u32[]{:S(2)}) copy-start(bf16[64,32,3,3,3]{0,1,4,3,2:T(8,128)(2,1)} %param.5) | copy-start | bytes 331780
  1.7 3.3 %collective-permute-start = (bf16[32,4,128]{2,0,1:T(8,128)(2,1)S(1)}, bf16[32,4,128]{2,0,1:T(8,128)(2,1)S(1)}, u32[]{:S(2)}, u32[]{:S(2)}) collective-permute-start(bf16[32,4,128]{2,0,1:T(8,128)(2,1)S(1)} %fusion), channel_id=1, source_target_pairs={{0,16},{16,0},{1,17},{17,1},{2,18},{18,2},{3,19},{19,3},{4,20},{20... | collective-permute-start | bytes 98312 | tf_op jit(solution)/shard_map/ppermute | solution.py:25
  2.7 0.7 %copy-start.2 = (f32[64]{0:T(128)S(1)}, f32[64]{0:T(128)}, u32[]{:S(2)}) copy-start(f32[64]{0:T(128)} %param.6) | copy-start | bytes 772
  3.8 1.0 %copy-start.1 = (bf16[1,64,8,4,128]{4,3,2,1,0:T(4,128)(2,1)S(1)}, bf16[1,64,8,4,128]{4,3,2,1,0:T(4,128)(2,1)}, u32[]{:S(2)}) copy-start(bf16[1,64,8,4,128]{4,3,2,1,0:T(4,128)(2,1)} %param.7) | copy-start | bytes 1572868
  5.1 8.8 %collective-permute-start.2 = (bf16[10,32,128]{2,1,0:T(8,128)(2,1)S(1)}, bf16[10,32,128]{2,1,0:T(8,128)(2,1)S(1)}, u32[]{:S(2)}, u32[]{:S(2)}) collective-permute-start(bf16[10,32,128]{2,1,0:T(8,128)(2,1)S(1)} %get-tuple-element.65), channel_id=1, source_target_pairs={{0,4},{4,0},{8,12},{12,8},{1,5},{5,1},{9,13},{13,9},{2,6},{6,2},{1... | collective-permute-start | bytes 245768 | tf_op jit(solution)/shard_map/ppermute | solution.py:25
  8.1 5.8 %collective-permute-start.1 = (bf16[10,32,128]{2,1,0:T(8,128)(2,1)S(1)}, bf16[10,32,128]{2,1,0:T(8,128)(2,1)S(1)}, u32[]{:S(2)}, u32[]{:S(2)}) collective-permute-start(bf16[10,32,128]{2,1,0:T(8,128)(2,1)S(1)} %get-tuple-element.66), channel_id=1, source_target_pairs={{0,12},{4,8},{8,4},{12,0},{1,13},{5,9},{9,5},{13,1},{2,14},{6,10},... | collective-permute-start | bytes 245768 | tf_op jit(solution)/shard_map/ppermute | solution.py:29
  18.3 1.3 %collective-permute-start.7 = (bf16[4,64,128]{2,1,0:T(8,128)(2,1)S(1)}, bf16[4,64,128]{2,1,0:T(8,128)(2,1)S(1)}, u32[]{:S(2)}, u32[]{:S(2)}) collective-permute-start(bf16[4,64,128]{2,1,0:T(8,128)(2,1)S(1)} %maximum_select_fusion), channel_id=1, source_target_pairs={{0,16},{16,0},{1,17},{17,1},{2,18},{18,2},{3,19},{19,3},{4,20},{20... | collective-permute-start | bytes 196616 | tf_op jit(solution)/shard_map/ppermute | solution.py:25
  18.4 1.5 %collective-permute-start.3 = (f32[224,128]{1,0:T(8,128)S(1)}, f32[224,128]{1,0:T(8,128)S(1)}, u32[]{:S(2)}, u32[]{:S(2)}) collective-permute-start(f32[224,128]{1,0:T(8,128)S(1)} %slice_select_fusion), channel_id=1, source_target_pairs={{0,16},{16,0},{1,17},{17,1},{2,18},{18,2},{3,19},{19,3},{4,20},{20... | collective-permute-start | bytes 344072 | tf_op jit(solution)/shard_map/ppermute | solution.py:43
  19.9 6.2 %collective-permute-start.6 = (bf16[224,128]{1,0:T(8,128)(2,1)S(1)}, bf16[224,128]{1,0:T(8,128)(2,1)S(1)}, u32[]{:S(2)}, u32[]{:S(2)}) collective-permute-start(bf16[224,128]{1,0:T(8,128)(2,1)S(1)} %get-tuple-element.43), channel_id=1, source_target_pairs={{0,12},{4,8},{8,4},{12,0},{1,13},{5,9},{9,5},{13,1},{2,14},{6,10},... | collective-permute-start | bytes 172040 | tf_op jit(solution)/shard_map/ppermute | solution.py:43
  21.4 4.9 %collective-permute-start.5 = (bf16[224,128]{1,0:T(8,128)(2,1)S(1)}, bf16[224,128]{1,0:T(8,128)(2,1)S(1)}, u32[]{:S(2)}, u32[]{:S(2)}) collective-permute-start(bf16[224,128]{1,0:T(8,128)(2,1)S(1)} %get-tuple-element.43), channel_id=1, source_target_pairs={{0,8},{4,12},{8,0},{12,4},{1,9},{5,13},{9,1},{13,5},{2,10},{6,14},... | collective-permute-start | bytes 172040 | tf_op jit(solution)/shard_map/ppermute | solution.py:43
  22.9 4.8 %collective-permute-start.4 = (bf16[224,128]{1,0:T(8,128)(2,1)S(1)}, bf16[224,128]{1,0:T(8,128)(2,1)S(1)}, u32[]{:S(2)}, u32[]{:S(2)}) collective-permute-start(bf16[224,128]{1,0:T(8,128)(2,1)S(1)} %get-tuple-element.43), channel_id=1, source_target_pairs={{0,4},{4,0},{8,12},{12,8},{1,5},{5,1},{9,13},{13,9},{2,6},{6,2},{1... | collective-permute-start | bytes 172040 | tf_op jit(solution)/shard_map/ppermute | solution.py:43
  23.5 7.7 %collective-permute-start.9 = (bf16[10,64,128]{2,1,0:T(8,128)(2,1)S(1)}, bf16[10,64,128]{2,1,0:T(8,128)(2,1)S(1)}, u32[]{:S(2)}, u32[]{:S(2)}) collective-permute-start(bf16[10,64,128]{2,1,0:T(8,128)(2,1)S(1)} %get-tuple-element.47), channel_id=1, source_target_pairs={{0,4},{4,0},{8,12},{12,8},{1,5},{5,1},{9,13},{13,9},{2,6},{6,2},{1... | collective-permute-start | bytes 491528 | tf_op jit(solution)/shard_map/ppermute | solution.py:25
  25.1 8.7 %collective-permute-start.8 = (bf16[10,64,128]{2,1,0:T(8,128)(2,1)S(1)}, bf16[10,64,128]{2,1,0:T(8,128)(2,1)S(1)}, u32[]{:S(2)}, u32[]{:S(2)}) collective-permute-start(bf16[10,64,128]{2,1,0:T(8,128)(2,1)S(1)} %get-tuple-element.48), channel_id=1, source_target_pairs={{0,12},{4,8},{8,4},{12,0},{1,13},{5,9},{9,5},{13,1},{2,14},{6,10},... | collective-permute-start | bytes 491528 | tf_op jit(solution)/shard_map/ppermute | solution.py:29
  33.9 6.5 %collective-permute-start.12 = (bf16[224,128]{1,0:T(8,128)(2,1)S(1)}, bf16[224,128]{1,0:T(8,128)(2,1)S(1)}, u32[]{:S(2)}, u32[]{:S(2)}) collective-permute-start(bf16[224,128]{1,0:T(8,128)(2,1)S(1)} %reduce-precision_convert_fusion), channel_id=1, source_target_pairs={{0,3},{1,2},{2,1},{3,0},{4,7},{5,6},{6,5},{7,4},{8,11},{9,10},{10,... | collective-permute-start | bytes 172040 | tf_op jit(solution)/shard_map/ppermute | solution.py:43
  37.5 5.1 %collective-permute-start.11 = (bf16[224,128]{1,0:T(8,128)(2,1)S(1)}, bf16[224,128]{1,0:T(8,128)(2,1)S(1)}, u32[]{:S(2)}, u32[]{:S(2)}) collective-permute-start(bf16[224,128]{1,0:T(8,128)(2,1)S(1)} %reduce-precision_convert_fusion), channel_id=1, source_target_pairs={{0,2},{1,3},{2,0},{3,1},{4,6},{5,7},{6,4},{7,5},{8,10},{9,11},{10,... | collective-permute-start | bytes 172040 | tf_op jit(solution)/shard_map/ppermute | solution.py:43
  37.6 5.1 %collective-permute-start.10 = (bf16[224,128]{1,0:T(8,128)(2,1)S(1)}, bf16[224,128]{1,0:T(8,128)(2,1)S(1)}, u32[]{:S(2)}, u32[]{:S(2)}) collective-permute-start(bf16[224,128]{1,0:T(8,128)(2,1)S(1)} %reduce-precision_convert_fusion), channel_id=1, source_target_pairs={{0,1},{1,0},{2,3},{3,2},{4,5},{5,4},{6,7},{7,6},{8,9},{9,8},{10,11... | collective-permute-start | bytes 172040 | tf_op jit(solution)/shard_map/ppermute | solution.py:43
  42.7 1.4 %collective-permute-start.13 = (f32[224,128]{1,0:T(8,128)S(1)}, f32[224,128]{1,0:T(8,128)S(1)}, u32[]{:S(2)}, u32[]{:S(2)}) collective-permute-start(f32[224,128]{1,0:T(8,128)S(1)} %add_add_fusion), channel_id=1, source_target_pairs={{0,16},{16,0},{1,17},{17,1},{2,18},{18,2},{3,19},{19,3},{4,20},{20... | collective-permute-start | bytes 344072 | tf_op jit(solution)/shard_map/ppermute | solution.py:43

commit v2 on v1

--- a/solution.py
+++ b/solution.py
@@ -210,8 +210,6 @@
     for axis in AXES:
         count = lax.axis_size(axis)
         assert count & (count - 1) == 0
-        if axis == AXES[-1]:
-            part, meanwhile = lax.optimization_barrier((part, meanwhile))
         bit = 2 if axis == "depth" else 1
         while bit < count:
             masks = [bit, 2 * bit, 3 * bit] if 2 * bit < count else [bit]

time: 45.2 us -> 39.1 us (0.87)
  waiting for transfers between devices: 12.2 us -> 6.11 us
    ppermute x4, waiting for transfers between devices: 4.14 us -> 0.67 us  [exchange(): got = lax.ppermute(jnp.where(even, high_edge, low_edge), axis, inner)]
    ppermute x8, waiting for transfers between devices: 5.5 us -> 3.85 us  [swap(): lax.ppermute(array, axis, [(i, i ^ mask) for i in range(lax.axis_size(axi...]
    ppermute x2, waiting for transfers between devices: 2.57 us -> 1.59 us  [exchange(): other = lax.ppermute(jnp.where(even, low_edge, high_edge), axis, outer)]
  transfers between devices with their start and end apart: 14 -> 14, of which waited for: 9 -> 7; matrix products, arithmetic and copies ran while one was open for 5% -> 6% of each run, Pallas kernels for 12% -> 14%
where the time goes in v2:
time: 39.1 us; the launch traced here: 38.9 us
  starting transfers between devices  16.3 us (42%)
  Pallas kernels  10.6 us (27%)
  waiting for transfers between devices  6.11 us (16%)
  local copies, waits for them, and re-layouts  4.69 us (12%)
  between operations  0.9 us (2%)
    pallas_call x4, Pallas kernels, call(): pl.pallas_call(kernel, out_shape=outs, scratch_shapes=scratch, compiler_p...  10.6 us
    ppermute x8, starting transfers between devices, swap(): lax.ppermute(array, axis, [(i, i ^ mask) for i in range(lax.axis_size(axi...  8.65 us
    ppermute x4, starting transfers between devices, exchange(): got = lax.ppermute(jnp.where(even, high_edge, low_edge), axis, inner)  5.15 us
    ppermute x8, waiting for transfers between devices, swap(): lax.ppermute(array, axis, [(i, i ^ mask) for i in range(lax.axis_size(axi...  3.85 us
    unnamed x9, local copies, waits for them, and re-layouts  3.65 us
    ppermute x2, starting transfers between devices, exchange(): other = lax.ppermute(jnp.where(even, low_edge, high_edge), axis, outer)  2.53 us
    ppermute x2, waiting for transfers between devices, exchange(): other = lax.ppermute(jnp.where(even, low_edge, high_edge), axis, outer)  1.59 us
  transfers between devices with their start and end apart: 14, of which 7 were waited for; matrix products, arithmetic and copies ran while one was open for 6% of the time, Pallas kernels for 14%

profile of v2, /device:TPU:0, one launch (start us, length us, event | category | flops | bytes accessed | tf_op | source)
XLA Modules:
  0.0 38.9 jit_solution(17292583424492452921)
XLA Ops:
  0.6 1.1 %copy.33 = bf16[1,32,8,4,128]{4,1,3,2,0:T(8,128)(2,1)S(1)} copy(bf16[1,32,8,4,128]{4,3,2,1,0:T(4,128)(2,1)} %param.4) | data formatting | bytes 524288 | tf_op args[0]
  1.7 0.5 %collective-permute-start = (bf16[32,4,128]{2,0,1:T(8,128)(2,1)S(1)}, bf16[32,4,128]{2,0,1:T(8,128)(2,1)S(1)}, u32[]{:S(2)}, u32[]{:S(2)}) collective-permute-start(bf16[32,4,128]{2,0,1:T(8,128)(2,1)S(1)} %fusion), channel_id=1, source_target_pairs={{0,16},{16,0},{1,17},{17,1},{2,18},{18,2},{3,19},{19,3},{4,20},{20... | collective-permute-start | bytes 98312 | tf_op jit(solution)/shard_map/ppermute | solution.py:25
  2.7 0.6 %copy-done.2 = f32[64]{0:T(128)S(1)} copy-done((f32[64]{0:T(128)S(1)}, f32[64]{0:T(128)}, u32[]{:S(2)}) %copy-start.2) | copy-done | bytes 280
  4.3 0.5 %copy-done.1 = bf16[1,64,8,4,128]{4,3,2,1,0:T(4,128)(2,1)S(1)} copy-done((bf16[1,64,8,4,128]{4,3,2,1,0:T(4,128)(2,1)S(1)}, bf16[1,64,8,4,128]{4,3,2,1,0:T(4,128)(2,1)}, u32[]{:S(2)}) %copy-start.1) | copy-done | bytes 524312
  5.1 3.0 %collective-permute-start.2 = (bf16[10,32,128]{2,1,0:T(8,128)(2,1)S(1)}, bf16[10,32,128]{2,1,0:T(8,128)(2,1)S(1)}, u32[]{:S(2)}, u32[]{:S(2)}) collective-permute-start(bf16[10,32,128]{2,1,0:T(8,128)(2,1)S(1)} %get-tuple-element.51), channel_id=1, source_target_pairs={{0,4},{4,0},{8,12},{12,8},{1,5},{5,1},{9,13},{13,9},{2,6},{6,2},{1... | collective-permute-start | bytes 245768 | tf_op jit(solution)/shard_map/ppermute | solution.py:25
  8.1 1.5 %collective-permute-start.1 = (bf16[10,32,128]{2,1,0:T(8,128)(2,1)S(1)}, bf16[10,32,128]{2,1,0:T(8,128)(2,1)S(1)}, u32[]{:S(2)}, u32[]{:S(2)}) collective-permute-start(bf16[10,32,128]{2,1,0:T(8,128)(2,1)S(1)} %get-tuple-element.52), channel_id=1, source_target_pairs={{0,12},{4,8},{8,4},{12,0},{1,13},{5,9},{9,5},{13,1},{2,14},{6,10},... | collective-permute-start | bytes 245768 | tf_op jit(solution)/shard_map/ppermute | solution.py:29
  9.6 4.3 %shard_map.67 = (bf16[2,8,64,128]{3,2,1,0:T(8,128)(2,1)S(1)}, f32[448,128]{1,0:T(8,128)S(1)}) custom-call(bf16[8,4,32,128]{3,2,1,0:T(8,128)(2,1)S(1)} %bitcast.53, bf16[4,32,128]{2,1,0:T(8,128)(2,1)S(1)} %get-tuple-element.64.below, bf16[4,32,128]{2,1,0:T(8,128)(2,1)S(1)} %get-tuple-element.63.above, bf16[192,288]{1,0:T(8,128)(2,1)S(1)} %copy.22.w1, ...), custom_call_target="tpu_custom_call" | custom-call | flops 452984832 | bytes 1454336 | tf_op jit(solution)/shard_map/pallas_call | solution.py:186
  14.0 4.2 %shard_map.68 = (bf16[2,8,64,128]{3,2,1,0:T(8,128)(2,1)S(1)}, f32[448,128]{1,0:T(8,128)S(1)}) custom-call(bf16[8,4,32,128]{3,2,1,0:T(8,128)(2,1)S(1)} %bitcast.54, bf16[4,32,128]{2,1,0:T(8,128)(2,1)S(1)} %get-tuple-element.64.below, bf16[4,32,128]{2,1,0:T(8,128)(2,1)S(1)} %get-tuple-element.63.above, bf16[10,32,128]{2,1,0:T(8,128)(2,1)S(1)} %get-tuple-element.50.left, ...), custom_call_target="tpu_custom_call" | custom-call | flops 452984832 | bytes 1847552 | tf_op jit(solution)/shard_map/pallas_call | solution.py:186
  18.4 0.6 %collective-permute-start.3 = (f32[224,128]{1,0:T(8,128)S(1)}, f32[224,128]{1,0:T(8,128)S(1)}, u32[]{:S(2)}, u32[]{:S(2)}) collective-permute-start(f32[224,128]{1,0:T(8,128)S(1)} %slice_select_fusion), channel_id=1, source_target_pairs={{0,16},{16,0},{1,17},{17,1},{2,18},{18,2},{3,19},{19,3},{4,20},{20... | collective-permute-start | bytes 344072 | tf_op jit(solution)/shard_map/ppermute | solution.py:43
  18.9 0.7 %collective-permute-done.10 = bf16[4,64,128]{2,1,0:T(8,128)(2,1)S(1)} collective-permute-done((bf16[4,64,128]{2,1,0:T(8,128)(2,1)S(1)}, bf16[4,64,128]{2,1,0:T(8,128)(2,1)S(1)}, u32[]{:S(2)}, u32[]{:S(2)}) %collective-permute-start.10) | collective-permute-done | bytes 65568 | tf_op jit(solution)/shard_map/ppermute | solution.py:25
  19.9 1.5 %collective-permute-start.6 = (bf16[224,128]{1,0:T(8,128)(2,1)S(1)}, bf16[224,128]{1,0:T(8,128)(2,1)S(1)}, u32[]{:S(2)}, u32[]{:S(2)}) collective-permute-start(bf16[224,128]{1,0:T(8,128)(2,1)S(1)} %get-tuple-element.29), channel_id=1, source_target_pairs={{0,12},{4,8},{8,4},{12,0},{1,13},{5,9},{9,5},{13,1},{2,14},{6,10},... | collective-permute-start | bytes 172040 | tf_op jit(solution)/shard_map/ppermute | solution.py:43
  21.4 1.5 %collective-permute-start.5 = (bf16[224,128]{1,0:T(8,128)(2,1)S(1)}, bf16[224,128]{1,0:T(8,128)(2,1)S(1)}, u32[]{:S(2)}, u32[]{:S(2)}) collective-permute-start(bf16[224,128]{1,0:T(8,128)(2,1)S(1)} %get-tuple-element.29), channel_id=1, source_target_pairs={{0,8},{4,12},{8,0},{12,4},{1,9},{5,13},{9,1},{13,5},{2,10},{6,14},... | collective-permute-start | bytes 172040 | tf_op jit(solution)/shard_map/ppermute | solution.py:43
  22.9 0.5 %collective-permute-start.4 = (bf16[224,128]{1,0:T(8,128)(2,1)S(1)}, bf16[224,128]{1,0:T(8,128)(2,1)S(1)}, u32[]{:S(2)}, u32[]{:S(2)}) collective-permute-start(bf16[224,128]{1,0:T(8,128)(2,1)S(1)} %get-tuple-element.29), channel_id=1, source_target_pairs={{0,4},{4,0},{8,12},{12,8},{1,5},{5,1},{9,13},{13,9},{2,6},{6,2},{1... | collective-permute-start | bytes 172040 | tf_op jit(solution)/shard_map/ppermute | solution.py:43
  23.5 1.6 %collective-permute-start.12 = (bf16[10,64,128]{2,1,0:T(8,128)(2,1)S(1)}, bf16[10,64,128]{2,1,0:T(8,128)(2,1)S(1)}, u32[]{:S(2)}, u32[]{:S(2)}) collective-permute-start(bf16[10,64,128]{2,1,0:T(8,128)(2,1)S(1)} %get-tuple-element.33), channel_id=1, source_target_pairs={{0,4},{4,0},{8,12},{12,8},{1,5},{5,1},{9,13},{13,9},{2,6},{6,2},{1... | collective-permute-start | bytes 491528 | tf_op jit(solution)/shard_map/ppermute | solution.py:25
  25.1 1.0 %collective-permute-start.11 = (bf16[10,64,128]{2,1,0:T(8,128)(2,1)S(1)}, bf16[10,64,128]{2,1,0:T(8,128)(2,1)S(1)}, u32[]{:S(2)}, u32[]{:S(2)}) collective-permute-start(bf16[10,64,128]{2,1,0:T(8,128)(2,1)S(1)} %get-tuple-element.34), channel_id=1, source_target_pairs={{0,12},{4,8},{8,4},{12,0},{1,13},{5,9},{9,5},{13,1},{2,14},{6,10},... | collective-permute-start | bytes 491528 | tf_op jit(solution)/shard_map/ppermute | solution.py:29
  26.3 1.5 %collective-permute-done.4 = bf16[224,128]{1,0:T(8,128)(2,1)S(1)} collective-permute-done((bf16[224,128]{1,0:T(8,128)(2,1)S(1)}, bf16[224,128]{1,0:T(8,128)(2,1)S(1)}, u32[]{:S(2)}, u32[]{:S(2)}) %collective-permute-start.4) | collective-permute-done | bytes 57376 | tf_op jit(solution)/shard_map/ppermute | solution.py:43
  27.8 3.7 %collective-permute-start.9 = (bf16[224,128]{1,0:T(8,128)(2,1)S(1)}, bf16[224,128]{1,0:T(8,128)(2,1)S(1)}, u32[]{:S(2)}, u32[]{:S(2)}) collective-permute-start(bf16[224,128]{1,0:T(8,128)(2,1)S(1)} %fusion.1), channel_id=1, source_target_pairs={{0,3},{1,2},{2,1},{3,0},{4,7},{5,6},{6,5},{7,4},{8,11},{9,10},{10,... | collective-permute-start | bytes 172040 | tf_op jit(solution)/shard_map/ppermute | solution.py:43
  31.5 0.8 %collective-permute-start.7 = (bf16[224,128]{1,0:T(8,128)(2,1)S(1)}, bf16[224,128]{1,0:T(8,128)(2,1)S(1)}, u32[]{:S(2)}, u32[]{:S(2)}) collective-permute-start(bf16[224,128]{1,0:T(8,128)(2,1)S(1)} %fusion.1), channel_id=1, source_target_pairs={{0,1},{1,0},{2,3},{3,2},{4,5},{5,4},{6,7},{7,6},{8,9},{9,8},{10,11... | collective-permute-start | bytes 172040 | tf_op jit(solution)/shard_map/ppermute | solution.py:43
  32.2 1.6 %collective-permute-done.11 = bf16[10,64,128]{2,1,0:T(8,128)(2,1)S(1)} collective-permute-done((bf16[10,64,128]{2,1,0:T(8,128)(2,1)S(1)}, bf16[10,64,128]{2,1,0:T(8,128)(2,1)S(1)}, u32[]{:S(2)}, u32[]{:S(2)}) %collective-permute-start.11) | collective-permute-done | bytes 163872 | tf_op jit(solution)/shard_map/ppermute | solution.py:29
  33.9 1.2 %shard_map.69 = bf16[8,4,32,128]{3,2,1,0:T(8,128)(2,1)S(1)} custom-call(bf16[2,8,64,128]{3,2,1,0:T(8,128)(2,1)S(1)} %get-tuple-element.16.inner, bf16[2,8,64,128]{3,2,1,0:T(8,128)(2,1)S(1)} %get-tuple-element.17.outer, bf16[4,64,128]{2,1,0:T(8,128)(2,1)S(1)} %get-tuple-element.58.below, bf16[4,64,128]{2,1,0:T(8,128)(2,1)S(1)} %get-tuple-element.57.above, ...), custom_call_target="tpu_custom_call" | custom-call | flops 452984832 | bytes 1355776 | tf_op jit(solution)/shard_map/pallas_call | solution.py:186
  35.1 1.5 %collective-permute-done.8 = bf16[224,128]{1,0:T(8,128)(2,1)S(1)} collective-permute-done((bf16[224,128]{1,0:T(8,128)(2,1)S(1)}, bf16[224,128]{1,0:T(8,128)(2,1)S(1)}, u32[]{:S(2)}, u32[]{:S(2)}) %collective-permute-start.8) | collective-permute-done | bytes 57376 | tf_op jit(solution)/shard_map/ppermute | solution.py:43
  36.7 0.8 %copy.26 = bf16[1,32,8,4,128]{4,3,2,1,0:T(4,128)(2,1)} copy(bf16[1,32,8,4,128]{4,1,3,2,0:T(8,128)(2,1)S(1)} %bitcast.57) | data formatting | bytes 524288
  37.5 0.5 %collective-permute-done.13 = f32[224,128]{1,0:T(8,128)S(1)} collective-permute-done((f32[224,128]{1,0:T(8,128)S(1)}, f32[224,128]{1,0:T(8,128)S(1)}, u32[]{:S(2)}, u32[]{:S(2)}) %collective-permute-start.13) | collective-permute-done | bytes 114720 | tf_op jit(solution)/shard_map/ppermute | solution.py:43
  38.0 0.9 %shard_map.70 = (f32[864,64]{1,0:T(8,128)}, f32[1,64]{1,0:T(1,128)}) custom-call(f32[224,128]{1,0:T(8,128)S(1)} %get-tuple-element.48.refs_0_, f32[224,128]{1,0:T(8,128)S(1)} %get-tuple-element.47.refs_1_), custom_call_target="tpu_custom_call" | custom-call | flops 57344 | bytes 450816 | tf_op jit(solution)/shard_map/pallas_call | solution.py:186
  (44 shorter events, 2.5 us)
Async XLA Ops:
  1.7 0.9 %copy-start = (bf16[64,32,3,3,3]{0,1,4,3,2:T(8,128)(2,1)S(1)}, bf16[64,32,3,3,3]{0,1,4,3,2:T(8,128)(2,1)}, u32[]{:S(2)}) copy-start(bf16[64,32,3,3,3]{0,1,4,3,2:T(8,128)(2,1)} %param.5) | copy-start | bytes 331780
  1.7 3.3 %collective-permute-start = (bf16[32,4,128]{2,0,1:T(8,128)(2,1)S(1)}, bf16[32,4,128]{2,0,1:T(8,128)(2,1)S(1)}, u32[]{:S(2)}, u32[]{:S(2)}) collective-permute-start(bf16[32,4,128]{2,0,1:T(8,128)(2,1)S(1)} %fusion), channel_id=1, source_target_pairs={{0,16},{16,0},{1,17},{17,1},{2,18},{18,2},{3,19},{19,3},{4,20},{20... | collective-permute-start | bytes 98312 | tf_op jit(solution)/shard_map/ppermute | solution.py:25
  2.7 0.7 %copy-start.2 = (f32[64]{0:T(128)S(1)}, f32[64]{0:T(128)}, u32[]{:S(2)}) copy-start(f32[64]{0:T(128)} %param.6) | copy-start | bytes 772
  3.8 1.0 %copy-start.1 = (bf16[1,64,8,4,128]{4,3,2,1,0:T(4,128)(2,1)S(1)}, bf16[1,64,8,4,128]{4,3,2,1,0:T(4,128)(2,1)}, u32[]{:S(2)}) copy-start(bf16[1,64,8,4,128]{4,3,2,1,0:T(4,128)(2,1)} %param.7) | copy-start | bytes 1572868
  5.1 8.8 %collective-permute-start.2 = (bf16[10,32,128]{2,1,0:T(8,128)(2,1)S(1)}, bf16[10,32,128]{2,1,0:T(8,128)(2,1)S(1)}, u32[]{:S(2)}, u32[]{:S(2)}) collective-permute-start(bf16[10,32,128]{2,1,0:T(8,128)(2,1)S(1)} %get-tuple-element.51), channel_id=1, source_target_pairs={{0,4},{4,0},{8,12},{12,8},{1,5},{5,1},{9,13},{13,9},{2,6},{6,2},{1... | collective-permute-start | bytes 245768 | tf_op jit(solution)/shard_map/ppermute | solution.py:25
  8.1 5.8 %collective-permute-start.1 = (bf16[10,32,128]{2,1,0:T(8,128)(2,1)S(1)}, bf16[10,32,128]{2,1,0:T(8,128)(2,1)S(1)}, u32[]{:S(2)}, u32[]{:S(2)}) collective-permute-start(bf16[10,32,128]{2,1,0:T(8,128)(2,1)S(1)} %get-tuple-element.52), channel_id=1, source_target_pairs={{0,12},{4,8},{8,4},{12,0},{1,13},{5,9},{9,5},{13,1},{2,14},{6,10},... | collective-permute-start | bytes 245768 | tf_op jit(solution)/shard_map/ppermute | solution.py:29
  18.3 1.3 %collective-permute-start.10 = (bf16[4,64,128]{2,1,0:T(8,128)(2,1)S(1)}, bf16[4,64,128]{2,1,0:T(8,128)(2,1)S(1)}, u32[]{:S(2)}, u32[]{:S(2)}) collective-permute-start(bf16[4,64,128]{2,1,0:T(8,128)(2,1)S(1)} %maximum_select_fusion), channel_id=1, source_target_pairs={{0,16},{16,0},{1,17},{17,1},{2,18},{18,2},{3,19},{19,3},{4,20},{20... | collective-permute-start | bytes 196616 | tf_op jit(solution)/shard_map/ppermute | solution.py:25
  18.4 1.5 %collective-permute-start.3 = (f32[224,128]{1,0:T(8,128)S(1)}, f32[224,128]{1,0:T(8,128)S(1)}, u32[]{:S(2)}, u32[]{:S(2)}) collective-permute-start(f32[224,128]{1,0:T(8,128)S(1)} %slice_select_fusion), channel_id=1, source_target_pairs={{0,16},{16,0},{1,17},{17,1},{2,18},{18,2},{3,19},{19,3},{4,20},{20... | collective-permute-start | bytes 344072 | tf_op jit(solution)/shard_map/ppermute | solution.py:43
  19.9 6.2 %collective-permute-start.6 = (bf16[224,128]{1,0:T(8,128)(2,1)S(1)}, bf16[224,128]{1,0:T(8,128)(2,1)S(1)}, u32[]{:S(2)}, u32[]{:S(2)}) collective-permute-start(bf16[224,128]{1,0:T(8,128)(2,1)S(1)} %get-tuple-element.29), channel_id=1, source_target_pairs={{0,12},{4,8},{8,4},{12,0},{1,13},{5,9},{9,5},{13,1},{2,14},{6,10},... | collective-permute-start | bytes 172040 | tf_op jit(solution)/shard_map/ppermute | solution.py:43
  21.4 4.9 %collective-permute-start.5 = (bf16[224,128]{1,0:T(8,128)(2,1)S(1)}, bf16[224,128]{1,0:T(8,128)(2,1)S(1)}, u32[]{:S(2)}, u32[]{:S(2)}) collective-permute-start(bf16[224,128]{1,0:T(8,128)(2,1)S(1)} %get-tuple-element.29), channel_id=1, source_target_pairs={{0,8},{4,12},{8,0},{12,4},{1,9},{5,13},{9,1},{13,5},{2,10},{6,14},... | collective-permute-start | bytes 172040 | tf_op jit(solution)/shard_map/ppermute | solution.py:43
  22.9 4.8 %collective-permute-start.4 = (bf16[224,128]{1,0:T(8,128)(2,1)S(1)}, bf16[224,128]{1,0:T(8,128)(2,1)S(1)}, u32[]{:S(2)}, u32[]{:S(2)}) collective-permute-start(bf16[224,128]{1,0:T(8,128)(2,1)S(1)} %get-tuple-element.29), channel_id=1, source_target_pairs={{0,4},{4,0},{8,12},{12,8},{1,5},{5,1},{9,13},{13,9},{2,6},{6,2},{1... | collective-permute-start | bytes 172040 | tf_op jit(solution)/shard_map/ppermute | solution.py:43
  23.5 8.7 %collective-permute-start.12 = (bf16[10,64,128]{2,1,0:T(8,128)(2,1)S(1)}, bf16[10,64,128]{2,1,0:T(8,128)(2,1)S(1)}, u32[]{:S(2)}, u32[]{:S(2)}) collective-permute-start(bf16[10,64,128]{2,1,0:T(8,128)(2,1)S(1)} %get-tuple-element.33), channel_id=1, source_target_pairs={{0,4},{4,0},{8,12},{12,8},{1,5},{5,1},{9,13},{13,9},{2,6},{6,2},{1... | collective-permute-start | bytes 491528 | tf_op jit(solution)/shard_map/ppermute | solution.py:25
  25.1 8.7 %collective-permute-start.11 = (bf16[10,64,128]{2,1,0:T(8,128)(2,1)S(1)}, bf16[10,64,128]{2,1,0:T(8,128)(2,1)S(1)}, u32[]{:S(2)}, u32[]{:S(2)}) collective-permute-start(bf16[10,64,128]{2,1,0:T(8,128)(2,1)S(1)} %get-tuple-element.34), channel_id=1, source_target_pairs={{0,12},{4,8},{8,4},{12,0},{1,13},{5,9},{9,5},{13,1},{2,14},{6,10},... | collective-permute-start | bytes 491528 | tf_op jit(solution)/shard_map/ppermute | solution.py:29
  27.8 7.3 %collective-permute-start.9 = (bf16[224,128]{1,0:T(8,128)(2,1)S(1)}, bf16[224,128]{1,0:T(8,128)(2,1)S(1)}, u32[]{:S(2)}, u32[]{:S(2)}) collective-permute-start(bf16[224,128]{1,0:T(8,128)(2,1)S(1)} %fusion.1), channel_id=1, source_target_pairs={{0,3},{1,2},{2,1},{3,0},{4,7},{5,6},{6,5},{7,4},{8,11},{9,10},{10,... | collective-permute-start | bytes 172040 | tf_op jit(solution)/shard_map/ppermute | solution.py:43
  31.5 5.1 %collective-permute-start.8 = (bf16[224,128]{1,0:T(8,128)(2,1)S(1)}, bf16[224,128]{1,0:T(8,128)(2,1)S(1)}, u32[]{:S(2)}, u32[]{:S(2)}) collective-permute-start(bf16[224,128]{1,0:T(8,128)(2,1)S(1)} %fusion.1), channel_id=1, source_target_pairs={{0,2},{1,3},{2,0},{3,1},{4,6},{5,7},{6,4},{7,5},{8,10},{9,11},{10,... | collective-permute-start | bytes 172040 | tf_op jit(solution)/shard_map/ppermute | solution.py:43
  31.5 5.1 %collective-permute-start.7 = (bf16[224,128]{1,0:T(8,128)(2,1)S(1)}, bf16[224,128]{1,0:T(8,128)(2,1)S(1)}, u32[]{:S(2)}, u32[]{:S(2)}) collective-permute-start(bf16[224,128]{1,0:T(8,128)(2,1)S(1)} %fusion.1), channel_id=1, source_target_pairs={{0,1},{1,0},{2,3},{3,2},{4,5},{5,4},{6,7},{7,6},{8,9},{9,8},{10,11... | collective-permute-start | bytes 172040 | tf_op jit(solution)/shard_map/ppermute | solution.py:43
  36.6 1.4 %collective-permute-start.13 = (f32[224,128]{1,0:T(8,128)S(1)}, f32[224,128]{1,0:T(8,128)S(1)}, u32[]{:S(2)}, u32[]{:S(2)}) collective-permute-start(f32[224,128]{1,0:T(8,128)S(1)} %add_add_fusion), channel_id=1, source_target_pairs={{0,16},{16,0},{1,17},{17,1},{2,18},{18,2},{3,19},{19,3},{4,20},{20... | collective-permute-start | bytes 344072 | tf_op jit(solution)/shard_map/ppermute | solution.py:43

commit v3 on v2

--- a/solution.py
+++ b/solution.py
@@ -2,6 +2,7 @@
 import jax.numpy as jnp
 from jax import lax
 from jax.experimental import pallas as pl
+from jax.experimental.layout import Layout, with_layout_constraint
 from jax.experimental.pallas import tpu as pltpu
 from jax.sharding import PartitionSpec as P
 
@@ -60,19 +61,22 @@
     return jnp.where(lane == edge, 0.0, pltpu.roll(value, (-step) % width, 1))
 
 
-def forward_rows(row_of, rows, w1, bias, cot, delta, before, payload, patches, grad):
-    depth, co = cot.shape[0], cot.shape[2]
-    width = cot.shape[3]
+def forward_rows(row_of, rows, w1, bias, cot, delta, before, payload, patches, taps, slopes, grad):
+    depth, co, width = cot.shape[0], cot.shape[2], cot.shape[3]
     ci = row_of(1, 1).shape[0]
-    fill_patches(row_of, depth, rows, patches)
+    count = len(rows)
+    for d in range(depth):
+        for at, h in enumerate(rows):
+            for a in range(3):
+                for b in range(3):
+                    lanes = pl.ds((d * count + at) * width, width)
+                    patches[pl.ds((a * 3 + b) * ci, ci), lanes] = row_of(d + a, h + b)
+    taps[...] = jnp.dot(w1[...], patches[...], preferred_element_type=F32)
     shift_bias = jnp.broadcast_to(bias[...], (co, width))
     bias_acc = jnp.zeros((co, width), F32)
     for d in range(depth):
-        window = pl.ds(d * 3 * ci, 9 * ci)
-        taps = jnp.dot(w1[...], patches[window, :], preferred_element_type=F32)
-        blocks = [[], [], []]
         for at, h in enumerate(rows):
-            lanes = slice(at * width, (at + 1) * width)
+            lanes = pl.ds((d * count + at) * width, width)
             linear = taps[co : 2 * co, lanes] + shift_bias
             linear = linear + shifted(taps[:co, lanes], -1) + shifted(taps[2 * co :, lanes], 1)
             sigma = 1.0 / (1.0 + jnp.exp(-linear))
@@ -81,17 +85,12 @@
             delta[at, d] = rounded
             wide = rounded.astype(F32)
             bias_acc = bias_acc + wide
-            blocks[0].append(shifted(wide, 1).astype(BF16))
-            blocks[1].append(rounded)
-            blocks[2].append(shifted(wide, -1).astype(BF16))
-        slopes = jnp.concatenate([jnp.concatenate(part, axis=1) for part in blocks], axis=0)
-        term = lax.dot_general(
-            patches[window, :], slopes, (((1,), (1,)), ((), ())), preferred_element_type=F32
-        )
-        if d == 0:
-            grad[...] = term
-        else:
-            grad[...] += term
+            slopes[:co, lanes] = shifted(wide, 1).astype(BF16)
+            slopes[co : 2 * co, lanes] = rounded
+            slopes[2 * co :, lanes] = shifted(wide, -1).astype(BF16)
+    grad[...] = lax.dot_general(
+        patches[...], slopes[...], (((1,), (1,)), ((), ())), preferred_element_type=F32
+    )
     taps_rows = 9 * ci
     tail = taps_rows + taps_rows // 2
     total = jnp.sum(bias_acc.T, axis=0, keepdims=True)
@@ -112,17 +111,17 @@
         payload[at, :] = value if before is None else before[at, :] + value
 
 
-def inner_kernel(x, below, above, w1, bias, cot, delta, payload, patches, grad):
+def inner_kernel(x, below, above, w1, bias, cot, delta, payload, *scratch):
     depth, height = x.shape[:2]
 
     def row_of(d, h):
         return below[h - 1] if d == 0 else above[h - 1] if d == depth + 1 else x[d - 1, h - 1]
 
     rows = range(1, height - 1)
-    forward_rows(row_of, rows, w1, bias, cot, delta, None, payload, patches, grad)
-
-
-def outer_kernel(x, below, above, left, right, w1, bias, cot, before, delta, payload, patches, grad):
+    forward_rows(row_of, rows, w1, bias, cot, delta, None, payload, *scratch)
+
+
+def outer_kernel(x, below, above, left, right, w1, bias, cot, before, delta, payload, *scratch):
     depth, height = x.shape[:2]
 
     def row_of(d, h):
@@ -133,7 +132,7 @@
         return below[h - 1] if d == 0 else above[h - 1] if d == depth + 1 else x[d - 1, h - 1]
 
     rows = (0, height - 1)
-    forward_rows(row_of, rows, w1, bias, cot, delta, before, payload, patches, grad)
+    forward_rows(row_of, rows, w1, bias, cot, delta, before, payload, *scratch)
 
 
 def input_kernel(inner, outer, below, above, left, right, w2, out, patches):
@@ -223,19 +222,19 @@
 def local(inputs, weight, bias, cotangent):
     cubes, ci, depth, height, width = inputs.shape
     co = cotangent.shape[1]
-    taps = weight.transpose(2, 3, 4, 1, 0)
-    w1 = taps.transpose(2, 4, 0, 1, 3).reshape(3 * co, 9 * ci)
-    w2 = jnp.flip(taps, (0, 1)).transpose(2, 3, 0, 1, 4).reshape(3 * ci, 9 * co)
-    w1, w2 = lax.optimization_barrier((w1, w2))
-    column = bias[:, None]
     payload_rows = 9 * ci + 9 * ci // 2 + 16
     payload_shape = jax.ShapeDtypeStruct((payload_rows, 2 * co), F32)
     flops = 2 * depth * width * 27 * ci * co
     total = None
     fields = []
+    edges = exchange(inputs[:, :, 0], inputs[:, :, -1], "depth")
+    edges = [with_layout_constraint(edge, Layout((0, 1, 2, 3))) for edge in edges]
+    edges, weight, bias, cotangent = lax.optimization_barrier((edges, weight, bias, cotangent))
+    taps = weight.transpose(2, 3, 4, 1, 0)
+    w1 = taps.transpose(2, 4, 0, 1, 3).reshape(3 * co, 9 * ci)
+    column = bias[:, None]
     for cube in range(cubes):
-        edges = exchange(inputs[cube][:, 0], inputs[cube][:, -1], "depth")
-        below, above = (edge.transpose(1, 0, 2) for edge in edges)
+        below, above = (edge[cube].transpose(1, 0, 2) for edge in edges)
         x = inputs[cube].transpose(1, 2, 0, 3)
         cot = cotangent[cube].transpose(1, 2, 0, 3)
 
@@ -244,7 +243,9 @@
                 kernel,
                 (jax.ShapeDtypeStruct((rows, depth, co, width), BF16), payload_shape),
                 [
-                    pltpu.VMEM(((depth + 2) * 3 * ci, rows * width), BF16),
+                    pltpu.VMEM((9 * ci, depth * rows * width), BF16),
+                    pltpu.VMEM((3 * co, depth * rows * width), F32),
+                    pltpu.VMEM((3 * co, depth * rows * width), BF16),
                     pltpu.VMEM((9 * ci, 3 * co), F32),
                 ],
                 2 * flops * rows,
@@ -262,6 +263,9 @@
         below, above = exchange(layer(0), layer(-1), "depth")
         sides = height_halo(outer[0], outer[1], below, above)
         fields.append((inner, outer, below, above, *sides))
+
+    total, taps = lax.optimization_barrier((total, taps))
+    w2 = jnp.flip(taps, (0, 1)).transpose(2, 3, 0, 1, 4).reshape(3 * ci, 9 * co)
 
     def input_gradients(fields):
         grads = []

time: 39.1 us -> 36.2 us (0.926)
  Pallas kernels: 10.6 us -> 5.18 us
  waiting for transfers between devices: 6.11 us -> 7.58 us
  other arithmetic: 0.32 us -> 1.13 us
  local copies, waits for them, and re-layouts: 4.69 us -> 5.3 us
  starting transfers between devices: 16.3 us -> 15.7 us
    pallas_call x4, Pallas kernels: 10.6 us -> 5.18 us  [call(): pl.pallas_call(kernel, out_shape=outs, scratch_shapes=scratch, compiler_p...]
    ppermute x2, waiting for transfers between devices: 1.59 us -> 3.17 us  [exchange(): other = lax.ppermute(jnp.where(even, low_edge, high_edge), axis, outer)]
    select_n x4, other arithmetic: 0.1 us -> 0.89 us  [exchange(): got = lax.ppermute(jnp.where(even, high_edge, low_edge), axis, inner)]
    ppermute x4, starting transfers between devices: 5.15 us -> 4.71 us  [exchange(): got = lax.ppermute(jnp.where(even, high_edge, low_edge), axis, inner)]
    ppermute x4, waiting for transfers between devices: 0.67 us -> 0.27 us  [exchange(): got = lax.ppermute(jnp.where(even, high_edge, low_edge), axis, inner)]
    unnamed x9 -> x10, local copies, waits for them, and re-layouts: 3.65 us -> 3.94 us
  transfers between devices with their start and end apart: 14 -> 14, of which waited for: 7 -> 8; matrix products, arithmetic and copies ran while one was open for 6% -> 9% of each run, Pallas kernels for 14% -> 8%
where the time goes in v3:
time: 36.2 us; the launch traced here: 35.8 us
  starting transfers between devices  15.7 us (43%)
  waiting for transfers between devices  7.58 us (21%)
  local copies, waits for them, and re-layouts  5.3 us (15%)
  Pallas kernels  5.18 us (14%)
  other arithmetic  1.13 us (3%)
  between operations  0.92 us (3%)
    ppermute x8, starting transfers between devices, swap(): lax.ppermute(array, axis, [(i, i ^ mask) for i in range(lax.axis_size(axi...  8.65 us
    pallas_call x4, Pallas kernels, call(): pl.pallas_call(kernel, out_shape=outs, scratch_shapes=scratch, compiler_p...  5.18 us
    ppermute x4, starting transfers between devices, exchange(): got = lax.ppermute(jnp.where(even, high_edge, low_edge), axis, inner)  4.71 us
    ppermute x8, waiting for transfers between devices, swap(): lax.ppermute(array, axis, [(i, i ^ mask) for i in range(lax.axis_size(axi...  4.14 us
    unnamed x10, local copies, waits for them, and re-layouts  3.94 us
    ppermute x2, waiting for transfers between devices, exchange(): other = lax.ppermute(jnp.where(even, low_edge, high_edge), axis, outer)  3.17 us
    ppermute x2, starting transfers between devices, exchange(): other = lax.ppermute(jnp.where(even, low_edge, high_edge), axis, outer)  2.38 us
    select_n x4, other arithmetic, exchange(): got = lax.ppermute(jnp.where(even, high_edge, low_edge), axis, inner)  0.89 us
  transfers between devices with their start and end apart: 14, of which 8 were waited for; matrix products, arithmetic and copies ran while one was open for 9% of the time, Pallas kernels for 8%

profile of v3, /device:TPU:0, one launch (start us, length us, event | category | flops | bytes accessed | tf_op | source)
XLA Modules:
  0.0 35.8 jit_solution(755296116029467412)
XLA Ops:
  0.6 0.8 %fusion = bf16[1,32,4,128]{3,2,1,0:T(4,128)(2,1)S(1)} fusion(bf16[1,32,8,4,128]{4,3,2,1,0:T(4,128)(2,1)} %param.4, pred[]{:T(512)S(6)} %eq.23), kind=kLoop, calls=%fused_computation.32 | loop fusion | flops 16384 | bytes 98305 | tf_op jit(solution)/shard_map/jit(_where)/select_n | solution.py:26
  2.0 1.1 %copy.51 = bf16[1,32,8,4,128]{4,1,2,3,0:T(8,128)(2,1)S(1)} copy(bf16[1,32,8,4,128]{4,3,2,1,0:T(4,128)(2,1)} %param.4) | data formatting | bytes 524288 | tf_op args[0]
  3.1 0.9 %copy-done = bf16[1,32,8,4,128]{4,3,2,1,0:T(4,128)(2,1)S(1)} copy-done((bf16[1,32,8,4,128]{4,3,2,1,0:T(4,128)(2,1)S(1)}, bf16[1,32,8,4,128]{4,3,2,1,0:T(4,128)(2,1)}, u32[]{:S(2)}) %copy-start) | copy-done | bytes 262168
  4.2 0.6 %copy-done.3 = f32[64]{0:T(128)S(1)} copy-done((f32[64]{0:T(128)S(1)}, f32[64]{0:T(128)}, u32[]{:S(2)}) %copy-start.3) | copy-done | bytes 280
  4.9 2.6 %collective-permute-start.2 = (bf16[10,32,128]{2,1,0:T(8,128)(2,1)S(1)}, bf16[10,32,128]{2,1,0:T(8,128)(2,1)S(1)}, u32[]{:S(2)}, u32[]{:S(2)}) collective-permute-start(bf16[10,32,128]{2,1,0:T(8,128)(2,1)S(1)} %get-tuple-element.59), channel_id=1, source_target_pairs={{0,4},{4,0},{8,12},{12,8},{1,5},{5,1},{9,13},{13,9},{2,6},{6,2},{1... | collective-permute-start | bytes 245768 | tf_op jit(solution)/shard_map/ppermute | solution.py:26
  7.5 1.5 %collective-permute-start.1 = (bf16[10,32,128]{2,1,0:T(8,128)(2,1)S(1)}, bf16[10,32,128]{2,1,0:T(8,128)(2,1)S(1)}, u32[]{:S(2)}, u32[]{:S(2)}) collective-permute-start(bf16[10,32,128]{2,1,0:T(8,128)(2,1)S(1)} %get-tuple-element.60), channel_id=1, source_target_pairs={{0,12},{4,8},{8,4},{12,0},{1,13},{5,9},{9,5},{13,1},{2,14},{6,10},... | collective-permute-start | bytes 245768 | tf_op jit(solution)/shard_map/ppermute | solution.py:30
  9.5 0.5 %copy-done.2 = bf16[1,64,8,4,128]{4,3,2,1,0:T(4,128)(2,1)S(1)} copy-done((bf16[1,64,8,4,128]{4,3,2,1,0:T(4,128)(2,1)S(1)}, bf16[1,64,8,4,128]{4,3,2,1,0:T(4,128)(2,1)}, u32[]{:S(2)}) %copy-start.2) | copy-done | bytes 524312
  10.2 1.6 %shard_map.67 = (bf16[2,8,64,128]{3,2,1,0:T(8,128)(2,1)S(1)}, f32[448,128]{1,0:T(8,128)S(1)}) custom-call(bf16[8,4,32,128]{3,2,1,0:T(8,128)(2,1)S(1)} %bitcast.65, bf16[4,32,128]{2,1,0:T(8,128)(2,1)S(1)} %get-tuple-element.74.below, bf16[4,32,128]{2,1,0:T(8,128)(2,1)S(1)} %get-tuple-element.73.above, bf16[192,288]{1,0:T(8,128)(2,1)S(1)} %copy.33.w1, ...), custom_call_target="tpu_custom_call" | custom-call | flops 452984832 | bytes 1454336 | tf_op jit(solution)/shard_map/pallas_call | solution.py:185
  11.8 1.7 %collective-permute-done.1 = bf16[10,32,128]{2,1,0:T(8,128)(2,1)S(1)} collective-permute-done((bf16[10,32,128]{2,1,0:T(8,128)(2,1)S(1)}, bf16[10,32,128]{2,1,0:T(8,128)(2,1)S(1)}, u32[]{:S(2)}, u32[]{:S(2)}) %collective-permute-start.1) | collective-permute-done | bytes 81952 | tf_op jit(solution)/shard_map/ppermute | solution.py:30
  13.6 1.6 %shard_map.68 = (bf16[2,8,64,128]{3,2,1,0:T(8,128)(2,1)S(1)}, f32[448,128]{1,0:T(8,128)S(1)}) custom-call(bf16[8,4,32,128]{3,2,1,0:T(8,128)(2,1)S(1)} %bitcast.66, bf16[4,32,128]{2,1,0:T(8,128)(2,1)S(1)} %get-tuple-element.74.below, bf16[4,32,128]{2,1,0:T(8,128)(2,1)S(1)} %get-tuple-element.73.above, bf16[10,32,128]{2,1,0:T(8,128)(2,1)S(1)} %get-tuple-element.58.left, ...), custom_call_target="tpu_custom_call" | custom-call | flops 452984832 | bytes 1847552 | tf_op jit(solution)/shard_map/pallas_call | solution.py:185
  15.3 0.6 %collective-permute-start.3 = (f32[224,128]{1,0:T(8,128)S(1)}, f32[224,128]{1,0:T(8,128)S(1)}, u32[]{:S(2)}, u32[]{:S(2)}) collective-permute-start(f32[224,128]{1,0:T(8,128)S(1)} %slice_select_fusion), channel_id=1, source_target_pairs={{0,16},{16,0},{1,17},{17,1},{2,18},{18,2},{3,19},{19,3},{4,20},{20... | collective-permute-start | bytes 344072 | tf_op jit(solution)/shard_map/ppermute | solution.py:44
  16.9 1.5 %collective-permute-start.6 = (bf16[224,128]{1,0:T(8,128)(2,1)S(1)}, bf16[224,128]{1,0:T(8,128)(2,1)S(1)}, u32[]{:S(2)}, u32[]{:S(2)}) collective-permute-start(bf16[224,128]{1,0:T(8,128)(2,1)S(1)} %get-tuple-element.39), channel_id=1, source_target_pairs={{0,12},{4,8},{8,4},{12,0},{1,13},{5,9},{9,5},{13,1},{2,14},{6,10},... | collective-permute-start | bytes 172040 | tf_op jit(solution)/shard_map/ppermute | solution.py:44
  18.4 1.5 %collective-permute-start.5 = (bf16[224,128]{1,0:T(8,128)(2,1)S(1)}, bf16[224,128]{1,0:T(8,128)(2,1)S(1)}, u32[]{:S(2)}, u32[]{:S(2)}) collective-permute-start(bf16[224,128]{1,0:T(8,128)(2,1)S(1)} %get-tuple-element.39), channel_id=1, source_target_pairs={{0,8},{4,12},{8,0},{12,4},{1,9},{5,13},{9,1},{13,5},{2,10},{6,14},... | collective-permute-start | bytes 172040 | tf_op jit(solution)/shard_map/ppermute | solution.py:44
  19.9 0.5 %collective-permute-start.4 = (bf16[224,128]{1,0:T(8,128)(2,1)S(1)}, bf16[224,128]{1,0:T(8,128)(2,1)S(1)}, u32[]{:S(2)}, u32[]{:S(2)}) collective-permute-start(bf16[224,128]{1,0:T(8,128)(2,1)S(1)} %get-tuple-element.39), channel_id=1, source_target_pairs={{0,4},{4,0},{8,12},{12,8},{1,5},{5,1},{9,13},{13,9},{2,6},{6,2},{1... | collective-permute-start | bytes 172040 | tf_op jit(solution)/shard_map/ppermute | solution.py:44
  20.5 1.6 %collective-permute-start.12 = (bf16[10,64,128]{2,1,0:T(8,128)(2,1)S(1)}, bf16[10,64,128]{2,1,0:T(8,128)(2,1)S(1)}, u32[]{:S(2)}, u32[]{:S(2)}) collective-permute-start(bf16[10,64,128]{2,1,0:T(8,128)(2,1)S(1)} %get-tuple-element.43), channel_id=1, source_target_pairs={{0,4},{4,0},{8,12},{12,8},{1,5},{5,1},{9,13},{13,9},{2,6},{6,2},{1... | collective-permute-start | bytes 491528 | tf_op jit(solution)/shard_map/ppermute | solution.py:26
  22.0 0.9 %collective-permute-start.11 = (bf16[10,64,128]{2,1,0:T(8,128)(2,1)S(1)}, bf16[10,64,128]{2,1,0:T(8,128)(2,1)S(1)}, u32[]{:S(2)}, u32[]{:S(2)}) collective-permute-start(bf16[10,64,128]{2,1,0:T(8,128)(2,1)S(1)} %get-tuple-element.44), channel_id=1, source_target_pairs={{0,12},{4,8},{8,4},{12,0},{1,13},{5,9},{9,5},{13,1},{2,14},{6,10},... | collective-permute-start | bytes 491528 | tf_op jit(solution)/shard_map/ppermute | solution.py:30
  23.2 1.5 %collective-permute-done.4 = bf16[224,128]{1,0:T(8,128)(2,1)S(1)} collective-permute-done((bf16[224,128]{1,0:T(8,128)(2,1)S(1)}, bf16[224,128]{1,0:T(8,128)(2,1)S(1)}, u32[]{:S(2)}, u32[]{:S(2)}) %collective-permute-start.4) | collective-permute-done | bytes 57376 | tf_op jit(solution)/shard_map/ppermute | solution.py:44
  24.7 3.7 %collective-permute-start.9 = (bf16[224,128]{1,0:T(8,128)(2,1)S(1)}, bf16[224,128]{1,0:T(8,128)(2,1)S(1)}, u32[]{:S(2)}, u32[]{:S(2)}) collective-permute-start(bf16[224,128]{1,0:T(8,128)(2,1)S(1)} %fusion.1), channel_id=1, source_target_pairs={{0,3},{1,2},{2,1},{3,0},{4,7},{5,6},{6,5},{7,4},{8,11},{9,10},{10,... | collective-permute-start | bytes 172040 | tf_op jit(solution)/shard_map/ppermute | solution.py:44
  28.4 0.8 %collective-permute-start.7 = (bf16[224,128]{1,0:T(8,128)(2,1)S(1)}, bf16[224,128]{1,0:T(8,128)(2,1)S(1)}, u32[]{:S(2)}, u32[]{:S(2)}) collective-permute-start(bf16[224,128]{1,0:T(8,128)(2,1)S(1)} %fusion.1), channel_id=1, source_target_pairs={{0,1},{1,0},{2,3},{3,2},{4,5},{5,4},{6,7},{7,6},{8,9},{9,8},{10,11... | collective-permute-start | bytes 172040 | tf_op jit(solution)/shard_map/ppermute | solution.py:44
  29.2 1.4 %collective-permute-done.11 = bf16[10,64,128]{2,1,0:T(8,128)(2,1)S(1)} collective-permute-done((bf16[10,64,128]{2,1,0:T(8,128)(2,1)S(1)}, bf16[10,64,128]{2,1,0:T(8,128)(2,1)S(1)}, u32[]{:S(2)}, u32[]{:S(2)}) %collective-permute-start.11) | collective-permute-done | bytes 163872 | tf_op jit(solution)/shard_map/ppermute | solution.py:30
  30.7 1.2 %shard_map.69 = bf16[8,4,32,128]{3,2,1,0:T(8,128)(2,1)S(1)} custom-call(bf16[2,8,64,128]{3,2,1,0:T(8,128)(2,1)S(1)} %get-tuple-element.26.inner, bf16[2,8,64,128]{3,2,1,0:T(8,128)(2,1)S(1)} %get-tuple-element.27.outer, bf16[4,64,128]{2,1,0:T(8,128)(2,1)S(1)} %get-tuple-element.66.below, bf16[4,64,128]{2,1,0:T(8,128)(2,1)S(1)} %get-tuple-element.65.above, ...), custom_call_target="tpu_custom_call" | custom-call | flops 452984832 | bytes 1355776 | tf_op jit(solution)/shard_map/pallas_call | solution.py:185
  31.9 1.6 %collective-permute-done.8 = bf16[224,128]{1,0:T(8,128)(2,1)S(1)} collective-permute-done((bf16[224,128]{1,0:T(8,128)(2,1)S(1)}, bf16[224,128]{1,0:T(8,128)(2,1)S(1)}, u32[]{:S(2)}, u32[]{:S(2)}) %collective-permute-start.8) | collective-permute-done | bytes 57376 | tf_op jit(solution)/shard_map/ppermute | solution.py:44
  33.6 0.8 %copy.38 = bf16[1,32,8,4,128]{4,3,2,1,0:T(4,128)(2,1)} copy(bf16[1,32,8,4,128]{4,1,3,2,0:T(8,128)(2,1)S(1)} %bitcast.67) | data formatting | bytes 524288
  35.0 0.9 %shard_map.70 = (f32[864,64]{1,0:T(8,128)}, f32[1,64]{1,0:T(1,128)}) custom-call(f32[224,128]{1,0:T(8,128)S(1)} %get-tuple-element.56.refs_0_, f32[224,128]{1,0:T(8,128)S(1)} %get-tuple-element.55.refs_1_), custom_call_target="tpu_custom_call" | custom-call | flops 57344 | bytes 450816 | tf_op jit(solution)/shard_map/pallas_call | solution.py:185
  (49 shorter events, 3.7 us)
Async XLA Ops:
  1.4 2.7 %collective-permute-start = (bf16[1,32,4,128]{3,2,1,0:T(4,128)(2,1)S(1)}, bf16[1,32,4,128]{3,2,1,0:T(4,128)(2,1)S(1)}, u32[]{:S(2)}, u32[]{:S(2)}) collective-permute-start(bf16[1,32,4,128]{3,2,1,0:T(4,128)(2,1)S(1)} %fusion), channel_id=1, source_target_pairs={{0,16},{16,0},{1,17},{17,1},{2,18},{18,2},{3,19},{19,3},{4,20},{20... | collective-permute-start | bytes 98312 | tf_op jit(solution)/shard_map/ppermute | solution.py:26
  3.0 1.0 %copy-start = (bf16[1,32,8,4,128]{4,3,2,1,0:T(4,128)(2,1)S(1)}, bf16[1,32,8,4,128]{4,3,2,1,0:T(4,128)(2,1)}, u32[]{:S(2)}) copy-start(bf16[1,32,8,4,128]{4,3,2,1,0:T(4,128)(2,1)} %param.4) | copy-start | bytes 786436
  4.1 0.7 %copy-start.3 = (f32[64]{0:T(128)S(1)}, f32[64]{0:T(128)}, u32[]{:S(2)}) copy-start(f32[64]{0:T(128)} %param.6) | copy-start | bytes 772
  4.2 4.8 %copy-start.1 = (bf16[64,32,3,3,3]{0,1,4,3,2:T(8,128)(2,1)S(1)}, bf16[64,32,3,3,3]{0,1,4,3,2:T(8,128)(2,1)}, u32[]{:S(2)}) copy-start(bf16[64,32,3,3,3]{0,1,4,3,2:T(8,128)(2,1)} %param.5) | copy-start | bytes 331780
  4.9 6.9 %collective-permute-start.2 = (bf16[10,32,128]{2,1,0:T(8,128)(2,1)S(1)}, bf16[10,32,128]{2,1,0:T(8,128)(2,1)S(1)}, u32[]{:S(2)}, u32[]{:S(2)}) collective-permute-start(bf16[10,32,128]{2,1,0:T(8,128)(2,1)S(1)} %get-tuple-element.59), channel_id=1, source_target_pairs={{0,4},{4,0},{8,12},{12,8},{1,5},{5,1},{9,13},{13,9},{2,6},{6,2},{1... | collective-permute-start | bytes 245768 | tf_op jit(solution)/shard_map/ppermute | solution.py:26
  7.5 6.1 %collective-permute-start.1 = (bf16[10,32,128]{2,1,0:T(8,128)(2,1)S(1)}, bf16[10,32,128]{2,1,0:T(8,128)(2,1)S(1)}, u32[]{:S(2)}, u32[]{:S(2)}) collective-permute-start(bf16[10,32,128]{2,1,0:T(8,128)(2,1)S(1)} %get-tuple-element.60), channel_id=1, source_target_pairs={{0,12},{4,8},{8,4},{12,0},{1,13},{5,9},{9,5},{13,1},{2,14},{6,10},... | collective-permute-start | bytes 245768 | tf_op jit(solution)/shard_map/ppermute | solution.py:30
  9.0 1.0 %copy-start.2 = (bf16[1,64,8,4,128]{4,3,2,1,0:T(4,128)(2,1)S(1)}, bf16[1,64,8,4,128]{4,3,2,1,0:T(4,128)(2,1)}, u32[]{:S(2)}) copy-start(bf16[1,64,8,4,128]{4,3,2,1,0:T(4,128)(2,1)} %param.7) | copy-start | bytes 1572868
  15.2 1.3 %collective-permute-start.10 = (bf16[4,64,128]{2,1,0:T(8,128)(2,1)S(1)}, bf16[4,64,128]{2,1,0:T(8,128)(2,1)S(1)}, u32[]{:S(2)}, u32[]{:S(2)}) collective-permute-start(bf16[4,64,128]{2,1,0:T(8,128)(2,1)S(1)} %maximum_select_fusion), channel_id=1, source_target_pairs={{0,16},{16,0},{1,17},{17,1},{2,18},{18,2},{3,19},{19,3},{4,20},{20... | collective-permute-start | bytes 196616 | tf_op jit(solution)/shard_map/ppermute | solution.py:26
  15.3 1.5 %collective-permute-start.3 = (f32[224,128]{1,0:T(8,128)S(1)}, f32[224,128]{1,0:T(8,128)S(1)}, u32[]{:S(2)}, u32[]{:S(2)}) collective-permute-start(f32[224,128]{1,0:T(8,128)S(1)} %slice_select_fusion), channel_id=1, source_target_pairs={{0,16},{16,0},{1,17},{17,1},{2,18},{18,2},{3,19},{19,3},{4,20},{20... | collective-permute-start | bytes 344072 | tf_op jit(solution)/shard_map/ppermute | solution.py:44
  16.9 6.1 %collective-permute-start.6 = (bf16[224,128]{1,0:T(8,128)(2,1)S(1)}, bf16[224,128]{1,0:T(8,128)(2,1)S(1)}, u32[]{:S(2)}, u32[]{:S(2)}) collective-permute-start(bf16[224,128]{1,0:T(8,128)(2,1)S(1)} %get-tuple-element.39), channel_id=1, source_target_pairs={{0,12},{4,8},{8,4},{12,0},{1,13},{5,9},{9,5},{13,1},{2,14},{6,10},... | collective-permute-start | bytes 172040 | tf_op jit(solution)/shard_map/ppermute | solution.py:44
  18.4 4.9 %collective-permute-start.5 = (bf16[224,128]{1,0:T(8,128)(2,1)S(1)}, bf16[224,128]{1,0:T(8,128)(2,1)S(1)}, u32[]{:S(2)}, u32[]{:S(2)}) collective-permute-start(bf16[224,128]{1,0:T(8,128)(2,1)S(1)} %get-tuple-element.39), channel_id=1, source_target_pairs={{0,8},{4,12},{8,0},{12,4},{1,9},{5,13},{9,1},{13,5},{2,10},{6,14},... | collective-permute-start | bytes 172040 | tf_op jit(solution)/shard_map/ppermute | solution.py:44
  19.9 4.8 %collective-permute-start.4 = (bf16[224,128]{1,0:T(8,128)(2,1)S(1)}, bf16[224,128]{1,0:T(8,128)(2,1)S(1)}, u32[]{:S(2)}, u32[]{:S(2)}) collective-permute-start(bf16[224,128]{1,0:T(8,128)(2,1)S(1)} %get-tuple-element.39), channel_id=1, source_target_pairs={{0,4},{4,0},{8,12},{12,8},{1,5},{5,1},{9,13},{13,9},{2,6},{6,2},{1... | collective-permute-start | bytes 172040 | tf_op jit(solution)/shard_map/ppermute | solution.py:44
  20.5 8.7 %collective-permute-start.12 = (bf16[10,64,128]{2,1,0:T(8,128)(2,1)S(1)}, bf16[10,64,128]{2,1,0:T(8,128)(2,1)S(1)}, u32[]{:S(2)}, u32[]{:S(2)}) collective-permute-start(bf16[10,64,128]{2,1,0:T(8,128)(2,1)S(1)} %get-tuple-element.43), channel_id=1, source_target_pairs={{0,4},{4,0},{8,12},{12,8},{1,5},{5,1},{9,13},{13,9},{2,6},{6,2},{1... | collective-permute-start | bytes 491528 | tf_op jit(solution)/shard_map/ppermute | solution.py:26
  22.0 8.6 %collective-permute-start.11 = (bf16[10,64,128]{2,1,0:T(8,128)(2,1)S(1)}, bf16[10,64,128]{2,1,0:T(8,128)(2,1)S(1)}, u32[]{:S(2)}, u32[]{:S(2)}) collective-permute-start(bf16[10,64,128]{2,1,0:T(8,128)(2,1)S(1)} %get-tuple-element.44), channel_id=1, source_target_pairs={{0,12},{4,8},{8,4},{12,0},{1,13},{5,9},{9,5},{13,1},{2,14},{6,10},... | collective-permute-start | bytes 491528 | tf_op jit(solution)/shard_map/ppermute | solution.py:30
  24.7 7.1 %collective-permute-start.9 = (bf16[224,128]{1,0:T(8,128)(2,1)S(1)}, bf16[224,128]{1,0:T(8,128)(2,1)S(1)}, u32[]{:S(2)}, u32[]{:S(2)}) collective-permute-start(bf16[224,128]{1,0:T(8,128)(2,1)S(1)} %fusion.1), channel_id=1, source_target_pairs={{0,3},{1,2},{2,1},{3,0},{4,7},{5,6},{6,5},{7,4},{8,11},{9,10},{10,... | collective-permute-start | bytes 172040 | tf_op jit(solution)/shard_map/ppermute | solution.py:44
  28.4 5.1 %collective-permute-start.8 = (bf16[224,128]{1,0:T(8,128)(2,1)S(1)}, bf16[224,128]{1,0:T(8,128)(2,1)S(1)}, u32[]{:S(2)}, u32[]{:S(2)}) collective-permute-start(bf16[224,128]{1,0:T(8,128)(2,1)S(1)} %fusion.1), channel_id=1, source_target_pairs={{0,2},{1,3},{2,0},{3,1},{4,6},{5,7},{6,4},{7,5},{8,10},{9,11},{10,... | collective-permute-start | bytes 172040 | tf_op jit(solution)/shard_map/ppermute | solution.py:44
  28.4 5.1 %collective-permute-start.7 = (bf16[224,128]{1,0:T(8,128)(2,1)S(1)}, bf16[224,128]{1,0:T(8,128)(2,1)S(1)}, u32[]{:S(2)}, u32[]{:S(2)}) collective-permute-start(bf16[224,128]{1,0:T(8,128)(2,1)S(1)} %fusion.1), channel_id=1, source_target_pairs={{0,1},{1,0},{2,3},{3,2},{4,5},{5,4},{6,7},{7,6},{8,9},{9,8},{10,11... | collective-permute-start | bytes 172040 | tf_op jit(solution)/shard_map/ppermute | solution.py:44
  33.5 1.4 %collective-permute-start.13 = (f32[224,128]{1,0:T(8,128)S(1)}, f32[224,128]{1,0:T(8,128)S(1)}, u32[]{:S(2)}, u32[]{:S(2)}) collective-permute-start(f32[224,128]{1,0:T(8,128)S(1)} %add_add_fusion), channel_id=1, source_target_pairs={{0,16},{16,0},{1,17},{17,1},{2,18},{18,2},{3,19},{19,3},{4,20},{20... | collective-permute-start | bytes 344072 | tf_op jit(solution)/shard_map/ppermute | solution.py:44

commit v4 on v3

--- a/solution.py
+++ b/solution.py
@@ -11,33 +11,40 @@
 AXES = ("depth", "height", "dp")
 
 
-def exchange(low_edge, high_edge, axis):
+def paired(axis):
+    return lax.axis_index(axis) % 2 == 0 if lax.axis_size(axis) % 2 == 0 else jnp.bool_(True)
+
+
+def meet(low_edge, high_edge, axis):
     count = lax.axis_size(axis)
     none = jnp.zeros_like(low_edge)
     if count == 1:
         return none, none
-    at = lax.axis_index(axis)
     if count % 2:
         up = [(i, i + 1) for i in range(count - 1)]
         down = [(i + 1, i) for i in range(count - 1)]
         return lax.ppermute(high_edge, axis, up), lax.ppermute(low_edge, axis, down)
-    even = at % 2 == 0
+    at, even = lax.axis_index(axis), paired(axis)
     inner = [(i, i ^ 1) for i in range(count)]
-    got = lax.ppermute(jnp.where(even, high_edge, low_edge), axis, inner)
+    first = lax.ppermute(jnp.where(even, high_edge, low_edge), axis, inner)
     if count == 2:
-        return jnp.where(even, none, got), jnp.where(even, got, none)
+        return none, first
     outer = [(i, (i - 1 if i % 2 == 0 else i + 1) % count) for i in range(count)]
-    other = lax.ppermute(jnp.where(even, low_edge, high_edge), axis, outer)
-    below = jnp.where(at == 0, none, jnp.where(even, other, got))
-    above = jnp.where(at == count - 1, none, jnp.where(even, got, other))
-    return below, above
-
-
-def height_halo(first_row, last_row, below, above):
+    second = lax.ppermute(jnp.where(even, low_edge, high_edge), axis, outer)
+    return jnp.where((at == 0) | (at == count - 1), none, second), first
+
+
+def exchange(low_edge, high_edge, axis):
+    second, first = meet(low_edge, high_edge, axis)
+    even = paired(axis)
+    return jnp.where(even, second, first), jnp.where(even, first, second)
+
+
+def columns(first_row, last_row, below, above):
     def column(rows, at):
         return jnp.concatenate([below[at][None], rows, above[at][None]], axis=0)
 
-    return exchange(column(first_row, 0), column(last_row, -1), "height")
+    return column(first_row, 0), column(last_row, -1)
 
 
 def swap(array, axis, mask):
@@ -61,26 +68,19 @@
     return jnp.where(lane == edge, 0.0, pltpu.roll(value, (-step) % width, 1))
 
 
-def forward_rows(row_of, rows, w1, bias, cot, delta, before, payload, patches, taps, slopes, grad):
-    depth, co, width = cot.shape[0], cot.shape[2], cot.shape[3]
-    ci = row_of(1, 1).shape[0]
-    count = len(rows)
-    for d in range(depth):
-        for at, h in enumerate(rows):
-            for a in range(3):
-                for b in range(3):
-                    lanes = pl.ds((d * count + at) * width, width)
-                    patches[pl.ds((a * 3 + b) * ci, ci), lanes] = row_of(d + a, h + b)
+def forward_rows(count, width, cot_of, w1, bias, delta, before, payload, patches, taps, slopes, grad):
+    co = bias.shape[1]
+    depth = patches.shape[1] // (count * width)
     taps[...] = jnp.dot(w1[...], patches[...], preferred_element_type=F32)
-    shift_bias = jnp.broadcast_to(bias[...], (co, width))
+    shift_bias = jnp.broadcast_to(bias[...], (width, co)).T
     bias_acc = jnp.zeros((co, width), F32)
     for d in range(depth):
-        for at, h in enumerate(rows):
+        for at in range(count):
             lanes = pl.ds((d * count + at) * width, width)
             linear = taps[co : 2 * co, lanes] + shift_bias
             linear = linear + shifted(taps[:co, lanes], -1) + shifted(taps[2 * co :, lanes], 1)
             sigma = 1.0 / (1.0 + jnp.exp(-linear))
-            slope = cot[d, h].astype(F32) * sigma * (1.0 + linear * (1.0 - sigma))
+            slope = cot_of(d, at).astype(F32) * sigma * (1.0 + linear * (1.0 - sigma))
             rounded = slope.astype(BF16)
             delta[at, d] = rounded
             wide = rounded.astype(F32)
@@ -91,53 +91,68 @@
     grad[...] = lax.dot_general(
         patches[...], slopes[...], (((1,), (1,)), ((), ())), preferred_element_type=F32
     )
-    taps_rows = 9 * ci
-    tail = taps_rows + taps_rows // 2
+    rows = grad.shape[0]
+    tail = rows + rows // 2
     total = jnp.sum(bias_acc.T, axis=0, keepdims=True)
     left_over = payload.shape[0] - tail
     row_at = lax.broadcasted_iota(jnp.int32, (left_over, co), 0)
     bias_rows = jnp.where(row_at == 0, jnp.broadcast_to(total, (left_over, co)), 0.0)
     zeros = jnp.zeros((left_over, payload.shape[1] - co), F32)
     for at, value in (
-        (pl.ds(0, taps_rows), grad[:, : 2 * co]),
+        (pl.ds(0, rows), grad[:, : 2 * co]),
         (
-            pl.ds(taps_rows, taps_rows // 2),
-            jnp.concatenate(
-                [grad[: taps_rows // 2, 2 * co :], grad[taps_rows // 2 :, 2 * co :]], axis=1
-            ),
+            pl.ds(rows, rows // 2),
+            jnp.concatenate([grad[: rows // 2, 2 * co :], grad[rows // 2 :, 2 * co :]], axis=1),
         ),
         (pl.ds(tail, left_over), jnp.concatenate([bias_rows, zeros], axis=1)),
     ):
         payload[at, :] = value if before is None else before[at, :] + value
 
 
-def inner_kernel(x, below, above, w1, bias, cot, delta, payload, *scratch):
-    depth, height = x.shape[:2]
-
-    def row_of(d, h):
-        return below[h - 1] if d == 0 else above[h - 1] if d == depth + 1 else x[d - 1, h - 1]
-
-    rows = range(1, height - 1)
-    forward_rows(row_of, rows, w1, bias, cot, delta, None, payload, *scratch)
-
-
-def outer_kernel(x, below, above, left, right, w1, bias, cot, before, delta, payload, *scratch):
-    depth, height = x.shape[:2]
-
-    def row_of(d, h):
-        if h == 0:
-            return left[d]
-        if h == height + 1:
-            return right[d]
-        return below[h - 1] if d == 0 else above[h - 1] if d == depth + 1 else x[d - 1, h - 1]
-
-    rows = (0, height - 1)
-    forward_rows(row_of, rows, w1, bias, cot, delta, before, payload, *scratch)
-
-
-def input_kernel(inner, outer, below, above, left, right, w2, out, patches):
-    co, width = inner.shape[2:]
-    depth, height, ci = out.shape[:3]
+def inner_kernel(x, below, above, w1, bias, cot, delta, payload, patches, *scratch):
+    depth, height, ci, width = x.shape
+    count = height - 2
+    for dd in range(depth + 2):
+        for hh in range(height):
+            row = below[hh] if dd == 0 else above[hh] if dd == depth + 1 else x[dd - 1, hh]
+            for a in range(3):
+                for b in range(3):
+                    d, at = dd - a, hh - b
+                    if 0 <= d < depth and 0 <= at < count:
+                        patches[pl.ds((a * 3 + b) * ci, ci), pl.ds((d * count + at) * width, width)] = row
+
+    def cot_of(d, at):
+        return cot[d, at + 1]
+
+    forward_rows(count, width, cot_of, w1, bias, delta, None, payload, patches, *scratch)
+
+
+def outer_kernel(last, x, below, above, side, w1, bias, cot, before, delta, payload, patches, *scratch):
+    depth, height, ci, width = x.shape
+    flag = last[0]
+    for dd in range(depth + 2):
+        for part in range(3):
+            if part == 2:
+                row, b = side[dd], 2 * flag
+            else:
+                h = flag * (height - 2) + part
+                row = below[h] if dd == 0 else above[h] if dd == depth + 1 else x[dd - 1, h]
+                b = part + 1 - flag
+            for a in range(3):
+                d = dd - a
+                if 0 <= d < depth:
+                    to = pl.ds(pl.multiple_of((a * 3 + b) * ci, ci), ci)
+                    patches[to, pl.ds(d * width, width)] = row
+
+    def cot_of(d, at):
+        return cot[d, flag * (height - 1)]
+
+    forward_rows(1, width, cot_of, w1, bias, delta, before, payload, patches, *scratch)
+
+
+def input_kernel(inner, top, bottom, below, above, left, right, w2, out, patches):
+    depth, co, width = top.shape
+    height, ci = out.shape[1:3]
 
     def row_of(d, h):
         if h == 0:
@@ -148,7 +163,7 @@
             return below[h - 1]
         if d == depth + 1:
             return above[h - 1]
-        return outer[0, d - 1] if h == 1 else outer[1, d - 1] if h == height else inner[h - 2, d - 1]
+        return top[d - 1] if h == 1 else bottom[d - 1] if h == height else inner[h - 2, d - 1]
 
     fill_patches(row_of, depth, range(height), patches)
     for d in range(depth):
@@ -180,14 +195,20 @@
     bias_out[...] = full[rows + rows // 2 : rows + rows // 2 + 1, :co]
 
 
-def call(kernel, outs, scratch, flops, *args):
+def call(kernel, outs, scratch, flops, *args, scalar=None):
     size = sum(a.size * a.dtype.itemsize for a in args) + sum(o.size * o.dtype.itemsize for o in outs)
+    specs = {}
+    if scalar is not None:
+        vmem = pl.BlockSpec(memory_space=pltpu.VMEM)
+        specs["in_specs"] = [pl.BlockSpec(memory_space=pltpu.SMEM)] + [vmem] * len(args)
+        args = (scalar.astype(jnp.int32).reshape(1), *args)
     return pl.pallas_call(
         kernel,
         out_shape=outs,
         scratch_shapes=scratch,
         compiler_params=pltpu.CompilerParams(vmem_limit_bytes=40 << 20),
         cost_estimate=pl.CostEstimate(flops=flops, bytes_accessed=size, transcendentals=0),
+        **specs,
     )(*args)
 
 
@@ -229,16 +250,25 @@
     fields = []
     edges = exchange(inputs[:, :, 0], inputs[:, :, -1], "depth")
     edges = [with_layout_constraint(edge, Layout((0, 1, 2, 3))) for edge in edges]
-    edges, weight, bias, cotangent = lax.optimization_barrier((edges, weight, bias, cotangent))
+    sides = []
+    for cube in range(cubes):
+        below, above = (edge[cube].transpose(1, 0, 2) for edge in edges)
+        first_row, last_row = (inputs[cube, :, :, at].transpose(1, 0, 2) for at in (0, -1))
+        sides.append(columns(first_row, last_row, below, above))
+    edges, sides, inputs, weight, bias, cotangent = lax.optimization_barrier(
+        (edges, sides, inputs, weight, bias, cotangent)
+    )
     taps = weight.transpose(2, 3, 4, 1, 0)
     w1 = taps.transpose(2, 4, 0, 1, 3).reshape(3 * co, 9 * ci)
-    column = bias[:, None]
+    bias_row = bias[None]
+    above_first = paired("height")
     for cube in range(cubes):
         below, above = (edge[cube].transpose(1, 0, 2) for edge in edges)
+        second, first = meet(*sides[cube], "height")
         x = inputs[cube].transpose(1, 2, 0, 3)
         cot = cotangent[cube].transpose(1, 2, 0, 3)
 
-        def forward(kernel, rows, *args):
+        def forward(kernel, rows, *args, scalar=None):
             return call(
                 kernel,
                 (jax.ShapeDtypeStruct((rows, depth, co, width), BF16), payload_shape),
@@ -250,20 +280,27 @@
                 ],
                 2 * flops * rows,
                 *args,
+                scalar=scalar,
             )
 
-        inner, part = forward(inner_kernel, height - 2, x, below, above, w1, column, cot)
-        sides = height_halo(x[:, 0], x[:, -1], below, above)
-        outer, part = forward(outer_kernel, 2, x, below, above, *sides, w1, column, cot, part)
+        shared = (x, below, above)
+        inner, part = forward(inner_kernel, height - 2, *shared, w1, bias_row, cot)
+        late, part = forward(
+            outer_kernel, 1, *shared, second, w1, bias_row, cot, part, scalar=~above_first
+        )
+        early, part = forward(
+            outer_kernel, 1, *shared, first, w1, bias_row, cot, part, scalar=above_first
+        )
         total = part if total is None else total + part
+        top = jnp.where(above_first, late[0], early[0])
+        bottom = jnp.where(above_first, early[0], late[0])
 
         def layer(at):
-            return jnp.concatenate([outer[:1, at], inner[:, at], outer[1:, at]], axis=0)
+            return jnp.concatenate([top[at][None], inner[:, at], bottom[at][None]], axis=0)
 
         below, above = exchange(layer(0), layer(-1), "depth")
-        sides = height_halo(outer[0], outer[1], below, above)
-        fields.append((inner, outer, below, above, *sides))
-
+        around = exchange(*columns(top, bottom, below, above), "height")
+        fields.append((inner, top, bottom, below, above, *around))
     total, taps = lax.optimization_barrier((total, taps))
     w2 = jnp.flip(taps, (0, 1)).transpose(2, 3, 0, 1, 4).reshape(3 * ci, 9 * co)
 

time: 36.2 us -> 34.8 us (0.961)
  waiting for transfers between devices: 7.58 us -> 5.82 us
  Pallas kernels: 5.18 us -> 6.23 us
  local copies, waits for them, and re-layouts: 5.3 us -> 4.88 us
    unnamed x10 -> x9, local copies, waits for them, and re-layouts: 3.94 us -> 2.32 us
    ppermute x6, waiting for transfers between devices: 3.44 us -> 2.14 us  [the longest x4 2.13 us: meet(): first = lax.ppermute(jnp.where(even, high_edge, low_edge), axis, inner)]
    slice x0 -> x3, local copies, waits for them, and re-layouts: none -> 1.27 us  [the longest x1 1.26 us: local(): inputs[cube, :, :, at].transpose(1, 0, 2)]
    pallas_call x4 -> x5, Pallas kernels: 5.18 us -> 6.23 us  [call(): pl.pallas_call(kernel, out_shape=outs, scratch_shapes=scratch, compiler_p...]
    ppermute x8, waiting for transfers between devices: 4.14 us -> 3.68 us  [swap(): lax.ppermute(array, axis, [(i, i ^ mask) for i in range(lax.axis_size(axi...]
    select_n x8 -> x9, other arithmetic: 0.98 us -> 0.99 us  [the longest x2 0.82 us: meet(): first = lax.ppermute(jnp.where(even, high_edge, low_edge), axis, inner)]
  transfers between devices with their start and end apart: 14 -> 14, of which waited for: 8 -> 6; matrix products, arithmetic and copies ran while one was open for 9% -> 10% of each run, Pallas kernels for 8% -> 12%
where the time goes in v4:
time: 34.8 us; the launch traced here: 34.5 us
  starting transfers between devices  15.4 us (44%)
  Pallas kernels  6.23 us (18%)
  waiting for transfers between devices  5.82 us (17%)
  local copies, waits for them, and re-layouts  4.88 us (14%)
  other arithmetic  1.17 us (3%)
  between operations  0.96 us (3%)
    ppermute x8, starting transfers between devices, swap(): lax.ppermute(array, axis, [(i, i ^ mask) for i in range(lax.axis_size(axi...  8.36 us
    pallas_call x5, Pallas kernels, call(): pl.pallas_call(kernel, out_shape=outs, scratch_shapes=scratch, compiler_p...  6.23 us
    ppermute x2, starting transfers between devices, meet(): second = lax.ppermute(jnp.where(even, low_edge, high_edge), axis, outer)  5.13 us
    ppermute x8, waiting for transfers between devices, swap(): lax.ppermute(array, axis, [(i, i ^ mask) for i in range(lax.axis_size(axi...  3.68 us
    unnamed x9, local copies, waits for them, and re-layouts  2.32 us
    ppermute x4, waiting for transfers between devices, meet(): first = lax.ppermute(jnp.where(even, high_edge, low_edge), axis, inner)  2.13 us
    ppermute x4, starting transfers between devices, meet(): first = lax.ppermute(jnp.where(even, high_edge, low_edge), axis, inner)  1.95 us
    slice x1, local copies, waits for them, and re-layouts, local(): inputs[cube, :, :, at].transpose(1, 0, 2)  1.26 us
  transfers between devices with their start and end apart: 14, of which 6 were waited for; matrix products, arithmetic and copies ran while one was open for 10% of the time, Pallas kernels for 12%

profile of v4, /device:TPU:0, one launch (start us, length us, event | category | flops | bytes accessed | tf_op | source)
XLA Modules:
  0.0 34.5 jit_solution(17767824024575647202)
XLA Ops:
  0.6 0.8 %fusion = bf16[1,32,4,128]{3,2,1,0:T(4,128)(2,1)S(1)} fusion(bf16[1,32,8,4,128]{4,3,2,1,0:T(4,128)(2,1)} %param.4, pred[]{:T(512)S(6)} %eq.31), kind=kLoop, calls=%fused_computation.31 | loop fusion | flops 16384 | bytes 98305 | tf_op jit(solution)/shard_map/jit(_where)/select_n | solution.py:29
  2.0 1.3 %fusion.3 = (bf16[1,32,8,1,128]{4,3,2,1,0:T(2,128)(2,1)S(1)}, bf16[1,32,8,1,128]{4,3,2,1,0:T(2,128)(2,1)S(1)}) fusion(bf16[1,32,8,4,128]{4,3,2,1,0:T(4,128)(2,1)} %param.4), kind=kLoop, calls=%fused_computation.44 | loop fusion | bytes 262144 | tf_op jit(solution)/shard_map/slice | solution.py:256
  3.5 3.5 %collective-permute-start.2 = (bf16[10,32,128]{2,1,0:T(8,128)(2,1)S(1)}, bf16[10,32,128]{2,1,0:T(8,128)(2,1)S(1)}, u32[]{:S(2)}, u32[]{:S(2)}) collective-permute-start(bf16[10,32,128]{2,1,0:T(8,128)(2,1)S(1)} %get-tuple-element.63), channel_id=1, source_target_pairs={{0,12},{4,8},{8,4},{12,0},{1,13},{5,9},{9,5},{13,1},{2,14},{6,10},... | collective-permute-start | bytes 245768 | tf_op jit(solution)/shard_map/ppermute | solution.py:33
  7.0 0.5 %collective-permute-start.1 = (bf16[10,32,128]{2,1,0:T(8,128)(2,1)S(1)}, bf16[10,32,128]{2,1,0:T(8,128)(2,1)S(1)}, u32[]{:S(2)}, u32[]{:S(2)}) collective-permute-start(bf16[10,32,128]{2,1,0:T(8,128)(2,1)S(1)} %get-tuple-element.64), channel_id=1, source_target_pairs={{0,4},{4,0},{8,12},{12,8},{1,5},{5,1},{9,13},{13,9},{2,6},{6,2},{1... | collective-permute-start | bytes 245768 | tf_op jit(solution)/shard_map/ppermute | solution.py:29
  8.5 0.5 %copy-done.3 = bf16[1,64,8,4,128]{4,3,2,1,0:T(4,128)(2,1)S(1)} copy-done((bf16[1,64,8,4,128]{4,3,2,1,0:T(4,128)(2,1)S(1)}, bf16[1,64,8,4,128]{4,3,2,1,0:T(4,128)(2,1)}, u32[]{:S(2)}) %copy-start.3) | copy-done | bytes 524312
  9.2 0.6 %copy-done = f32[64]{0:T(128)S(1)} copy-done((f32[64]{0:T(128)S(1)}, f32[64]{0:T(128)}, u32[]{:S(2)}) %copy-start) | copy-done | bytes 280
  9.9 1.7 %shard_map.67 = (bf16[2,8,64,128]{3,2,1,0:T(8,128)(2,1)S(1)}, f32[448,128]{1,0:T(8,128)S(1)}) custom-call(bf16[8,4,32,128]{3,2,1,0:T(8,128)(2,1)S(1)} %bitcast.77, bf16[4,32,128]{2,1,0:T(8,128)(2,1)S(1)} %bitcast.84, bf16[4,32,128]{2,1,0:T(8,128)(2,1)S(1)} %bitcast.87, bf16[192,288]{1,0:T(8,128)(2,1)S(1)} %copy.35.w1, f32[1,64]{1,0:T(1,128)S(1)} %bitcast.91, ...), custom_call_target="tpu_custom_call" | custom-call | flops 452984832 | bytes 1454336 | tf_op jit(solution)/shard_map/pallas_call | solution.py:205
  11.6 1.2 %shard_map.68 = (bf16[1,8,64,128]{3,2,1,0:T(8,128)(2,1)S(1)}, f32[448,128]{1,0:T(8,128)S(1)}) custom-call(s32[1]{0:T(128)} %bitcast.22.last, bf16[8,4,32,128]{3,2,1,0:T(8,128)(2,1)S(1)} %bitcast.78, bf16[4,32,128]{2,1,0:T(8,128)(2,1)S(1)} %bitcast.85, bf16[4,32,128]{2,1,0:T(8,128)(2,1)S(1)} %bitcast.88, ...), custom_call_target="tpu_custom_call" | custom-call | flops 226492416 | bytes 1634560 | tf_op jit(solution)/shard_map/pallas_call | solution.py:205
  12.8 1.2 %shard_map.69 = (bf16[1,8,64,128]{3,2,1,0:T(8,128)(2,1)S(1)}, f32[448,128]{1,0:T(8,128)S(1)}) custom-call(s32[1]{0:T(128)} %bitcast.last, bf16[8,4,32,128]{3,2,1,0:T(8,128)(2,1)S(1)} %bitcast.79, bf16[4,32,128]{2,1,0:T(8,128)(2,1)S(1)} %bitcast.86, bf16[4,32,128]{2,1,0:T(8,128)(2,1)S(1)} %bitcast.89, bf16[10,32,128]{2,1,0:T(8,128)(2,1)S(1)} %collective-permute-done.1.side, ...), custom_call_target="tpu_custom_call" | custom-call | flops 226492416 | bytes 1634560 | tf_op jit(solution)/shard_map/pallas_call | solution.py:205
  15.2 0.6 %collective-permute-done.10 = bf16[4,64,128]{2,1,0:T(8,128)(2,1)S(1)} collective-permute-done((bf16[4,64,128]{2,1,0:T(8,128)(2,1)S(1)}, bf16[4,64,128]{2,1,0:T(8,128)(2,1)S(1)}, u32[]{:S(2)}, u32[]{:S(2)}) %collective-permute-start.10) | collective-permute-done | bytes 65568 | tf_op jit(solution)/shard_map/ppermute | solution.py:29
  15.9 1.6 %collective-permute-start.6 = (bf16[224,128]{1,0:T(8,128)(2,1)S(1)}, bf16[224,128]{1,0:T(8,128)(2,1)S(1)}, u32[]{:S(2)}, u32[]{:S(2)}) collective-permute-start(bf16[224,128]{1,0:T(8,128)(2,1)S(1)} %get-tuple-element.49), channel_id=1, source_target_pairs={{0,12},{4,8},{8,4},{12,0},{1,13},{5,9},{9,5},{13,1},{2,14},{6,10},... | collective-permute-start | bytes 172040 | tf_op jit(solution)/shard_map/ppermute | solution.py:51
  17.5 1.1 %collective-permute-start.5 = (bf16[224,128]{1,0:T(8,128)(2,1)S(1)}, bf16[224,128]{1,0:T(8,128)(2,1)S(1)}, u32[]{:S(2)}, u32[]{:S(2)}) collective-permute-start(bf16[224,128]{1,0:T(8,128)(2,1)S(1)} %get-tuple-element.49), channel_id=1, source_target_pairs={{0,8},{4,12},{8,0},{12,4},{1,9},{5,13},{9,1},{13,5},{2,10},{6,14},... | collective-permute-start | bytes 172040 | tf_op jit(solution)/shard_map/ppermute | solution.py:51
  18.6 0.9 %collective-permute-start.4 = (bf16[224,128]{1,0:T(8,128)(2,1)S(1)}, bf16[224,128]{1,0:T(8,128)(2,1)S(1)}, u32[]{:S(2)}, u32[]{:S(2)}) collective-permute-start(bf16[224,128]{1,0:T(8,128)(2,1)S(1)} %get-tuple-element.49), channel_id=1, source_target_pairs={{0,4},{4,0},{8,12},{12,8},{1,5},{5,1},{9,13},{13,9},{2,6},{6,2},{1... | collective-permute-start | bytes 172040 | tf_op jit(solution)/shard_map/ppermute | solution.py:51
  19.5 1.6 %collective-permute-start.11 = (bf16[10,64,128]{2,1,0:T(8,128)(2,1)S(1)}, bf16[10,64,128]{2,1,0:T(8,128)(2,1)S(1)}, u32[]{:S(2)}, u32[]{:S(2)}) collective-permute-start(bf16[10,64,128]{2,1,0:T(8,128)(2,1)S(1)} %get-tuple-element.53), channel_id=1, source_target_pairs={{0,12},{4,8},{8,4},{12,0},{1,13},{5,9},{9,5},{13,1},{2,14},{6,10},... | collective-permute-start | bytes 491528 | tf_op jit(solution)/shard_map/ppermute | solution.py:33
  21.1 0.5 %collective-permute-start.12 = (bf16[10,64,128]{2,1,0:T(8,128)(2,1)S(1)}, bf16[10,64,128]{2,1,0:T(8,128)(2,1)S(1)}, u32[]{:S(2)}, u32[]{:S(2)}) collective-permute-start(bf16[10,64,128]{2,1,0:T(8,128)(2,1)S(1)} %get-tuple-element.54), channel_id=1, source_target_pairs={{0,4},{4,0},{8,12},{12,8},{1,5},{5,1},{9,13},{13,9},{2,6},{6,2},{1... | collective-permute-start | bytes 491528 | tf_op jit(solution)/shard_map/ppermute | solution.py:29
  21.6 0.6 %collective-permute-done.5 = bf16[224,128]{1,0:T(8,128)(2,1)S(1)} collective-permute-done((bf16[224,128]{1,0:T(8,128)(2,1)S(1)}, bf16[224,128]{1,0:T(8,128)(2,1)S(1)}, u32[]{:S(2)}, u32[]{:S(2)}) %collective-permute-start.5) | collective-permute-done | bytes 57376 | tf_op jit(solution)/shard_map/ppermute | solution.py:51
  22.2 1.1 %collective-permute-done.4 = bf16[224,128]{1,0:T(8,128)(2,1)S(1)} collective-permute-done((bf16[224,128]{1,0:T(8,128)(2,1)S(1)}, bf16[224,128]{1,0:T(8,128)(2,1)S(1)}, u32[]{:S(2)}, u32[]{:S(2)}) %collective-permute-start.4) | collective-permute-done | bytes 57376 | tf_op jit(solution)/shard_map/ppermute | solution.py:51
  23.3 3.7 %collective-permute-start.9 = (bf16[224,128]{1,0:T(8,128)(2,1)S(1)}, bf16[224,128]{1,0:T(8,128)(2,1)S(1)}, u32[]{:S(2)}, u32[]{:S(2)}) collective-permute-start(bf16[224,128]{1,0:T(8,128)(2,1)S(1)} %fusion.1), channel_id=1, source_target_pairs={{0,3},{1,2},{2,1},{3,0},{4,7},{5,6},{6,5},{7,4},{8,11},{9,10},{10,... | collective-permute-start | bytes 172040 | tf_op jit(solution)/shard_map/ppermute | solution.py:51
  27.0 0.8 %collective-permute-start.7 = (bf16[224,128]{1,0:T(8,128)(2,1)S(1)}, bf16[224,128]{1,0:T(8,128)(2,1)S(1)}, u32[]{:S(2)}, u32[]{:S(2)}) collective-permute-start(bf16[224,128]{1,0:T(8,128)(2,1)S(1)} %fusion.1), channel_id=1, source_target_pairs={{0,1},{1,0},{2,3},{3,2},{4,5},{5,4},{6,7},{7,6},{8,9},{9,8},{10,11... | collective-permute-start | bytes 172040 | tf_op jit(solution)/shard_map/ppermute | solution.py:51
  27.8 1.6 %collective-permute-done.12 = bf16[10,64,128]{2,1,0:T(8,128)(2,1)S(1)} collective-permute-done((bf16[10,64,128]{2,1,0:T(8,128)(2,1)S(1)}, bf16[10,64,128]{2,1,0:T(8,128)(2,1)S(1)}, u32[]{:S(2)}, u32[]{:S(2)}) %collective-permute-start.12) | collective-permute-done | bytes 163872 | tf_op jit(solution)/shard_map/ppermute | solution.py:29
  29.4 1.2 %shard_map.70 = bf16[8,4,32,128]{3,2,1,0:T(8,128)(2,1)S(1)} custom-call(bf16[2,8,64,128]{3,2,1,0:T(8,128)(2,1)S(1)} %get-tuple-element.35.inner, bf16[8,64,128]{2,1,0:T(8,128)(2,1)S(1)} %bitcast.83, bf16[8,64,128]{2,1,0:T(8,128)(2,1)S(1)} %bitcast.81, bf16[4,64,128]{2,1,0:T(8,128)(2,1)S(1)} %get-tuple-element.74.below, ...), custom_call_target="tpu_custom_call" | custom-call | flops 452984832 | bytes 1355776 | tf_op jit(solution)/shard_map/pallas_call | solution.py:205
  30.6 1.6 %collective-permute-done.8 = bf16[224,128]{1,0:T(8,128)(2,1)S(1)} collective-permute-done((bf16[224,128]{1,0:T(8,128)(2,1)S(1)}, bf16[224,128]{1,0:T(8,128)(2,1)S(1)}, u32[]{:S(2)}, u32[]{:S(2)}) %collective-permute-start.8) | collective-permute-done | bytes 57376 | tf_op jit(solution)/shard_map/ppermute | solution.py:51
  32.3 0.8 %copy.39 = bf16[1,32,8,4,128]{4,3,2,1,0:T(4,128)(2,1)} copy(bf16[1,32,8,4,128]{4,1,3,2,0:T(8,128)(2,1)S(1)} %bitcast.90) | data formatting | bytes 524288
  33.6 0.9 %shard_map.71 = (f32[864,64]{1,0:T(8,128)}, f32[1,64]{1,0:T(1,128)}) custom-call(f32[224,128]{1,0:T(8,128)S(1)} %get-tuple-element.62.refs_0_, f32[224,128]{1,0:T(8,128)S(1)} %get-tuple-element.61.refs_1_), custom_call_target="tpu_custom_call" | custom-call | flops 57344 | bytes 450816 | tf_op jit(solution)/shard_map/pallas_call | solution.py:205
  (54 shorter events, 3.7 us)
Async XLA Ops:
  1.4 1.9 %collective-permute-start = (bf16[1,32,4,128]{3,2,1,0:T(4,128)(2,1)S(1)}, bf16[1,32,4,128]{3,2,1,0:T(4,128)(2,1)S(1)}, u32[]{:S(2)}, u32[]{:S(2)}) collective-permute-start(bf16[1,32,4,128]{3,2,1,0:T(4,128)(2,1)S(1)} %fusion), channel_id=1, source_target_pairs={{0,16},{16,0},{1,17},{17,1},{2,18},{18,2},{3,19},{19,3},{4,20},{20... | collective-permute-start | bytes 98312 | tf_op jit(solution)/shard_map/ppermute | solution.py:29
  3.4 4.1 %copy-start.1 = (bf16[1,32,8,4,128]{4,3,2,1,0:T(4,128)(2,1)S(1)}, bf16[1,32,8,4,128]{4,3,2,1,0:T(4,128)(2,1)}, u32[]{:S(2)}) copy-start(bf16[1,32,8,4,128]{4,3,2,1,0:T(4,128)(2,1)} %param.4) | copy-start | bytes 786436
  3.5 8.0 %collective-permute-start.2 = (bf16[10,32,128]{2,1,0:T(8,128)(2,1)S(1)}, bf16[10,32,128]{2,1,0:T(8,128)(2,1)S(1)}, u32[]{:S(2)}, u32[]{:S(2)}) collective-permute-start(bf16[10,32,128]{2,1,0:T(8,128)(2,1)S(1)} %get-tuple-element.63), channel_id=1, source_target_pairs={{0,12},{4,8},{8,4},{12,0},{1,13},{5,9},{9,5},{13,1},{2,14},{6,10},... | collective-permute-start | bytes 245768 | tf_op jit(solution)/shard_map/ppermute | solution.py:33
  7.0 0.9 %copy-start.2 = (bf16[64,32,3,3,3]{0,1,4,3,2:T(8,128)(2,1)S(1)}, bf16[64,32,3,3,3]{0,1,4,3,2:T(8,128)(2,1)}, u32[]{:S(2)}) copy-start(bf16[64,32,3,3,3]{0,1,4,3,2:T(8,128)(2,1)} %param.5) | copy-start | bytes 331780
  7.0 5.8 %collective-permute-start.1 = (bf16[10,32,128]{2,1,0:T(8,128)(2,1)S(1)}, bf16[10,32,128]{2,1,0:T(8,128)(2,1)S(1)}, u32[]{:S(2)}, u32[]{:S(2)}) collective-permute-start(bf16[10,32,128]{2,1,0:T(8,128)(2,1)S(1)} %get-tuple-element.64), channel_id=1, source_target_pairs={{0,4},{4,0},{8,12},{12,8},{1,5},{5,1},{9,13},{13,9},{2,6},{6,2},{1... | collective-permute-start | bytes 245768 | tf_op jit(solution)/shard_map/ppermute | solution.py:29
  8.0 1.0 %copy-start.3 = (bf16[1,64,8,4,128]{4,3,2,1,0:T(4,128)(2,1)S(1)}, bf16[1,64,8,4,128]{4,3,2,1,0:T(4,128)(2,1)}, u32[]{:S(2)}) copy-start(bf16[1,64,8,4,128]{4,3,2,1,0:T(4,128)(2,1)} %param.7) | copy-start | bytes 1572868
  9.2 0.7 %copy-start = (f32[64]{0:T(128)S(1)}, f32[64]{0:T(128)}, u32[]{:S(2)}) copy-start(f32[64]{0:T(128)} %param.6) | copy-start | bytes 772
  14.1 1.7 %collective-permute-start.3 = (f32[224,128]{1,0:T(8,128)S(1)}, f32[224,128]{1,0:T(8,128)S(1)}, u32[]{:S(2)}, u32[]{:S(2)}) collective-permute-start(f32[224,128]{1,0:T(8,128)S(1)} %slice_select_fusion), channel_id=1, source_target_pairs={{0,16},{16,0},{1,17},{17,1},{2,18},{18,2},{3,19},{19,3},{4,20},{20... | collective-permute-start | bytes 344072 | tf_op jit(solution)/shard_map/ppermute | solution.py:51
  14.5 1.3 %collective-permute-start.10 = (bf16[4,64,128]{2,1,0:T(8,128)(2,1)S(1)}, bf16[4,64,128]{2,1,0:T(8,128)(2,1)S(1)}, u32[]{:S(2)}, u32[]{:S(2)}) collective-permute-start(bf16[4,64,128]{2,1,0:T(8,128)(2,1)S(1)} %maximum_select_fusion), channel_id=1, source_target_pairs={{0,16},{16,0},{1,17},{17,1},{2,18},{18,2},{3,19},{19,3},{4,20},{20... | collective-permute-start | bytes 196616 | tf_op jit(solution)/shard_map/ppermute | solution.py:29
  15.9 5.8 %collective-permute-start.6 = (bf16[224,128]{1,0:T(8,128)(2,1)S(1)}, bf16[224,128]{1,0:T(8,128)(2,1)S(1)}, u32[]{:S(2)}, u32[]{:S(2)}) collective-permute-start(bf16[224,128]{1,0:T(8,128)(2,1)S(1)} %get-tuple-element.49), channel_id=1, source_target_pairs={{0,12},{4,8},{8,4},{12,0},{1,13},{5,9},{9,5},{13,1},{2,14},{6,10},... | collective-permute-start | bytes 172040 | tf_op jit(solution)/shard_map/ppermute | solution.py:51
  17.5 4.7 %collective-permute-start.5 = (bf16[224,128]{1,0:T(8,128)(2,1)S(1)}, bf16[224,128]{1,0:T(8,128)(2,1)S(1)}, u32[]{:S(2)}, u32[]{:S(2)}) collective-permute-start(bf16[224,128]{1,0:T(8,128)(2,1)S(1)} %get-tuple-element.49), channel_id=1, source_target_pairs={{0,8},{4,12},{8,0},{12,4},{1,9},{5,13},{9,1},{13,5},{2,10},{6,14},... | collective-permute-start | bytes 172040 | tf_op jit(solution)/shard_map/ppermute | solution.py:51
  18.6 4.7 %collective-permute-start.4 = (bf16[224,128]{1,0:T(8,128)(2,1)S(1)}, bf16[224,128]{1,0:T(8,128)(2,1)S(1)}, u32[]{:S(2)}, u32[]{:S(2)}) collective-permute-start(bf16[224,128]{1,0:T(8,128)(2,1)S(1)} %get-tuple-element.49), channel_id=1, source_target_pairs={{0,4},{4,0},{8,12},{12,8},{1,5},{5,1},{9,13},{13,9},{2,6},{6,2},{1... | collective-permute-start | bytes 172040 | tf_op jit(solution)/shard_map/ppermute | solution.py:51
  19.5 8.3 %collective-permute-start.11 = (bf16[10,64,128]{2,1,0:T(8,128)(2,1)S(1)}, bf16[10,64,128]{2,1,0:T(8,128)(2,1)S(1)}, u32[]{:S(2)}, u32[]{:S(2)}) collective-permute-start(bf16[10,64,128]{2,1,0:T(8,128)(2,1)S(1)} %get-tuple-element.53), channel_id=1, source_target_pairs={{0,12},{4,8},{8,4},{12,0},{1,13},{5,9},{9,5},{13,1},{2,14},{6,10},... | collective-permute-start | bytes 491528 | tf_op jit(solution)/shard_map/ppermute | solution.py:33
  21.1 8.3 %collective-permute-start.12 = (bf16[10,64,128]{2,1,0:T(8,128)(2,1)S(1)}, bf16[10,64,128]{2,1,0:T(8,128)(2,1)S(1)}, u32[]{:S(2)}, u32[]{:S(2)}) collective-permute-start(bf16[10,64,128]{2,1,0:T(8,128)(2,1)S(1)} %get-tuple-element.54), channel_id=1, source_target_pairs={{0,4},{4,0},{8,12},{12,8},{1,5},{5,1},{9,13},{13,9},{2,6},{6,2},{1... | collective-permute-start | bytes 491528 | tf_op jit(solution)/shard_map/ppermute | solution.py:29
  23.3 7.3 %collective-permute-start.9 = (bf16[224,128]{1,0:T(8,128)(2,1)S(1)}, bf16[224,128]{1,0:T(8,128)(2,1)S(1)}, u32[]{:S(2)}, u32[]{:S(2)}) collective-permute-start(bf16[224,128]{1,0:T(8,128)(2,1)S(1)} %fusion.1), channel_id=1, source_target_pairs={{0,3},{1,2},{2,1},{3,0},{4,7},{5,6},{6,5},{7,4},{8,11},{9,10},{10,... | collective-permute-start | bytes 172040 | tf_op jit(solution)/shard_map/ppermute | solution.py:51
  27.0 5.2 %collective-permute-start.8 = (bf16[224,128]{1,0:T(8,128)(2,1)S(1)}, bf16[224,128]{1,0:T(8,128)(2,1)S(1)}, u32[]{:S(2)}, u32[]{:S(2)}) collective-permute-start(bf16[224,128]{1,0:T(8,128)(2,1)S(1)} %fusion.1), channel_id=1, source_target_pairs={{0,2},{1,3},{2,0},{3,1},{4,6},{5,7},{6,4},{7,5},{8,10},{9,11},{10,... | collective-permute-start | bytes 172040 | tf_op jit(solution)/shard_map/ppermute | solution.py:51
  27.0 5.2 %collective-permute-start.7 = (bf16[224,128]{1,0:T(8,128)(2,1)S(1)}, bf16[224,128]{1,0:T(8,128)(2,1)S(1)}, u32[]{:S(2)}, u32[]{:S(2)}) collective-permute-start(bf16[224,128]{1,0:T(8,128)(2,1)S(1)} %fusion.1), channel_id=1, source_target_pairs={{0,1},{1,0},{2,3},{3,2},{4,5},{5,4},{6,7},{7,6},{8,9},{9,8},{10,11... | collective-permute-start | bytes 172040 | tf_op jit(solution)/shard_map/ppermute | solution.py:51
  32.2 1.4 %collective-permute-start.13 = (f32[224,128]{1,0:T(8,128)S(1)}, f32[224,128]{1,0:T(8,128)S(1)}, u32[]{:S(2)}, u32[]{:S(2)}) collective-permute-start(f32[224,128]{1,0:T(8,128)S(1)} %add_add_fusion), channel_id=1, source_target_pairs={{0,16},{16,0},{1,17},{17,1},{2,18},{18,2},{3,19},{19,3},{4,20},{20... | collective-permute-start | bytes 344072 | tf_op jit(solution)/shard_map/ppermute | solution.py:51

commit v5 on v4

--- a/solution.py
+++ b/solution.py
@@ -2,7 +2,6 @@
 import jax.numpy as jnp
 from jax import lax
 from jax.experimental import pallas as pl
-from jax.experimental.layout import Layout, with_layout_constraint
 from jax.experimental.pallas import tpu as pltpu
 from jax.sharding import PartitionSpec as P
 
@@ -195,6 +194,27 @@
     bias_out[...] = full[rows + rows // 2 : rows + rows // 2 + 1, :co]
 
 
+def load_kernel(*refs):
+    count = len(refs) // 2
+    done = refs[-1]
+    copies = [pltpu.make_async_copy(refs[i], refs[count + i], done.at[i]) for i in range(count)]
+    for copy in copies:
+        copy.start()
+    for copy in copies:
+        copy.wait()
+
+
+def loaded(*arrays):
+    return pl.pallas_call(
+        load_kernel,
+        out_shape=[jax.ShapeDtypeStruct(a.shape, a.dtype) for a in arrays],
+        in_specs=[pl.BlockSpec(memory_space=pltpu.HBM) for a in arrays],
+        out_specs=[pl.BlockSpec(memory_space=pltpu.VMEM) for a in arrays],
+        scratch_shapes=[pltpu.SemaphoreType.DMA((len(arrays),))],
+        compiler_params=pltpu.CompilerParams(vmem_limit_bytes=16 << 20),
+    )(*(pltpu.with_memory_space_constraint(a, pltpu.HBM) for a in arrays))
+
+
 def call(kernel, outs, scratch, flops, *args, scalar=None):
     size = sum(a.size * a.dtype.itemsize for a in args) + sum(o.size * o.dtype.itemsize for o in outs)
     specs = {}
@@ -248,19 +268,16 @@
     flops = 2 * depth * width * 27 * ci * co
     total = None
     fields = []
+    inputs, taps, bias_row, cotangent = loaded(
+        inputs, weight.transpose(2, 3, 4, 1, 0), bias[None], cotangent
+    )
     edges = exchange(inputs[:, :, 0], inputs[:, :, -1], "depth")
-    edges = [with_layout_constraint(edge, Layout((0, 1, 2, 3))) for edge in edges]
     sides = []
     for cube in range(cubes):
         below, above = (edge[cube].transpose(1, 0, 2) for edge in edges)
         first_row, last_row = (inputs[cube, :, :, at].transpose(1, 0, 2) for at in (0, -1))
         sides.append(columns(first_row, last_row, below, above))
-    edges, sides, inputs, weight, bias, cotangent = lax.optimization_barrier(
-        (edges, sides, inputs, weight, bias, cotangent)
-    )
-    taps = weight.transpose(2, 3, 4, 1, 0)
     w1 = taps.transpose(2, 4, 0, 1, 3).reshape(3 * co, 9 * ci)
-    bias_row = bias[None]
     above_first = paired("height")
     for cube in range(cubes):
         below, above = (edge[cube].transpose(1, 0, 2) for edge in edges)

time: 34.8 us -> 34.9 us (level)
  local copies, waits for them, and re-layouts: 4.88 us -> 2.18 us
  waiting for transfers between devices: 5.82 us -> 7.17 us
  Pallas kernels: 6.23 us -> 7.49 us
  starting transfers between devices: 15.4 us -> 16.6 us
  other arithmetic: 1.17 us -> 0.34 us
    unnamed x9 -> x1, local copies, waits for them, and re-layouts: 2.32 us -> 0.84 us
    ppermute x2, starting transfers between devices: 5.13 us -> 6.53 us  [meet(): second = lax.ppermute(jnp.where(even, low_edge, high_edge), axis, outer)]
    pallas_call x0 -> x1, Pallas kernels: none -> 1.28 us  [loaded(): pl.pallas_call(load_kernel, out_shape=[jax.ShapeDtypeStruct(a.shape, a.dt...]
    slice x1 -> x0, local copies, waits for them, and re-layouts: 1.26 us -> none  [local(): inputs[cube, :, :, at].transpose(1, 0, 2)]
    ppermute x2, waiting for transfers between devices: 0.01 us -> 0.98 us  [meet(): second = lax.ppermute(jnp.where(even, low_edge, high_edge), axis, outer)]
    select_n x2, other arithmetic: 0.82 us -> 0.03 us  [meet(): first = lax.ppermute(jnp.where(even, high_edge, low_edge), axis, inner)]
    ppermute x4, starting transfers between devices: 1.95 us -> 1.47 us  [meet(): first = lax.ppermute(jnp.where(even, high_edge, low_edge), axis, inner)]
    pallas_call x0 -> x3, local copies, waits for them, and re-layouts: none -> 0.42 us  [loaded(): pl.pallas_call(load_kernel, out_shape=[jax.ShapeDtypeStruct(a.shape, a.dt...]
  transfers between devices with their start and end apart: 14 -> 14, of which waited for: 6 -> 9; matrix products, arithmetic and copies ran while one was open for 10% -> 6% of each run, Pallas kernels for 12% -> 12%
where the time goes in v5:
time: 34.9 us; the launch traced here: 34.7 us
  starting transfers between devices  16.6 us (48%)
  Pallas kernels  7.49 us (21%)
  waiting for transfers between devices  7.17 us (21%)
  local copies, waits for them, and re-layouts  2.18 us (6%)
  between operations  0.91 us (3%)
    ppermute x8, starting transfers between devices, swap(): lax.ppermute(array, axis, [(i, i ^ mask) for i in range(lax.axis_size(axi...  8.65 us
    ppermute x2, starting transfers between devices, meet(): second = lax.ppermute(jnp.where(even, low_edge, high_edge), axis, outer)  6.53 us
    pallas_call x5, Pallas kernels, call(): pl.pallas_call(kernel, out_shape=outs, scratch_shapes=scratch, compiler_p...  6.2 us
    ppermute x8, waiting for transfers between devices, swap(): lax.ppermute(array, axis, [(i, i ^ mask) for i in range(lax.axis_size(axi...  3.68 us
    ppermute x4, waiting for transfers between devices, meet(): first = lax.ppermute(jnp.where(even, high_edge, low_edge), axis, inner)  2.51 us
    ppermute x4, starting transfers between devices, meet(): first = lax.ppermute(jnp.where(even, high_edge, low_edge), axis, inner)  1.47 us
    pallas_call x1, Pallas kernels, loaded(): pl.pallas_call(load_kernel, out_shape=[jax.ShapeDtypeStruct(a.shape, a.dt...  1.28 us
    ppermute x2, waiting for transfers between devices, meet(): second = lax.ppermute(jnp.where(even, low_edge, high_edge), axis, outer)  0.98 us
  transfers between devices with their start and end apart: 14, of which 9 were waited for; matrix products, arithmetic and copies ran while one was open for 6% of the time, Pallas kernels for 12%

profile of v5, /device:TPU:0, one launch (start us, length us, event | category | flops | bytes accessed | tf_op | source)
XLA Modules:
  0.0 34.7 jit_solution(4785232776264656604)
XLA Ops:
  0.6 1.3 %shard_map.67 = (bf16[1,32,8,4,128]{4,3,2,1,0:T(4,128)(2,1)S(1)}, bf16[3,3,3,32,64]{4,3,2,1,0:T(8,128)(2,1)S(1)}, f32[1,64]{1,0:T(1,128)S(1)}, bf16[1,64,8,4,128]{4,3,2,1,0:T(4,128)(2,1)S(1)}) custom-call(bf16[1,32,8,4,128]{4,3,2,1,0:T(4,128)(2,1)} %refs_0_.1, bf16[3,3,3,32,64]{4,3,2,1,0:T(8,128)(2,1)} %bitcast.69, f32[1,64]{1,0:T(1,128)} %bitcast.70, ...), custom_call_target="tpu_custom_call" | custom-call | tf_op jit(solution)/shard_map/pallas_call | solution.py:208
  2.1 0.5 %collective-permute-start = (bf16[1,32,4,128]{3,1,2,0:T(8,128)(2,1)S(1)}, bf16[1,32,4,128]{3,1,2,0:T(8,128)(2,1)S(1)}, u32[]{:S(2)}, u32[]{:S(2)}) collective-permute-start(bf16[1,32,4,128]{3,1,2,0:T(8,128)(2,1)S(1)} %fusion), channel_id=1, source_target_pairs={{0,16},{16,0},{1,17},{17,1},{2,18},{18,2},{3,19},{19,3},{4,20},{20... | collective-permute-start | bytes 98312 | tf_op jit(solution)/shard_map/ppermute | solution.py:28
  3.5 3.8 %collective-permute-start.2 = (bf16[10,32,128]{2,1,0:T(8,128)(2,1)S(1)}, bf16[10,32,128]{2,1,0:T(8,128)(2,1)S(1)}, u32[]{:S(2)}, u32[]{:S(2)}) collective-permute-start(bf16[10,32,128]{2,1,0:T(8,128)(2,1)S(1)} %get-tuple-element.57), channel_id=1, source_target_pairs={{0,12},{4,8},{8,4},{12,0},{1,13},{5,9},{9,5},{13,1},{2,14},{6,10},... | collective-permute-start | bytes 245768 | tf_op jit(solution)/shard_map/ppermute | solution.py:32
  7.4 0.5 %collective-permute-start.1 = (bf16[10,32,128]{2,1,0:T(8,128)(2,1)S(1)}, bf16[10,32,128]{2,1,0:T(8,128)(2,1)S(1)}, u32[]{:S(2)}, u32[]{:S(2)}) collective-permute-start(bf16[10,32,128]{2,1,0:T(8,128)(2,1)S(1)} %get-tuple-element.58), channel_id=1, source_target_pairs={{0,4},{4,0},{8,12},{12,8},{1,5},{5,1},{9,13},{13,9},{2,6},{6,2},{1... | collective-permute-start | bytes 245768 | tf_op jit(solution)/shard_map/ppermute | solution.py:28
  7.9 1.6 %shard_map.68 = (bf16[2,8,64,128]{3,2,1,0:T(8,128)(2,1)S(1)}, f32[448,128]{1,0:T(8,128)S(1)}) custom-call(bf16[8,4,32,128]{3,2,1,0:T(8,128)(2,1)S(1)} %bitcast.60, bf16[4,32,128]{2,1,0:T(8,128)(2,1)S(1)} %get-tuple-element.74.below, bf16[4,32,128]{2,1,0:T(8,128)(2,1)S(1)} %get-tuple-element.73.above, bf16[192,288]{1,0:T(8,128)(2,1)S(1)} %copy.27.w1, ...), custom_call_target="tpu_custom_call" | custom-call | flops 452984832 | bytes 1454336 | tf_op jit(solution)/shard_map/pallas_call | solution.py:225
  9.6 1.0 %collective-permute-done.2 = bf16[10,32,128]{2,1,0:T(8,128)(2,1)S(1)} collective-permute-done((bf16[10,32,128]{2,1,0:T(8,128)(2,1)S(1)}, bf16[10,32,128]{2,1,0:T(8,128)(2,1)S(1)}, u32[]{:S(2)}, u32[]{:S(2)}) %collective-permute-start.2) | collective-permute-done | bytes 81952 | tf_op jit(solution)/shard_map/ppermute | solution.py:32
  10.5 1.2 %shard_map.69 = (bf16[1,8,64,128]{3,2,1,0:T(8,128)(2,1)S(1)}, f32[448,128]{1,0:T(8,128)S(1)}) custom-call(s32[1]{0:T(128)} %bitcast.19.last, bf16[8,4,32,128]{3,2,1,0:T(8,128)(2,1)S(1)} %bitcast.61, bf16[4,32,128]{2,1,0:T(8,128)(2,1)S(1)} %get-tuple-element.74.below, bf16[4,32,128]{2,1,0:T(8,128)(2,1)S(1)} %get-tuple-element.73.above, ...), custom_call_target="tpu_custom_call" | custom-call | flops 226492416 | bytes 1634560 | tf_op jit(solution)/shard_map/pallas_call | solution.py:225
  11.8 0.4 %collective-permute-done.1.side = bf16[10,32,128]{2,1,0:T(8,128)(2,1)S(1)} collective-permute-done((bf16[10,32,128]{2,1,0:T(8,128)(2,1)S(1)}, bf16[10,32,128]{2,1,0:T(8,128)(2,1)S(1)}, u32[]{:S(2)}, u32[]{:S(2)}) %collective-permute-start.1) | collective-permute-done | bytes 81952 | tf_op jit(solution)/shard_map/ppermute | solution.py:28
  12.2 1.2 %shard_map.70 = (bf16[1,8,64,128]{3,2,1,0:T(8,128)(2,1)S(1)}, f32[448,128]{1,0:T(8,128)S(1)}) custom-call(s32[1]{0:T(128)} %bitcast.last, bf16[8,4,32,128]{3,2,1,0:T(8,128)(2,1)S(1)} %bitcast.62, bf16[4,32,128]{2,1,0:T(8,128)(2,1)S(1)} %get-tuple-element.74.below, bf16[4,32,128]{2,1,0:T(8,128)(2,1)S(1)} %get-tuple-element.73.above, ...), custom_call_target="tpu_custom_call" | custom-call | flops 226492416 | bytes 1634560 | tf_op jit(solution)/shard_map/pallas_call | solution.py:225
  14.0 0.6 %collective-permute-start.3 = (f32[224,128]{1,0:T(8,128)S(1)}, f32[224,128]{1,0:T(8,128)S(1)}, u32[]{:S(2)}, u32[]{:S(2)}) collective-permute-start(f32[224,128]{1,0:T(8,128)S(1)} %slice_select_fusion), channel_id=1, source_target_pairs={{0,16},{16,0},{1,17},{17,1},{2,18},{18,2},{3,19},{19,3},{4,20},{20... | collective-permute-start | bytes 344072 | tf_op jit(solution)/shard_map/ppermute | solution.py:50
  14.9 0.6 %collective-permute-done.3 = f32[224,128]{1,0:T(8,128)S(1)} collective-permute-done((f32[224,128]{1,0:T(8,128)S(1)}, f32[224,128]{1,0:T(8,128)S(1)}, u32[]{:S(2)}, u32[]{:S(2)}) %collective-permute-start.3) | collective-permute-done | bytes 114720 | tf_op jit(solution)/shard_map/ppermute | solution.py:50
  15.6 2.7 %collective-permute-start.6 = (bf16[224,128]{1,0:T(8,128)(2,1)S(1)}, bf16[224,128]{1,0:T(8,128)(2,1)S(1)}, u32[]{:S(2)}, u32[]{:S(2)}) collective-permute-start(bf16[224,128]{1,0:T(8,128)(2,1)S(1)} %get-tuple-element.41), channel_id=1, source_target_pairs={{0,12},{4,8},{8,4},{12,0},{1,13},{5,9},{9,5},{13,1},{2,14},{6,10},... | collective-permute-start | bytes 172040 | tf_op jit(solution)/shard_map/ppermute | solution.py:50
  18.3 0.5 %collective-permute-start.5 = (bf16[224,128]{1,0:T(8,128)(2,1)S(1)}, bf16[224,128]{1,0:T(8,128)(2,1)S(1)}, u32[]{:S(2)}, u32[]{:S(2)}) collective-permute-start(bf16[224,128]{1,0:T(8,128)(2,1)S(1)} %get-tuple-element.41), channel_id=1, source_target_pairs={{0,8},{4,12},{8,0},{12,4},{1,9},{5,13},{9,1},{13,5},{2,10},{6,14},... | collective-permute-start | bytes 172040 | tf_op jit(solution)/shard_map/ppermute | solution.py:50
  19.2 2.7 %collective-permute-start.11 = (bf16[10,64,128]{2,1,0:T(8,128)(2,1)S(1)}, bf16[10,64,128]{2,1,0:T(8,128)(2,1)S(1)}, u32[]{:S(2)}, u32[]{:S(2)}) collective-permute-start(bf16[10,64,128]{2,1,0:T(8,128)(2,1)S(1)} %get-tuple-element.45), channel_id=1, source_target_pairs={{0,12},{4,8},{8,4},{12,0},{1,13},{5,9},{9,5},{13,1},{2,14},{6,10},... | collective-permute-start | bytes 491528 | tf_op jit(solution)/shard_map/ppermute | solution.py:32
  21.9 0.3 collective-permute-start.12
  22.5 1.1 %collective-permute-done.4 = bf16[224,128]{1,0:T(8,128)(2,1)S(1)} collective-permute-done((bf16[224,128]{1,0:T(8,128)(2,1)S(1)}, bf16[224,128]{1,0:T(8,128)(2,1)S(1)}, u32[]{:S(2)}, u32[]{:S(2)}) %collective-permute-start.4) | collective-permute-done | bytes 57376 | tf_op jit(solution)/shard_map/ppermute | solution.py:50
  23.6 3.7 %collective-permute-start.9 = (bf16[224,128]{1,0:T(8,128)(2,1)S(1)}, bf16[224,128]{1,0:T(8,128)(2,1)S(1)}, u32[]{:S(2)}, u32[]{:S(2)}) collective-permute-start(bf16[224,128]{1,0:T(8,128)(2,1)S(1)} %fusion.1), channel_id=1, source_target_pairs={{0,3},{1,2},{2,1},{3,0},{4,7},{5,6},{6,5},{7,4},{8,11},{9,10},{10,... | collective-permute-start | bytes 172040 | tf_op jit(solution)/shard_map/ppermute | solution.py:50
  27.3 0.8 %collective-permute-start.7 = (bf16[224,128]{1,0:T(8,128)(2,1)S(1)}, bf16[224,128]{1,0:T(8,128)(2,1)S(1)}, u32[]{:S(2)}, u32[]{:S(2)}) collective-permute-start(bf16[224,128]{1,0:T(8,128)(2,1)S(1)} %fusion.1), channel_id=1, source_target_pairs={{0,1},{1,0},{2,3},{3,2},{4,5},{5,4},{6,7},{7,6},{8,9},{9,8},{10,11... | collective-permute-start | bytes 172040 | tf_op jit(solution)/shard_map/ppermute | solution.py:50
  28.1 1.9 %collective-permute-done.12 = bf16[10,64,128]{2,1,0:T(8,128)(2,1)S(1)} collective-permute-done((bf16[10,64,128]{2,1,0:T(8,128)(2,1)S(1)}, bf16[10,64,128]{2,1,0:T(8,128)(2,1)S(1)}, u32[]{:S(2)}, u32[]{:S(2)}) %collective-permute-start.12) | collective-permute-done | bytes 163872 | tf_op jit(solution)/shard_map/ppermute | solution.py:28
  30.0 1.2 %shard_map.71 = bf16[8,4,32,128]{3,2,1,0:T(8,128)(2,1)S(1)} custom-call(bf16[2,8,64,128]{3,2,1,0:T(8,128)(2,1)S(1)} %get-tuple-element.27.inner, bf16[8,64,128]{2,1,0:T(8,128)(2,1)S(1)} %bitcast.67, bf16[8,64,128]{2,1,0:T(8,128)(2,1)S(1)} %bitcast.65, bf16[4,64,128]{2,1,0:T(8,128)(2,1)S(1)} %get-tuple-element.68.below, ...), custom_call_target="tpu_custom_call" | custom-call | flops 452984832 | bytes 1355776 | tf_op jit(solution)/shard_map/pallas_call | solution.py:225
  31.2 1.2 %collective-permute-done.8 = bf16[224,128]{1,0:T(8,128)(2,1)S(1)} collective-permute-done((bf16[224,128]{1,0:T(8,128)(2,1)S(1)}, bf16[224,128]{1,0:T(8,128)(2,1)S(1)}, u32[]{:S(2)}, u32[]{:S(2)}) %collective-permute-start.8) | collective-permute-done | bytes 57376 | tf_op jit(solution)/shard_map/ppermute | solution.py:50
  32.5 0.8 %copy.31 = bf16[1,32,8,4,128]{4,3,2,1,0:T(4,128)(2,1)} copy(bf16[1,32,8,4,128]{4,1,3,2,0:T(8,128)(2,1)S(1)} %bitcast.68) | data formatting | bytes 524288
  33.3 0.5 %collective-permute-done.13 = f32[224,128]{1,0:T(8,128)S(1)} collective-permute-done((f32[224,128]{1,0:T(8,128)S(1)}, f32[224,128]{1,0:T(8,128)S(1)}, u32[]{:S(2)}, u32[]{:S(2)}) %collective-permute-start.13) | collective-permute-done | bytes 114720 | tf_op jit(solution)/shard_map/ppermute | solution.py:50
  33.8 0.9 %shard_map.72 = (f32[864,64]{1,0:T(8,128)}, f32[1,64]{1,0:T(1,128)}) custom-call(f32[224,128]{1,0:T(8,128)S(1)} %get-tuple-element.56.refs_0_, f32[224,128]{1,0:T(8,128)S(1)} %get-tuple-element.55.refs_1_), custom_call_target="tpu_custom_call" | custom-call | flops 57344 | bytes 450816 | tf_op jit(solution)/shard_map/pallas_call | solution.py:225
  (41 shorter events, 2.7 us)
Async XLA Ops:
  2.1 1.4 %collective-permute-start = (bf16[1,32,4,128]{3,1,2,0:T(8,128)(2,1)S(1)}, bf16[1,32,4,128]{3,1,2,0:T(8,128)(2,1)S(1)}, u32[]{:S(2)}, u32[]{:S(2)}) collective-permute-start(bf16[1,32,4,128]{3,1,2,0:T(8,128)(2,1)S(1)} %fusion), channel_id=1, source_target_pairs={{0,16},{16,0},{1,17},{17,1},{2,18},{18,2},{3,19},{19,3},{4,20},{20... | collective-permute-start | bytes 98312 | tf_op jit(solution)/shard_map/ppermute | solution.py:28
  3.5 7.0 %collective-permute-start.2 = (bf16[10,32,128]{2,1,0:T(8,128)(2,1)S(1)}, bf16[10,32,128]{2,1,0:T(8,128)(2,1)S(1)}, u32[]{:S(2)}, u32[]{:S(2)}) collective-permute-start(bf16[10,32,128]{2,1,0:T(8,128)(2,1)S(1)} %get-tuple-element.57), channel_id=1, source_target_pairs={{0,12},{4,8},{8,4},{12,0},{1,13},{5,9},{9,5},{13,1},{2,14},{6,10},... | collective-permute-start | bytes 245768 | tf_op jit(solution)/shard_map/ppermute | solution.py:32
  7.4 4.8 %collective-permute-start.1 = (bf16[10,32,128]{2,1,0:T(8,128)(2,1)S(1)}, bf16[10,32,128]{2,1,0:T(8,128)(2,1)S(1)}, u32[]{:S(2)}, u32[]{:S(2)}) collective-permute-start(bf16[10,32,128]{2,1,0:T(8,128)(2,1)S(1)} %get-tuple-element.58), channel_id=1, source_target_pairs={{0,4},{4,0},{8,12},{12,8},{1,5},{5,1},{9,13},{13,9},{2,6},{6,2},{1... | collective-permute-start | bytes 245768 | tf_op jit(solution)/shard_map/ppermute | solution.py:28
  13.5 1.3 %collective-permute-start.10 = (bf16[4,64,128]{2,1,0:T(8,128)(2,1)S(1)}, bf16[4,64,128]{2,1,0:T(8,128)(2,1)S(1)}, u32[]{:S(2)}, u32[]{:S(2)}) collective-permute-start(bf16[4,64,128]{2,1,0:T(8,128)(2,1)S(1)} %maximum_select_fusion), channel_id=1, source_target_pairs={{0,16},{16,0},{1,17},{17,1},{2,18},{18,2},{3,19},{19,3},{4,20},{20... | collective-permute-start | bytes 196616 | tf_op jit(solution)/shard_map/ppermute | solution.py:28
  14.0 1.5 %collective-permute-start.3 = (f32[224,128]{1,0:T(8,128)S(1)}, f32[224,128]{1,0:T(8,128)S(1)}, u32[]{:S(2)}, u32[]{:S(2)}) collective-permute-start(f32[224,128]{1,0:T(8,128)S(1)} %slice_select_fusion), channel_id=1, source_target_pairs={{0,16},{16,0},{1,17},{17,1},{2,18},{18,2},{3,19},{19,3},{4,20},{20... | collective-permute-start | bytes 344072 | tf_op jit(solution)/shard_map/ppermute | solution.py:50
  15.6 6.7 %collective-permute-start.6 = (bf16[224,128]{1,0:T(8,128)(2,1)S(1)}, bf16[224,128]{1,0:T(8,128)(2,1)S(1)}, u32[]{:S(2)}, u32[]{:S(2)}) collective-permute-start(bf16[224,128]{1,0:T(8,128)(2,1)S(1)} %get-tuple-element.41), channel_id=1, source_target_pairs={{0,12},{4,8},{8,4},{12,0},{1,13},{5,9},{9,5},{13,1},{2,14},{6,10},... | collective-permute-start | bytes 172040 | tf_op jit(solution)/shard_map/ppermute | solution.py:50
  18.3 4.2 %collective-permute-start.5 = (bf16[224,128]{1,0:T(8,128)(2,1)S(1)}, bf16[224,128]{1,0:T(8,128)(2,1)S(1)}, u32[]{:S(2)}, u32[]{:S(2)}) collective-permute-start(bf16[224,128]{1,0:T(8,128)(2,1)S(1)} %get-tuple-element.41), channel_id=1, source_target_pairs={{0,8},{4,12},{8,0},{12,4},{1,9},{5,13},{9,1},{13,5},{2,10},{6,14},... | collective-permute-start | bytes 172040 | tf_op jit(solution)/shard_map/ppermute | solution.py:50
  18.8 4.8 %collective-permute-start.4 = (bf16[224,128]{1,0:T(8,128)(2,1)S(1)}, bf16[224,128]{1,0:T(8,128)(2,1)S(1)}, u32[]{:S(2)}, u32[]{:S(2)}) collective-permute-start(bf16[224,128]{1,0:T(8,128)(2,1)S(1)} %get-tuple-element.41), channel_id=1, source_target_pairs={{0,4},{4,0},{8,12},{12,8},{1,5},{5,1},{9,13},{13,9},{2,6},{6,2},{1... | collective-permute-start | bytes 172040 | tf_op jit(solution)/shard_map/ppermute | solution.py:50
  19.2 8.9 %collective-permute-start.11 = (bf16[10,64,128]{2,1,0:T(8,128)(2,1)S(1)}, bf16[10,64,128]{2,1,0:T(8,128)(2,1)S(1)}, u32[]{:S(2)}, u32[]{:S(2)}) collective-permute-start(bf16[10,64,128]{2,1,0:T(8,128)(2,1)S(1)} %get-tuple-element.45), channel_id=1, source_target_pairs={{0,12},{4,8},{8,4},{12,0},{1,13},{5,9},{9,5},{13,1},{2,14},{6,10},... | collective-permute-start | bytes 491528 | tf_op jit(solution)/shard_map/ppermute | solution.py:32
  21.9 8.1 %collective-permute-start.12 = (bf16[10,64,128]{2,1,0:T(8,128)(2,1)S(1)}, bf16[10,64,128]{2,1,0:T(8,128)(2,1)S(1)}, u32[]{:S(2)}, u32[]{:S(2)}) collective-permute-start(bf16[10,64,128]{2,1,0:T(8,128)(2,1)S(1)} %get-tuple-element.46), channel_id=1, source_target_pairs={{0,4},{4,0},{8,12},{12,8},{1,5},{5,1},{9,13},{13,9},{2,6},{6,2},{1... | collective-permute-start | bytes 491528 | tf_op jit(solution)/shard_map/ppermute | solution.py:28
  23.6 7.5 %collective-permute-start.9 = (bf16[224,128]{1,0:T(8,128)(2,1)S(1)}, bf16[224,128]{1,0:T(8,128)(2,1)S(1)}, u32[]{:S(2)}, u32[]{:S(2)}) collective-permute-start(bf16[224,128]{1,0:T(8,128)(2,1)S(1)} %fusion.1), channel_id=1, source_target_pairs={{0,3},{1,2},{2,1},{3,0},{4,7},{5,6},{6,5},{7,4},{8,11},{9,10},{10,... | collective-permute-start | bytes 172040 | tf_op jit(solution)/shard_map/ppermute | solution.py:50
  27.3 5.1 %collective-permute-start.8 = (bf16[224,128]{1,0:T(8,128)(2,1)S(1)}, bf16[224,128]{1,0:T(8,128)(2,1)S(1)}, u32[]{:S(2)}, u32[]{:S(2)}) collective-permute-start(bf16[224,128]{1,0:T(8,128)(2,1)S(1)} %fusion.1), channel_id=1, source_target_pairs={{0,2},{1,3},{2,0},{3,1},{4,6},{5,7},{6,4},{7,5},{8,10},{9,11},{10,... | collective-permute-start | bytes 172040 | tf_op jit(solution)/shard_map/ppermute | solution.py:50
  27.3 5.1 %collective-permute-start.7 = (bf16[224,128]{1,0:T(8,128)(2,1)S(1)}, bf16[224,128]{1,0:T(8,128)(2,1)S(1)}, u32[]{:S(2)}, u32[]{:S(2)}) collective-permute-start(bf16[224,128]{1,0:T(8,128)(2,1)S(1)} %fusion.1), channel_id=1, source_target_pairs={{0,1},{1,0},{2,3},{3,2},{4,5},{5,4},{6,7},{7,6},{8,9},{9,8},{10,11... | collective-permute-start | bytes 172040 | tf_op jit(solution)/shard_map/ppermute | solution.py:50
  32.4 1.4 %collective-permute-start.13 = (f32[224,128]{1,0:T(8,128)S(1)}, f32[224,128]{1,0:T(8,128)S(1)}, u32[]{:S(2)}, u32[]{:S(2)}) collective-permute-start(f32[224,128]{1,0:T(8,128)S(1)} %add_add_fusion), channel_id=1, source_target_pairs={{0,16},{16,0},{1,17},{17,1},{2,18},{18,2},{3,19},{19,3},{4,20},{20... | collective-permute-start | bytes 344072 | tf_op jit(solution)/shard_map/ppermute | solution.py:50

commit v6 on v5

--- a/solution.py
+++ b/solution.py
@@ -194,10 +194,18 @@
     bias_out[...] = full[rows + rows // 2 : rows + rows // 2 + 1, :co]
 
 
+def chunks(shape):
+    parts = 8 if shape[1] % 8 == 0 and len(shape) > 2 else 1
+    step = shape[1] // parts
+    return [(slice(None), slice(i * step, (i + 1) * step)) for i in range(parts)]
+
+
 def load_kernel(*refs):
     count = len(refs) // 2
-    done = refs[-1]
-    copies = [pltpu.make_async_copy(refs[i], refs[count + i], done.at[i]) for i in range(count)]
+    copies = []
+    for source, target in zip(refs[:count], refs[count : 2 * count]):
+        for at in chunks(source.shape):
+            copies.append(pltpu.make_async_copy(source.at[at], target.at[at], refs[-1].at[len(copies)]))
     for copy in copies:
         copy.start()
     for copy in copies:
@@ -210,7 +218,7 @@
         out_shape=[jax.ShapeDtypeStruct(a.shape, a.dtype) for a in arrays],
         in_specs=[pl.BlockSpec(memory_space=pltpu.HBM) for a in arrays],
         out_specs=[pl.BlockSpec(memory_space=pltpu.VMEM) for a in arrays],
-        scratch_shapes=[pltpu.SemaphoreType.DMA((len(arrays),))],
+        scratch_shapes=[pltpu.SemaphoreType.DMA((sum(len(chunks(a.shape)) for a in arrays),))],
         compiler_params=pltpu.CompilerParams(vmem_limit_bytes=16 << 20),
     )(*(pltpu.with_memory_space_constraint(a, pltpu.HBM) for a in arrays))
 
@@ -247,7 +255,7 @@
     first = lax.axis_index("depth") % 2 == 0
     got = swap(jnp.where(first, high, low), "depth", 1)
     part = jnp.where(first, low, high) + got
-    for axis in AXES:
+    for axis in ("depth", "dp", "height"):
         count = lax.axis_size(axis)
         assert count & (count - 1) == 0
         bit = 2 if axis == "depth" else 1
@@ -302,6 +310,9 @@
 
         shared = (x, below, above)
         inner, part = forward(inner_kernel, height - 2, *shared, w1, bias_row, cot)
+        part, taps = lax.optimization_barrier((part, taps))
+        w2 = jnp.flip(taps, (0, 1)).transpose(2, 3, 0, 1, 4).reshape(3 * ci, 9 * co)
+        part, w2 = lax.optimization_barrier((part, w2))
         late, part = forward(
             outer_kernel, 1, *shared, second, w1, bias_row, cot, part, scalar=~above_first
         )
@@ -318,9 +329,6 @@
         below, above = exchange(layer(0), layer(-1), "depth")
         around = exchange(*columns(top, bottom, below, above), "height")
         fields.append((inner, top, bottom, below, above, *around))
-    total, taps = lax.optimization_barrier((total, taps))
-    w2 = jnp.flip(taps, (0, 1)).transpose(2, 3, 0, 1, 4).reshape(3 * ci, 9 * co)
-
     def input_gradients(fields):
         grads = []
         for field in fields:

time: 34.9 us -> 36 us (1.032)
  waiting for transfers between devices: 7.17 us -> 8.51 us
  starting transfers between devices: 16.6 us -> 16.2 us
    ppermute x2, waiting for transfers between devices: 0.98 us -> 5.14 us  [meet(): second = lax.ppermute(jnp.where(even, low_edge, high_edge), axis, outer)]
    ppermute x2, starting transfers between devices: 6.53 us -> 2.55 us  [meet(): second = lax.ppermute(jnp.where(even, low_edge, high_edge), axis, outer)]
    ppermute x4, starting transfers between devices: 1.47 us -> 4.99 us  [meet(): first = lax.ppermute(jnp.where(even, high_edge, low_edge), axis, inner)]
    ppermute x4, waiting for transfers between devices: 2.51 us -> 0.67 us  [meet(): first = lax.ppermute(jnp.where(even, high_edge, low_edge), axis, inner)]
    ppermute x8, waiting for transfers between devices: 3.68 us -> 2.7 us  [swap(): lax.ppermute(array, axis, [(i, i ^ mask) for i in range(lax.axis_size(axi...]
  transfers between devices with their start and end apart: 14 -> 14, of which waited for: 9 -> 6; matrix products, arithmetic and copies ran while one was open for 6% -> 6% of each run, Pallas kernels for 12% -> 11%
where the time goes in v6:
time: 36 us; the launch traced here: 35.8 us
  starting transfers between devices  16.2 us (45%)
  waiting for transfers between devices  8.51 us (24%)
  Pallas kernels  7.63 us (21%)
  local copies, waits for them, and re-layouts  2.19 us (6%)
  between operations  0.95 us (3%)
    ppermute x8, starting transfers between devices, swap(): lax.ppermute(array, axis, [(i, i ^ mask) for i in range(lax.axis_size(axi...  8.65 us
    pallas_call x5, Pallas kernels, call(): pl.pallas_call(kernel, out_shape=outs, scratch_shapes=scratch, compiler_p...  6.22 us
    ppermute x2, waiting for transfers between devices, meet(): second = lax.ppermute(jnp.where(even, low_edge, high_edge), axis, outer)  5.14 us
    ppermute x4, starting transfers between devices, meet(): first = lax.ppermute(jnp.where(even, high_edge, low_edge), axis, inner)  4.99 us
    ppermute x8, waiting for transfers between devices, swap(): lax.ppermute(array, axis, [(i, i ^ mask) for i in range(lax.axis_size(axi...  2.7 us
    ppermute x2, starting transfers between devices, meet(): second = lax.ppermute(jnp.where(even, low_edge, high_edge), axis, outer)  2.55 us
    pallas_call x1, Pallas kernels, loaded(): pl.pallas_call(load_kernel, out_shape=[jax.ShapeDtypeStruct(a.shape, a.dt...  1.41 us
    unnamed x1, local copies, waits for them, and re-layouts  0.84 us
  transfers between devices with their start and end apart: 14, of which 6 were waited for; matrix products, arithmetic and copies ran while one was open for 6% of the time, Pallas kernels for 11%

profile of v6, /device:TPU:0, one launch (start us, length us, event | category | flops | bytes accessed | tf_op | source)
XLA Modules:
  0.0 35.8 jit_solution(9995484772494471418)
XLA Ops:
  0.6 1.4 %shard_map.67 = (bf16[1,32,8,4,128]{4,3,2,1,0:T(4,128)(2,1)S(1)}, bf16[3,3,3,32,64]{4,3,2,1,0:T(8,128)(2,1)S(1)}, f32[1,64]{1,0:T(1,128)S(1)}, bf16[1,64,8,4,128]{4,3,2,1,0:T(4,128)(2,1)S(1)}) custom-call(bf16[1,32,8,4,128]{4,3,2,1,0:T(4,128)(2,1)} %refs_0_.1, bf16[3,3,3,32,64]{4,3,2,1,0:T(8,128)(2,1)} %bitcast.69, f32[1,64]{1,0:T(1,128)} %bitcast.70, ...), custom_call_target="tpu_custom_call" | custom-call | tf_op jit(solution)/shard_map/pallas_call | solution.py:216
  2.2 0.5 %collective-permute-start = (bf16[1,32,4,128]{3,1,2,0:T(8,128)(2,1)S(1)}, bf16[1,32,4,128]{3,1,2,0:T(8,128)(2,1)S(1)}, u32[]{:S(2)}, u32[]{:S(2)}) collective-permute-start(bf16[1,32,4,128]{3,1,2,0:T(8,128)(2,1)S(1)} %fusion), channel_id=1, source_target_pairs={{0,16},{16,0},{1,17},{17,1},{2,18},{18,2},{3,19},{19,3},{4,20},{20... | collective-permute-start | bytes 98312 | tf_op jit(solution)/shard_map/ppermute | solution.py:28
  3.7 2.9 %collective-permute-start.1 = (bf16[10,32,128]{2,1,0:T(8,128)(2,1)S(1)}, bf16[10,32,128]{2,1,0:T(8,128)(2,1)S(1)}, u32[]{:S(2)}, u32[]{:S(2)}) collective-permute-start(bf16[10,32,128]{2,1,0:T(8,128)(2,1)S(1)} %get-tuple-element.62), channel_id=1, source_target_pairs={{0,4},{4,0},{8,12},{12,8},{1,5},{5,1},{9,13},{13,9},{2,6},{6,2},{1... | collective-permute-start | bytes 245768 | tf_op jit(solution)/shard_map/ppermute | solution.py:28
  6.5 1.5 %collective-permute-start.2 = (bf16[10,32,128]{2,1,0:T(8,128)(2,1)S(1)}, bf16[10,32,128]{2,1,0:T(8,128)(2,1)S(1)}, u32[]{:S(2)}, u32[]{:S(2)}) collective-permute-start(bf16[10,32,128]{2,1,0:T(8,128)(2,1)S(1)} %get-tuple-element.61), channel_id=1, source_target_pairs={{0,12},{4,8},{8,4},{12,0},{1,13},{5,9},{9,5},{13,1},{2,14},{6,10},... | collective-permute-start | bytes 245768 | tf_op jit(solution)/shard_map/ppermute | solution.py:32
  8.0 1.6 %shard_map.68 = (bf16[2,8,64,128]{3,2,1,0:T(8,128)(2,1)S(1)}, f32[448,128]{1,0:T(8,128)S(1)}) custom-call(bf16[8,4,32,128]{3,2,1,0:T(8,128)(2,1)S(1)} %bitcast.60, bf16[4,32,128]{2,1,0:T(8,128)(2,1)S(1)} %get-tuple-element.78.below, bf16[4,32,128]{2,1,0:T(8,128)(2,1)S(1)} %get-tuple-element.77.above, bf16[192,288]{1,0:T(8,128)(2,1)S(1)} %copy.28.w1, ...), custom_call_target="tpu_custom_call" | custom-call | flops 452984832 | bytes 1454336 | tf_op jit(solution)/shard_map/pallas_call | solution.py:233
  10.1 2.2 %collective-permute-done.2 = bf16[10,32,128]{2,1,0:T(8,128)(2,1)S(1)} collective-permute-done((bf16[10,32,128]{2,1,0:T(8,128)(2,1)S(1)}, bf16[10,32,128]{2,1,0:T(8,128)(2,1)S(1)}, u32[]{:S(2)}, u32[]{:S(2)}) %collective-permute-start.2) | collective-permute-done | bytes 81952 | tf_op jit(solution)/shard_map/ppermute | solution.py:32
  12.3 1.2 %shard_map.69 = (bf16[1,8,64,128]{3,2,1,0:T(8,128)(2,1)S(1)}, f32[448,128]{1,0:T(8,128)S(1)}) custom-call(s32[1]{0:T(128)} %bitcast.19.last, bf16[8,4,32,128]{3,2,1,0:T(8,128)(2,1)S(1)} %bitcast.61, bf16[4,32,128]{2,1,0:T(8,128)(2,1)S(1)} %get-tuple-element.78.below, bf16[4,32,128]{2,1,0:T(8,128)(2,1)S(1)} %get-tuple-element.77.above, ...), custom_call_target="tpu_custom_call" | custom-call | flops 226492416 | bytes 1634560 | tf_op jit(solution)/shard_map/pallas_call | solution.py:233
  13.6 1.2 %shard_map.70 = (bf16[1,8,64,128]{3,2,1,0:T(8,128)(2,1)S(1)}, f32[448,128]{1,0:T(8,128)S(1)}) custom-call(s32[1]{0:T(128)} %bitcast.last, bf16[8,4,32,128]{3,2,1,0:T(8,128)(2,1)S(1)} %bitcast.62, bf16[4,32,128]{2,1,0:T(8,128)(2,1)S(1)} %get-tuple-element.78.below, bf16[4,32,128]{2,1,0:T(8,128)(2,1)S(1)} %get-tuple-element.77.above, ...), custom_call_target="tpu_custom_call" | custom-call | flops 226492416 | bytes 1634560 | tf_op jit(solution)/shard_map/pallas_call | solution.py:233
  15.0 0.6 %collective-permute-start.3 = (f32[224,128]{1,0:T(8,128)S(1)}, f32[224,128]{1,0:T(8,128)S(1)}, u32[]{:S(2)}, u32[]{:S(2)}) collective-permute-start(f32[224,128]{1,0:T(8,128)S(1)} %slice_select_fusion), channel_id=1, source_target_pairs={{0,16},{16,0},{1,17},{17,1},{2,18},{18,2},{3,19},{19,3},{4,20},{20... | collective-permute-start | bytes 344072 | tf_op jit(solution)/shard_map/ppermute | solution.py:50
  15.6 0.7 %collective-permute-done.10 = bf16[4,64,128]{2,1,0:T(8,128)(2,1)S(1)} collective-permute-done((bf16[4,64,128]{2,1,0:T(8,128)(2,1)S(1)}, bf16[4,64,128]{2,1,0:T(8,128)(2,1)S(1)}, u32[]{:S(2)}, u32[]{:S(2)}) %collective-permute-start.10) | collective-permute-done | bytes 65568 | tf_op jit(solution)/shard_map/ppermute | solution.py:28
  16.3 0.3 collective-permute-done.3
  16.6 3.7 %collective-permute-start.6 = (bf16[224,128]{1,0:T(8,128)(2,1)S(1)}, bf16[224,128]{1,0:T(8,128)(2,1)S(1)}, u32[]{:S(2)}, u32[]{:S(2)}) collective-permute-start(bf16[224,128]{1,0:T(8,128)(2,1)S(1)} %get-tuple-element.45), channel_id=1, source_target_pairs={{0,3},{1,2},{2,1},{3,0},{4,7},{5,6},{6,5},{7,4},{8,11},{9,10},{10,... | collective-permute-start | bytes 172040 | tf_op jit(solution)/shard_map/ppermute | solution.py:50
  20.2 0.8 %collective-permute-start.4 = (bf16[224,128]{1,0:T(8,128)(2,1)S(1)}, bf16[224,128]{1,0:T(8,128)(2,1)S(1)}, u32[]{:S(2)}, u32[]{:S(2)}) collective-permute-start(bf16[224,128]{1,0:T(8,128)(2,1)S(1)} %get-tuple-element.45), channel_id=1, source_target_pairs={{0,1},{1,0},{2,3},{3,2},{4,5},{5,4},{6,7},{7,6},{8,9},{9,8},{10,11... | collective-permute-start | bytes 172040 | tf_op jit(solution)/shard_map/ppermute | solution.py:50
  21.1 1.5 %collective-permute-start.12 = (bf16[10,64,128]{2,1,0:T(8,128)(2,1)S(1)}, bf16[10,64,128]{2,1,0:T(8,128)(2,1)S(1)}, u32[]{:S(2)}, u32[]{:S(2)}) collective-permute-start(bf16[10,64,128]{2,1,0:T(8,128)(2,1)S(1)} %get-tuple-element.50), channel_id=1, source_target_pairs={{0,4},{4,0},{8,12},{12,8},{1,5},{5,1},{9,13},{13,9},{2,6},{6,2},{1... | collective-permute-start | bytes 491528 | tf_op jit(solution)/shard_map/ppermute | solution.py:28
  22.6 1.1 %collective-permute-start.11 = (bf16[10,64,128]{2,1,0:T(8,128)(2,1)S(1)}, bf16[10,64,128]{2,1,0:T(8,128)(2,1)S(1)}, u32[]{:S(2)}, u32[]{:S(2)}) collective-permute-start(bf16[10,64,128]{2,1,0:T(8,128)(2,1)S(1)} %get-tuple-element.49), channel_id=1, source_target_pairs={{0,12},{4,8},{8,4},{12,0},{1,13},{5,9},{9,5},{13,1},{2,14},{6,10},... | collective-permute-start | bytes 491528 | tf_op jit(solution)/shard_map/ppermute | solution.py:32
  23.7 1.9 %collective-permute-done.5 = bf16[224,128]{1,0:T(8,128)(2,1)S(1)} collective-permute-done((bf16[224,128]{1,0:T(8,128)(2,1)S(1)}, bf16[224,128]{1,0:T(8,128)(2,1)S(1)}, u32[]{:S(2)}, u32[]{:S(2)}) %collective-permute-start.5) | collective-permute-done | bytes 57376 | tf_op jit(solution)/shard_map/ppermute | solution.py:50
  25.7 1.5 %collective-permute-start.9 = (bf16[224,128]{1,0:T(8,128)(2,1)S(1)}, bf16[224,128]{1,0:T(8,128)(2,1)S(1)}, u32[]{:S(2)}, u32[]{:S(2)}) collective-permute-start(bf16[224,128]{1,0:T(8,128)(2,1)S(1)} %fusion.1), channel_id=1, source_target_pairs={{0,12},{4,8},{8,4},{12,0},{1,13},{5,9},{9,5},{13,1},{2,14},{6,10},... | collective-permute-start | bytes 172040 | tf_op jit(solution)/shard_map/ppermute | solution.py:50
  27.2 1.5 %collective-permute-start.8 = (bf16[224,128]{1,0:T(8,128)(2,1)S(1)}, bf16[224,128]{1,0:T(8,128)(2,1)S(1)}, u32[]{:S(2)}, u32[]{:S(2)}) collective-permute-start(bf16[224,128]{1,0:T(8,128)(2,1)S(1)} %fusion.1), channel_id=1, source_target_pairs={{0,8},{4,12},{8,0},{12,4},{1,9},{5,13},{9,1},{13,5},{2,10},{6,14},... | collective-permute-start | bytes 172040 | tf_op jit(solution)/shard_map/ppermute | solution.py:50
  28.7 0.5 %collective-permute-start.7 = (bf16[224,128]{1,0:T(8,128)(2,1)S(1)}, bf16[224,128]{1,0:T(8,128)(2,1)S(1)}, u32[]{:S(2)}, u32[]{:S(2)}) collective-permute-start(bf16[224,128]{1,0:T(8,128)(2,1)S(1)} %fusion.1), channel_id=1, source_target_pairs={{0,4},{4,0},{8,12},{12,8},{1,5},{5,1},{9,13},{13,9},{2,6},{6,2},{1... | collective-permute-start | bytes 172040 | tf_op jit(solution)/shard_map/ppermute | solution.py:50
  29.3 2.9 %collective-permute-done.11 = bf16[10,64,128]{2,1,0:T(8,128)(2,1)S(1)} collective-permute-done((bf16[10,64,128]{2,1,0:T(8,128)(2,1)S(1)}, bf16[10,64,128]{2,1,0:T(8,128)(2,1)S(1)}, u32[]{:S(2)}, u32[]{:S(2)}) %collective-permute-start.11) | collective-permute-done | bytes 163872 | tf_op jit(solution)/shard_map/ppermute | solution.py:32
  32.2 1.2 %shard_map.71 = bf16[8,4,32,128]{3,2,1,0:T(8,128)(2,1)S(1)} custom-call(bf16[2,8,64,128]{3,2,1,0:T(8,128)(2,1)S(1)} %get-tuple-element.31.inner, bf16[8,64,128]{2,1,0:T(8,128)(2,1)S(1)} %bitcast.67, bf16[8,64,128]{2,1,0:T(8,128)(2,1)S(1)} %bitcast.65, bf16[4,64,128]{2,1,0:T(8,128)(2,1)S(1)} %get-tuple-element.72.below, ...), custom_call_target="tpu_custom_call" | custom-call | flops 452984832 | bytes 1355776 | tf_op jit(solution)/shard_map/pallas_call | solution.py:233
  33.6 0.8 %copy.31 = bf16[1,32,8,4,128]{4,3,2,1,0:T(4,128)(2,1)} copy(bf16[1,32,8,4,128]{4,1,3,2,0:T(8,128)(2,1)S(1)} %bitcast.68) | data formatting | bytes 524288
  34.4 0.5 %collective-permute-done.13 = f32[224,128]{1,0:T(8,128)S(1)} collective-permute-done((f32[224,128]{1,0:T(8,128)S(1)}, f32[224,128]{1,0:T(8,128)S(1)}, u32[]{:S(2)}, u32[]{:S(2)}) %collective-permute-start.13) | collective-permute-done | bytes 114720 | tf_op jit(solution)/shard_map/ppermute | solution.py:50
  34.9 0.9 %shard_map.72 = (f32[864,64]{1,0:T(8,128)}, f32[1,64]{1,0:T(1,128)}) custom-call(f32[224,128]{1,0:T(8,128)S(1)} %get-tuple-element.60.refs_0_, f32[224,128]{1,0:T(8,128)S(1)} %get-tuple-element.59.refs_1_), custom_call_target="tpu_custom_call" | custom-call | flops 57344 | bytes 450816 | tf_op jit(solution)/shard_map/pallas_call | solution.py:233
  (41 shorter events, 1.9 us)
Async XLA Ops:
  2.2 1.4 %collective-permute-start = (bf16[1,32,4,128]{3,1,2,0:T(8,128)(2,1)S(1)}, bf16[1,32,4,128]{3,1,2,0:T(8,128)(2,1)S(1)}, u32[]{:S(2)}, u32[]{:S(2)}) collective-permute-start(bf16[1,32,4,128]{3,1,2,0:T(8,128)(2,1)S(1)} %fusion), channel_id=1, source_target_pairs={{0,16},{16,0},{1,17},{17,1},{2,18},{18,2},{3,19},{19,3},{4,20},{20... | collective-permute-start | bytes 98312 | tf_op jit(solution)/shard_map/ppermute | solution.py:28
  3.7 9.9 %collective-permute-start.1 = (bf16[10,32,128]{2,1,0:T(8,128)(2,1)S(1)}, bf16[10,32,128]{2,1,0:T(8,128)(2,1)S(1)}, u32[]{:S(2)}, u32[]{:S(2)}) collective-permute-start(bf16[10,32,128]{2,1,0:T(8,128)(2,1)S(1)} %get-tuple-element.62), channel_id=1, source_target_pairs={{0,4},{4,0},{8,12},{12,8},{1,5},{5,1},{9,13},{13,9},{2,6},{6,2},{1... | collective-permute-start | bytes 245768 | tf_op jit(solution)/shard_map/ppermute | solution.py:28
  6.5 5.8 %collective-permute-start.2 = (bf16[10,32,128]{2,1,0:T(8,128)(2,1)S(1)}, bf16[10,32,128]{2,1,0:T(8,128)(2,1)S(1)}, u32[]{:S(2)}, u32[]{:S(2)}) collective-permute-start(bf16[10,32,128]{2,1,0:T(8,128)(2,1)S(1)} %get-tuple-element.61), channel_id=1, source_target_pairs={{0,12},{4,8},{8,4},{12,0},{1,13},{5,9},{9,5},{13,1},{2,14},{6,10},... | collective-permute-start | bytes 245768 | tf_op jit(solution)/shard_map/ppermute | solution.py:32
  14.9 1.3 %collective-permute-start.10 = (bf16[4,64,128]{2,1,0:T(8,128)(2,1)S(1)}, bf16[4,64,128]{2,1,0:T(8,128)(2,1)S(1)}, u32[]{:S(2)}, u32[]{:S(2)}) collective-permute-start(bf16[4,64,128]{2,1,0:T(8,128)(2,1)S(1)} %maximum_select_fusion), channel_id=1, source_target_pairs={{0,16},{16,0},{1,17},{17,1},{2,18},{18,2},{3,19},{19,3},{4,20},{20... | collective-permute-start | bytes 196616 | tf_op jit(solution)/shard_map/ppermute | solution.py:28
  15.0 1.5 %collective-permute-start.3 = (f32[224,128]{1,0:T(8,128)S(1)}, f32[224,128]{1,0:T(8,128)S(1)}, u32[]{:S(2)}, u32[]{:S(2)}) collective-permute-start(f32[224,128]{1,0:T(8,128)S(1)} %slice_select_fusion), channel_id=1, source_target_pairs={{0,16},{16,0},{1,17},{17,1},{2,18},{18,2},{3,19},{19,3},{4,20},{20... | collective-permute-start | bytes 344072 | tf_op jit(solution)/shard_map/ppermute | solution.py:50
  16.6 7.1 %collective-permute-start.6 = (bf16[224,128]{1,0:T(8,128)(2,1)S(1)}, bf16[224,128]{1,0:T(8,128)(2,1)S(1)}, u32[]{:S(2)}, u32[]{:S(2)}) collective-permute-start(bf16[224,128]{1,0:T(8,128)(2,1)S(1)} %get-tuple-element.45), channel_id=1, source_target_pairs={{0,3},{1,2},{2,1},{3,0},{4,7},{5,6},{6,5},{7,4},{8,11},{9,10},{10,... | collective-permute-start | bytes 172040 | tf_op jit(solution)/shard_map/ppermute | solution.py:50
  20.2 5.4 %collective-permute-start.5 = (bf16[224,128]{1,0:T(8,128)(2,1)S(1)}, bf16[224,128]{1,0:T(8,128)(2,1)S(1)}, u32[]{:S(2)}, u32[]{:S(2)}) collective-permute-start(bf16[224,128]{1,0:T(8,128)(2,1)S(1)} %get-tuple-element.45), channel_id=1, source_target_pairs={{0,2},{1,3},{2,0},{3,1},{4,6},{5,7},{6,4},{7,5},{8,10},{9,11},{10,... | collective-permute-start | bytes 172040 | tf_op jit(solution)/shard_map/ppermute | solution.py:50
  20.2 5.4 %collective-permute-start.4 = (bf16[224,128]{1,0:T(8,128)(2,1)S(1)}, bf16[224,128]{1,0:T(8,128)(2,1)S(1)}, u32[]{:S(2)}, u32[]{:S(2)}) collective-permute-start(bf16[224,128]{1,0:T(8,128)(2,1)S(1)} %get-tuple-element.45), channel_id=1, source_target_pairs={{0,1},{1,0},{2,3},{3,2},{4,5},{5,4},{6,7},{7,6},{8,9},{9,8},{10,11... | collective-permute-start | bytes 172040 | tf_op jit(solution)/shard_map/ppermute | solution.py:50
  21.1 8.2 %collective-permute-start.12 = (bf16[10,64,128]{2,1,0:T(8,128)(2,1)S(1)}, bf16[10,64,128]{2,1,0:T(8,128)(2,1)S(1)}, u32[]{:S(2)}, u32[]{:S(2)}) collective-permute-start(bf16[10,64,128]{2,1,0:T(8,128)(2,1)S(1)} %get-tuple-element.50), channel_id=1, source_target_pairs={{0,4},{4,0},{8,12},{12,8},{1,5},{5,1},{9,13},{13,9},{2,6},{6,2},{1... | collective-permute-start | bytes 491528 | tf_op jit(solution)/shard_map/ppermute | solution.py:28
  22.6 9.5 %collective-permute-start.11 = (bf16[10,64,128]{2,1,0:T(8,128)(2,1)S(1)}, bf16[10,64,128]{2,1,0:T(8,128)(2,1)S(1)}, u32[]{:S(2)}, u32[]{:S(2)}) collective-permute-start(bf16[10,64,128]{2,1,0:T(8,128)(2,1)S(1)} %get-tuple-element.49), channel_id=1, source_target_pairs={{0,12},{4,8},{8,4},{12,0},{1,13},{5,9},{9,5},{13,1},{2,14},{6,10},... | collective-permute-start | bytes 491528 | tf_op jit(solution)/shard_map/ppermute | solution.py:32
  25.7 7.7 %collective-permute-start.9 = (bf16[224,128]{1,0:T(8,128)(2,1)S(1)}, bf16[224,128]{1,0:T(8,128)(2,1)S(1)}, u32[]{:S(2)}, u32[]{:S(2)}) collective-permute-start(bf16[224,128]{1,0:T(8,128)(2,1)S(1)} %fusion.1), channel_id=1, source_target_pairs={{0,12},{4,8},{8,4},{12,0},{1,13},{5,9},{9,5},{13,1},{2,14},{6,10},... | collective-permute-start | bytes 172040 | tf_op jit(solution)/shard_map/ppermute | solution.py:50
  27.2 6.2 %collective-permute-start.8 = (bf16[224,128]{1,0:T(8,128)(2,1)S(1)}, bf16[224,128]{1,0:T(8,128)(2,1)S(1)}, u32[]{:S(2)}, u32[]{:S(2)}) collective-permute-start(bf16[224,128]{1,0:T(8,128)(2,1)S(1)} %fusion.1), channel_id=1, source_target_pairs={{0,8},{4,12},{8,0},{12,4},{1,9},{5,13},{9,1},{13,5},{2,10},{6,14},... | collective-permute-start | bytes 172040 | tf_op jit(solution)/shard_map/ppermute | solution.py:50
  28.7 4.7 %collective-permute-start.7 = (bf16[224,128]{1,0:T(8,128)(2,1)S(1)}, bf16[224,128]{1,0:T(8,128)(2,1)S(1)}, u32[]{:S(2)}, u32[]{:S(2)}) collective-permute-start(bf16[224,128]{1,0:T(8,128)(2,1)S(1)} %fusion.1), channel_id=1, source_target_pairs={{0,4},{4,0},{8,12},{12,8},{1,5},{5,1},{9,13},{13,9},{2,6},{6,2},{1... | collective-permute-start | bytes 172040 | tf_op jit(solution)/shard_map/ppermute | solution.py:50
  33.5 1.4 %collective-permute-start.13 = (f32[224,128]{1,0:T(8,128)S(1)}, f32[224,128]{1,0:T(8,128)S(1)}, u32[]{:S(2)}, u32[]{:S(2)}) collective-permute-start(f32[224,128]{1,0:T(8,128)S(1)} %add_add_fusion), channel_id=1, source_target_pairs={{0,16},{16,0},{1,17},{17,1},{2,18},{18,2},{3,19},{19,3},{4,20},{20... | collective-permute-start | bytes 344072 | tf_op jit(solution)/shard_map/ppermute | solution.py:50

commit v7 on v5

--- a/solution.py
+++ b/solution.py
@@ -8,6 +8,7 @@
 F32 = jnp.float32
 BF16 = jnp.bfloat16
 AXES = ("depth", "height", "dp")
+WAYS = {"depth": (3, 2, 1), "height": (3, 2, 1), "dp": (2, 1, 3)}
 
 
 def paired(axis):
@@ -108,45 +109,52 @@
         payload[at, :] = value if before is None else before[at, :] + value
 
 
-def inner_kernel(x, below, above, w1, bias, cot, delta, payload, patches, *scratch):
-    depth, height, ci, width = x.shape
-    count = height - 2
-    for dd in range(depth + 2):
-        for hh in range(height):
-            row = below[hh] if dd == 0 else above[hh] if dd == depth + 1 else x[dd - 1, hh]
+def fill_taps(row_of, depth, rows, patches):
+    ci, width = row_of(1, 1).shape
+    count = len(rows)
+    for d in range(depth):
+        for at, h in enumerate(rows):
             for a in range(3):
                 for b in range(3):
-                    d, at = dd - a, hh - b
-                    if 0 <= d < depth and 0 <= at < count:
-                        patches[pl.ds((a * 3 + b) * ci, ci), pl.ds((d * count + at) * width, width)] = row
+                    lanes = pl.ds((d * count + at) * width, width)
+                    patches[pl.ds((a * 3 + b) * ci, ci), lanes] = row_of(d + a, h + b)
+
+
+def inner_kernel(x, below, above, w1, bias, cot, delta, payload, patches, *scratch):
+    depth, height = x.shape[:2]
+
+    def row_of(d, h):
+        return below[h - 1] if d == 0 else above[h - 1] if d == depth + 1 else x[d - 1, h - 1]
 
     def cot_of(d, at):
         return cot[d, at + 1]
 
-    forward_rows(count, width, cot_of, w1, bias, delta, None, payload, patches, *scratch)
-
-
-def outer_kernel(last, x, below, above, side, w1, bias, cot, before, delta, payload, patches, *scratch):
-    depth, height, ci, width = x.shape
-    flag = last[0]
-    for dd in range(depth + 2):
-        for part in range(3):
-            if part == 2:
-                row, b = side[dd], 2 * flag
-            else:
-                h = flag * (height - 2) + part
-                row = below[h] if dd == 0 else above[h] if dd == depth + 1 else x[dd - 1, h]
-                b = part + 1 - flag
-            for a in range(3):
-                d = dd - a
-                if 0 <= d < depth:
-                    to = pl.ds(pl.multiple_of((a * 3 + b) * ci, ci), ci)
-                    patches[to, pl.ds(d * width, width)] = row
+    fill_taps(row_of, depth, range(1, height - 1), patches)
+    width = x.shape[3]
+    forward_rows(height - 2, width, cot_of, w1, bias, delta, None, payload, patches, *scratch)
+
+
+def outer_kernel(
+    x, below, above, left, right, corners_below, corners_above, w1, bias, cot, before, *refs
+):
+    delta, payload, patches, *scratch = refs
+    depth, height = x.shape[:2]
+
+    def row_of(d, h):
+        if 0 < h <= height:
+            return below[h - 1] if d == 0 else above[h - 1] if d == depth + 1 else x[d - 1, h - 1]
+        side = 0 if h == 0 else 1
+        if d == 0:
+            return corners_below[side]
+        if d == depth + 1:
+            return corners_above[side]
+        return right[d - 1] if side else left[d - 1]
 
     def cot_of(d, at):
-        return cot[d, flag * (height - 1)]
-
-    forward_rows(1, width, cot_of, w1, bias, delta, before, payload, patches, *scratch)
+        return cot[d, at * (height - 1)]
+
+    fill_taps(row_of, depth, (0, height - 1), patches)
+    forward_rows(2, x.shape[3], cot_of, w1, bias, delta, before, payload, patches, *scratch)
 
 
 def input_kernel(inner, top, bottom, below, above, left, right, w2, out, patches):
@@ -215,20 +223,14 @@
     )(*(pltpu.with_memory_space_constraint(a, pltpu.HBM) for a in arrays))
 
 
-def call(kernel, outs, scratch, flops, *args, scalar=None):
+def call(kernel, outs, scratch, flops, *args):
     size = sum(a.size * a.dtype.itemsize for a in args) + sum(o.size * o.dtype.itemsize for o in outs)
-    specs = {}
-    if scalar is not None:
-        vmem = pl.BlockSpec(memory_space=pltpu.VMEM)
-        specs["in_specs"] = [pl.BlockSpec(memory_space=pltpu.SMEM)] + [vmem] * len(args)
-        args = (scalar.astype(jnp.int32).reshape(1), *args)
     return pl.pallas_call(
         kernel,
         out_shape=outs,
         scratch_shapes=scratch,
         compiler_params=pltpu.CompilerParams(vmem_limit_bytes=40 << 20),
         cost_estimate=pl.CostEstimate(flops=flops, bytes_accessed=size, transcendentals=0),
-        **specs,
     )(*args)
 
 
@@ -252,7 +254,7 @@
         assert count & (count - 1) == 0
         bit = 2 if axis == "depth" else 1
         while bit < count:
-            masks = [bit, 2 * bit, 3 * bit] if 2 * bit < count else [bit]
+            masks = [bit * way for way in WAYS[axis]] if 2 * bit < count else [bit]
             part = gathered_sum(part, axis, masks)
             bit *= len(masks) + 1
     part, done = lax.optimization_barrier((part, work(meanwhile)))
@@ -268,24 +270,20 @@
     flops = 2 * depth * width * 27 * ci * co
     total = None
     fields = []
-    inputs, taps, bias_row, cotangent = loaded(
-        inputs, weight.transpose(2, 3, 4, 1, 0), bias[None], cotangent
+    fields_in = [inputs[cube].transpose(1, 2, 0, 3) for cube in range(cubes)]
+    rows = [(x[:, 0], x[:, -1]) for x in fields_in]
+    rows, fields_in, weight, bias, cotangent = lax.optimization_barrier(
+        (rows, fields_in, weight, bias, cotangent)
     )
-    edges = exchange(inputs[:, :, 0], inputs[:, :, -1], "depth")
-    sides = []
+    taps, bias_row, cotangent = loaded(weight.transpose(2, 3, 4, 1, 0), bias[None], cotangent)
+    w1 = taps.transpose(2, 4, 0, 1, 3).reshape(3 * co, 9 * ci)
     for cube in range(cubes):
-        below, above = (edge[cube].transpose(1, 0, 2) for edge in edges)
-        first_row, last_row = (inputs[cube, :, :, at].transpose(1, 0, 2) for at in (0, -1))
-        sides.append(columns(first_row, last_row, below, above))
-    w1 = taps.transpose(2, 4, 0, 1, 3).reshape(3 * co, 9 * ci)
-    above_first = paired("height")
-    for cube in range(cubes):
-        below, above = (edge[cube].transpose(1, 0, 2) for edge in edges)
-        second, first = meet(*sides[cube], "height")
-        x = inputs[cube].transpose(1, 2, 0, 3)
+        x = fields_in[cube]
+        left, right = exchange(*rows[cube], "height")
+        below, above = exchange(x[0], x[-1], "depth")
         cot = cotangent[cube].transpose(1, 2, 0, 3)
 
-        def forward(kernel, rows, *args, scalar=None):
+        def forward(kernel, rows, *args):
             return call(
                 kernel,
                 (jax.ShapeDtypeStruct((rows, depth, co, width), BF16), payload_shape),
@@ -297,20 +295,19 @@
                 ],
                 2 * flops * rows,
                 *args,
-                scalar=scalar,
             )
 
         shared = (x, below, above)
         inner, part = forward(inner_kernel, height - 2, *shared, w1, bias_row, cot)
-        late, part = forward(
-            outer_kernel, 1, *shared, second, w1, bias_row, cot, part, scalar=~above_first
-        )
-        early, part = forward(
-            outer_kernel, 1, *shared, first, w1, bias_row, cot, part, scalar=above_first
+        part, taps = lax.optimization_barrier((part, taps))
+        w2 = jnp.flip(taps, (0, 1)).transpose(2, 3, 0, 1, 4).reshape(3 * ci, 9 * co)
+        part, w2 = lax.optimization_barrier((part, w2))
+        corners = exchange(jnp.stack([left[0], right[0]]), jnp.stack([left[-1], right[-1]]), "depth")
+        outer, part = forward(
+            outer_kernel, 2, *shared, left, right, *corners, w1, bias_row, cot, part
         )
         total = part if total is None else total + part
-        top = jnp.where(above_first, late[0], early[0])
-        bottom = jnp.where(above_first, early[0], late[0])
+        top, bottom = outer[0], outer[1]
 
         def layer(at):
             return jnp.concatenate([top[at][None], inner[:, at], bottom[at][None]], axis=0)
@@ -318,9 +315,6 @@
         below, above = exchange(layer(0), layer(-1), "depth")
         around = exchange(*columns(top, bottom, below, above), "height")
         fields.append((inner, top, bottom, below, above, *around))
-    total, taps = lax.optimization_barrier((total, taps))
-    w2 = jnp.flip(taps, (0, 1)).transpose(2, 3, 0, 1, 4).reshape(3 * ci, 9 * co)
-
     def input_gradients(fields):
         grads = []
         for field in fields:

time: 34.9 us -> 34.1 us (0.977)
  starting transfers between devices: 16.6 us -> 15.3 us
  local copies, waits for them, and re-layouts: 2.18 us -> 3.07 us
  Pallas kernels: 7.49 us -> 6.61 us
  waiting for transfers between devices: 7.17 us -> 7.69 us
    ppermute x2, starting transfers between devices: 6.53 us -> 5.04 us  [meet(): second = lax.ppermute(jnp.where(even, low_edge, high_edge), axis, outer)]
    ppermute x8, waiting for transfers between devices: 3.68 us -> 4.79 us  [swap(): lax.ppermute(array, axis, [(i, i ^ mask) for i in range(lax.axis_size(axi...]
    unnamed x1 -> x2, local copies, waits for them, and re-layouts: 0.84 us -> 1.89 us
    ppermute x2, waiting for transfers between devices: 0.98 us -> 0.01 us  [meet(): second = lax.ppermute(jnp.where(even, low_edge, high_edge), axis, outer)]
    pallas_call x5 -> x4, Pallas kernels: 6.2 us -> 5.4 us  [call(): pl.pallas_call(kernel, out_shape=outs, scratch_shapes=scratch, compiler_p...]
    ppermute x4 -> x5, waiting for transfers between devices: 2.51 us -> 2.9 us  [meet(): first = lax.ppermute(jnp.where(even, high_edge, low_edge), axis, inner)]
    ppermute x4 -> x5, starting transfers between devices: 1.47 us -> 1.77 us  [meet(): first = lax.ppermute(jnp.where(even, high_edge, low_edge), axis, inner)]
  transfers between devices with their start and end apart: 14 -> 15, of which waited for: 9 -> 9; matrix products, arithmetic and copies ran while one was open for 6% -> 6% of each run, Pallas kernels for 12% -> 12%
where the time goes in v7:
time: 34.1 us; the launch traced here: 33.9 us
  starting transfers between devices  15.3 us (45%)
  waiting for transfers between devices  7.69 us (23%)
  Pallas kernels  6.61 us (19%)
  local copies, waits for them, and re-layouts  3.07 us (9%)
  between operations  0.89 us (3%)
    ppermute x8, starting transfers between devices, swap(): lax.ppermute(array, axis, [(i, i ^ mask) for i in range(lax.axis_size(axi...  8.49 us
    pallas_call x4, Pallas kernels, call(): pl.pallas_call(kernel, out_shape=outs, scratch_shapes=scratch, compiler_p...  5.4 us
    ppermute x2, starting transfers between devices, meet(): second = lax.ppermute(jnp.where(even, low_edge, high_edge), axis, outer)  5.04 us
    ppermute x8, waiting for transfers between devices, swap(): lax.ppermute(array, axis, [(i, i ^ mask) for i in range(lax.axis_size(axi...  4.79 us
    ppermute x5, waiting for transfers between devices, meet(): first = lax.ppermute(jnp.where(even, high_edge, low_edge), axis, inner)  2.9 us
    unnamed x2, local copies, waits for them, and re-layouts  1.89 us
    ppermute x5, starting transfers between devices, meet(): first = lax.ppermute(jnp.where(even, high_edge, low_edge), axis, inner)  1.77 us
    pallas_call x1, Pallas kernels, loaded(): pl.pallas_call(load_kernel, out_shape=[jax.ShapeDtypeStruct(a.shape, a.dt...  1.21 us
  transfers between devices with their start and end apart: 15, of which 9 were waited for; matrix products, arithmetic and copies ran while one was open for 6% of the time, Pallas kernels for 12%

profile of v7, /device:TPU:0, one launch (start us, length us, event | category | flops | bytes accessed | tf_op | source)
XLA Modules:
  0.0 33.9 jit_solution(6900279732239303847)
XLA Ops:
  0.6 1.1 %copy.32 = bf16[1,32,8,4,128]{4,1,2,3,0:T(8,128)(2,1)S(1)} copy(bf16[1,32,8,4,128]{4,3,2,1,0:T(4,128)(2,1)} %param.4) | data formatting | bytes 524288 | tf_op args[0]
  1.7 0.5 %collective-permute-start = (bf16[4,32,128]{2,1,0:T(8,128)(2,1)S(1)}, bf16[4,32,128]{2,1,0:T(8,128)(2,1)S(1)}, u32[]{:S(2)}, u32[]{:S(2)}) collective-permute-start(bf16[4,32,128]{2,1,0:T(8,128)(2,1)S(1)} %select_bitcast_fusion), channel_id=1, source_target_pairs={{0,16},{16,0},{1,17},{17,1},{2,18},{18,2},{3,19},{19,3},{4,20},{20... | collective-permute-start | bytes 98312 | tf_op jit(solution)/shard_map/ppermute | solution.py:29
  2.3 3.5 %collective-permute-start.1 = (bf16[8,32,128]{2,1,0:T(8,128)(2,1)S(1)}, bf16[8,32,128]{2,1,0:T(8,128)(2,1)S(1)}, u32[]{:S(2)}, u32[]{:S(2)}) collective-permute-start(bf16[8,32,128]{2,1,0:T(8,128)(2,1)S(1)} %get-tuple-element.71), channel_id=1, source_target_pairs={{0,12},{4,8},{8,4},{12,0},{1,13},{5,9},{9,5},{13,1},{2,14},{6,10},... | collective-permute-start | bytes 196616 | tf_op jit(solution)/shard_map/ppermute | solution.py:33
  5.8 0.5 %collective-permute-start.2 = (bf16[8,32,128]{2,1,0:T(8,128)(2,1)S(1)}, bf16[8,32,128]{2,1,0:T(8,128)(2,1)S(1)}, u32[]{:S(2)}, u32[]{:S(2)}) collective-permute-start(bf16[8,32,128]{2,1,0:T(8,128)(2,1)S(1)} %get-tuple-element.72), channel_id=1, source_target_pairs={{0,4},{4,0},{8,12},{12,8},{1,5},{5,1},{9,13},{13,9},{2,6},{6,2},{1... | collective-permute-start | bytes 196616 | tf_op jit(solution)/shard_map/ppermute | solution.py:29
  6.4 1.2 %shard_map.67 = (bf16[3,3,3,32,64]{4,3,2,1,0:T(8,128)(2,1)S(1)}, f32[1,64]{1,0:T(1,128)S(1)}, bf16[1,64,8,4,128]{4,3,2,1,0:T(4,128)(2,1)S(1)}) custom-call(bf16[3,3,3,32,64]{4,3,2,1,0:T(8,128)(2,1)} %bitcast.53, f32[1,64]{1,0:T(1,128)} %bitcast.54, bf16[1,64,8,4,128]{4,3,2,1,0:T(4,128)(2,1)} %refs_2_), custom_call_target="tpu_custom_call" | custom-call | tf_op jit(solution)/shard_map/pallas_call | solution.py:216
  8.4 1.7 %shard_map.68 = (bf16[2,8,64,128]{3,2,1,0:T(8,128)(2,1)S(1)}, f32[448,128]{1,0:T(8,128)S(1)}) custom-call(bf16[8,4,32,128]{3,2,1,0:T(8,128)(2,1)S(1)} %copy.22.x, bf16[4,32,128]{2,1,0:T(8,128)(2,1)S(1)} %get-tuple-element.84.below, bf16[4,32,128]{2,1,0:T(8,128)(2,1)S(1)} %get-tuple-element.83.above, bf16[192,288]{1,0:T(8,128)(2,1)S(1)} %copy.23.w1, ...), custom_call_target="tpu_custom_call" | custom-call | flops 452984832 | bytes 1454336 | tf_op jit(solution)/shard_map/pallas_call | solution.py:228
  10.7 0.8 %collective-permute-done.3 = bf16[2,32,128]{2,1,0:T(8,128)(2,1)S(1)} collective-permute-done((bf16[2,32,128]{2,1,0:T(8,128)(2,1)S(1)}, bf16[2,32,128]{2,1,0:T(8,128)(2,1)S(1)}, u32[]{:S(2)}, u32[]{:S(2)}) %collective-permute-start.3) | collective-permute-done | bytes 16416 | tf_op jit(solution)/shard_map/ppermute | solution.py:29
  11.5 1.7 %shard_map.69 = (bf16[2,8,64,128]{3,2,1,0:T(8,128)(2,1)S(1)}, f32[448,128]{1,0:T(8,128)S(1)}) custom-call(bf16[8,4,32,128]{3,2,1,0:T(8,128)(2,1)S(1)} %copy.22.x, bf16[4,32,128]{2,1,0:T(8,128)(2,1)S(1)} %get-tuple-element.84.below, bf16[4,32,128]{2,1,0:T(8,128)(2,1)S(1)} %get-tuple-element.83.above, bf16[8,32,128]{2,1,0:T(8,128)(2,1)S(1)} %get-tuple-element.70.left, ...), custom_call_target="tpu_custom_call" | custom-call | flops 452984832 | bytes 1847552 | tf_op jit(solution)/shard_map/pallas_call | solution.py:228
  13.9 0.7 %collective-permute-done.11 = bf16[4,64,128]{2,1,0:T(8,128)(2,1)S(1)} collective-permute-done((bf16[4,64,128]{2,1,0:T(8,128)(2,1)S(1)}, bf16[4,64,128]{2,1,0:T(8,128)(2,1)S(1)}, u32[]{:S(2)}, u32[]{:S(2)}) %collective-permute-start.11) | collective-permute-done | bytes 65568 | tf_op jit(solution)/shard_map/ppermute | solution.py:29
  14.9 1.5 %collective-permute-start.5 = (bf16[224,128]{1,0:T(8,128)(2,1)S(1)}, bf16[224,128]{1,0:T(8,128)(2,1)S(1)}, u32[]{:S(2)}, u32[]{:S(2)}) collective-permute-start(bf16[224,128]{1,0:T(8,128)(2,1)S(1)} %get-tuple-element.51), channel_id=1, source_target_pairs={{0,12},{4,8},{8,4},{12,0},{1,13},{5,9},{9,5},{13,1},{2,14},{6,10},... | collective-permute-start | bytes 172040 | tf_op jit(solution)/shard_map/ppermute | solution.py:51
  16.4 1.5 %collective-permute-start.6 = (bf16[224,128]{1,0:T(8,128)(2,1)S(1)}, bf16[224,128]{1,0:T(8,128)(2,1)S(1)}, u32[]{:S(2)}, u32[]{:S(2)}) collective-permute-start(bf16[224,128]{1,0:T(8,128)(2,1)S(1)} %get-tuple-element.51), channel_id=1, source_target_pairs={{0,8},{4,12},{8,0},{12,4},{1,9},{5,13},{9,1},{13,5},{2,10},{6,14},... | collective-permute-start | bytes 172040 | tf_op jit(solution)/shard_map/ppermute | solution.py:51
  17.9 0.5 %collective-permute-start.7 = (bf16[224,128]{1,0:T(8,128)(2,1)S(1)}, bf16[224,128]{1,0:T(8,128)(2,1)S(1)}, u32[]{:S(2)}, u32[]{:S(2)}) collective-permute-start(bf16[224,128]{1,0:T(8,128)(2,1)S(1)} %get-tuple-element.51), channel_id=1, source_target_pairs={{0,4},{4,0},{8,12},{12,8},{1,5},{5,1},{9,13},{13,9},{2,6},{6,2},{1... | collective-permute-start | bytes 172040 | tf_op jit(solution)/shard_map/ppermute | solution.py:51
  18.5 1.5 %collective-permute-start.12 = (bf16[10,64,128]{2,1,0:T(8,128)(2,1)S(1)}, bf16[10,64,128]{2,1,0:T(8,128)(2,1)S(1)}, u32[]{:S(2)}, u32[]{:S(2)}) collective-permute-start(bf16[10,64,128]{2,1,0:T(8,128)(2,1)S(1)} %get-tuple-element.55), channel_id=1, source_target_pairs={{0,12},{4,8},{8,4},{12,0},{1,13},{5,9},{9,5},{13,1},{2,14},{6,10},... | collective-permute-start | bytes 491528 | tf_op jit(solution)/shard_map/ppermute | solution.py:33
  20.0 0.4 %collective-permute-start.13 = (bf16[10,64,128]{2,1,0:T(8,128)(2,1)S(1)}, bf16[10,64,128]{2,1,0:T(8,128)(2,1)S(1)}, u32[]{:S(2)}, u32[]{:S(2)}) collective-permute-start(bf16[10,64,128]{2,1,0:T(8,128)(2,1)S(1)} %get-tuple-element.56), channel_id=1, source_target_pairs={{0,4},{4,0},{8,12},{12,8},{1,5},{5,1},{9,13},{13,9},{2,6},{6,2},{1... | collective-permute-start | bytes 491528 | tf_op jit(solution)/shard_map/ppermute | solution.py:29
  20.4 0.8 %collective-permute-done.6 = bf16[224,128]{1,0:T(8,128)(2,1)S(1)} collective-permute-done((bf16[224,128]{1,0:T(8,128)(2,1)S(1)}, bf16[224,128]{1,0:T(8,128)(2,1)S(1)}, u32[]{:S(2)}, u32[]{:S(2)}) %collective-permute-start.6) | collective-permute-done | bytes 57376 | tf_op jit(solution)/shard_map/ppermute | solution.py:51
  21.3 1.5 %collective-permute-done.7 = bf16[224,128]{1,0:T(8,128)(2,1)S(1)} collective-permute-done((bf16[224,128]{1,0:T(8,128)(2,1)S(1)}, bf16[224,128]{1,0:T(8,128)(2,1)S(1)}, u32[]{:S(2)}, u32[]{:S(2)}) %collective-permute-start.7) | collective-permute-done | bytes 57376 | tf_op jit(solution)/shard_map/ppermute | solution.py:51
  22.8 3.7 %collective-permute-start.10 = (bf16[224,128]{1,0:T(8,128)(2,1)S(1)}, bf16[224,128]{1,0:T(8,128)(2,1)S(1)}, u32[]{:S(2)}, u32[]{:S(2)}) collective-permute-start(bf16[224,128]{1,0:T(8,128)(2,1)S(1)} %fusion), channel_id=1, source_target_pairs={{0,3},{1,2},{2,1},{3,0},{4,7},{5,6},{6,5},{7,4},{8,11},{9,10},{10,... | collective-permute-start | bytes 172040 | tf_op jit(solution)/shard_map/ppermute | solution.py:51
  26.4 0.8 %collective-permute-start.9 = (bf16[224,128]{1,0:T(8,128)(2,1)S(1)}, bf16[224,128]{1,0:T(8,128)(2,1)S(1)}, u32[]{:S(2)}, u32[]{:S(2)}) collective-permute-start(bf16[224,128]{1,0:T(8,128)(2,1)S(1)} %fusion), channel_id=1, source_target_pairs={{0,1},{1,0},{2,3},{3,2},{4,5},{5,4},{6,7},{7,6},{8,9},{9,8},{10,11... | collective-permute-start | bytes 172040 | tf_op jit(solution)/shard_map/ppermute | solution.py:51
  27.2 1.3 %collective-permute-done.13 = bf16[10,64,128]{2,1,0:T(8,128)(2,1)S(1)} collective-permute-done((bf16[10,64,128]{2,1,0:T(8,128)(2,1)S(1)}, bf16[10,64,128]{2,1,0:T(8,128)(2,1)S(1)}, u32[]{:S(2)}, u32[]{:S(2)}) %collective-permute-start.13) | collective-permute-done | bytes 163872 | tf_op jit(solution)/shard_map/ppermute | solution.py:29
  28.6 1.2 %shard_map.70 = bf16[8,4,32,128]{3,2,1,0:T(8,128)(2,1)S(1)} custom-call(bf16[2,8,64,128]{3,2,1,0:T(8,128)(2,1)S(1)} %get-tuple-element.38.inner, bf16[8,64,128]{2,1,0:T(8,128)(2,1)S(1)} %get-tuple-element.64.top, bf16[8,64,128]{2,1,0:T(8,128)(2,1)S(1)} %get-tuple-element.63.bottom, bf16[4,64,128]{2,1,0:T(8,128)(2,1)S(1)} %get-tuple-element.78.below, ...), custom_call_target="tpu_custom_call" | custom-call | flops 452984832 | bytes 1355776 | tf_op jit(solution)/shard_map/pallas_call | solution.py:228
  29.8 1.7 %collective-permute-done.8 = bf16[224,128]{1,0:T(8,128)(2,1)S(1)} collective-permute-done((bf16[224,128]{1,0:T(8,128)(2,1)S(1)}, bf16[224,128]{1,0:T(8,128)(2,1)S(1)}, u32[]{:S(2)}, u32[]{:S(2)}) %collective-permute-start.8) | collective-permute-done | bytes 57376 | tf_op jit(solution)/shard_map/ppermute | solution.py:51
  31.7 0.8 %copy.26 = bf16[1,32,8,4,128]{4,3,2,1,0:T(4,128)(2,1)} copy(bf16[1,32,8,4,128]{4,1,3,2,0:T(8,128)(2,1)S(1)} %bitcast.49) | data formatting | bytes 524288
  32.5 0.5 %collective-permute-done.14 = f32[224,128]{1,0:T(8,128)S(1)} collective-permute-done((f32[224,128]{1,0:T(8,128)S(1)}, f32[224,128]{1,0:T(8,128)S(1)}, u32[]{:S(2)}, u32[]{:S(2)}) %collective-permute-start.14) | collective-permute-done | bytes 114720 | tf_op jit(solution)/shard_map/ppermute | solution.py:51
  33.0 0.9 %shard_map.71 = (f32[864,64]{1,0:T(8,128)}, f32[1,64]{1,0:T(1,128)}) custom-call(f32[224,128]{1,0:T(8,128)S(1)} %get-tuple-element.68.refs_0_, f32[224,128]{1,0:T(8,128)S(1)} %get-tuple-element.67.refs_1_), custom_call_target="tpu_custom_call" | custom-call | flops 57344 | bytes 450816 | tf_op jit(solution)/shard_map/pallas_call | solution.py:228
  (43 shorter events, 2.7 us)
Async XLA Ops:
  1.7 6.6 %collective-permute-start = (bf16[4,32,128]{2,1,0:T(8,128)(2,1)S(1)}, bf16[4,32,128]{2,1,0:T(8,128)(2,1)S(1)}, u32[]{:S(2)}, u32[]{:S(2)}) collective-permute-start(bf16[4,32,128]{2,1,0:T(8,128)(2,1)S(1)} %select_bitcast_fusion), channel_id=1, source_target_pairs={{0,16},{16,0},{1,17},{17,1},{2,18},{18,2},{3,19},{19,3},{4,20},{20... | collective-permute-start | bytes 98312 | tf_op jit(solution)/shard_map/ppermute | solution.py:29
  2.3 7.8 %collective-permute-start.1 = (bf16[8,32,128]{2,1,0:T(8,128)(2,1)S(1)}, bf16[8,32,128]{2,1,0:T(8,128)(2,1)S(1)}, u32[]{:S(2)}, u32[]{:S(2)}) collective-permute-start(bf16[8,32,128]{2,1,0:T(8,128)(2,1)S(1)} %get-tuple-element.71), channel_id=1, source_target_pairs={{0,12},{4,8},{8,4},{12,0},{1,13},{5,9},{9,5},{13,1},{2,14},{6,10},... | collective-permute-start | bytes 196616 | tf_op jit(solution)/shard_map/ppermute | solution.py:33
  5.8 4.4 %collective-permute-start.2 = (bf16[8,32,128]{2,1,0:T(8,128)(2,1)S(1)}, bf16[8,32,128]{2,1,0:T(8,128)(2,1)S(1)}, u32[]{:S(2)}, u32[]{:S(2)}) collective-permute-start(bf16[8,32,128]{2,1,0:T(8,128)(2,1)S(1)} %get-tuple-element.72), channel_id=1, source_target_pairs={{0,4},{4,0},{8,12},{12,8},{1,5},{5,1},{9,13},{13,9},{2,6},{6,2},{1... | collective-permute-start | bytes 196616 | tf_op jit(solution)/shard_map/ppermute | solution.py:29
  10.2 1.2 %collective-permute-start.3 = (bf16[2,32,128]{2,1,0:T(8,128)(2,1)S(1)}, bf16[2,32,128]{2,1,0:T(8,128)(2,1)S(1)}, u32[]{:S(2)}, u32[]{:S(2)}) collective-permute-start(bf16[2,32,128]{2,1,0:T(8,128)(2,1)S(1)} %maximum_select_fusion.1), channel_id=1, source_target_pairs={{0,16},{16,0},{1,17},{17,1},{2,18},{18,2},{3,19},{19,3},{4,20},{20... | collective-permute-start | bytes 49160 | tf_op jit(solution)/shard_map/ppermute | solution.py:29
  13.2 1.3 %collective-permute-start.11 = (bf16[4,64,128]{2,1,0:T(8,128)(2,1)S(1)}, bf16[4,64,128]{2,1,0:T(8,128)(2,1)S(1)}, u32[]{:S(2)}, u32[]{:S(2)}) collective-permute-start(bf16[4,64,128]{2,1,0:T(8,128)(2,1)S(1)} %maximum_select_fusion), channel_id=1, source_target_pairs={{0,16},{16,0},{1,17},{17,1},{2,18},{18,2},{3,19},{19,3},{4,20},{20... | collective-permute-start | bytes 196616 | tf_op jit(solution)/shard_map/ppermute | solution.py:29
  13.5 1.4 %collective-permute-start.4 = (f32[224,128]{1,0:T(8,128)S(1)}, f32[224,128]{1,0:T(8,128)S(1)}, u32[]{:S(2)}, u32[]{:S(2)}) collective-permute-start(f32[224,128]{1,0:T(8,128)S(1)} %slice_select_fusion), channel_id=1, source_target_pairs={{0,16},{16,0},{1,17},{17,1},{2,18},{18,2},{3,19},{19,3},{4,20},{20... | collective-permute-start | bytes 344072 | tf_op jit(solution)/shard_map/ppermute | solution.py:51
  14.9 5.5 %collective-permute-start.5 = (bf16[224,128]{1,0:T(8,128)(2,1)S(1)}, bf16[224,128]{1,0:T(8,128)(2,1)S(1)}, u32[]{:S(2)}, u32[]{:S(2)}) collective-permute-start(bf16[224,128]{1,0:T(8,128)(2,1)S(1)} %get-tuple-element.51), channel_id=1, source_target_pairs={{0,12},{4,8},{8,4},{12,0},{1,13},{5,9},{9,5},{13,1},{2,14},{6,10},... | collective-permute-start | bytes 172040 | tf_op jit(solution)/shard_map/ppermute | solution.py:51
  16.4 4.9 %collective-permute-start.6 = (bf16[224,128]{1,0:T(8,128)(2,1)S(1)}, bf16[224,128]{1,0:T(8,128)(2,1)S(1)}, u32[]{:S(2)}, u32[]{:S(2)}) collective-permute-start(bf16[224,128]{1,0:T(8,128)(2,1)S(1)} %get-tuple-element.51), channel_id=1, source_target_pairs={{0,8},{4,12},{8,0},{12,4},{1,9},{5,13},{9,1},{13,5},{2,10},{6,14},... | collective-permute-start | bytes 172040 | tf_op jit(solution)/shard_map/ppermute | solution.py:51
  17.9 4.8 %collective-permute-start.7 = (bf16[224,128]{1,0:T(8,128)(2,1)S(1)}, bf16[224,128]{1,0:T(8,128)(2,1)S(1)}, u32[]{:S(2)}, u32[]{:S(2)}) collective-permute-start(bf16[224,128]{1,0:T(8,128)(2,1)S(1)} %get-tuple-element.51), channel_id=1, source_target_pairs={{0,4},{4,0},{8,12},{12,8},{1,5},{5,1},{9,13},{13,9},{2,6},{6,2},{1... | collective-permute-start | bytes 172040 | tf_op jit(solution)/shard_map/ppermute | solution.py:51
  18.5 8.7 %collective-permute-start.12 = (bf16[10,64,128]{2,1,0:T(8,128)(2,1)S(1)}, bf16[10,64,128]{2,1,0:T(8,128)(2,1)S(1)}, u32[]{:S(2)}, u32[]{:S(2)}) collective-permute-start(bf16[10,64,128]{2,1,0:T(8,128)(2,1)S(1)} %get-tuple-element.55), channel_id=1, source_target_pairs={{0,12},{4,8},{8,4},{12,0},{1,13},{5,9},{9,5},{13,1},{2,14},{6,10},... | collective-permute-start | bytes 491528 | tf_op jit(solution)/shard_map/ppermute | solution.py:33
  20.0 8.5 %collective-permute-start.13 = (bf16[10,64,128]{2,1,0:T(8,128)(2,1)S(1)}, bf16[10,64,128]{2,1,0:T(8,128)(2,1)S(1)}, u32[]{:S(2)}, u32[]{:S(2)}) collective-permute-start(bf16[10,64,128]{2,1,0:T(8,128)(2,1)S(1)} %get-tuple-element.56), channel_id=1, source_target_pairs={{0,4},{4,0},{8,12},{12,8},{1,5},{5,1},{9,13},{13,9},{2,6},{6,2},{1... | collective-permute-start | bytes 491528 | tf_op jit(solution)/shard_map/ppermute | solution.py:29
  22.8 7.0 %collective-permute-start.10 = (bf16[224,128]{1,0:T(8,128)(2,1)S(1)}, bf16[224,128]{1,0:T(8,128)(2,1)S(1)}, u32[]{:S(2)}, u32[]{:S(2)}) collective-permute-start(bf16[224,128]{1,0:T(8,128)(2,1)S(1)} %fusion), channel_id=1, source_target_pairs={{0,3},{1,2},{2,1},{3,0},{4,7},{5,6},{6,5},{7,4},{8,11},{9,10},{10,... | collective-permute-start | bytes 172040 | tf_op jit(solution)/shard_map/ppermute | solution.py:51
  26.4 5.1 %collective-permute-start.8 = (bf16[224,128]{1,0:T(8,128)(2,1)S(1)}, bf16[224,128]{1,0:T(8,128)(2,1)S(1)}, u32[]{:S(2)}, u32[]{:S(2)}) collective-permute-start(bf16[224,128]{1,0:T(8,128)(2,1)S(1)} %fusion), channel_id=1, source_target_pairs={{0,2},{1,3},{2,0},{3,1},{4,6},{5,7},{6,4},{7,5},{8,10},{9,11},{10,... | collective-permute-start | bytes 172040 | tf_op jit(solution)/shard_map/ppermute | solution.py:51
  26.4 5.1 %collective-permute-start.9 = (bf16[224,128]{1,0:T(8,128)(2,1)S(1)}, bf16[224,128]{1,0:T(8,128)(2,1)S(1)}, u32[]{:S(2)}, u32[]{:S(2)}) collective-permute-start(bf16[224,128]{1,0:T(8,128)(2,1)S(1)} %fusion), channel_id=1, source_target_pairs={{0,1},{1,0},{2,3},{3,2},{4,5},{5,4},{6,7},{7,6},{8,9},{9,8},{10,11... | collective-permute-start | bytes 172040 | tf_op jit(solution)/shard_map/ppermute | solution.py:51
  31.6 1.4 %collective-permute-start.14 = (f32[224,128]{1,0:T(8,128)S(1)}, f32[224,128]{1,0:T(8,128)S(1)}, u32[]{:S(2)}, u32[]{:S(2)}) collective-permute-start(f32[224,128]{1,0:T(8,128)S(1)} %add_add_fusion), channel_id=1, source_target_pairs={{0,16},{16,0},{1,17},{17,1},{2,18},{18,2},{3,19},{19,3},{4,20},{20... | collective-permute-start | bytes 344072 | tf_op jit(solution)/shard_map/ppermute | solution.py:51

commit v8 on v7

--- a/solution.py
+++ b/solution.py
@@ -1,3 +1,5 @@
+import functools
+
 import jax
 import jax.numpy as jnp
 from jax import lax
@@ -8,7 +10,7 @@
 F32 = jnp.float32
 BF16 = jnp.bfloat16
 AXES = ("depth", "height", "dp")
-WAYS = {"depth": (3, 2, 1), "height": (3, 2, 1), "dp": (2, 1, 3)}
+WAYS = {"depth": (1, 2, 3), "height": (1, 2, 3), "dp": (1, 2, 3)}
 
 
 def paired(axis):
@@ -68,26 +70,29 @@
     return jnp.where(lane == edge, 0.0, pltpu.roll(value, (-step) % width, 1))
 
 
-def forward_rows(count, width, cot_of, w1, bias, delta, before, payload, patches, taps, slopes, grad):
-    co = bias.shape[1]
-    depth = patches.shape[1] // (count * width)
+def forward_rows(positions, row_of, w1, bias, cot, delta, before, payload, patches, taps, slopes, grad):
+    co, width = bias.shape[1], cot.shape[3]
+    ci = patches.shape[0] // 9
+    for at, (d, h) in enumerate(positions):
+        for a in range(3):
+            for b in range(3):
+                patches[pl.ds((a * 3 + b) * ci, ci), pl.ds(at * width, width)] = row_of(d + a, h + b)
     taps[...] = jnp.dot(w1[...], patches[...], preferred_element_type=F32)
     shift_bias = jnp.broadcast_to(bias[...], (width, co)).T
     bias_acc = jnp.zeros((co, width), F32)
-    for d in range(depth):
-        for at in range(count):
-            lanes = pl.ds((d * count + at) * width, width)
-            linear = taps[co : 2 * co, lanes] + shift_bias
-            linear = linear + shifted(taps[:co, lanes], -1) + shifted(taps[2 * co :, lanes], 1)
-            sigma = 1.0 / (1.0 + jnp.exp(-linear))
-            slope = cot_of(d, at).astype(F32) * sigma * (1.0 + linear * (1.0 - sigma))
-            rounded = slope.astype(BF16)
-            delta[at, d] = rounded
-            wide = rounded.astype(F32)
-            bias_acc = bias_acc + wide
-            slopes[:co, lanes] = shifted(wide, 1).astype(BF16)
-            slopes[co : 2 * co, lanes] = rounded
-            slopes[2 * co :, lanes] = shifted(wide, -1).astype(BF16)
+    for at, (d, h) in enumerate(positions):
+        lanes = pl.ds(at * width, width)
+        linear = taps[co : 2 * co, lanes] + shift_bias
+        linear = linear + shifted(taps[:co, lanes], -1) + shifted(taps[2 * co :, lanes], 1)
+        sigma = 1.0 / (1.0 + jnp.exp(-linear))
+        slope = cot[d, h].astype(F32) * sigma * (1.0 + linear * (1.0 - sigma))
+        rounded = slope.astype(BF16)
+        delta[at] = rounded
+        wide = rounded.astype(F32)
+        bias_acc = bias_acc + wide
+        slopes[:co, lanes] = shifted(wide, 1).astype(BF16)
+        slopes[co : 2 * co, lanes] = rounded
+        slopes[2 * co :, lanes] = shifted(wide, -1).astype(BF16)
     grad[...] = lax.dot_general(
         patches[...], slopes[...], (((1,), (1,)), ((), ())), preferred_element_type=F32
     )
@@ -109,57 +114,38 @@
         payload[at, :] = value if before is None else before[at, :] + value
 
 
-def fill_taps(row_of, depth, rows, patches):
-    ci, width = row_of(1, 1).shape
-    count = len(rows)
-    for d in range(depth):
-        for at, h in enumerate(rows):
-            for a in range(3):
-                for b in range(3):
-                    lanes = pl.ds((d * count + at) * width, width)
-                    patches[pl.ds((a * 3 + b) * ci, ci), lanes] = row_of(d + a, h + b)
-
-
-def inner_kernel(x, below, above, w1, bias, cot, delta, payload, patches, *scratch):
+def parts_of(depth, height):
+    layers, rows = range(1, depth - 1), range(1, height - 1)
+    return (
+        [(d, h) for d in layers for h in rows],
+        [(d, h) for h in (0, height - 1) for d in layers],
+        [(d, h) for d in (0, depth - 1) for h in range(height)],
+    )
+
+
+def forward_kernel(positions, halos, x, *refs):
+    left, right, low, high = (*refs[:halos], None, None, None, None)[:4]
+    w1, bias, cot, *refs = refs[halos:]
+    before, *refs = refs if halos else (None, *refs)
     depth, height = x.shape[:2]
 
     def row_of(d, h):
-        return below[h - 1] if d == 0 else above[h - 1] if d == depth + 1 else x[d - 1, h - 1]
-
-    def cot_of(d, at):
-        return cot[d, at + 1]
-
-    fill_taps(row_of, depth, range(1, height - 1), patches)
-    width = x.shape[3]
-    forward_rows(height - 2, width, cot_of, w1, bias, delta, None, payload, patches, *scratch)
-
-
-def outer_kernel(
-    x, below, above, left, right, corners_below, corners_above, w1, bias, cot, before, *refs
-):
-    delta, payload, patches, *scratch = refs
-    depth, height = x.shape[:2]
-
-    def row_of(d, h):
-        if 0 < h <= height:
-            return below[h - 1] if d == 0 else above[h - 1] if d == depth + 1 else x[d - 1, h - 1]
-        side = 0 if h == 0 else 1
         if d == 0:
-            return corners_below[side]
+            return low[h]
         if d == depth + 1:
-            return corners_above[side]
-        return right[d - 1] if side else left[d - 1]
-
-    def cot_of(d, at):
-        return cot[d, at * (height - 1)]
-
-    fill_taps(row_of, depth, (0, height - 1), patches)
-    forward_rows(2, x.shape[3], cot_of, w1, bias, delta, before, payload, patches, *scratch)
-
-
-def input_kernel(inner, top, bottom, below, above, left, right, w2, out, patches):
-    depth, co, width = top.shape
-    height, ci = out.shape[1:3]
+            return high[h]
+        return left[d - 1] if h == 0 else right[d - 1] if h == height + 1 else x[d - 1, h - 1]
+
+    delta, *refs = refs
+    forward_rows(positions, row_of, w1, bias, cot, delta, before, *refs)
+
+
+def input_kernel(inner, sides, ends, below, above, left, right, w2, out, patches):
+    depth, height, ci, width = out.shape
+    co = inner.shape[1]
+    place = {}
+    for ref, positions in zip((inner, sides, ends), parts_of(depth, height)):
+        place.update({position: (ref, at) for at, position in enumerate(positions)})
 
     def row_of(d, h):
         if h == 0:
@@ -170,7 +156,8 @@
             return below[h - 1]
         if d == depth + 1:
             return above[h - 1]
-        return top[d - 1] if h == 1 else bottom[d - 1] if h == height else inner[h - 2, d - 1]
+        ref, at = place[d - 1, h - 1]
+        return ref[at]
 
     fill_patches(row_of, depth, range(height), patches)
     for d in range(depth):
@@ -267,7 +254,7 @@
     co = cotangent.shape[1]
     payload_rows = 9 * ci + 9 * ci // 2 + 16
     payload_shape = jax.ShapeDtypeStruct((payload_rows, 2 * co), F32)
-    flops = 2 * depth * width * 27 * ci * co
+    flops = 4 * width * 27 * ci * co
     total = None
     fields = []
     fields_in = [inputs[cube].transpose(1, 2, 0, 3) for cube in range(cubes)]
@@ -279,42 +266,48 @@
     w1 = taps.transpose(2, 4, 0, 1, 3).reshape(3 * co, 9 * ci)
     for cube in range(cubes):
         x = fields_in[cube]
-        left, right = exchange(*rows[cube], "height")
-        below, above = exchange(x[0], x[-1], "depth")
         cot = cotangent[cube].transpose(1, 2, 0, 3)
-
-        def forward(kernel, rows, *args):
+        parts = parts_of(depth, height)
+
+        def forward(which, halos, so_far):
+            count = len(parts[which])
             return call(
-                kernel,
-                (jax.ShapeDtypeStruct((rows, depth, co, width), BF16), payload_shape),
+                functools.partial(forward_kernel, parts[which], len(halos)),
+                (jax.ShapeDtypeStruct((count, co, width), BF16), payload_shape),
                 [
-                    pltpu.VMEM((9 * ci, depth * rows * width), BF16),
-                    pltpu.VMEM((3 * co, depth * rows * width), F32),
-                    pltpu.VMEM((3 * co, depth * rows * width), BF16),
+                    pltpu.VMEM((9 * ci, count * width), BF16),
+                    pltpu.VMEM((3 * co, count * width), F32),
+                    pltpu.VMEM((3 * co, count * width), BF16),
                     pltpu.VMEM((9 * ci, 3 * co), F32),
                 ],
-                2 * flops * rows,
-                *args,
+                flops * count,
+                x,
+                *halos,
+                w1,
+                bias_row,
+                cot,
+                *so_far,
             )
 
-        shared = (x, below, above)
-        inner, part = forward(inner_kernel, height - 2, *shared, w1, bias_row, cot)
-        part, taps = lax.optimization_barrier((part, taps))
-        w2 = jnp.flip(taps, (0, 1)).transpose(2, 3, 0, 1, 4).reshape(3 * ci, 9 * co)
-        part, w2 = lax.optimization_barrier((part, w2))
-        corners = exchange(jnp.stack([left[0], right[0]]), jnp.stack([left[-1], right[-1]]), "depth")
-        outer, part = forward(
-            outer_kernel, 2, *shared, left, right, *corners, w1, bias_row, cot, part
-        )
+        inner, part = forward(0, (), ())
+        left, right = exchange(*rows[cube], "height")
+        part, left, right = lax.optimization_barrier((part, left, right))
+
+        def layer(at):
+            return jnp.concatenate([left[at][None], x[at], right[at][None]], axis=0)
+
+        low, high = exchange(layer(0), layer(-1), "depth")
+        sides, part = forward(1, (left, right), (part,))
+        ends, part = forward(2, (left, right, low, high), (part,))
         total = part if total is None else total + part
-        top, bottom = outer[0], outer[1]
-
-        def layer(at):
-            return jnp.concatenate([top[at][None], inner[:, at], bottom[at][None]], axis=0)
-
-        below, above = exchange(layer(0), layer(-1), "depth")
-        around = exchange(*columns(top, bottom, below, above), "height")
-        fields.append((inner, top, bottom, below, above, *around))
+        below, above = exchange(ends[:height], ends[height:], "depth")
+        below, above, taps = lax.optimization_barrier((below, above, taps))
+        first_row = jnp.concatenate([ends[:1], sides[: depth - 2], ends[height : height + 1]], axis=0)
+        last_row = jnp.concatenate([ends[height - 1 : height], sides[depth - 2 :], ends[-1:]], axis=0)
+        around = exchange(*columns(first_row, last_row, below, above), "height")
+        fields.append((inner, sides, ends, below, above, *around))
+    w2 = jnp.flip(taps, (0, 1)).transpose(2, 3, 0, 1, 4).reshape(3 * ci, 9 * co)
+
     def input_gradients(fields):
         grads = []
         for field in fields:
@@ -322,7 +315,7 @@
                 input_kernel,
                 (jax.ShapeDtypeStruct((depth, height, ci, width), BF16),),
                 [pltpu.VMEM(((depth + 2) * 3 * co, height * width), BF16)],
-                flops * height,
+                flops // 2 * depth * height,
                 *field,
                 w2,
             )

time: 34.1 us -> 33.4 us (0.979)
  waiting for transfers between devices: 7.69 us -> 6.44 us
  Pallas kernels: 6.61 us -> 7.06 us
    ppermute x8, waiting for transfers between devices: 4.79 us -> 3.49 us  [swap(): lax.ppermute(array, axis, [(i, i ^ mask) for i in range(lax.axis_size(axi...]
    pallas_call x4 -> x5, Pallas kernels: 5.4 us -> 5.85 us  [call(): pl.pallas_call(kernel, out_shape=outs, scratch_shapes=scratch, compiler_p...]
    ppermute x5 -> x4, starting transfers between devices: 1.77 us -> 2.06 us  [meet(): first = lax.ppermute(jnp.where(even, high_edge, low_edge), axis, inner)]
    ppermute x5 -> x4, waiting for transfers between devices: 2.9 us -> 2.78 us  [meet(): first = lax.ppermute(jnp.where(even, high_edge, low_edge), axis, inner)]
    unnamed x2 -> x6, local copies, waits for them, and re-layouts: 1.89 us -> 1.95 us
  transfers between devices with their start and end apart: 15 -> 14, of which waited for: 9 -> 9; matrix products, arithmetic and copies ran while one was open for 6% -> 6% of each run, Pallas kernels for 12% -> 15%
where the time goes in v8:
time: 33.4 us; the launch traced here: 33.2 us
  starting transfers between devices  15.4 us (46%)
  Pallas kernels  7.06 us (21%)
  waiting for transfers between devices  6.44 us (19%)
  local copies, waits for them, and re-layouts  3.1 us (9%)
  between operations  0.89 us (3%)
    ppermute x8, starting transfers between devices, swap(): lax.ppermute(array, axis, [(i, i ^ mask) for i in range(lax.axis_size(axi...  8.16 us
    pallas_call x5, Pallas kernels, call(): pl.pallas_call(kernel, out_shape=outs, scratch_shapes=scratch, compiler_p...  5.85 us
    ppermute x2, starting transfers between devices, meet(): second = lax.ppermute(jnp.where(even, low_edge, high_edge), axis, outer)  5.2 us
    ppermute x8, waiting for transfers between devices, swap(): lax.ppermute(array, axis, [(i, i ^ mask) for i in range(lax.axis_size(axi...  3.49 us
    ppermute x4, waiting for transfers between devices, meet(): first = lax.ppermute(jnp.where(even, high_edge, low_edge), axis, inner)  2.78 us
    ppermute x4, starting transfers between devices, meet(): first = lax.ppermute(jnp.where(even, high_edge, low_edge), axis, inner)  2.06 us
    unnamed x6, local copies, waits for them, and re-layouts  1.95 us
    pallas_call x1, Pallas kernels, loaded(): pl.pallas_call(load_kernel, out_shape=[jax.ShapeDtypeStruct(a.shape, a.dt...  1.21 us
  transfers between devices with their start and end apart: 14, of which 9 were waited for; matrix products, arithmetic and copies ran while one was open for 6% of the time, Pallas kernels for 15%

profile of v8, /device:TPU:0, one launch (start us, length us, event | category | flops | bytes accessed | tf_op | source)
XLA Modules:
  0.0 33.2 jit_solution(10735999313617529112)
XLA Ops:
  0.6 1.1 %copy.29 = bf16[1,32,8,4,128]{4,1,2,3,0:T(8,128)(2,1)S(1)} copy(bf16[1,32,8,4,128]{4,3,2,1,0:T(4,128)(2,1)} %param.4) | data formatting | bytes 524288 | tf_op args[0]
  1.7 4.0 %collective-permute-start = (bf16[8,32,128]{2,1,0:T(8,128)(2,1)S(1)}, bf16[8,32,128]{2,1,0:T(8,128)(2,1)S(1)}, u32[]{:S(2)}, u32[]{:S(2)}) collective-permute-start(bf16[8,32,128]{2,1,0:T(8,128)(2,1)S(1)} %get-tuple-element.79), channel_id=1, source_target_pairs={{0,12},{4,8},{8,4},{12,0},{1,13},{5,9},{9,5},{13,1},{2,14},{6,10},... | collective-permute-start | bytes 196616 | tf_op jit(solution)/shard_map/ppermute | solution.py:35
  5.7 0.5 %collective-permute-start.1 = (bf16[8,32,128]{2,1,0:T(8,128)(2,1)S(1)}, bf16[8,32,128]{2,1,0:T(8,128)(2,1)S(1)}, u32[]{:S(2)}, u32[]{:S(2)}) collective-permute-start(bf16[8,32,128]{2,1,0:T(8,128)(2,1)S(1)} %get-tuple-element.80), channel_id=1, source_target_pairs={{0,4},{4,0},{8,12},{12,8},{1,5},{5,1},{9,13},{13,9},{2,6},{6,2},{1... | collective-permute-start | bytes 196616 | tf_op jit(solution)/shard_map/ppermute | solution.py:31
  6.3 1.2 %shard_map.67 = (bf16[3,3,3,32,64]{4,3,2,1,0:T(8,128)(2,1)S(1)}, f32[1,64]{1,0:T(1,128)S(1)}, bf16[1,64,8,4,128]{4,3,2,1,0:T(4,128)(2,1)S(1)}) custom-call(bf16[3,3,3,32,64]{4,3,2,1,0:T(8,128)(2,1)} %bitcast.40, f32[1,64]{1,0:T(1,128)} %bitcast.41, bf16[1,64,8,4,128]{4,3,2,1,0:T(4,128)(2,1)} %refs_2_), custom_call_target="tpu_custom_call" | custom-call | tf_op jit(solution)/shard_map/pallas_call | solution.py:203
  8.2 1.3 %shard_map.68 = (bf16[12,64,128]{2,1,0:T(8,128)(2,1)S(1)}, f32[448,128]{1,0:T(8,128)S(1)}) custom-call(bf16[8,4,32,128]{3,2,1,0:T(8,128)(2,1)S(1)} %copy.22.x, bf16[192,288]{1,0:T(8,128)(2,1)S(1)} %copy.19.refs_0_.refs_2_.refs_4_, f32[1,64]{1,0:T(1,128)S(1)} %get-tuple-element.33.refs_1_.refs_3_.refs_5_, bf16[8,4,64,128]{3,2,1,0:T(8,128)(2,1)S(1)} %bitcast.32), custom_call_target="tpu_custom_call" | custom-call | flops 339738624 | bytes 1323264 | tf_op jit(solution)/shard_map/pallas_call | solution.py:215
  9.5 0.4 %collective-permute-done.1 = bf16[8,32,128]{2,1,0:T(8,128)(2,1)S(1)} collective-permute-done((bf16[8,32,128]{2,1,0:T(8,128)(2,1)S(1)}, bf16[8,32,128]{2,1,0:T(8,128)(2,1)S(1)}, u32[]{:S(2)}, u32[]{:S(2)}) %collective-permute-start.1) | collective-permute-done | bytes 65568 | tf_op jit(solution)/shard_map/ppermute | solution.py:31
  10.1 1.3 %shard_map.69 = (bf16[12,64,128]{2,1,0:T(8,128)(2,1)S(1)}, f32[448,128]{1,0:T(8,128)S(1)}) custom-call(bf16[8,4,32,128]{3,2,1,0:T(8,128)(2,1)S(1)} %copy.22.x, bf16[8,32,128]{2,1,0:T(8,128)(2,1)S(1)} %get-tuple-element.38.refs_0_, bf16[8,32,128]{2,1,0:T(8,128)(2,1)S(1)} %get-tuple-element.39.refs_1_, bf16[192,288]{1,0:T(8,128)(2,1)S(1)} %copy.19.refs_0_.refs_2_.refs_4_, ...), custom_call_target="tpu_custom_call" | custom-call | flops 339738624 | bytes 1683712 | tf_op jit(solution)/shard_map/pallas_call | solution.py:215
  11.4 1.2 %shard_map.70 = (bf16[8,64,128]{2,1,0:T(8,128)(2,1)S(1)}, f32[448,128]{1,0:T(8,128)S(1)}) custom-call(bf16[8,4,32,128]{3,2,1,0:T(8,128)(2,1)S(1)} %copy.22.x, bf16[8,32,128]{2,1,0:T(8,128)(2,1)S(1)} %get-tuple-element.38.refs_0_, bf16[8,32,128]{2,1,0:T(8,128)(2,1)S(1)} %get-tuple-element.39.refs_1_, bf16[6,32,128]{2,1,0:T(8,128)(2,1)S(1)} %get-tuple-element.92.refs_2_, ...), custom_call_target="tpu_custom_call" | custom-call | flops 226492416 | bytes 1716480 | tf_op jit(solution)/shard_map/pallas_call | solution.py:215
  12.6 0.6 %collective-permute-start.10 = (bf16[4,64,128]{2,1,0:T(8,128)(2,1)S(1)}, bf16[4,64,128]{2,1,0:T(8,128)(2,1)S(1)}, u32[]{:S(2)}, u32[]{:S(2)}) collective-permute-start(bf16[4,64,128]{2,1,0:T(8,128)(2,1)S(1)} %slice_select_fusion.1), channel_id=1, source_target_pairs={{0,16},{16,0},{1,17},{17,1},{2,18},{18,2},{3,19},{19,3},{4,20},{20... | collective-permute-start | bytes 196616 | tf_op jit(solution)/shard_map/ppermute | solution.py:31
  13.3 0.8 %collective-permute-done.10 = bf16[4,64,128]{2,1,0:T(8,128)(2,1)S(1)} collective-permute-done((bf16[4,64,128]{2,1,0:T(8,128)(2,1)S(1)}, bf16[4,64,128]{2,1,0:T(8,128)(2,1)S(1)}, u32[]{:S(2)}, u32[]{:S(2)}) %collective-permute-start.10) | collective-permute-done | bytes 65568 | tf_op jit(solution)/shard_map/ppermute | solution.py:31
  14.6 1.2 %collective-permute-start.6 = (bf16[224,128]{1,0:T(8,128)(2,1)S(1)}, bf16[224,128]{1,0:T(8,128)(2,1)S(1)}, u32[]{:S(2)}, u32[]{:S(2)}) collective-permute-start(bf16[224,128]{1,0:T(8,128)(2,1)S(1)} %get-tuple-element.59), channel_id=1, source_target_pairs={{0,12},{4,8},{8,4},{12,0},{1,13},{5,9},{9,5},{13,1},{2,14},{6,10},... | collective-permute-start | bytes 172040 | tf_op jit(solution)/shard_map/ppermute | solution.py:53
  15.9 1.4 %collective-permute-start.5 = (bf16[224,128]{1,0:T(8,128)(2,1)S(1)}, bf16[224,128]{1,0:T(8,128)(2,1)S(1)}, u32[]{:S(2)}, u32[]{:S(2)}) collective-permute-start(bf16[224,128]{1,0:T(8,128)(2,1)S(1)} %get-tuple-element.59), channel_id=1, source_target_pairs={{0,8},{4,12},{8,0},{12,4},{1,9},{5,13},{9,1},{13,5},{2,10},{6,14},... | collective-permute-start | bytes 172040 | tf_op jit(solution)/shard_map/ppermute | solution.py:53
  17.3 0.9 %collective-permute-start.4 = (bf16[224,128]{1,0:T(8,128)(2,1)S(1)}, bf16[224,128]{1,0:T(8,128)(2,1)S(1)}, u32[]{:S(2)}, u32[]{:S(2)}) collective-permute-start(bf16[224,128]{1,0:T(8,128)(2,1)S(1)} %get-tuple-element.59), channel_id=1, source_target_pairs={{0,4},{4,0},{8,12},{12,8},{1,5},{5,1},{9,13},{13,9},{2,6},{6,2},{1... | collective-permute-start | bytes 172040 | tf_op jit(solution)/shard_map/ppermute | solution.py:53
  18.6 1.2 %collective-permute-start.11 = (bf16[10,64,128]{2,1,0:T(8,128)(2,1)S(1)}, bf16[10,64,128]{2,1,0:T(8,128)(2,1)S(1)}, u32[]{:S(2)}, u32[]{:S(2)}) collective-permute-start(bf16[10,64,128]{2,1,0:T(8,128)(2,1)S(1)} %get-tuple-element.63), channel_id=1, source_target_pairs={{0,12},{4,8},{8,4},{12,0},{1,13},{5,9},{9,5},{13,1},{2,14},{6,10},... | collective-permute-start | bytes 491528 | tf_op jit(solution)/shard_map/ppermute | solution.py:35
  19.8 0.9 %collective-permute-start.12 = (bf16[10,64,128]{2,1,0:T(8,128)(2,1)S(1)}, bf16[10,64,128]{2,1,0:T(8,128)(2,1)S(1)}, u32[]{:S(2)}, u32[]{:S(2)}) collective-permute-start(bf16[10,64,128]{2,1,0:T(8,128)(2,1)S(1)} %get-tuple-element.64), channel_id=1, source_target_pairs={{0,4},{4,0},{8,12},{12,8},{1,5},{5,1},{9,13},{13,9},{2,6},{6,2},{1... | collective-permute-start | bytes 491528 | tf_op jit(solution)/shard_map/ppermute | solution.py:31
  20.8 1.2 %collective-permute-done.4 = bf16[224,128]{1,0:T(8,128)(2,1)S(1)} collective-permute-done((bf16[224,128]{1,0:T(8,128)(2,1)S(1)}, bf16[224,128]{1,0:T(8,128)(2,1)S(1)}, u32[]{:S(2)}, u32[]{:S(2)}) %collective-permute-start.4) | collective-permute-done | bytes 57376 | tf_op jit(solution)/shard_map/ppermute | solution.py:53
  22.1 3.7 %collective-permute-start.9 = (bf16[224,128]{1,0:T(8,128)(2,1)S(1)}, bf16[224,128]{1,0:T(8,128)(2,1)S(1)}, u32[]{:S(2)}, u32[]{:S(2)}) collective-permute-start(bf16[224,128]{1,0:T(8,128)(2,1)S(1)} %fusion), channel_id=1, source_target_pairs={{0,3},{1,2},{2,1},{3,0},{4,7},{5,6},{6,5},{7,4},{8,11},{9,10},{10,... | collective-permute-start | bytes 172040 | tf_op jit(solution)/shard_map/ppermute | solution.py:53
  25.7 0.8 %collective-permute-start.7 = (bf16[224,128]{1,0:T(8,128)(2,1)S(1)}, bf16[224,128]{1,0:T(8,128)(2,1)S(1)}, u32[]{:S(2)}, u32[]{:S(2)}) collective-permute-start(bf16[224,128]{1,0:T(8,128)(2,1)S(1)} %fusion), channel_id=1, source_target_pairs={{0,1},{1,0},{2,3},{3,2},{4,5},{5,4},{6,7},{7,6},{8,9},{9,8},{10,11... | collective-permute-start | bytes 172040 | tf_op jit(solution)/shard_map/ppermute | solution.py:53
  26.7 1.5 %collective-permute-done.12 = bf16[10,64,128]{2,1,0:T(8,128)(2,1)S(1)} collective-permute-done((bf16[10,64,128]{2,1,0:T(8,128)(2,1)S(1)}, bf16[10,64,128]{2,1,0:T(8,128)(2,1)S(1)}, u32[]{:S(2)}, u32[]{:S(2)}) %collective-permute-start.12) | collective-permute-done | bytes 163872 | tf_op jit(solution)/shard_map/ppermute | solution.py:31
  28.3 1.2 %shard_map.71 = bf16[8,4,32,128]{3,2,1,0:T(8,128)(2,1)S(1)} custom-call(bf16[12,64,128]{2,1,0:T(8,128)(2,1)S(1)} %get-tuple-element.43.inner, bf16[12,64,128]{2,1,0:T(8,128)(2,1)S(1)} %get-tuple-element.44.sides, bf16[8,64,128]{2,1,0:T(8,128)(2,1)S(1)} %get-tuple-element.45.ends, bf16[4,64,128]{2,1,0:T(8,128)(2,1)S(1)} %get-tuple-element.46.below, ...), custom_call_target="tpu_custom_call" | custom-call | flops 452984832 | bytes 1355776 | tf_op jit(solution)/shard_map/pallas_call | solution.py:215
  29.5 1.4 %collective-permute-done.8 = bf16[224,128]{1,0:T(8,128)(2,1)S(1)} collective-permute-done((bf16[224,128]{1,0:T(8,128)(2,1)S(1)}, bf16[224,128]{1,0:T(8,128)(2,1)S(1)}, u32[]{:S(2)}, u32[]{:S(2)}) %collective-permute-start.8) | collective-permute-done | bytes 57376 | tf_op jit(solution)/shard_map/ppermute | solution.py:53
  31.0 0.8 %copy.25 = bf16[1,32,8,4,128]{4,3,2,1,0:T(4,128)(2,1)} copy(bf16[1,32,8,4,128]{4,1,3,2,0:T(8,128)(2,1)S(1)} %bitcast.36) | data formatting | bytes 524288
  31.8 0.5 %collective-permute-done.13 = f32[224,128]{1,0:T(8,128)S(1)} collective-permute-done((f32[224,128]{1,0:T(8,128)S(1)}, f32[224,128]{1,0:T(8,128)S(1)}, u32[]{:S(2)}, u32[]{:S(2)}) %collective-permute-start.13) | collective-permute-done | bytes 114720 | tf_op jit(solution)/shard_map/ppermute | solution.py:53
  32.3 0.9 %shard_map.72 = (f32[864,64]{1,0:T(8,128)}, f32[1,64]{1,0:T(1,128)}) custom-call(f32[224,128]{1,0:T(8,128)S(1)} %get-tuple-element.70.refs_0_, f32[224,128]{1,0:T(8,128)S(1)} %get-tuple-element.69.refs_1_), custom_call_target="tpu_custom_call" | custom-call | flops 57344 | bytes 450816 | tf_op jit(solution)/shard_map/pallas_call | solution.py:215
  (41 shorter events, 2.3 us)
Async XLA Ops:
  1.7 7.8 %collective-permute-start = (bf16[8,32,128]{2,1,0:T(8,128)(2,1)S(1)}, bf16[8,32,128]{2,1,0:T(8,128)(2,1)S(1)}, u32[]{:S(2)}, u32[]{:S(2)}) collective-permute-start(bf16[8,32,128]{2,1,0:T(8,128)(2,1)S(1)} %get-tuple-element.79), channel_id=1, source_target_pairs={{0,12},{4,8},{8,4},{12,0},{1,13},{5,9},{9,5},{13,1},{2,14},{6,10},... | collective-permute-start | bytes 196616 | tf_op jit(solution)/shard_map/ppermute | solution.py:35
  5.7 4.3 %collective-permute-start.1 = (bf16[8,32,128]{2,1,0:T(8,128)(2,1)S(1)}, bf16[8,32,128]{2,1,0:T(8,128)(2,1)S(1)}, u32[]{:S(2)}, u32[]{:S(2)}) collective-permute-start(bf16[8,32,128]{2,1,0:T(8,128)(2,1)S(1)} %get-tuple-element.80), channel_id=1, source_target_pairs={{0,4},{4,0},{8,12},{12,8},{1,5},{5,1},{9,13},{13,9},{2,6},{6,2},{1... | collective-permute-start | bytes 196616 | tf_op jit(solution)/shard_map/ppermute | solution.py:31
  10.0 1.4 %collective-permute-start.2 = (bf16[6,32,128]{2,1,0:T(8,128)(2,1)S(1)}, bf16[6,32,128]{2,1,0:T(8,128)(2,1)S(1)}, u32[]{:S(2)}, u32[]{:S(2)}) collective-permute-start(bf16[6,32,128]{2,1,0:T(8,128)(2,1)S(1)} %maximum_select_fusion), channel_id=1, source_target_pairs={{0,16},{16,0},{1,17},{17,1},{2,18},{18,2},{3,19},{19,3},{4,20},{20... | collective-permute-start | bytes 147464 | tf_op jit(solution)/shard_map/ppermute | solution.py:31
  12.6 1.5 %collective-permute-start.10 = (bf16[4,64,128]{2,1,0:T(8,128)(2,1)S(1)}, bf16[4,64,128]{2,1,0:T(8,128)(2,1)S(1)}, u32[]{:S(2)}, u32[]{:S(2)}) collective-permute-start(bf16[4,64,128]{2,1,0:T(8,128)(2,1)S(1)} %slice_select_fusion.1), channel_id=1, source_target_pairs={{0,16},{16,0},{1,17},{17,1},{2,18},{18,2},{3,19},{19,3},{4,20},{20... | collective-permute-start | bytes 196616 | tf_op jit(solution)/shard_map/ppermute | solution.py:31
  13.2 1.4 %collective-permute-start.3 = (f32[224,128]{1,0:T(8,128)S(1)}, f32[224,128]{1,0:T(8,128)S(1)}, u32[]{:S(2)}, u32[]{:S(2)}) collective-permute-start(f32[224,128]{1,0:T(8,128)S(1)} %slice_select_fusion), channel_id=1, source_target_pairs={{0,16},{16,0},{1,17},{17,1},{2,18},{18,2},{3,19},{19,3},{4,20},{20... | collective-permute-start | bytes 344072 | tf_op jit(solution)/shard_map/ppermute | solution.py:53
  14.6 6.1 %collective-permute-start.6 = (bf16[224,128]{1,0:T(8,128)(2,1)S(1)}, bf16[224,128]{1,0:T(8,128)(2,1)S(1)}, u32[]{:S(2)}, u32[]{:S(2)}) collective-permute-start(bf16[224,128]{1,0:T(8,128)(2,1)S(1)} %get-tuple-element.59), channel_id=1, source_target_pairs={{0,12},{4,8},{8,4},{12,0},{1,13},{5,9},{9,5},{13,1},{2,14},{6,10},... | collective-permute-start | bytes 172040 | tf_op jit(solution)/shard_map/ppermute | solution.py:53
  15.9 4.9 %collective-permute-start.5 = (bf16[224,128]{1,0:T(8,128)(2,1)S(1)}, bf16[224,128]{1,0:T(8,128)(2,1)S(1)}, u32[]{:S(2)}, u32[]{:S(2)}) collective-permute-start(bf16[224,128]{1,0:T(8,128)(2,1)S(1)} %get-tuple-element.59), channel_id=1, source_target_pairs={{0,8},{4,12},{8,0},{12,4},{1,9},{5,13},{9,1},{13,5},{2,10},{6,14},... | collective-permute-start | bytes 172040 | tf_op jit(solution)/shard_map/ppermute | solution.py:53
  17.3 4.8 %collective-permute-start.4 = (bf16[224,128]{1,0:T(8,128)(2,1)S(1)}, bf16[224,128]{1,0:T(8,128)(2,1)S(1)}, u32[]{:S(2)}, u32[]{:S(2)}) collective-permute-start(bf16[224,128]{1,0:T(8,128)(2,1)S(1)} %get-tuple-element.59), channel_id=1, source_target_pairs={{0,4},{4,0},{8,12},{12,8},{1,5},{5,1},{9,13},{13,9},{2,6},{6,2},{1... | collective-permute-start | bytes 172040 | tf_op jit(solution)/shard_map/ppermute | solution.py:53
  18.6 8.1 %collective-permute-start.11 = (bf16[10,64,128]{2,1,0:T(8,128)(2,1)S(1)}, bf16[10,64,128]{2,1,0:T(8,128)(2,1)S(1)}, u32[]{:S(2)}, u32[]{:S(2)}) collective-permute-start(bf16[10,64,128]{2,1,0:T(8,128)(2,1)S(1)} %get-tuple-element.63), channel_id=1, source_target_pairs={{0,12},{4,8},{8,4},{12,0},{1,13},{5,9},{9,5},{13,1},{2,14},{6,10},... | collective-permute-start | bytes 491528 | tf_op jit(solution)/shard_map/ppermute | solution.py:35
  19.8 8.4 %collective-permute-start.12 = (bf16[10,64,128]{2,1,0:T(8,128)(2,1)S(1)}, bf16[10,64,128]{2,1,0:T(8,128)(2,1)S(1)}, u32[]{:S(2)}, u32[]{:S(2)}) collective-permute-start(bf16[10,64,128]{2,1,0:T(8,128)(2,1)S(1)} %get-tuple-element.64), channel_id=1, source_target_pairs={{0,4},{4,0},{8,12},{12,8},{1,5},{5,1},{9,13},{13,9},{2,6},{6,2},{1... | collective-permute-start | bytes 491528 | tf_op jit(solution)/shard_map/ppermute | solution.py:31
  22.1 7.4 %collective-permute-start.9 = (bf16[224,128]{1,0:T(8,128)(2,1)S(1)}, bf16[224,128]{1,0:T(8,128)(2,1)S(1)}, u32[]{:S(2)}, u32[]{:S(2)}) collective-permute-start(bf16[224,128]{1,0:T(8,128)(2,1)S(1)} %fusion), channel_id=1, source_target_pairs={{0,3},{1,2},{2,1},{3,0},{4,7},{5,6},{6,5},{7,4},{8,11},{9,10},{10,... | collective-permute-start | bytes 172040 | tf_op jit(solution)/shard_map/ppermute | solution.py:53
  25.7 5.1 %collective-permute-start.8 = (bf16[224,128]{1,0:T(8,128)(2,1)S(1)}, bf16[224,128]{1,0:T(8,128)(2,1)S(1)}, u32[]{:S(2)}, u32[]{:S(2)}) collective-permute-start(bf16[224,128]{1,0:T(8,128)(2,1)S(1)} %fusion), channel_id=1, source_target_pairs={{0,2},{1,3},{2,0},{3,1},{4,6},{5,7},{6,4},{7,5},{8,10},{9,11},{10,... | collective-permute-start | bytes 172040 | tf_op jit(solution)/shard_map/ppermute | solution.py:53
  25.7 5.1 %collective-permute-start.7 = (bf16[224,128]{1,0:T(8,128)(2,1)S(1)}, bf16[224,128]{1,0:T(8,128)(2,1)S(1)}, u32[]{:S(2)}, u32[]{:S(2)}) collective-permute-start(bf16[224,128]{1,0:T(8,128)(2,1)S(1)} %fusion), channel_id=1, source_target_pairs={{0,1},{1,0},{2,3},{3,2},{4,5},{5,4},{6,7},{7,6},{8,9},{9,8},{10,11... | collective-permute-start | bytes 172040 | tf_op jit(solution)/shard_map/ppermute | solution.py:53
  30.9 1.4 %collective-permute-start.13 = (f32[224,128]{1,0:T(8,128)S(1)}, f32[224,128]{1,0:T(8,128)S(1)}, u32[]{:S(2)}, u32[]{:S(2)}) collective-permute-start(f32[224,128]{1,0:T(8,128)S(1)} %add_add_fusion), channel_id=1, source_target_pairs={{0,16},{16,0},{1,17},{17,1},{2,18},{18,2},{3,19},{19,3},{4,20},{20... | collective-permute-start | bytes 344072 | tf_op jit(solution)/shard_map/ppermute | solution.py:53

commit v9 on v8

--- a/solution.py
+++ b/solution.py
@@ -17,7 +17,7 @@
     return lax.axis_index(axis) % 2 == 0 if lax.axis_size(axis) % 2 == 0 else jnp.bool_(True)
 
 
-def meet(low_edge, high_edge, axis):
+def meet(low_edge, high_edge, axis, first=None):
     count = lax.axis_size(axis)
     none = jnp.zeros_like(low_edge)
     if count == 1:
@@ -28,7 +28,8 @@
         return lax.ppermute(high_edge, axis, up), lax.ppermute(low_edge, axis, down)
     at, even = lax.axis_index(axis), paired(axis)
     inner = [(i, i ^ 1) for i in range(count)]
-    first = lax.ppermute(jnp.where(even, high_edge, low_edge), axis, inner)
+    if first is None:
+        first = lax.ppermute(jnp.where(even, high_edge, low_edge), axis, inner)
     if count == 2:
         return none, first
     outer = [(i, (i - 1 if i % 2 == 0 else i + 1) % count) for i in range(count)]
@@ -36,8 +37,8 @@
     return jnp.where((at == 0) | (at == count - 1), none, second), first
 
 
-def exchange(low_edge, high_edge, axis):
-    second, first = meet(low_edge, high_edge, axis)
+def exchange(low_edge, high_edge, axis, first=None):
+    second, first = meet(low_edge, high_edge, axis, first)
     even = paired(axis)
     return jnp.where(even, second, first), jnp.where(even, first, second)
 
@@ -221,28 +222,44 @@
     )(*args)
 
 
-def gathered_sum(part, axis, masks):
+def gathered_sum(part, axis, masks, meanwhile):
     own = lax.reduce_precision(part, 8, 7)
     sent = own.astype(BF16)
-    terms = [own] + [swap(sent, axis, mask).astype(F32) for mask in masks]
+    near, meanwhile = lax.optimization_barrier((sent, meanwhile))
+    terms = [own]
+    for mask in masks:
+        terms.append(swap(near if mask == min(masks) else sent, axis, mask).astype(F32))
     while len(terms) > 1:
         terms = [terms[i] + terms[i + 1] for i in range(0, len(terms), 2)]
-    return terms[0]
-
-
-def summed(total, meanwhile, work):
-    half = total.shape[0] // 2
+    return terms[0], meanwhile
+
+
+def halved(total, edges):
+    half, lanes = total.shape[0] // 2, total.shape[1]
+    first = lax.axis_index("depth") % 2 == 0
     low, high = total[:half], total[half:]
+    flat = [edge.astype(F32).reshape(-1, lanes) for edge in edges]
+    got = swap(jnp.concatenate([jnp.where(first, high, low), *flat], axis=0), "depth", 1)
+    part = jnp.where(first, low, high) + got[:half]
+    received, at = [], half
+    for edge, rows in zip(edges, flat):
+        received.append(got[at : at + rows.shape[0]].reshape(edge.shape).astype(BF16))
+        at += rows.shape[0]
+    return part, received
+
+
+def summed(part, meanwhile, work):
     first = lax.axis_index("depth") % 2 == 0
-    got = swap(jnp.where(first, high, low), "depth", 1)
-    part = jnp.where(first, low, high) + got
     for axis in AXES:
         count = lax.axis_size(axis)
         assert count & (count - 1) == 0
         bit = 2 if axis == "depth" else 1
         while bit < count:
             masks = [bit * way for way in WAYS[axis]] if 2 * bit < count else [bit]
-            part = gathered_sum(part, axis, masks)
+            if axis == AXES[-1]:
+                part, meanwhile = gathered_sum(part, axis, masks, meanwhile)
+            else:
+                part, _ = gathered_sum(part, axis, masks, ())
             bit *= len(masks) + 1
     part, done = lax.optimization_barrier((part, work(meanwhile)))
     other = swap(part, "depth", 1)
@@ -256,7 +273,7 @@
     payload_shape = jax.ShapeDtypeStruct((payload_rows, 2 * co), F32)
     flops = 4 * width * 27 * ci * co
     total = None
-    fields = []
+    deltas, fields = [], []
     fields_in = [inputs[cube].transpose(1, 2, 0, 3) for cube in range(cubes)]
     rows = [(x[:, 0], x[:, -1]) for x in fields_in]
     rows, fields_in, weight, bias, cotangent = lax.optimization_barrier(
@@ -264,6 +281,8 @@
     )
     taps, bias_row, cotangent = loaded(weight.transpose(2, 3, 4, 1, 0), bias[None], cotangent)
     w1 = taps.transpose(2, 4, 0, 1, 3).reshape(3 * co, 9 * ci)
+    w2 = jnp.flip(taps, (0, 1)).transpose(2, 3, 0, 1, 4).reshape(3 * ci, 9 * co)
+    w1, w2 = lax.optimization_barrier((w1, w2))
     for cube in range(cubes):
         x = fields_in[cube]
         cot = cotangent[cube].transpose(1, 2, 0, 3)
@@ -300,13 +319,17 @@
         sides, part = forward(1, (left, right), (part,))
         ends, part = forward(2, (left, right, low, high), (part,))
         total = part if total is None else total + part
-        below, above = exchange(ends[:height], ends[height:], "depth")
-        below, above, taps = lax.optimization_barrier((below, above, taps))
+        deltas.append((inner, sides, ends))
+    even = paired("depth")
+    part, edges = halved(
+        total, [jnp.where(even, ends[height:], ends[:height]) for _, _, ends in deltas]
+    )
+    for (inner, sides, ends), edge in zip(deltas, edges):
+        below, above = exchange(ends[:height], ends[height:], "depth", edge)
         first_row = jnp.concatenate([ends[:1], sides[: depth - 2], ends[height : height + 1]], axis=0)
         last_row = jnp.concatenate([ends[height - 1 : height], sides[depth - 2 :], ends[-1:]], axis=0)
         around = exchange(*columns(first_row, last_row, below, above), "height")
         fields.append((inner, sides, ends, below, above, *around))
-    w2 = jnp.flip(taps, (0, 1)).transpose(2, 3, 0, 1, 4).reshape(3 * ci, 9 * co)
 
     def input_gradients(fields):
         grads = []
@@ -322,7 +345,7 @@
             grads.append(grad.transpose(2, 0, 1, 3))
         return jnp.stack(grads)
 
-    low, high, grads = summed(total, fields, input_gradients)
+    low, high, grads = summed(part, fields, input_gradients)
     voxels = cubes * depth * height * width
     for axis in AXES:
         voxels *= lax.axis_size(axis)

time: 33.4 us -> 34.9 us (1.045)
  starting transfers between devices: 15.4 us -> 16.2 us
  waiting for transfers between devices: 6.44 us -> 7.18 us
    ppermute x8, waiting for transfers between devices: 3.49 us -> 5.04 us  [swap(): lax.ppermute(array, axis, [(i, i ^ mask) for i in range(lax.axis_size(axi...]
    ppermute x8, starting transfers between devices: 8.16 us -> 9.51 us  [swap(): lax.ppermute(array, axis, [(i, i ^ mask) for i in range(lax.axis_size(axi...]
    ppermute x4 -> x3, waiting for transfers between devices: 2.78 us -> 1.87 us  [meet(): first = lax.ppermute(jnp.where(even, high_edge, low_edge), axis, inner)]
    ppermute x4 -> x3, starting transfers between devices: 2.06 us -> 1.23 us  [meet(): first = lax.ppermute(jnp.where(even, high_edge, low_edge), axis, inner)]
  transfers between devices with their start and end apart: 14 -> 13, of which waited for: 9 -> 7; matrix products, arithmetic and copies ran while one was open for 6% -> 6% of each run, Pallas kernels for 15% -> 14%
where the time goes in v9:
time: 34.9 us; the launch traced here: 34.8 us
  starting transfers between devices  16.2 us (46%)
  waiting for transfers between devices  7.18 us (21%)
  Pallas kernels  7.04 us (20%)
  local copies, waits for them, and re-layouts  3.1 us (9%)
  between operations  0.93 us (3%)
    ppermute x8, starting transfers between devices, swap(): lax.ppermute(array, axis, [(i, i ^ mask) for i in range(lax.axis_size(axi...  9.51 us
    pallas_call x5, Pallas kernels, call(): pl.pallas_call(kernel, out_shape=outs, scratch_shapes=scratch, compiler_p...  5.84 us
    ppermute x2, starting transfers between devices, meet(): second = lax.ppermute(jnp.where(even, low_edge, high_edge), axis, outer)  5.46 us
    ppermute x8, waiting for transfers between devices, swap(): lax.ppermute(array, axis, [(i, i ^ mask) for i in range(lax.axis_size(axi...  5.04 us
    unnamed x6, local copies, waits for them, and re-layouts  1.95 us
    ppermute x3, waiting for transfers between devices, meet(): first = lax.ppermute(jnp.where(even, high_edge, low_edge), axis, inner)  1.87 us
    ppermute x3, starting transfers between devices, meet(): first = lax.ppermute(jnp.where(even, high_edge, low_edge), axis, inner)  1.23 us
    pallas_call x1, Pallas kernels, loaded(): pl.pallas_call(load_kernel, out_shape=[jax.ShapeDtypeStruct(a.shape, a.dt...  1.2 us
  transfers between devices with their start and end apart: 13, of which 7 were waited for; matrix products, arithmetic and copies ran while one was open for 6% of the time, Pallas kernels for 14%

profile of v9, /device:TPU:0, one launch (start us, length us, event | category | flops | bytes accessed | tf_op | source)
XLA Modules:
  0.0 34.8 jit_solution(9937260674536532823)
XLA Ops:
  0.6 1.1 %copy.29 = bf16[1,32,8,4,128]{4,1,2,3,0:T(8,128)(2,1)S(1)} copy(bf16[1,32,8,4,128]{4,3,2,1,0:T(4,128)(2,1)} %param.4) | data formatting | bytes 524288 | tf_op args[0]
  1.7 4.0 %collective-permute-start = (bf16[8,32,128]{2,1,0:T(8,128)(2,1)S(1)}, bf16[8,32,128]{2,1,0:T(8,128)(2,1)S(1)}, u32[]{:S(2)}, u32[]{:S(2)}) collective-permute-start(bf16[8,32,128]{2,1,0:T(8,128)(2,1)S(1)} %get-tuple-element.95), channel_id=1, source_target_pairs={{0,12},{4,8},{8,4},{12,0},{1,13},{5,9},{9,5},{13,1},{2,14},{6,10},... | collective-permute-start | bytes 196616 | tf_op jit(solution)/shard_map/ppermute | solution.py:36
  5.7 0.5 %collective-permute-start.1 = (bf16[8,32,128]{2,1,0:T(8,128)(2,1)S(1)}, bf16[8,32,128]{2,1,0:T(8,128)(2,1)S(1)}, u32[]{:S(2)}, u32[]{:S(2)}) collective-permute-start(bf16[8,32,128]{2,1,0:T(8,128)(2,1)S(1)} %get-tuple-element.96), channel_id=1, source_target_pairs={{0,4},{4,0},{8,12},{12,8},{1,5},{5,1},{9,13},{13,9},{2,6},{6,2},{1... | collective-permute-start | bytes 196616 | tf_op jit(solution)/shard_map/ppermute | solution.py:32
  6.2 1.2 %shard_map.67 = (bf16[3,3,3,32,64]{4,3,2,1,0:T(8,128)(2,1)S(1)}, f32[1,64]{1,0:T(1,128)S(1)}, bf16[1,64,8,4,128]{4,3,2,1,0:T(4,128)(2,1)S(1)}) custom-call(bf16[3,3,3,32,64]{4,3,2,1,0:T(8,128)(2,1)} %bitcast.63, f32[1,64]{1,0:T(1,128)} %bitcast.64, bf16[1,64,8,4,128]{4,3,2,1,0:T(4,128)(2,1)} %refs_2_), custom_call_target="tpu_custom_call" | custom-call | tf_op jit(solution)/shard_map/pallas_call | solution.py:204
  8.7 1.3 %shard_map.68 = (bf16[12,64,128]{2,1,0:T(8,128)(2,1)S(1)}, f32[448,128]{1,0:T(8,128)S(1)}) custom-call(bf16[8,4,32,128]{3,2,1,0:T(8,128)(2,1)S(1)} %copy.23.x, bf16[192,288]{1,0:T(8,128)(2,1)S(1)} %copy.20.refs_0_.refs_2_.refs_4_, f32[1,64]{1,0:T(1,128)S(1)} %get-tuple-element.41.refs_1_.refs_3_.refs_5_, bf16[8,4,64,128]{3,2,1,0:T(8,128)(2,1)S(1)} %bitcast.53), custom_call_target="tpu_custom_call" | custom-call | flops 339738624 | bytes 1323264 | tf_op jit(solution)/shard_map/pallas_call | solution.py:216
  10.1 1.3 %shard_map.69 = (bf16[12,64,128]{2,1,0:T(8,128)(2,1)S(1)}, f32[448,128]{1,0:T(8,128)S(1)}) custom-call(bf16[8,4,32,128]{3,2,1,0:T(8,128)(2,1)S(1)} %copy.23.x, bf16[8,32,128]{2,1,0:T(8,128)(2,1)S(1)} %get-tuple-element.46.refs_0_, bf16[8,32,128]{2,1,0:T(8,128)(2,1)S(1)} %get-tuple-element.47.refs_1_, bf16[192,288]{1,0:T(8,128)(2,1)S(1)} %copy.20.refs_0_.refs_2_.refs_4_, ...), custom_call_target="tpu_custom_call" | custom-call | flops 339738624 | bytes 1683712 | tf_op jit(solution)/shard_map/pallas_call | solution.py:216
  11.4 1.2 %shard_map.70 = (bf16[8,64,128]{2,1,0:T(8,128)(2,1)S(1)}, f32[448,128]{1,0:T(8,128)S(1)}) custom-call(bf16[8,4,32,128]{3,2,1,0:T(8,128)(2,1)S(1)} %copy.23.x, bf16[8,32,128]{2,1,0:T(8,128)(2,1)S(1)} %get-tuple-element.46.refs_0_, bf16[8,32,128]{2,1,0:T(8,128)(2,1)S(1)} %get-tuple-element.47.refs_1_, bf16[6,32,128]{2,1,0:T(8,128)(2,1)S(1)} %get-tuple-element.106.refs_2_, ...), custom_call_target="tpu_custom_call" | custom-call | flops 226492416 | bytes 1716480 | tf_op jit(solution)/shard_map/pallas_call | solution.py:216
  12.7 0.6 %collective-permute-start.3 = (f32[480,128]{1,0:T(8,128)S(1)}, f32[480,128]{1,0:T(8,128)S(1)}, u32[]{:S(2)}, u32[]{:S(2)}) collective-permute-start(f32[480,128]{1,0:T(8,128)S(1)} %pad_maximum_fusion), channel_id=1, source_target_pairs={{0,16},{16,0},{1,17},{17,1},{2,18},{18,2},{3,19},{19,3},{4,20},{20... | collective-permute-start | bytes 737288 | tf_op jit(solution)/shard_map/ppermute | solution.py:54
  13.3 1.1 %collective-permute-done.3 = f32[480,128]{1,0:T(8,128)S(1)} collective-permute-done((f32[480,128]{1,0:T(8,128)S(1)}, f32[480,128]{1,0:T(8,128)S(1)}, u32[]{:S(2)}, u32[]{:S(2)}) %collective-permute-start.3) | collective-permute-done | bytes 245792 | tf_op jit(solution)/shard_map/ppermute | solution.py:54
  14.5 1.5 %collective-permute-start.6 = (bf16[224,128]{1,0:T(8,128)(2,1)S(1)}, bf16[224,128]{1,0:T(8,128)(2,1)S(1)}, u32[]{:S(2)}, u32[]{:S(2)}) collective-permute-start(bf16[224,128]{1,0:T(8,128)(2,1)S(1)} %get-tuple-element.73), channel_id=1, source_target_pairs={{0,12},{4,8},{8,4},{12,0},{1,13},{5,9},{9,5},{13,1},{2,14},{6,10},... | collective-permute-start | bytes 172040 | tf_op jit(solution)/shard_map/ppermute | solution.py:54
  16.0 1.5 %collective-permute-start.5 = (bf16[224,128]{1,0:T(8,128)(2,1)S(1)}, bf16[224,128]{1,0:T(8,128)(2,1)S(1)}, u32[]{:S(2)}, u32[]{:S(2)}) collective-permute-start(bf16[224,128]{1,0:T(8,128)(2,1)S(1)} %get-tuple-element.73), channel_id=1, source_target_pairs={{0,8},{4,12},{8,0},{12,4},{1,9},{5,13},{9,1},{13,5},{2,10},{6,14},... | collective-permute-start | bytes 172040 | tf_op jit(solution)/shard_map/ppermute | solution.py:54
  17.5 0.5 %collective-permute-start.4 = (bf16[224,128]{1,0:T(8,128)(2,1)S(1)}, bf16[224,128]{1,0:T(8,128)(2,1)S(1)}, u32[]{:S(2)}, u32[]{:S(2)}) collective-permute-start(bf16[224,128]{1,0:T(8,128)(2,1)S(1)} %get-tuple-element.73), channel_id=1, source_target_pairs={{0,4},{4,0},{8,12},{12,8},{1,5},{5,1},{9,13},{13,9},{2,6},{6,2},{1... | collective-permute-start | bytes 172040 | tf_op jit(solution)/shard_map/ppermute | solution.py:54
  18.2 1.5 %collective-permute-start.7 = (bf16[10,64,128]{2,1,0:T(8,128)(2,1)S(1)}, bf16[10,64,128]{2,1,0:T(8,128)(2,1)S(1)}, u32[]{:S(2)}, u32[]{:S(2)}) collective-permute-start(bf16[10,64,128]{2,1,0:T(8,128)(2,1)S(1)} %get-tuple-element.77), channel_id=1, source_target_pairs={{0,12},{4,8},{8,4},{12,0},{1,13},{5,9},{9,5},{13,1},{2,14},{6,10},... | collective-permute-start | bytes 491528 | tf_op jit(solution)/shard_map/ppermute | solution.py:36
  19.7 0.6 %collective-permute-start.8 = (bf16[10,64,128]{2,1,0:T(8,128)(2,1)S(1)}, bf16[10,64,128]{2,1,0:T(8,128)(2,1)S(1)}, u32[]{:S(2)}, u32[]{:S(2)}) collective-permute-start(bf16[10,64,128]{2,1,0:T(8,128)(2,1)S(1)} %get-tuple-element.78), channel_id=1, source_target_pairs={{0,4},{4,0},{8,12},{12,8},{1,5},{5,1},{9,13},{13,9},{2,6},{6,2},{1... | collective-permute-start | bytes 491528 | tf_op jit(solution)/shard_map/ppermute | solution.py:32
  20.3 2.0 %collective-permute-done.4 = bf16[224,128]{1,0:T(8,128)(2,1)S(1)} collective-permute-done((bf16[224,128]{1,0:T(8,128)(2,1)S(1)}, bf16[224,128]{1,0:T(8,128)(2,1)S(1)}, u32[]{:S(2)}, u32[]{:S(2)}) %collective-permute-start.4) | collective-permute-done | bytes 57376 | tf_op jit(solution)/shard_map/ppermute | solution.py:54
  22.3 3.7 %collective-permute-start.11 = (bf16[224,128]{1,0:T(8,128)(2,1)S(1)}, bf16[224,128]{1,0:T(8,128)(2,1)S(1)}, u32[]{:S(2)}, u32[]{:S(2)}) collective-permute-start(bf16[224,128]{1,0:T(8,128)(2,1)S(1)} %fusion.1), channel_id=1, source_target_pairs={{0,3},{1,2},{2,1},{3,0},{4,7},{5,6},{6,5},{7,4},{8,11},{9,10},{10,... | collective-permute-start | bytes 172040 | tf_op jit(solution)/shard_map/ppermute | solution.py:54
  26.0 0.3 collective-permute-done.7
  26.3 1.9 %collective-permute-done.8 = bf16[10,64,128]{2,1,0:T(8,128)(2,1)S(1)} collective-permute-done((bf16[10,64,128]{2,1,0:T(8,128)(2,1)S(1)}, bf16[10,64,128]{2,1,0:T(8,128)(2,1)S(1)}, u32[]{:S(2)}, u32[]{:S(2)}) %collective-permute-start.8) | collective-permute-done | bytes 163872 | tf_op jit(solution)/shard_map/ppermute | solution.py:32
  28.2 1.6 %collective-permute-start.9 = (bf16[224,128]{1,0:T(8,128)(2,1)S(1)}, bf16[224,128]{1,0:T(8,128)(2,1)S(1)}, u32[]{:S(2)}, u32[]{:S(2)}) collective-permute-start(bf16[224,128]{1,0:T(8,128)(2,1)S(1)} %fusion.1), channel_id=1, source_target_pairs={{0,1},{1,0},{2,3},{3,2},{4,5},{5,4},{6,7},{7,6},{8,9},{9,8},{10,11... | collective-permute-start | bytes 172040 | tf_op jit(solution)/shard_map/ppermute | solution.py:54
  29.8 1.2 %shard_map.71 = bf16[8,4,32,128]{3,2,1,0:T(8,128)(2,1)S(1)} custom-call(bf16[12,64,128]{2,1,0:T(8,128)(2,1)S(1)} %get-tuple-element.55.inner, bf16[12,64,128]{2,1,0:T(8,128)(2,1)S(1)} %get-tuple-element.56.sides, bf16[8,64,128]{2,1,0:T(8,128)(2,1)S(1)} %get-tuple-element.57.ends, bf16[4,64,128]{2,1,0:T(8,128)(2,1)S(1)} %bitcast.59, ...), custom_call_target="tpu_custom_call" | custom-call | flops 452984832 | bytes 1355776 | tf_op jit(solution)/shard_map/pallas_call | solution.py:216
  31.1 1.3 %collective-permute-done.9 = bf16[224,128]{1,0:T(8,128)(2,1)S(1)} collective-permute-done((bf16[224,128]{1,0:T(8,128)(2,1)S(1)}, bf16[224,128]{1,0:T(8,128)(2,1)S(1)}, u32[]{:S(2)}, u32[]{:S(2)}) %collective-permute-start.9) | collective-permute-done | bytes 57376 | tf_op jit(solution)/shard_map/ppermute | solution.py:54
  32.5 0.8 %copy.25 = bf16[1,32,8,4,128]{4,3,2,1,0:T(4,128)(2,1)} copy(bf16[1,32,8,4,128]{4,1,3,2,0:T(8,128)(2,1)S(1)} %bitcast.57) | data formatting | bytes 524288
  33.4 0.5 %collective-permute-done.12 = f32[224,128]{1,0:T(8,128)S(1)} collective-permute-done((f32[224,128]{1,0:T(8,128)S(1)}, f32[224,128]{1,0:T(8,128)S(1)}, u32[]{:S(2)}, u32[]{:S(2)}) %collective-permute-start.12) | collective-permute-done | bytes 114720 | tf_op jit(solution)/shard_map/ppermute | solution.py:54
  33.9 0.9 %shard_map.72 = (f32[864,64]{1,0:T(8,128)}, f32[1,64]{1,0:T(1,128)}) custom-call(f32[224,128]{1,0:T(8,128)S(1)} %get-tuple-element.86.refs_0_, f32[224,128]{1,0:T(8,128)S(1)} %get-tuple-element.85.refs_1_), custom_call_target="tpu_custom_call" | custom-call | flops 57344 | bytes 450816 | tf_op jit(solution)/shard_map/pallas_call | solution.py:216
  (41 shorter events, 1.8 us)
Async XLA Ops:
  1.7 8.2 %collective-permute-start = (bf16[8,32,128]{2,1,0:T(8,128)(2,1)S(1)}, bf16[8,32,128]{2,1,0:T(8,128)(2,1)S(1)}, u32[]{:S(2)}, u32[]{:S(2)}) collective-permute-start(bf16[8,32,128]{2,1,0:T(8,128)(2,1)S(1)} %get-tuple-element.95), channel_id=1, source_target_pairs={{0,12},{4,8},{8,4},{12,0},{1,13},{5,9},{9,5},{13,1},{2,14},{6,10},... | collective-permute-start | bytes 196616 | tf_op jit(solution)/shard_map/ppermute | solution.py:36
  5.7 4.3 %collective-permute-start.1 = (bf16[8,32,128]{2,1,0:T(8,128)(2,1)S(1)}, bf16[8,32,128]{2,1,0:T(8,128)(2,1)S(1)}, u32[]{:S(2)}, u32[]{:S(2)}) collective-permute-start(bf16[8,32,128]{2,1,0:T(8,128)(2,1)S(1)} %get-tuple-element.96), channel_id=1, source_target_pairs={{0,4},{4,0},{8,12},{12,8},{1,5},{5,1},{9,13},{13,9},{2,6},{6,2},{1... | collective-permute-start | bytes 196616 | tf_op jit(solution)/shard_map/ppermute | solution.py:32
  10.0 1.4 %collective-permute-start.2 = (bf16[6,32,128]{2,1,0:T(8,128)(2,1)S(1)}, bf16[6,32,128]{2,1,0:T(8,128)(2,1)S(1)}, u32[]{:S(2)}, u32[]{:S(2)}) collective-permute-start(bf16[6,32,128]{2,1,0:T(8,128)(2,1)S(1)} %maximum_select_fusion), channel_id=1, source_target_pairs={{0,16},{16,0},{1,17},{17,1},{2,18},{18,2},{3,19},{19,3},{4,20},{20... | collective-permute-start | bytes 147464 | tf_op jit(solution)/shard_map/ppermute | solution.py:32
  12.7 1.7 %collective-permute-start.3 = (f32[480,128]{1,0:T(8,128)S(1)}, f32[480,128]{1,0:T(8,128)S(1)}, u32[]{:S(2)}, u32[]{:S(2)}) collective-permute-start(f32[480,128]{1,0:T(8,128)S(1)} %pad_maximum_fusion), channel_id=1, source_target_pairs={{0,16},{16,0},{1,17},{17,1},{2,18},{18,2},{3,19},{19,3},{4,20},{20... | collective-permute-start | bytes 737288 | tf_op jit(solution)/shard_map/ppermute | solution.py:54
  14.5 7.8 %collective-permute-start.6 = (bf16[224,128]{1,0:T(8,128)(2,1)S(1)}, bf16[224,128]{1,0:T(8,128)(2,1)S(1)}, u32[]{:S(2)}, u32[]{:S(2)}) collective-permute-start(bf16[224,128]{1,0:T(8,128)(2,1)S(1)} %get-tuple-element.73), channel_id=1, source_target_pairs={{0,12},{4,8},{8,4},{12,0},{1,13},{5,9},{9,5},{13,1},{2,14},{6,10},... | collective-permute-start | bytes 172040 | tf_op jit(solution)/shard_map/ppermute | solution.py:54
  16.0 6.3 %collective-permute-start.5 = (bf16[224,128]{1,0:T(8,128)(2,1)S(1)}, bf16[224,128]{1,0:T(8,128)(2,1)S(1)}, u32[]{:S(2)}, u32[]{:S(2)}) collective-permute-start(bf16[224,128]{1,0:T(8,128)(2,1)S(1)} %get-tuple-element.73), channel_id=1, source_target_pairs={{0,8},{4,12},{8,0},{12,4},{1,9},{5,13},{9,1},{13,5},{2,10},{6,14},... | collective-permute-start | bytes 172040 | tf_op jit(solution)/shard_map/ppermute | solution.py:54
  17.5 4.8 %collective-permute-start.4 = (bf16[224,128]{1,0:T(8,128)(2,1)S(1)}, bf16[224,128]{1,0:T(8,128)(2,1)S(1)}, u32[]{:S(2)}, u32[]{:S(2)}) collective-permute-start(bf16[224,128]{1,0:T(8,128)(2,1)S(1)} %get-tuple-element.73), channel_id=1, source_target_pairs={{0,4},{4,0},{8,12},{12,8},{1,5},{5,1},{9,13},{13,9},{2,6},{6,2},{1... | collective-permute-start | bytes 172040 | tf_op jit(solution)/shard_map/ppermute | solution.py:54
  18.2 8.1 %collective-permute-start.7 = (bf16[10,64,128]{2,1,0:T(8,128)(2,1)S(1)}, bf16[10,64,128]{2,1,0:T(8,128)(2,1)S(1)}, u32[]{:S(2)}, u32[]{:S(2)}) collective-permute-start(bf16[10,64,128]{2,1,0:T(8,128)(2,1)S(1)} %get-tuple-element.77), channel_id=1, source_target_pairs={{0,12},{4,8},{8,4},{12,0},{1,13},{5,9},{9,5},{13,1},{2,14},{6,10},... | collective-permute-start | bytes 491528 | tf_op jit(solution)/shard_map/ppermute | solution.py:36
  19.7 8.5 %collective-permute-start.8 = (bf16[10,64,128]{2,1,0:T(8,128)(2,1)S(1)}, bf16[10,64,128]{2,1,0:T(8,128)(2,1)S(1)}, u32[]{:S(2)}, u32[]{:S(2)}) collective-permute-start(bf16[10,64,128]{2,1,0:T(8,128)(2,1)S(1)} %get-tuple-element.78), channel_id=1, source_target_pairs={{0,4},{4,0},{8,12},{12,8},{1,5},{5,1},{9,13},{13,9},{2,6},{6,2},{1... | collective-permute-start | bytes 491528 | tf_op jit(solution)/shard_map/ppermute | solution.py:32
  22.3 8.6 %collective-permute-start.11 = (bf16[224,128]{1,0:T(8,128)(2,1)S(1)}, bf16[224,128]{1,0:T(8,128)(2,1)S(1)}, u32[]{:S(2)}, u32[]{:S(2)}) collective-permute-start(bf16[224,128]{1,0:T(8,128)(2,1)S(1)} %fusion.1), channel_id=1, source_target_pairs={{0,3},{1,2},{2,1},{3,0},{4,7},{5,6},{6,5},{7,4},{8,11},{9,10},{10,... | collective-permute-start | bytes 172040 | tf_op jit(solution)/shard_map/ppermute | solution.py:54
  26.0 5.1 %collective-permute-start.10 = (bf16[224,128]{1,0:T(8,128)(2,1)S(1)}, bf16[224,128]{1,0:T(8,128)(2,1)S(1)}, u32[]{:S(2)}, u32[]{:S(2)}) collective-permute-start(bf16[224,128]{1,0:T(8,128)(2,1)S(1)} %fusion.1), channel_id=1, source_target_pairs={{0,2},{1,3},{2,0},{3,1},{4,6},{5,7},{6,4},{7,5},{8,10},{9,11},{10,... | collective-permute-start | bytes 172040 | tf_op jit(solution)/shard_map/ppermute | solution.py:54
  28.2 4.2 %collective-permute-start.9 = (bf16[224,128]{1,0:T(8,128)(2,1)S(1)}, bf16[224,128]{1,0:T(8,128)(2,1)S(1)}, u32[]{:S(2)}, u32[]{:S(2)}) collective-permute-start(bf16[224,128]{1,0:T(8,128)(2,1)S(1)} %fusion.1), channel_id=1, source_target_pairs={{0,1},{1,0},{2,3},{3,2},{4,5},{5,4},{6,7},{7,6},{8,9},{9,8},{10,11... | collective-permute-start | bytes 172040 | tf_op jit(solution)/shard_map/ppermute | solution.py:54
  32.5 1.4 %collective-permute-start.12 = (f32[224,128]{1,0:T(8,128)S(1)}, f32[224,128]{1,0:T(8,128)S(1)}, u32[]{:S(2)}, u32[]{:S(2)}) collective-permute-start(f32[224,128]{1,0:T(8,128)S(1)} %add_add_fusion), channel_id=1, source_target_pairs={{0,16},{16,0},{1,17},{17,1},{2,18},{18,2},{3,19},{19,3},{4,20},{20... | collective-permute-start | bytes 344072 | tf_op jit(solution)/shard_map/ppermute | solution.py:54

commit v10 on v8

--- a/solution.py
+++ b/solution.py
@@ -9,6 +9,7 @@
 
 F32 = jnp.float32
 BF16 = jnp.bfloat16
+GROUP = 4
 AXES = ("depth", "height", "dp")
 WAYS = {"depth": (1, 2, 3), "height": (1, 2, 3), "dp": (1, 2, 3)}
 
@@ -70,6 +71,14 @@
     return jnp.where(lane == edge, 0.0, pltpu.roll(value, (-step) % width, 1))
 
 
+def rowwise(value, width):
+    return [value[:, at : at + width] for at in range(0, value.shape[1], width)]
+
+
+def beside(rows):
+    return rows[0] if len(rows) == 1 else jnp.concatenate(rows, axis=1)
+
+
 def forward_rows(positions, row_of, w1, bias, cot, delta, before, payload, patches, taps, slopes, grad):
     co, width = bias.shape[1], cot.shape[3]
     ci = patches.shape[0] // 9
@@ -80,22 +89,41 @@
     taps[...] = jnp.dot(w1[...], patches[...], preferred_element_type=F32)
     shift_bias = jnp.broadcast_to(bias[...], (width, co)).T
     bias_acc = jnp.zeros((co, width), F32)
-    for at, (d, h) in enumerate(positions):
-        lanes = pl.ds(at * width, width)
-        linear = taps[co : 2 * co, lanes] + shift_bias
-        linear = linear + shifted(taps[:co, lanes], -1) + shifted(taps[2 * co :, lanes], 1)
+    starts = range(0, len(positions), GROUP)
+    per_group = len(starts) > 2
+    product = functools.partial(
+        lax.dot_general,
+        dimension_numbers=(((1,), (1,)), ((), ())),
+        preferred_element_type=F32,
+    )
+    for start in starts:
+        group = positions[start : start + GROUP]
+        lanes = pl.ds(start * width, len(group) * width)
+        low, middle, high = (rowwise(taps[i * co : (i + 1) * co, lanes], width) for i in range(3))
+        linear = beside(
+            [
+                m + shift_bias + shifted(l, -1) + shifted(h, 1)
+                for l, m, h in zip(low, middle, high)
+            ]
+        )
         sigma = 1.0 / (1.0 + jnp.exp(-linear))
-        slope = cot[d, h].astype(F32) * sigma * (1.0 + linear * (1.0 - sigma))
-        rounded = slope.astype(BF16)
-        delta[at] = rounded
-        wide = rounded.astype(F32)
-        bias_acc = bias_acc + wide
-        slopes[:co, lanes] = shifted(wide, 1).astype(BF16)
-        slopes[co : 2 * co, lanes] = rounded
-        slopes[2 * co :, lanes] = shifted(wide, -1).astype(BF16)
-    grad[...] = lax.dot_general(
-        patches[...], slopes[...], (((1,), (1,)), ((), ())), preferred_element_type=F32
-    )
+        incoming = beside([cot[d, h].astype(F32) for d, h in group])
+        rounded = (incoming * sigma * (1.0 + linear * (1.0 - sigma))).astype(BF16)
+        wide = rowwise(rounded.astype(F32), width)
+        for at, row in enumerate(rowwise(rounded, width)):
+            delta[start + at] = row
+            bias_acc = bias_acc + wide[at]
+        before_it = beside([shifted(row, 1) for row in wide]).astype(BF16)
+        after_it = beside([shifted(row, -1) for row in wide]).astype(BF16)
+        if per_group:
+            term = product(patches[:, lanes], jnp.concatenate([before_it, rounded, after_it], axis=0))
+            grad[...] = term if start == 0 else grad[...] + term
+        else:
+            slopes[:co, lanes] = before_it
+            slopes[co : 2 * co, lanes] = rounded
+            slopes[2 * co :, lanes] = after_it
+    if not per_group:
+        grad[...] = product(patches[...], slopes[...])
     rows = grad.shape[0]
     tail = rows + rows // 2
     total = jnp.sum(bias_acc.T, axis=0, keepdims=True)

time: 33.4 us -> 33 us (0.988)
  Pallas kernels: 7.06 us -> 6.62 us
    pallas_call x5, Pallas kernels: 5.85 us -> 5.42 us  [call(): pl.pallas_call(kernel, out_shape=outs, scratch_shapes=scratch, compiler_p...]
  transfers between devices with their start and end apart: 14 -> 14, of which waited for: 9 -> 10; matrix products, arithmetic and copies ran while one was open for 6% -> 7% of each run, Pallas kernels for 15% -> 14%
where the time goes in v10:
time: 33 us; the launch traced here: 32.8 us
  starting transfers between devices  15.4 us (47%)
  Pallas kernels  6.62 us (20%)
  waiting for transfers between devices  6.54 us (20%)
  local copies, waits for them, and re-layouts  3.1 us (9%)
  between operations  0.87 us (3%)
    ppermute x8, starting transfers between devices, swap(): lax.ppermute(array, axis, [(i, i ^ mask) for i in range(lax.axis_size(axi...  8.26 us
    pallas_call x5, Pallas kernels, call(): pl.pallas_call(kernel, out_shape=outs, scratch_shapes=scratch, compiler_p...  5.42 us
    ppermute x2, starting transfers between devices, meet(): second = lax.ppermute(jnp.where(even, low_edge, high_edge), axis, outer)  5.2 us
    ppermute x8, waiting for transfers between devices, swap(): lax.ppermute(array, axis, [(i, i ^ mask) for i in range(lax.axis_size(axi...  3.28 us
    ppermute x4, waiting for transfers between devices, meet(): first = lax.ppermute(jnp.where(even, high_edge, low_edge), axis, inner)  2.98 us
    ppermute x4, starting transfers between devices, meet(): first = lax.ppermute(jnp.where(even, high_edge, low_edge), axis, inner)  1.96 us
    unnamed x6, local copies, waits for them, and re-layouts  1.95 us
    pallas_call x1, Pallas kernels, loaded(): pl.pallas_call(load_kernel, out_shape=[jax.ShapeDtypeStruct(a.shape, a.dt...  1.21 us
  transfers between devices with their start and end apart: 14, of which 10 were waited for; matrix products, arithmetic and copies ran while one was open for 7% of the time, Pallas kernels for 14%

profile of v10, /device:TPU:0, one launch (start us, length us, event | category | flops | bytes accessed | tf_op | source)
XLA Modules:
  0.0 32.8 jit_solution(9294959894634912959)
XLA Ops:
  0.6 1.1 %copy.29 = bf16[1,32,8,4,128]{4,1,2,3,0:T(8,128)(2,1)S(1)} copy(bf16[1,32,8,4,128]{4,3,2,1,0:T(4,128)(2,1)} %param.4) | data formatting | bytes 524288 | tf_op args[0]
  1.7 4.0 %collective-permute-start = (bf16[8,32,128]{2,1,0:T(8,128)(2,1)S(1)}, bf16[8,32,128]{2,1,0:T(8,128)(2,1)S(1)}, u32[]{:S(2)}, u32[]{:S(2)}) collective-permute-start(bf16[8,32,128]{2,1,0:T(8,128)(2,1)S(1)} %get-tuple-element.79), channel_id=1, source_target_pairs={{0,12},{4,8},{8,4},{12,0},{1,13},{5,9},{9,5},{13,1},{2,14},{6,10},... | collective-permute-start | bytes 196616 | tf_op jit(solution)/shard_map/ppermute | solution.py:36
  5.7 0.5 %collective-permute-start.1 = (bf16[8,32,128]{2,1,0:T(8,128)(2,1)S(1)}, bf16[8,32,128]{2,1,0:T(8,128)(2,1)S(1)}, u32[]{:S(2)}, u32[]{:S(2)}) collective-permute-start(bf16[8,32,128]{2,1,0:T(8,128)(2,1)S(1)} %get-tuple-element.80), channel_id=1, source_target_pairs={{0,4},{4,0},{8,12},{12,8},{1,5},{5,1},{9,13},{13,9},{2,6},{6,2},{1... | collective-permute-start | bytes 196616 | tf_op jit(solution)/shard_map/ppermute | solution.py:32
  6.3 1.2 %shard_map.67 = (bf16[3,3,3,32,64]{4,3,2,1,0:T(8,128)(2,1)S(1)}, f32[1,64]{1,0:T(1,128)S(1)}, bf16[1,64,8,4,128]{4,3,2,1,0:T(4,128)(2,1)S(1)}) custom-call(bf16[3,3,3,32,64]{4,3,2,1,0:T(8,128)(2,1)} %bitcast.40, f32[1,64]{1,0:T(1,128)} %bitcast.41, bf16[1,64,8,4,128]{4,3,2,1,0:T(4,128)(2,1)} %refs_2_), custom_call_target="tpu_custom_call" | custom-call | tf_op jit(solution)/shard_map/pallas_call | solution.py:231
  8.2 1.1 %shard_map.68 = (bf16[12,64,128]{2,1,0:T(8,128)(2,1)S(1)}, f32[448,128]{1,0:T(8,128)S(1)}) custom-call(bf16[8,4,32,128]{3,2,1,0:T(8,128)(2,1)S(1)} %copy.22.x, bf16[192,288]{1,0:T(8,128)(2,1)S(1)} %copy.19.refs_0_.refs_2_.refs_4_, f32[1,64]{1,0:T(1,128)S(1)} %get-tuple-element.33.refs_1_.refs_3_.refs_5_, bf16[8,4,64,128]{3,2,1,0:T(8,128)(2,1)S(1)} %bitcast.32), custom_call_target="tpu_custom_call" | custom-call | flops 339738624 | bytes 1323264 | tf_op jit(solution)/shard_map/pallas_call | solution.py:243
  9.3 0.6 %collective-permute-done.1 = bf16[8,32,128]{2,1,0:T(8,128)(2,1)S(1)} collective-permute-done((bf16[8,32,128]{2,1,0:T(8,128)(2,1)S(1)}, bf16[8,32,128]{2,1,0:T(8,128)(2,1)S(1)}, u32[]{:S(2)}, u32[]{:S(2)}) %collective-permute-start.1) | collective-permute-done | bytes 65568 | tf_op jit(solution)/shard_map/ppermute | solution.py:32
  10.1 1.1 %shard_map.69 = (bf16[12,64,128]{2,1,0:T(8,128)(2,1)S(1)}, f32[448,128]{1,0:T(8,128)S(1)}) custom-call(bf16[8,4,32,128]{3,2,1,0:T(8,128)(2,1)S(1)} %copy.22.x, bf16[8,32,128]{2,1,0:T(8,128)(2,1)S(1)} %get-tuple-element.38.refs_0_, bf16[8,32,128]{2,1,0:T(8,128)(2,1)S(1)} %get-tuple-element.39.refs_1_, bf16[192,288]{1,0:T(8,128)(2,1)S(1)} %copy.19.refs_0_.refs_2_.refs_4_, ...), custom_call_target="tpu_custom_call" | custom-call | flops 339738624 | bytes 1683712 | tf_op jit(solution)/shard_map/pallas_call | solution.py:243
  11.3 1.1 %shard_map.70 = (bf16[8,64,128]{2,1,0:T(8,128)(2,1)S(1)}, f32[448,128]{1,0:T(8,128)S(1)}) custom-call(bf16[8,4,32,128]{3,2,1,0:T(8,128)(2,1)S(1)} %copy.22.x, bf16[8,32,128]{2,1,0:T(8,128)(2,1)S(1)} %get-tuple-element.38.refs_0_, bf16[8,32,128]{2,1,0:T(8,128)(2,1)S(1)} %get-tuple-element.39.refs_1_, bf16[6,32,128]{2,1,0:T(8,128)(2,1)S(1)} %get-tuple-element.92.refs_2_, ...), custom_call_target="tpu_custom_call" | custom-call | flops 226492416 | bytes 1716480 | tf_op jit(solution)/shard_map/pallas_call | solution.py:243
  12.5 0.5 %collective-permute-start.10 = (bf16[4,64,128]{2,1,0:T(8,128)(2,1)S(1)}, bf16[4,64,128]{2,1,0:T(8,128)(2,1)S(1)}, u32[]{:S(2)}, u32[]{:S(2)}) collective-permute-start(bf16[4,64,128]{2,1,0:T(8,128)(2,1)S(1)} %slice_select_fusion.1), channel_id=1, source_target_pairs={{0,16},{16,0},{1,17},{17,1},{2,18},{18,2},{3,19},{19,3},{4,20},{20... | collective-permute-start | bytes 196616 | tf_op jit(solution)/shard_map/ppermute | solution.py:32
  13.2 0.7 %collective-permute-done.10 = bf16[4,64,128]{2,1,0:T(8,128)(2,1)S(1)} collective-permute-done((bf16[4,64,128]{2,1,0:T(8,128)(2,1)S(1)}, bf16[4,64,128]{2,1,0:T(8,128)(2,1)S(1)}, u32[]{:S(2)}, u32[]{:S(2)}) %collective-permute-start.10) | collective-permute-done | bytes 65568 | tf_op jit(solution)/shard_map/ppermute | solution.py:32
  14.4 1.2 %collective-permute-start.6 = (bf16[224,128]{1,0:T(8,128)(2,1)S(1)}, bf16[224,128]{1,0:T(8,128)(2,1)S(1)}, u32[]{:S(2)}, u32[]{:S(2)}) collective-permute-start(bf16[224,128]{1,0:T(8,128)(2,1)S(1)} %get-tuple-element.59), channel_id=1, source_target_pairs={{0,12},{4,8},{8,4},{12,0},{1,13},{5,9},{9,5},{13,1},{2,14},{6,10},... | collective-permute-start | bytes 172040 | tf_op jit(solution)/shard_map/ppermute | solution.py:54
  15.6 1.3 %collective-permute-start.5 = (bf16[224,128]{1,0:T(8,128)(2,1)S(1)}, bf16[224,128]{1,0:T(8,128)(2,1)S(1)}, u32[]{:S(2)}, u32[]{:S(2)}) collective-permute-start(bf16[224,128]{1,0:T(8,128)(2,1)S(1)} %get-tuple-element.59), channel_id=1, source_target_pairs={{0,8},{4,12},{8,0},{12,4},{1,9},{5,13},{9,1},{13,5},{2,10},{6,14},... | collective-permute-start | bytes 172040 | tf_op jit(solution)/shard_map/ppermute | solution.py:54
  16.9 1.1 %collective-permute-start.4 = (bf16[224,128]{1,0:T(8,128)(2,1)S(1)}, bf16[224,128]{1,0:T(8,128)(2,1)S(1)}, u32[]{:S(2)}, u32[]{:S(2)}) collective-permute-start(bf16[224,128]{1,0:T(8,128)(2,1)S(1)} %get-tuple-element.59), channel_id=1, source_target_pairs={{0,4},{4,0},{8,12},{12,8},{1,5},{5,1},{9,13},{13,9},{2,6},{6,2},{1... | collective-permute-start | bytes 172040 | tf_op jit(solution)/shard_map/ppermute | solution.py:54
  18.4 1.2 %collective-permute-start.11 = (bf16[10,64,128]{2,1,0:T(8,128)(2,1)S(1)}, bf16[10,64,128]{2,1,0:T(8,128)(2,1)S(1)}, u32[]{:S(2)}, u32[]{:S(2)}) collective-permute-start(bf16[10,64,128]{2,1,0:T(8,128)(2,1)S(1)} %get-tuple-element.63), channel_id=1, source_target_pairs={{0,12},{4,8},{8,4},{12,0},{1,13},{5,9},{9,5},{13,1},{2,14},{6,10},... | collective-permute-start | bytes 491528 | tf_op jit(solution)/shard_map/ppermute | solution.py:36
  19.6 0.9 %collective-permute-start.12 = (bf16[10,64,128]{2,1,0:T(8,128)(2,1)S(1)}, bf16[10,64,128]{2,1,0:T(8,128)(2,1)S(1)}, u32[]{:S(2)}, u32[]{:S(2)}) collective-permute-start(bf16[10,64,128]{2,1,0:T(8,128)(2,1)S(1)} %get-tuple-element.64), channel_id=1, source_target_pairs={{0,4},{4,0},{8,12},{12,8},{1,5},{5,1},{9,13},{13,9},{2,6},{6,2},{1... | collective-permute-start | bytes 491528 | tf_op jit(solution)/shard_map/ppermute | solution.py:32
  20.6 1.1 %collective-permute-done.4 = bf16[224,128]{1,0:T(8,128)(2,1)S(1)} collective-permute-done((bf16[224,128]{1,0:T(8,128)(2,1)S(1)}, bf16[224,128]{1,0:T(8,128)(2,1)S(1)}, u32[]{:S(2)}, u32[]{:S(2)}) %collective-permute-start.4) | collective-permute-done | bytes 57376 | tf_op jit(solution)/shard_map/ppermute | solution.py:54
  21.7 3.7 %collective-permute-start.9 = (bf16[224,128]{1,0:T(8,128)(2,1)S(1)}, bf16[224,128]{1,0:T(8,128)(2,1)S(1)}, u32[]{:S(2)}, u32[]{:S(2)}) collective-permute-start(bf16[224,128]{1,0:T(8,128)(2,1)S(1)} %fusion), channel_id=1, source_target_pairs={{0,3},{1,2},{2,1},{3,0},{4,7},{5,6},{6,5},{7,4},{8,11},{9,10},{10,... | collective-permute-start | bytes 172040 | tf_op jit(solution)/shard_map/ppermute | solution.py:54
  25.4 0.8 %collective-permute-start.7 = (bf16[224,128]{1,0:T(8,128)(2,1)S(1)}, bf16[224,128]{1,0:T(8,128)(2,1)S(1)}, u32[]{:S(2)}, u32[]{:S(2)}) collective-permute-start(bf16[224,128]{1,0:T(8,128)(2,1)S(1)} %fusion), channel_id=1, source_target_pairs={{0,1},{1,0},{2,3},{3,2},{4,5},{5,4},{6,7},{7,6},{8,9},{9,8},{10,11... | collective-permute-start | bytes 172040 | tf_op jit(solution)/shard_map/ppermute | solution.py:54
  26.5 1.5 %collective-permute-done.12 = bf16[10,64,128]{2,1,0:T(8,128)(2,1)S(1)} collective-permute-done((bf16[10,64,128]{2,1,0:T(8,128)(2,1)S(1)}, bf16[10,64,128]{2,1,0:T(8,128)(2,1)S(1)}, u32[]{:S(2)}, u32[]{:S(2)}) %collective-permute-start.12) | collective-permute-done | bytes 163872 | tf_op jit(solution)/shard_map/ppermute | solution.py:32
  28.0 1.2 %shard_map.71 = bf16[8,4,32,128]{3,2,1,0:T(8,128)(2,1)S(1)} custom-call(bf16[12,64,128]{2,1,0:T(8,128)(2,1)S(1)} %get-tuple-element.43.inner, bf16[12,64,128]{2,1,0:T(8,128)(2,1)S(1)} %get-tuple-element.44.sides, bf16[8,64,128]{2,1,0:T(8,128)(2,1)S(1)} %get-tuple-element.45.ends, bf16[4,64,128]{2,1,0:T(8,128)(2,1)S(1)} %get-tuple-element.46.below, ...), custom_call_target="tpu_custom_call" | custom-call | flops 452984832 | bytes 1355776 | tf_op jit(solution)/shard_map/pallas_call | solution.py:243
  29.2 1.2 %collective-permute-done.8 = bf16[224,128]{1,0:T(8,128)(2,1)S(1)} collective-permute-done((bf16[224,128]{1,0:T(8,128)(2,1)S(1)}, bf16[224,128]{1,0:T(8,128)(2,1)S(1)}, u32[]{:S(2)}, u32[]{:S(2)}) %collective-permute-start.8) | collective-permute-done | bytes 57376 | tf_op jit(solution)/shard_map/ppermute | solution.py:54
  30.6 0.8 %copy.25 = bf16[1,32,8,4,128]{4,3,2,1,0:T(4,128)(2,1)} copy(bf16[1,32,8,4,128]{4,1,3,2,0:T(8,128)(2,1)S(1)} %bitcast.36) | data formatting | bytes 524288
  31.5 0.5 %collective-permute-done.13 = f32[224,128]{1,0:T(8,128)S(1)} collective-permute-done((f32[224,128]{1,0:T(8,128)S(1)}, f32[224,128]{1,0:T(8,128)S(1)}, u32[]{:S(2)}, u32[]{:S(2)}) %collective-permute-start.13) | collective-permute-done | bytes 114720 | tf_op jit(solution)/shard_map/ppermute | solution.py:54
  32.0 0.9 %shard_map.72 = (f32[864,64]{1,0:T(8,128)}, f32[1,64]{1,0:T(1,128)}) custom-call(f32[224,128]{1,0:T(8,128)S(1)} %get-tuple-element.70.refs_0_, f32[224,128]{1,0:T(8,128)S(1)} %get-tuple-element.69.refs_1_), custom_call_target="tpu_custom_call" | custom-call | flops 57344 | bytes 450816 | tf_op jit(solution)/shard_map/pallas_call | solution.py:243
  (41 shorter events, 2.6 us)
Async XLA Ops:
  1.7 7.6 %collective-permute-start = (bf16[8,32,128]{2,1,0:T(8,128)(2,1)S(1)}, bf16[8,32,128]{2,1,0:T(8,128)(2,1)S(1)}, u32[]{:S(2)}, u32[]{:S(2)}) collective-permute-start(bf16[8,32,128]{2,1,0:T(8,128)(2,1)S(1)} %get-tuple-element.79), channel_id=1, source_target_pairs={{0,12},{4,8},{8,4},{12,0},{1,13},{5,9},{9,5},{13,1},{2,14},{6,10},... | collective-permute-start | bytes 196616 | tf_op jit(solution)/shard_map/ppermute | solution.py:36
  5.7 4.3 %collective-permute-start.1 = (bf16[8,32,128]{2,1,0:T(8,128)(2,1)S(1)}, bf16[8,32,128]{2,1,0:T(8,128)(2,1)S(1)}, u32[]{:S(2)}, u32[]{:S(2)}) collective-permute-start(bf16[8,32,128]{2,1,0:T(8,128)(2,1)S(1)} %get-tuple-element.80), channel_id=1, source_target_pairs={{0,4},{4,0},{8,12},{12,8},{1,5},{5,1},{9,13},{13,9},{2,6},{6,2},{1... | collective-permute-start | bytes 196616 | tf_op jit(solution)/shard_map/ppermute | solution.py:32
  10.0 1.3 %collective-permute-start.2 = (bf16[6,32,128]{2,1,0:T(8,128)(2,1)S(1)}, bf16[6,32,128]{2,1,0:T(8,128)(2,1)S(1)}, u32[]{:S(2)}, u32[]{:S(2)}) collective-permute-start(bf16[6,32,128]{2,1,0:T(8,128)(2,1)S(1)} %maximum_select_fusion), channel_id=1, source_target_pairs={{0,16},{16,0},{1,17},{17,1},{2,18},{18,2},{3,19},{19,3},{4,20},{20... | collective-permute-start | bytes 147464 | tf_op jit(solution)/shard_map/ppermute | solution.py:32
  12.5 1.4 %collective-permute-start.10 = (bf16[4,64,128]{2,1,0:T(8,128)(2,1)S(1)}, bf16[4,64,128]{2,1,0:T(8,128)(2,1)S(1)}, u32[]{:S(2)}, u32[]{:S(2)}) collective-permute-start(bf16[4,64,128]{2,1,0:T(8,128)(2,1)S(1)} %slice_select_fusion.1), channel_id=1, source_target_pairs={{0,16},{16,0},{1,17},{17,1},{2,18},{18,2},{3,19},{19,3},{4,20},{20... | collective-permute-start | bytes 196616 | tf_op jit(solution)/shard_map/ppermute | solution.py:32
  13.0 1.4 %collective-permute-start.3 = (f32[224,128]{1,0:T(8,128)S(1)}, f32[224,128]{1,0:T(8,128)S(1)}, u32[]{:S(2)}, u32[]{:S(2)}) collective-permute-start(f32[224,128]{1,0:T(8,128)S(1)} %slice_select_fusion), channel_id=1, source_target_pairs={{0,16},{16,0},{1,17},{17,1},{2,18},{18,2},{3,19},{19,3},{4,20},{20... | collective-permute-start | bytes 344072 | tf_op jit(solution)/shard_map/ppermute | solution.py:54
  14.4 6.1 %collective-permute-start.6 = (bf16[224,128]{1,0:T(8,128)(2,1)S(1)}, bf16[224,128]{1,0:T(8,128)(2,1)S(1)}, u32[]{:S(2)}, u32[]{:S(2)}) collective-permute-start(bf16[224,128]{1,0:T(8,128)(2,1)S(1)} %get-tuple-element.59), channel_id=1, source_target_pairs={{0,12},{4,8},{8,4},{12,0},{1,13},{5,9},{9,5},{13,1},{2,14},{6,10},... | collective-permute-start | bytes 172040 | tf_op jit(solution)/shard_map/ppermute | solution.py:54
  15.6 4.9 %collective-permute-start.5 = (bf16[224,128]{1,0:T(8,128)(2,1)S(1)}, bf16[224,128]{1,0:T(8,128)(2,1)S(1)}, u32[]{:S(2)}, u32[]{:S(2)}) collective-permute-start(bf16[224,128]{1,0:T(8,128)(2,1)S(1)} %get-tuple-element.59), channel_id=1, source_target_pairs={{0,8},{4,12},{8,0},{12,4},{1,9},{5,13},{9,1},{13,5},{2,10},{6,14},... | collective-permute-start | bytes 172040 | tf_op jit(solution)/shard_map/ppermute | solution.py:54
  16.9 4.8 %collective-permute-start.4 = (bf16[224,128]{1,0:T(8,128)(2,1)S(1)}, bf16[224,128]{1,0:T(8,128)(2,1)S(1)}, u32[]{:S(2)}, u32[]{:S(2)}) collective-permute-start(bf16[224,128]{1,0:T(8,128)(2,1)S(1)} %get-tuple-element.59), channel_id=1, source_target_pairs={{0,4},{4,0},{8,12},{12,8},{1,5},{5,1},{9,13},{13,9},{2,6},{6,2},{1... | collective-permute-start | bytes 172040 | tf_op jit(solution)/shard_map/ppermute | solution.py:54
  18.4 8.1 %collective-permute-start.11 = (bf16[10,64,128]{2,1,0:T(8,128)(2,1)S(1)}, bf16[10,64,128]{2,1,0:T(8,128)(2,1)S(1)}, u32[]{:S(2)}, u32[]{:S(2)}) collective-permute-start(bf16[10,64,128]{2,1,0:T(8,128)(2,1)S(1)} %get-tuple-element.63), channel_id=1, source_target_pairs={{0,12},{4,8},{8,4},{12,0},{1,13},{5,9},{9,5},{13,1},{2,14},{6,10},... | collective-permute-start | bytes 491528 | tf_op jit(solution)/shard_map/ppermute | solution.py:36
  19.6 8.4 %collective-permute-start.12 = (bf16[10,64,128]{2,1,0:T(8,128)(2,1)S(1)}, bf16[10,64,128]{2,1,0:T(8,128)(2,1)S(1)}, u32[]{:S(2)}, u32[]{:S(2)}) collective-permute-start(bf16[10,64,128]{2,1,0:T(8,128)(2,1)S(1)} %get-tuple-element.64), channel_id=1, source_target_pairs={{0,4},{4,0},{8,12},{12,8},{1,5},{5,1},{9,13},{13,9},{2,6},{6,2},{1... | collective-permute-start | bytes 491528 | tf_op jit(solution)/shard_map/ppermute | solution.py:32
  21.7 7.5 %collective-permute-start.9 = (bf16[224,128]{1,0:T(8,128)(2,1)S(1)}, bf16[224,128]{1,0:T(8,128)(2,1)S(1)}, u32[]{:S(2)}, u32[]{:S(2)}) collective-permute-start(bf16[224,128]{1,0:T(8,128)(2,1)S(1)} %fusion), channel_id=1, source_target_pairs={{0,3},{1,2},{2,1},{3,0},{4,7},{5,6},{6,5},{7,4},{8,11},{9,10},{10,... | collective-permute-start | bytes 172040 | tf_op jit(solution)/shard_map/ppermute | solution.py:54
  25.4 5.1 %collective-permute-start.8 = (bf16[224,128]{1,0:T(8,128)(2,1)S(1)}, bf16[224,128]{1,0:T(8,128)(2,1)S(1)}, u32[]{:S(2)}, u32[]{:S(2)}) collective-permute-start(bf16[224,128]{1,0:T(8,128)(2,1)S(1)} %fusion), channel_id=1, source_target_pairs={{0,2},{1,3},{2,0},{3,1},{4,6},{5,7},{6,4},{7,5},{8,10},{9,11},{10,... | collective-permute-start | bytes 172040 | tf_op jit(solution)/shard_map/ppermute | solution.py:54
  25.4 5.1 %collective-permute-start.7 = (bf16[224,128]{1,0:T(8,128)(2,1)S(1)}, bf16[224,128]{1,0:T(8,128)(2,1)S(1)}, u32[]{:S(2)}, u32[]{:S(2)}) collective-permute-start(bf16[224,128]{1,0:T(8,128)(2,1)S(1)} %fusion), channel_id=1, source_target_pairs={{0,1},{1,0},{2,3},{3,2},{4,5},{5,4},{6,7},{7,6},{8,9},{9,8},{10,11... | collective-permute-start | bytes 172040 | tf_op jit(solution)/shard_map/ppermute | solution.py:54
  30.5 1.4 %collective-permute-start.13 = (f32[224,128]{1,0:T(8,128)S(1)}, f32[224,128]{1,0:T(8,128)S(1)}, u32[]{:S(2)}, u32[]{:S(2)}) collective-permute-start(f32[224,128]{1,0:T(8,128)S(1)} %add_add_fusion), channel_id=1, source_target_pairs={{0,16},{16,0},{1,17},{17,1},{2,18},{18,2},{3,19},{19,3},{4,20},{20... | collective-permute-start | bytes 344072 | tf_op jit(solution)/shard_map/ppermute | solution.py:54

commit v11 on v10

--- a/solution.py
+++ b/solution.py
@@ -285,6 +285,7 @@
     flops = 4 * width * 27 * ci * co
     total = None
     fields = []
+    (inputs,) = loaded(inputs)
     fields_in = [inputs[cube].transpose(1, 2, 0, 3) for cube in range(cubes)]
     rows = [(x[:, 0], x[:, -1]) for x in fields_in]
     rows, fields_in, weight, bias, cotangent = lax.optimization_barrier(

time: 33 us -> 33 us (level)
  Pallas kernels: 6.62 us -> 7.58 us
  local copies, waits for them, and re-layouts: 3.1 us -> 2.15 us
    unnamed x6 -> x5, local copies, waits for them, and re-layouts: 1.95 us -> 0.89 us
    pallas_call x1 -> x2, Pallas kernels: 1.21 us -> 2.17 us  [loaded(): pl.pallas_call(load_kernel, out_shape=[jax.ShapeDtypeStruct(a.shape, a.dt...]
where the time goes in v11:
time: 33 us; the launch traced here: 32.9 us
  starting transfers between devices  15.4 us (47%)
  Pallas kernels  7.58 us (23%)
  waiting for transfers between devices  6.54 us (20%)
  local copies, waits for them, and re-layouts  2.15 us (7%)
  between operations  0.89 us (3%)
    ppermute x8, starting transfers between devices, swap(): lax.ppermute(array, axis, [(i, i ^ mask) for i in range(lax.axis_size(axi...  8.25 us
    pallas_call x5, Pallas kernels, call(): pl.pallas_call(kernel, out_shape=outs, scratch_shapes=scratch, compiler_p...  5.42 us
    ppermute x2, starting transfers between devices, meet(): second = lax.ppermute(jnp.where(even, low_edge, high_edge), axis, outer)  5.2 us
    ppermute x8, waiting for transfers between devices, swap(): lax.ppermute(array, axis, [(i, i ^ mask) for i in range(lax.axis_size(axi...  3.27 us
    ppermute x4, waiting for transfers between devices, meet(): first = lax.ppermute(jnp.where(even, high_edge, low_edge), axis, inner)  2.99 us
    pallas_call x2, Pallas kernels, loaded(): pl.pallas_call(load_kernel, out_shape=[jax.ShapeDtypeStruct(a.shape, a.dt...  2.17 us
    ppermute x4, starting transfers between devices, meet(): first = lax.ppermute(jnp.where(even, high_edge, low_edge), axis, inner)  1.96 us
    unnamed x5, local copies, waits for them, and re-layouts  0.89 us
  transfers between devices with their start and end apart: 14, of which 10 were waited for; matrix products, arithmetic and copies ran while one was open for 7% of the time, Pallas kernels for 14%

profile of v11, /device:TPU:0, one launch (start us, length us, event | category | flops | bytes accessed | tf_op | source)
XLA Modules:
  0.0 32.9 jit_solution(10353541835373109946)
XLA Ops:
  0.6 1.0 %shard_map.67 = bf16[1,32,8,4,128]{4,3,2,1,0:T(4,128)(2,1)S(1)} custom-call(bf16[1,32,8,4,128]{4,3,2,1,0:T(4,128)(2,1)} %refs_0_.1), custom_call_target="tpu_custom_call" | custom-call | tf_op jit(solution)/shard_map/pallas_call | solution.py:231
  1.8 4.0 %collective-permute-start = (bf16[8,32,128]{2,1,0:T(8,128)(2,1)S(1)}, bf16[8,32,128]{2,1,0:T(8,128)(2,1)S(1)}, u32[]{:S(2)}, u32[]{:S(2)}) collective-permute-start(bf16[8,32,128]{2,1,0:T(8,128)(2,1)S(1)} %get-tuple-element.79), channel_id=1, source_target_pairs={{0,12},{4,8},{8,4},{12,0},{1,13},{5,9},{9,5},{13,1},{2,14},{6,10},... | collective-permute-start | bytes 196616 | tf_op jit(solution)/shard_map/ppermute | solution.py:36
  5.7 0.5 %collective-permute-start.1 = (bf16[8,32,128]{2,1,0:T(8,128)(2,1)S(1)}, bf16[8,32,128]{2,1,0:T(8,128)(2,1)S(1)}, u32[]{:S(2)}, u32[]{:S(2)}) collective-permute-start(bf16[8,32,128]{2,1,0:T(8,128)(2,1)S(1)} %get-tuple-element.80), channel_id=1, source_target_pairs={{0,4},{4,0},{8,12},{12,8},{1,5},{5,1},{9,13},{13,9},{2,6},{6,2},{1... | collective-permute-start | bytes 196616 | tf_op jit(solution)/shard_map/ppermute | solution.py:32
  6.3 1.2 %shard_map.68 = (bf16[3,3,3,32,64]{4,3,2,1,0:T(8,128)(2,1)S(1)}, f32[1,64]{1,0:T(1,128)S(1)}, bf16[1,64,8,4,128]{4,3,2,1,0:T(4,128)(2,1)S(1)}) custom-call(bf16[3,3,3,32,64]{4,3,2,1,0:T(8,128)(2,1)} %bitcast.40, f32[1,64]{1,0:T(1,128)} %bitcast.41, bf16[1,64,8,4,128]{4,3,2,1,0:T(4,128)(2,1)} %refs_2_), custom_call_target="tpu_custom_call" | custom-call | tf_op jit(solution)/shard_map/pallas_call | solution.py:231
  8.3 1.1 %shard_map.69 = (bf16[12,64,128]{2,1,0:T(8,128)(2,1)S(1)}, f32[448,128]{1,0:T(8,128)S(1)}) custom-call(bf16[8,4,32,128]{3,2,1,0:T(8,128)(2,1)S(1)} %copy.22.x, bf16[192,288]{1,0:T(8,128)(2,1)S(1)} %copy.19.refs_0_.refs_2_.refs_4_, f32[1,64]{1,0:T(1,128)S(1)} %get-tuple-element.33.refs_1_.refs_3_.refs_5_, bf16[8,4,64,128]{3,2,1,0:T(8,128)(2,1)S(1)} %bitcast.32), custom_call_target="tpu_custom_call" | custom-call | flops 339738624 | bytes 1323264 | tf_op jit(solution)/shard_map/pallas_call | solution.py:243
  9.4 0.6 %collective-permute-done.1 = bf16[8,32,128]{2,1,0:T(8,128)(2,1)S(1)} collective-permute-done((bf16[8,32,128]{2,1,0:T(8,128)(2,1)S(1)}, bf16[8,32,128]{2,1,0:T(8,128)(2,1)S(1)}, u32[]{:S(2)}, u32[]{:S(2)}) %collective-permute-start.1) | collective-permute-done | bytes 65568 | tf_op jit(solution)/shard_map/ppermute | solution.py:32
  10.1 1.1 %shard_map.70 = (bf16[12,64,128]{2,1,0:T(8,128)(2,1)S(1)}, f32[448,128]{1,0:T(8,128)S(1)}) custom-call(bf16[8,4,32,128]{3,2,1,0:T(8,128)(2,1)S(1)} %copy.22.x, bf16[8,32,128]{2,1,0:T(8,128)(2,1)S(1)} %get-tuple-element.38.refs_0_, bf16[8,32,128]{2,1,0:T(8,128)(2,1)S(1)} %get-tuple-element.39.refs_1_, bf16[192,288]{1,0:T(8,128)(2,1)S(1)} %copy.19.refs_0_.refs_2_.refs_4_, ...), custom_call_target="tpu_custom_call" | custom-call | flops 339738624 | bytes 1683712 | tf_op jit(solution)/shard_map/pallas_call | solution.py:243
  11.4 1.1 %shard_map.71 = (bf16[8,64,128]{2,1,0:T(8,128)(2,1)S(1)}, f32[448,128]{1,0:T(8,128)S(1)}) custom-call(bf16[8,4,32,128]{3,2,1,0:T(8,128)(2,1)S(1)} %copy.22.x, bf16[8,32,128]{2,1,0:T(8,128)(2,1)S(1)} %get-tuple-element.38.refs_0_, bf16[8,32,128]{2,1,0:T(8,128)(2,1)S(1)} %get-tuple-element.39.refs_1_, bf16[6,32,128]{2,1,0:T(8,128)(2,1)S(1)} %get-tuple-element.92.refs_2_, ...), custom_call_target="tpu_custom_call" | custom-call | flops 226492416 | bytes 1716480 | tf_op jit(solution)/shard_map/pallas_call | solution.py:243
  12.5 0.5 %collective-permute-start.10 = (bf16[4,64,128]{2,1,0:T(8,128)(2,1)S(1)}, bf16[4,64,128]{2,1,0:T(8,128)(2,1)S(1)}, u32[]{:S(2)}, u32[]{:S(2)}) collective-permute-start(bf16[4,64,128]{2,1,0:T(8,128)(2,1)S(1)} %slice_select_fusion.1), channel_id=1, source_target_pairs={{0,16},{16,0},{1,17},{17,1},{2,18},{18,2},{3,19},{19,3},{4,20},{20... | collective-permute-start | bytes 196616 | tf_op jit(solution)/shard_map/ppermute | solution.py:32
  13.2 0.7 %collective-permute-done.10 = bf16[4,64,128]{2,1,0:T(8,128)(2,1)S(1)} collective-permute-done((bf16[4,64,128]{2,1,0:T(8,128)(2,1)S(1)}, bf16[4,64,128]{2,1,0:T(8,128)(2,1)S(1)}, u32[]{:S(2)}, u32[]{:S(2)}) %collective-permute-start.10) | collective-permute-done | bytes 65568 | tf_op jit(solution)/shard_map/ppermute | solution.py:32
  14.4 1.2 %collective-permute-start.6 = (bf16[224,128]{1,0:T(8,128)(2,1)S(1)}, bf16[224,128]{1,0:T(8,128)(2,1)S(1)}, u32[]{:S(2)}, u32[]{:S(2)}) collective-permute-start(bf16[224,128]{1,0:T(8,128)(2,1)S(1)} %get-tuple-element.59), channel_id=1, source_target_pairs={{0,12},{4,8},{8,4},{12,0},{1,13},{5,9},{9,5},{13,1},{2,14},{6,10},... | collective-permute-start | bytes 172040 | tf_op jit(solution)/shard_map/ppermute | solution.py:54
  15.7 1.3 %collective-permute-start.5 = (bf16[224,128]{1,0:T(8,128)(2,1)S(1)}, bf16[224,128]{1,0:T(8,128)(2,1)S(1)}, u32[]{:S(2)}, u32[]{:S(2)}) collective-permute-start(bf16[224,128]{1,0:T(8,128)(2,1)S(1)} %get-tuple-element.59), channel_id=1, source_target_pairs={{0,8},{4,12},{8,0},{12,4},{1,9},{5,13},{9,1},{13,5},{2,10},{6,14},... | collective-permute-start | bytes 172040 | tf_op jit(solution)/shard_map/ppermute | solution.py:54
  16.9 1.1 %collective-permute-start.4 = (bf16[224,128]{1,0:T(8,128)(2,1)S(1)}, bf16[224,128]{1,0:T(8,128)(2,1)S(1)}, u32[]{:S(2)}, u32[]{:S(2)}) collective-permute-start(bf16[224,128]{1,0:T(8,128)(2,1)S(1)} %get-tuple-element.59), channel_id=1, source_target_pairs={{0,4},{4,0},{8,12},{12,8},{1,5},{5,1},{9,13},{13,9},{2,6},{6,2},{1... | collective-permute-start | bytes 172040 | tf_op jit(solution)/shard_map/ppermute | solution.py:54
  18.4 1.2 %collective-permute-start.11 = (bf16[10,64,128]{2,1,0:T(8,128)(2,1)S(1)}, bf16[10,64,128]{2,1,0:T(8,128)(2,1)S(1)}, u32[]{:S(2)}, u32[]{:S(2)}) collective-permute-start(bf16[10,64,128]{2,1,0:T(8,128)(2,1)S(1)} %get-tuple-element.63), channel_id=1, source_target_pairs={{0,12},{4,8},{8,4},{12,0},{1,13},{5,9},{9,5},{13,1},{2,14},{6,10},... | collective-permute-start | bytes 491528 | tf_op jit(solution)/shard_map/ppermute | solution.py:36
  19.6 0.9 %collective-permute-start.12 = (bf16[10,64,128]{2,1,0:T(8,128)(2,1)S(1)}, bf16[10,64,128]{2,1,0:T(8,128)(2,1)S(1)}, u32[]{:S(2)}, u32[]{:S(2)}) collective-permute-start(bf16[10,64,128]{2,1,0:T(8,128)(2,1)S(1)} %get-tuple-element.64), channel_id=1, source_target_pairs={{0,4},{4,0},{8,12},{12,8},{1,5},{5,1},{9,13},{13,9},{2,6},{6,2},{1... | collective-permute-start | bytes 491528 | tf_op jit(solution)/shard_map/ppermute | solution.py:32
  20.6 1.1 %collective-permute-done.4 = bf16[224,128]{1,0:T(8,128)(2,1)S(1)} collective-permute-done((bf16[224,128]{1,0:T(8,128)(2,1)S(1)}, bf16[224,128]{1,0:T(8,128)(2,1)S(1)}, u32[]{:S(2)}, u32[]{:S(2)}) %collective-permute-start.4) | collective-permute-done | bytes 57376 | tf_op jit(solution)/shard_map/ppermute | solution.py:54
  21.8 3.7 %collective-permute-start.9 = (bf16[224,128]{1,0:T(8,128)(2,1)S(1)}, bf16[224,128]{1,0:T(8,128)(2,1)S(1)}, u32[]{:S(2)}, u32[]{:S(2)}) collective-permute-start(bf16[224,128]{1,0:T(8,128)(2,1)S(1)} %fusion), channel_id=1, source_target_pairs={{0,3},{1,2},{2,1},{3,0},{4,7},{5,6},{6,5},{7,4},{8,11},{9,10},{10,... | collective-permute-start | bytes 172040 | tf_op jit(solution)/shard_map/ppermute | solution.py:54
  25.4 0.8 %collective-permute-start.7 = (bf16[224,128]{1,0:T(8,128)(2,1)S(1)}, bf16[224,128]{1,0:T(8,128)(2,1)S(1)}, u32[]{:S(2)}, u32[]{:S(2)}) collective-permute-start(bf16[224,128]{1,0:T(8,128)(2,1)S(1)} %fusion), channel_id=1, source_target_pairs={{0,1},{1,0},{2,3},{3,2},{4,5},{5,4},{6,7},{7,6},{8,9},{9,8},{10,11... | collective-permute-start | bytes 172040 | tf_op jit(solution)/shard_map/ppermute | solution.py:54
  26.5 1.5 %collective-permute-done.12 = bf16[10,64,128]{2,1,0:T(8,128)(2,1)S(1)} collective-permute-done((bf16[10,64,128]{2,1,0:T(8,128)(2,1)S(1)}, bf16[10,64,128]{2,1,0:T(8,128)(2,1)S(1)}, u32[]{:S(2)}, u32[]{:S(2)}) %collective-permute-start.12) | collective-permute-done | bytes 163872 | tf_op jit(solution)/shard_map/ppermute | solution.py:32
  28.1 1.2 %shard_map.72 = bf16[8,4,32,128]{3,2,1,0:T(8,128)(2,1)S(1)} custom-call(bf16[12,64,128]{2,1,0:T(8,128)(2,1)S(1)} %get-tuple-element.43.inner, bf16[12,64,128]{2,1,0:T(8,128)(2,1)S(1)} %get-tuple-element.44.sides, bf16[8,64,128]{2,1,0:T(8,128)(2,1)S(1)} %get-tuple-element.45.ends, bf16[4,64,128]{2,1,0:T(8,128)(2,1)S(1)} %get-tuple-element.46.below, ...), custom_call_target="tpu_custom_call" | custom-call | flops 452984832 | bytes 1355776 | tf_op jit(solution)/shard_map/pallas_call | solution.py:243
  29.3 1.2 %collective-permute-done.8 = bf16[224,128]{1,0:T(8,128)(2,1)S(1)} collective-permute-done((bf16[224,128]{1,0:T(8,128)(2,1)S(1)}, bf16[224,128]{1,0:T(8,128)(2,1)S(1)}, u32[]{:S(2)}, u32[]{:S(2)}) %collective-permute-start.8) | collective-permute-done | bytes 57376 | tf_op jit(solution)/shard_map/ppermute | solution.py:54
  30.6 0.8 %copy.25 = bf16[1,32,8,4,128]{4,3,2,1,0:T(4,128)(2,1)} copy(bf16[1,32,8,4,128]{4,1,3,2,0:T(8,128)(2,1)S(1)} %bitcast.36) | data formatting | bytes 524288
  31.5 0.5 %collective-permute-done.13 = f32[224,128]{1,0:T(8,128)S(1)} collective-permute-done((f32[224,128]{1,0:T(8,128)S(1)}, f32[224,128]{1,0:T(8,128)S(1)}, u32[]{:S(2)}, u32[]{:S(2)}) %collective-permute-start.13) | collective-permute-done | bytes 114720 | tf_op jit(solution)/shard_map/ppermute | solution.py:54
  32.0 0.9 %shard_map.73 = (f32[864,64]{1,0:T(8,128)}, f32[1,64]{1,0:T(1,128)}) custom-call(f32[224,128]{1,0:T(8,128)S(1)} %get-tuple-element.70.refs_0_, f32[224,128]{1,0:T(8,128)S(1)} %get-tuple-element.69.refs_1_), custom_call_target="tpu_custom_call" | custom-call | flops 57344 | bytes 450816 | tf_op jit(solution)/shard_map/pallas_call | solution.py:243
  (42 shorter events, 2.7 us)
Async XLA Ops:
  1.8 7.6 %collective-permute-start = (bf16[8,32,128]{2,1,0:T(8,128)(2,1)S(1)}, bf16[8,32,128]{2,1,0:T(8,128)(2,1)S(1)}, u32[]{:S(2)}, u32[]{:S(2)}) collective-permute-start(bf16[8,32,128]{2,1,0:T(8,128)(2,1)S(1)} %get-tuple-element.79), channel_id=1, source_target_pairs={{0,12},{4,8},{8,4},{12,0},{1,13},{5,9},{9,5},{13,1},{2,14},{6,10},... | collective-permute-start | bytes 196616 | tf_op jit(solution)/shard_map/ppermute | solution.py:36
  5.7 4.3 %collective-permute-start.1 = (bf16[8,32,128]{2,1,0:T(8,128)(2,1)S(1)}, bf16[8,32,128]{2,1,0:T(8,128)(2,1)S(1)}, u32[]{:S(2)}, u32[]{:S(2)}) collective-permute-start(bf16[8,32,128]{2,1,0:T(8,128)(2,1)S(1)} %get-tuple-element.80), channel_id=1, source_target_pairs={{0,4},{4,0},{8,12},{12,8},{1,5},{5,1},{9,13},{13,9},{2,6},{6,2},{1... | collective-permute-start | bytes 196616 | tf_op jit(solution)/shard_map/ppermute | solution.py:32
  10.0 1.3 %collective-permute-start.2 = (bf16[6,32,128]{2,1,0:T(8,128)(2,1)S(1)}, bf16[6,32,128]{2,1,0:T(8,128)(2,1)S(1)}, u32[]{:S(2)}, u32[]{:S(2)}) collective-permute-start(bf16[6,32,128]{2,1,0:T(8,128)(2,1)S(1)} %maximum_select_fusion), channel_id=1, source_target_pairs={{0,16},{16,0},{1,17},{17,1},{2,18},{18,2},{3,19},{19,3},{4,20},{20... | collective-permute-start | bytes 147464 | tf_op jit(solution)/shard_map/ppermute | solution.py:32
  12.5 1.4 %collective-permute-start.10 = (bf16[4,64,128]{2,1,0:T(8,128)(2,1)S(1)}, bf16[4,64,128]{2,1,0:T(8,128)(2,1)S(1)}, u32[]{:S(2)}, u32[]{:S(2)}) collective-permute-start(bf16[4,64,128]{2,1,0:T(8,128)(2,1)S(1)} %slice_select_fusion.1), channel_id=1, source_target_pairs={{0,16},{16,0},{1,17},{17,1},{2,18},{18,2},{3,19},{19,3},{4,20},{20... | collective-permute-start | bytes 196616 | tf_op jit(solution)/shard_map/ppermute | solution.py:32
  13.0 1.4 %collective-permute-start.3 = (f32[224,128]{1,0:T(8,128)S(1)}, f32[224,128]{1,0:T(8,128)S(1)}, u32[]{:S(2)}, u32[]{:S(2)}) collective-permute-start(f32[224,128]{1,0:T(8,128)S(1)} %slice_select_fusion), channel_id=1, source_target_pairs={{0,16},{16,0},{1,17},{17,1},{2,18},{18,2},{3,19},{19,3},{4,20},{20... | collective-permute-start | bytes 344072 | tf_op jit(solution)/shard_map/ppermute | solution.py:54
  14.4 6.1 %collective-permute-start.6 = (bf16[224,128]{1,0:T(8,128)(2,1)S(1)}, bf16[224,128]{1,0:T(8,128)(2,1)S(1)}, u32[]{:S(2)}, u32[]{:S(2)}) collective-permute-start(bf16[224,128]{1,0:T(8,128)(2,1)S(1)} %get-tuple-element.59), channel_id=1, source_target_pairs={{0,12},{4,8},{8,4},{12,0},{1,13},{5,9},{9,5},{13,1},{2,14},{6,10},... | collective-permute-start | bytes 172040 | tf_op jit(solution)/shard_map/ppermute | solution.py:54
  15.7 4.9 %collective-permute-start.5 = (bf16[224,128]{1,0:T(8,128)(2,1)S(1)}, bf16[224,128]{1,0:T(8,128)(2,1)S(1)}, u32[]{:S(2)}, u32[]{:S(2)}) collective-permute-start(bf16[224,128]{1,0:T(8,128)(2,1)S(1)} %get-tuple-element.59), channel_id=1, source_target_pairs={{0,8},{4,12},{8,0},{12,4},{1,9},{5,13},{9,1},{13,5},{2,10},{6,14},... | collective-permute-start | bytes 172040 | tf_op jit(solution)/shard_map/ppermute | solution.py:54
  16.9 4.8 %collective-permute-start.4 = (bf16[224,128]{1,0:T(8,128)(2,1)S(1)}, bf16[224,128]{1,0:T(8,128)(2,1)S(1)}, u32[]{:S(2)}, u32[]{:S(2)}) collective-permute-start(bf16[224,128]{1,0:T(8,128)(2,1)S(1)} %get-tuple-element.59), channel_id=1, source_target_pairs={{0,4},{4,0},{8,12},{12,8},{1,5},{5,1},{9,13},{13,9},{2,6},{6,2},{1... | collective-permute-start | bytes 172040 | tf_op jit(solution)/shard_map/ppermute | solution.py:54
  18.4 8.1 %collective-permute-start.11 = (bf16[10,64,128]{2,1,0:T(8,128)(2,1)S(1)}, bf16[10,64,128]{2,1,0:T(8,128)(2,1)S(1)}, u32[]{:S(2)}, u32[]{:S(2)}) collective-permute-start(bf16[10,64,128]{2,1,0:T(8,128)(2,1)S(1)} %get-tuple-element.63), channel_id=1, source_target_pairs={{0,12},{4,8},{8,4},{12,0},{1,13},{5,9},{9,5},{13,1},{2,14},{6,10},... | collective-permute-start | bytes 491528 | tf_op jit(solution)/shard_map/ppermute | solution.py:36
  19.6 8.4 %collective-permute-start.12 = (bf16[10,64,128]{2,1,0:T(8,128)(2,1)S(1)}, bf16[10,64,128]{2,1,0:T(8,128)(2,1)S(1)}, u32[]{:S(2)}, u32[]{:S(2)}) collective-permute-start(bf16[10,64,128]{2,1,0:T(8,128)(2,1)S(1)} %get-tuple-element.64), channel_id=1, source_target_pairs={{0,4},{4,0},{8,12},{12,8},{1,5},{5,1},{9,13},{13,9},{2,6},{6,2},{1... | collective-permute-start | bytes 491528 | tf_op jit(solution)/shard_map/ppermute | solution.py:32
  21.8 7.5 %collective-permute-start.9 = (bf16[224,128]{1,0:T(8,128)(2,1)S(1)}, bf16[224,128]{1,0:T(8,128)(2,1)S(1)}, u32[]{:S(2)}, u32[]{:S(2)}) collective-permute-start(bf16[224,128]{1,0:T(8,128)(2,1)S(1)} %fusion), channel_id=1, source_target_pairs={{0,3},{1,2},{2,1},{3,0},{4,7},{5,6},{6,5},{7,4},{8,11},{9,10},{10,... | collective-permute-start | bytes 172040 | tf_op jit(solution)/shard_map/ppermute | solution.py:54
  25.4 5.1 %collective-permute-start.8 = (bf16[224,128]{1,0:T(8,128)(2,1)S(1)}, bf16[224,128]{1,0:T(8,128)(2,1)S(1)}, u32[]{:S(2)}, u32[]{:S(2)}) collective-permute-start(bf16[224,128]{1,0:T(8,128)(2,1)S(1)} %fusion), channel_id=1, source_target_pairs={{0,2},{1,3},{2,0},{3,1},{4,6},{5,7},{6,4},{7,5},{8,10},{9,11},{10,... | collective-permute-start | bytes 172040 | tf_op jit(solution)/shard_map/ppermute | solution.py:54
  25.4 5.1 %collective-permute-start.7 = (bf16[224,128]{1,0:T(8,128)(2,1)S(1)}, bf16[224,128]{1,0:T(8,128)(2,1)S(1)}, u32[]{:S(2)}, u32[]{:S(2)}) collective-permute-start(bf16[224,128]{1,0:T(8,128)(2,1)S(1)} %fusion), channel_id=1, source_target_pairs={{0,1},{1,0},{2,3},{3,2},{4,5},{5,4},{6,7},{7,6},{8,9},{9,8},{10,11... | collective-permute-start | bytes 172040 | tf_op jit(solution)/shard_map/ppermute | solution.py:54
  30.6 1.4 %collective-permute-start.13 = (f32[224,128]{1,0:T(8,128)S(1)}, f32[224,128]{1,0:T(8,128)S(1)}, u32[]{:S(2)}, u32[]{:S(2)}) collective-permute-start(f32[224,128]{1,0:T(8,128)S(1)} %add_add_fusion), channel_id=1, source_target_pairs={{0,16},{16,0},{1,17},{17,1},{2,18},{18,2},{3,19},{19,3},{4,20},{20... | collective-permute-start | bytes 344072 | tf_op jit(solution)/shard_map/ppermute | solution.py:54

commit v12 on v10

--- a/solution.py
+++ b/solution.py
@@ -18,7 +18,7 @@
     return lax.axis_index(axis) % 2 == 0 if lax.axis_size(axis) % 2 == 0 else jnp.bool_(True)
 
 
-def meet(low_edge, high_edge, axis):
+def meet(low_edge, high_edge, axis, first=None):
     count = lax.axis_size(axis)
     none = jnp.zeros_like(low_edge)
     if count == 1:
@@ -29,7 +29,8 @@
         return lax.ppermute(high_edge, axis, up), lax.ppermute(low_edge, axis, down)
     at, even = lax.axis_index(axis), paired(axis)
     inner = [(i, i ^ 1) for i in range(count)]
-    first = lax.ppermute(jnp.where(even, high_edge, low_edge), axis, inner)
+    if first is None:
+        first = lax.ppermute(jnp.where(even, high_edge, low_edge), axis, inner)
     if count == 2:
         return none, first
     outer = [(i, (i - 1 if i % 2 == 0 else i + 1) % count) for i in range(count)]
@@ -37,8 +38,8 @@
     return jnp.where((at == 0) | (at == count - 1), none, second), first
 
 
-def exchange(low_edge, high_edge, axis):
-    second, first = meet(low_edge, high_edge, axis)
+def exchange(low_edge, high_edge, axis, first=None):
+    second, first = meet(low_edge, high_edge, axis, first)
     even = paired(axis)
     return jnp.where(even, second, first), jnp.where(even, first, second)
 
@@ -249,28 +250,44 @@
     )(*args)
 
 
-def gathered_sum(part, axis, masks):
+def gathered_sum(part, axis, masks, meanwhile):
     own = lax.reduce_precision(part, 8, 7)
     sent = own.astype(BF16)
-    terms = [own] + [swap(sent, axis, mask).astype(F32) for mask in masks]
+    near, meanwhile = lax.optimization_barrier((sent, meanwhile))
+    terms = [own]
+    for mask in masks:
+        terms.append(swap(near if mask == min(masks) else sent, axis, mask).astype(F32))
     while len(terms) > 1:
         terms = [terms[i] + terms[i + 1] for i in range(0, len(terms), 2)]
-    return terms[0]
-
-
-def summed(total, meanwhile, work):
-    half = total.shape[0] // 2
+    return terms[0], meanwhile
+
+
+def halved(total, edges):
+    half, lanes = total.shape[0] // 2, total.shape[1]
+    first = lax.axis_index("depth") % 2 == 0
     low, high = total[:half], total[half:]
+    flat = [edge.astype(F32).reshape(-1, lanes) for edge in edges]
+    got = swap(jnp.concatenate([jnp.where(first, high, low), *flat], axis=0), "depth", 1)
+    part = jnp.where(first, low, high) + got[:half]
+    received, at = [], half
+    for edge, rows in zip(edges, flat):
+        received.append(got[at : at + rows.shape[0]].reshape(edge.shape).astype(BF16))
+        at += rows.shape[0]
+    return part, received
+
+
+def summed(part, first_halos, meanwhile, work):
     first = lax.axis_index("depth") % 2 == 0
-    got = swap(jnp.where(first, high, low), "depth", 1)
-    part = jnp.where(first, low, high) + got
     for axis in AXES:
         count = lax.axis_size(axis)
         assert count & (count - 1) == 0
         bit = 2 if axis == "depth" else 1
         while bit < count:
             masks = [bit * way for way in WAYS[axis]] if 2 * bit < count else [bit]
-            part = gathered_sum(part, axis, masks)
+            if axis == AXES[-1]:
+                part, _ = gathered_sum(part, axis, masks, first_halos)
+            else:
+                part, _ = gathered_sum(part, axis, masks, ())
             bit *= len(masks) + 1
     part, done = lax.optimization_barrier((part, work(meanwhile)))
     other = swap(part, "depth", 1)
@@ -284,7 +301,7 @@
     payload_shape = jax.ShapeDtypeStruct((payload_rows, 2 * co), F32)
     flops = 4 * width * 27 * ci * co
     total = None
-    fields = []
+    deltas, fields = [], []
     fields_in = [inputs[cube].transpose(1, 2, 0, 3) for cube in range(cubes)]
     rows = [(x[:, 0], x[:, -1]) for x in fields_in]
     rows, fields_in, weight, bias, cotangent = lax.optimization_barrier(
@@ -328,11 +345,22 @@
         sides, part = forward(1, (left, right), (part,))
         ends, part = forward(2, (left, right, low, high), (part,))
         total = part if total is None else total + part
-        below, above = exchange(ends[:height], ends[height:], "depth")
+        deltas.append((inner, sides, ends))
+    even = paired("depth")
+    part, edges = halved(
+        total, [jnp.where(even, ends[height:], ends[:height]) for _, _, ends in deltas]
+    )
+    first_halos = []
+    for (inner, sides, ends), edge in zip(deltas, edges):
+        below, above = exchange(ends[:height], ends[height:], "depth", edge)
         below, above, taps = lax.optimization_barrier((below, above, taps))
         first_row = jnp.concatenate([ends[:1], sides[: depth - 2], ends[height : height + 1]], axis=0)
         last_row = jnp.concatenate([ends[height - 1 : height], sides[depth - 2 :], ends[-1:]], axis=0)
-        around = exchange(*columns(first_row, last_row, below, above), "height")
+        second, first = meet(*columns(first_row, last_row, below, above), "height")
+        first = lax.optimization_barrier(first)
+        first_halos.append(first)
+        up = paired("height")
+        around = jnp.where(up, second, first), jnp.where(up, first, second)
         fields.append((inner, sides, ends, below, above, *around))
     w2 = jnp.flip(taps, (0, 1)).transpose(2, 3, 0, 1, 4).reshape(3 * ci, 9 * co)
 
@@ -350,7 +378,7 @@
             grads.append(grad.transpose(2, 0, 1, 3))
         return jnp.stack(grads)
 
-    low, high, grads = summed(total, fields, input_gradients)
+    low, high, grads = summed(part, first_halos, fields, input_gradients)
     voxels = cubes * depth * height * width
     for axis in AXES:
         voxels *= lax.axis_size(axis)

time: 33 us -> 34.7 us (1.052)
  waiting for transfers between devices: 6.54 us -> 7.5 us
  starting transfers between devices: 15.4 us -> 16.1 us
    ppermute x8, starting transfers between devices: 8.26 us -> 9.4 us  [swap(): lax.ppermute(array, axis, [(i, i ^ mask) for i in range(lax.axis_size(axi...]
    ppermute x4 -> x3, waiting for transfers between devices: 2.98 us -> 3.67 us  [meet(): first = lax.ppermute(jnp.where(even, high_edge, low_edge), axis, inner)]
    ppermute x8, waiting for transfers between devices: 3.28 us -> 3.82 us  [swap(): lax.ppermute(array, axis, [(i, i ^ mask) for i in range(lax.axis_size(axi...]
    ppermute x4 -> x3, starting transfers between devices: 1.96 us -> 1.5 us  [meet(): first = lax.ppermute(jnp.where(even, high_edge, low_edge), axis, inner)]
  transfers between devices with their start and end apart: 14 -> 13, of which waited for: 10 -> 7; matrix products, arithmetic and copies ran while one was open for 7% -> 6% of each run, Pallas kernels for 14% -> 13%
where the time goes in v12:
time: 34.7 us; the launch traced here: 34.5 us
  starting transfers between devices  16.1 us (46%)
  waiting for transfers between devices  7.5 us (22%)
  Pallas kernels  6.63 us (19%)
  local copies, waits for them, and re-layouts  3.1 us (9%)
  between operations  0.89 us (3%)
    ppermute x8, starting transfers between devices, swap(): lax.ppermute(array, axis, [(i, i ^ mask) for i in range(lax.axis_size(axi...  9.4 us
    pallas_call x5, Pallas kernels, call(): pl.pallas_call(kernel, out_shape=outs, scratch_shapes=scratch, compiler_p...  5.42 us
    ppermute x2, starting transfers between devices, meet(): second = lax.ppermute(jnp.where(even, low_edge, high_edge), axis, outer)  5.2 us
    ppermute x8, waiting for transfers between devices, swap(): lax.ppermute(array, axis, [(i, i ^ mask) for i in range(lax.axis_size(axi...  3.82 us
    ppermute x3, waiting for transfers between devices, meet(): first = lax.ppermute(jnp.where(even, high_edge, low_edge), axis, inner)  3.67 us
    unnamed x6, local copies, waits for them, and re-layouts  1.95 us
    ppermute x3, starting transfers between devices, meet(): first = lax.ppermute(jnp.where(even, high_edge, low_edge), axis, inner)  1.5 us
    pallas_call x1, Pallas kernels, loaded(): pl.pallas_call(load_kernel, out_shape=[jax.ShapeDtypeStruct(a.shape, a.dt...  1.21 us
  transfers between devices with their start and end apart: 13, of which 7 were waited for; matrix products, arithmetic and copies ran while one was open for 6% of the time, Pallas kernels for 13%

profile of v12, /device:TPU:0, one launch (start us, length us, event | category | flops | bytes accessed | tf_op | source)
XLA Modules:
  0.0 34.5 jit_solution(15752883644991878037)
XLA Ops:
  0.6 1.1 %copy.29 = bf16[1,32,8,4,128]{4,1,2,3,0:T(8,128)(2,1)S(1)} copy(bf16[1,32,8,4,128]{4,3,2,1,0:T(4,128)(2,1)} %param.4) | data formatting | bytes 524288 | tf_op args[0]
  1.7 4.0 %collective-permute-start = (bf16[8,32,128]{2,1,0:T(8,128)(2,1)S(1)}, bf16[8,32,128]{2,1,0:T(8,128)(2,1)S(1)}, u32[]{:S(2)}, u32[]{:S(2)}) collective-permute-start(bf16[8,32,128]{2,1,0:T(8,128)(2,1)S(1)} %get-tuple-element.83), channel_id=1, source_target_pairs={{0,12},{4,8},{8,4},{12,0},{1,13},{5,9},{9,5},{13,1},{2,14},{6,10},... | collective-permute-start | bytes 196616 | tf_op jit(solution)/shard_map/ppermute | solution.py:37
  5.7 0.5 %collective-permute-start.1 = (bf16[8,32,128]{2,1,0:T(8,128)(2,1)S(1)}, bf16[8,32,128]{2,1,0:T(8,128)(2,1)S(1)}, u32[]{:S(2)}, u32[]{:S(2)}) collective-permute-start(bf16[8,32,128]{2,1,0:T(8,128)(2,1)S(1)} %get-tuple-element.84), channel_id=1, source_target_pairs={{0,4},{4,0},{8,12},{12,8},{1,5},{5,1},{9,13},{13,9},{2,6},{6,2},{1... | collective-permute-start | bytes 196616 | tf_op jit(solution)/shard_map/ppermute | solution.py:33
  6.3 1.2 %shard_map.67 = (bf16[3,3,3,32,64]{4,3,2,1,0:T(8,128)(2,1)S(1)}, f32[1,64]{1,0:T(1,128)S(1)}, bf16[1,64,8,4,128]{4,3,2,1,0:T(4,128)(2,1)S(1)}) custom-call(bf16[3,3,3,32,64]{4,3,2,1,0:T(8,128)(2,1)} %bitcast.49, f32[1,64]{1,0:T(1,128)} %bitcast.50, bf16[1,64,8,4,128]{4,3,2,1,0:T(4,128)(2,1)} %refs_2_), custom_call_target="tpu_custom_call" | custom-call | tf_op jit(solution)/shard_map/pallas_call | solution.py:232
  8.2 1.1 %shard_map.68 = (bf16[12,64,128]{2,1,0:T(8,128)(2,1)S(1)}, f32[448,128]{1,0:T(8,128)S(1)}) custom-call(bf16[8,4,32,128]{3,2,1,0:T(8,128)(2,1)S(1)} %copy.22.x, bf16[192,288]{1,0:T(8,128)(2,1)S(1)} %copy.19.refs_0_.refs_2_.refs_4_, f32[1,64]{1,0:T(1,128)S(1)} %get-tuple-element.34.refs_1_.refs_3_.refs_5_, bf16[8,4,64,128]{3,2,1,0:T(8,128)(2,1)S(1)} %bitcast.37), custom_call_target="tpu_custom_call" | custom-call | flops 339738624 | bytes 1323264 | tf_op jit(solution)/shard_map/pallas_call | solution.py:244
  9.3 0.6 %collective-permute-done.1 = bf16[8,32,128]{2,1,0:T(8,128)(2,1)S(1)} collective-permute-done((bf16[8,32,128]{2,1,0:T(8,128)(2,1)S(1)}, bf16[8,32,128]{2,1,0:T(8,128)(2,1)S(1)}, u32[]{:S(2)}, u32[]{:S(2)}) %collective-permute-start.1) | collective-permute-done | bytes 65568 | tf_op jit(solution)/shard_map/ppermute | solution.py:33
  10.1 1.1 %shard_map.69 = (bf16[12,64,128]{2,1,0:T(8,128)(2,1)S(1)}, f32[448,128]{1,0:T(8,128)S(1)}) custom-call(bf16[8,4,32,128]{3,2,1,0:T(8,128)(2,1)S(1)} %copy.22.x, bf16[8,32,128]{2,1,0:T(8,128)(2,1)S(1)} %get-tuple-element.39.refs_0_, bf16[8,32,128]{2,1,0:T(8,128)(2,1)S(1)} %get-tuple-element.40.refs_1_, bf16[192,288]{1,0:T(8,128)(2,1)S(1)} %copy.19.refs_0_.refs_2_.refs_4_, ...), custom_call_target="tpu_custom_call" | custom-call | flops 339738624 | bytes 1683712 | tf_op jit(solution)/shard_map/pallas_call | solution.py:244
  11.3 1.1 %shard_map.70 = (bf16[8,64,128]{2,1,0:T(8,128)(2,1)S(1)}, f32[448,128]{1,0:T(8,128)S(1)}) custom-call(bf16[8,4,32,128]{3,2,1,0:T(8,128)(2,1)S(1)} %copy.22.x, bf16[8,32,128]{2,1,0:T(8,128)(2,1)S(1)} %get-tuple-element.39.refs_0_, bf16[8,32,128]{2,1,0:T(8,128)(2,1)S(1)} %get-tuple-element.40.refs_1_, bf16[6,32,128]{2,1,0:T(8,128)(2,1)S(1)} %get-tuple-element.94.refs_2_, ...), custom_call_target="tpu_custom_call" | custom-call | flops 226492416 | bytes 1716480 | tf_op jit(solution)/shard_map/pallas_call | solution.py:244
  12.6 0.5 %collective-permute-start.3 = (f32[480,128]{1,0:T(8,128)S(1)}, f32[480,128]{1,0:T(8,128)S(1)}, u32[]{:S(2)}, u32[]{:S(2)}) collective-permute-start(f32[480,128]{1,0:T(8,128)S(1)} %pad_maximum_fusion), channel_id=1, source_target_pairs={{0,16},{16,0},{1,17},{17,1},{2,18},{18,2},{3,19},{19,3},{4,20},{20... | collective-permute-start | bytes 737288 | tf_op jit(solution)/shard_map/ppermute | solution.py:55
  13.0 1.1 %collective-permute-done.3 = f32[480,128]{1,0:T(8,128)S(1)} collective-permute-done((f32[480,128]{1,0:T(8,128)S(1)}, f32[480,128]{1,0:T(8,128)S(1)}, u32[]{:S(2)}, u32[]{:S(2)}) %collective-permute-start.3) | collective-permute-done | bytes 245792 | tf_op jit(solution)/shard_map/ppermute | solution.py:55
  14.2 1.3 %collective-permute-start.6 = (bf16[224,128]{1,0:T(8,128)(2,1)S(1)}, bf16[224,128]{1,0:T(8,128)(2,1)S(1)}, u32[]{:S(2)}, u32[]{:S(2)}) collective-permute-start(bf16[224,128]{1,0:T(8,128)(2,1)S(1)} %get-tuple-element.61), channel_id=1, source_target_pairs={{0,12},{4,8},{8,4},{12,0},{1,13},{5,9},{9,5},{13,1},{2,14},{6,10},... | collective-permute-start | bytes 172040 | tf_op jit(solution)/shard_map/ppermute | solution.py:55
  15.5 1.3 %collective-permute-start.5 = (bf16[224,128]{1,0:T(8,128)(2,1)S(1)}, bf16[224,128]{1,0:T(8,128)(2,1)S(1)}, u32[]{:S(2)}, u32[]{:S(2)}) collective-permute-start(bf16[224,128]{1,0:T(8,128)(2,1)S(1)} %get-tuple-element.61), channel_id=1, source_target_pairs={{0,8},{4,12},{8,0},{12,4},{1,9},{5,13},{9,1},{13,5},{2,10},{6,14},... | collective-permute-start | bytes 172040 | tf_op jit(solution)/shard_map/ppermute | solution.py:55
  16.7 1.1 %collective-permute-start.4 = (bf16[224,128]{1,0:T(8,128)(2,1)S(1)}, bf16[224,128]{1,0:T(8,128)(2,1)S(1)}, u32[]{:S(2)}, u32[]{:S(2)}) collective-permute-start(bf16[224,128]{1,0:T(8,128)(2,1)S(1)} %get-tuple-element.61), channel_id=1, source_target_pairs={{0,4},{4,0},{8,12},{12,8},{1,5},{5,1},{9,13},{13,9},{2,6},{6,2},{1... | collective-permute-start | bytes 172040 | tf_op jit(solution)/shard_map/ppermute | solution.py:55
  18.4 1.2 %collective-permute-start.11 = (bf16[10,64,128]{2,1,0:T(8,128)(2,1)S(1)}, bf16[10,64,128]{2,1,0:T(8,128)(2,1)S(1)}, u32[]{:S(2)}, u32[]{:S(2)}) collective-permute-start(bf16[10,64,128]{2,1,0:T(8,128)(2,1)S(1)} %get-tuple-element.65), channel_id=1, source_target_pairs={{0,12},{4,8},{8,4},{12,0},{1,13},{5,9},{9,5},{13,1},{2,14},{6,10},... | collective-permute-start | bytes 491528 | tf_op jit(solution)/shard_map/ppermute | solution.py:37
  19.6 0.9 %collective-permute-start.7 = (bf16[10,64,128]{2,1,0:T(8,128)(2,1)S(1)}, bf16[10,64,128]{2,1,0:T(8,128)(2,1)S(1)}, u32[]{:S(2)}, u32[]{:S(2)}) collective-permute-start(bf16[10,64,128]{2,1,0:T(8,128)(2,1)S(1)} %get-tuple-element.66), channel_id=1, source_target_pairs={{0,4},{4,0},{8,12},{12,8},{1,5},{5,1},{9,13},{13,9},{2,6},{6,2},{1... | collective-permute-start | bytes 491528 | tf_op jit(solution)/shard_map/ppermute | solution.py:33
  20.5 0.8 %collective-permute-done.4 = bf16[224,128]{1,0:T(8,128)(2,1)S(1)} collective-permute-done((bf16[224,128]{1,0:T(8,128)(2,1)S(1)}, bf16[224,128]{1,0:T(8,128)(2,1)S(1)}, u32[]{:S(2)}, u32[]{:S(2)}) %collective-permute-start.4) | collective-permute-done | bytes 57376 | tf_op jit(solution)/shard_map/ppermute | solution.py:55
  21.4 3.7 %collective-permute-start.10 = (bf16[224,128]{1,0:T(8,128)(2,1)S(1)}, bf16[224,128]{1,0:T(8,128)(2,1)S(1)}, u32[]{:S(2)}, u32[]{:S(2)}) collective-permute-start(bf16[224,128]{1,0:T(8,128)(2,1)S(1)} %fusion.1), channel_id=1, source_target_pairs={{0,3},{1,2},{2,1},{3,0},{4,7},{5,6},{6,5},{7,4},{8,11},{9,10},{10,... | collective-permute-start | bytes 172040 | tf_op jit(solution)/shard_map/ppermute | solution.py:55
  25.1 2.9 %collective-permute-done.7 = bf16[10,64,128]{2,1,0:T(8,128)(2,1)S(1)} collective-permute-done((bf16[10,64,128]{2,1,0:T(8,128)(2,1)S(1)}, bf16[10,64,128]{2,1,0:T(8,128)(2,1)S(1)}, u32[]{:S(2)}, u32[]{:S(2)}) %collective-permute-start.7) | collective-permute-done | bytes 163872 | tf_op jit(solution)/shard_map/ppermute | solution.py:33
  28.0 1.6 %collective-permute-start.8 = (bf16[224,128]{1,0:T(8,128)(2,1)S(1)}, bf16[224,128]{1,0:T(8,128)(2,1)S(1)}, u32[]{:S(2)}, u32[]{:S(2)}) collective-permute-start(bf16[224,128]{1,0:T(8,128)(2,1)S(1)} %fusion.1), channel_id=1, source_target_pairs={{0,1},{1,0},{2,3},{3,2},{4,5},{5,4},{6,7},{7,6},{8,9},{9,8},{10,11... | collective-permute-start | bytes 172040 | tf_op jit(solution)/shard_map/ppermute | solution.py:55
  29.6 1.2 %shard_map.71 = bf16[8,4,32,128]{3,2,1,0:T(8,128)(2,1)S(1)} custom-call(bf16[12,64,128]{2,1,0:T(8,128)(2,1)S(1)} %get-tuple-element.49.inner, bf16[12,64,128]{2,1,0:T(8,128)(2,1)S(1)} %get-tuple-element.46.sides, bf16[8,64,128]{2,1,0:T(8,128)(2,1)S(1)} %get-tuple-element.44.ends, bf16[4,64,128]{2,1,0:T(8,128)(2,1)S(1)} %bitcast.45, ...), custom_call_target="tpu_custom_call" | custom-call | flops 452984832 | bytes 1355776 | tf_op jit(solution)/shard_map/pallas_call | solution.py:244
  30.8 1.4 %collective-permute-done.8 = bf16[224,128]{1,0:T(8,128)(2,1)S(1)} collective-permute-done((bf16[224,128]{1,0:T(8,128)(2,1)S(1)}, bf16[224,128]{1,0:T(8,128)(2,1)S(1)}, u32[]{:S(2)}, u32[]{:S(2)}) %collective-permute-start.8) | collective-permute-done | bytes 57376 | tf_op jit(solution)/shard_map/ppermute | solution.py:55
  32.3 0.8 %copy.25 = bf16[1,32,8,4,128]{4,3,2,1,0:T(4,128)(2,1)} copy(bf16[1,32,8,4,128]{4,1,3,2,0:T(8,128)(2,1)S(1)} %bitcast.41) | data formatting | bytes 524288
  33.2 0.5 %collective-permute-done.12 = f32[224,128]{1,0:T(8,128)S(1)} collective-permute-done((f32[224,128]{1,0:T(8,128)S(1)}, f32[224,128]{1,0:T(8,128)S(1)}, u32[]{:S(2)}, u32[]{:S(2)}) %collective-permute-start.12) | collective-permute-done | bytes 114720 | tf_op jit(solution)/shard_map/ppermute | solution.py:55
  33.7 0.9 %shard_map.72 = (f32[864,64]{1,0:T(8,128)}, f32[1,64]{1,0:T(1,128)}) custom-call(f32[224,128]{1,0:T(8,128)S(1)} %get-tuple-element.74.refs_0_, f32[224,128]{1,0:T(8,128)S(1)} %get-tuple-element.73.refs_1_), custom_call_target="tpu_custom_call" | custom-call | flops 57344 | bytes 450816 | tf_op jit(solution)/shard_map/pallas_call | solution.py:244
  (41 shorter events, 1.8 us)
Async XLA Ops:
  1.7 7.6 %collective-permute-start = (bf16[8,32,128]{2,1,0:T(8,128)(2,1)S(1)}, bf16[8,32,128]{2,1,0:T(8,128)(2,1)S(1)}, u32[]{:S(2)}, u32[]{:S(2)}) collective-permute-start(bf16[8,32,128]{2,1,0:T(8,128)(2,1)S(1)} %get-tuple-element.83), channel_id=1, source_target_pairs={{0,12},{4,8},{8,4},{12,0},{1,13},{5,9},{9,5},{13,1},{2,14},{6,10},... | collective-permute-start | bytes 196616 | tf_op jit(solution)/shard_map/ppermute | solution.py:37
  5.7 4.3 %collective-permute-start.1 = (bf16[8,32,128]{2,1,0:T(8,128)(2,1)S(1)}, bf16[8,32,128]{2,1,0:T(8,128)(2,1)S(1)}, u32[]{:S(2)}, u32[]{:S(2)}) collective-permute-start(bf16[8,32,128]{2,1,0:T(8,128)(2,1)S(1)} %get-tuple-element.84), channel_id=1, source_target_pairs={{0,4},{4,0},{8,12},{12,8},{1,5},{5,1},{9,13},{13,9},{2,6},{6,2},{1... | collective-permute-start | bytes 196616 | tf_op jit(solution)/shard_map/ppermute | solution.py:33
  10.0 1.3 %collective-permute-start.2 = (bf16[6,32,128]{2,1,0:T(8,128)(2,1)S(1)}, bf16[6,32,128]{2,1,0:T(8,128)(2,1)S(1)}, u32[]{:S(2)}, u32[]{:S(2)}) collective-permute-start(bf16[6,32,128]{2,1,0:T(8,128)(2,1)S(1)} %maximum_select_fusion), channel_id=1, source_target_pairs={{0,16},{16,0},{1,17},{17,1},{2,18},{18,2},{3,19},{19,3},{4,20},{20... | collective-permute-start | bytes 147464 | tf_op jit(solution)/shard_map/ppermute | solution.py:33
  12.6 1.6 %collective-permute-start.3 = (f32[480,128]{1,0:T(8,128)S(1)}, f32[480,128]{1,0:T(8,128)S(1)}, u32[]{:S(2)}, u32[]{:S(2)}) collective-permute-start(f32[480,128]{1,0:T(8,128)S(1)} %pad_maximum_fusion), channel_id=1, source_target_pairs={{0,16},{16,0},{1,17},{17,1},{2,18},{18,2},{3,19},{19,3},{4,20},{20... | collective-permute-start | bytes 737288 | tf_op jit(solution)/shard_map/ppermute | solution.py:55
  14.2 7.2 %collective-permute-start.6 = (bf16[224,128]{1,0:T(8,128)(2,1)S(1)}, bf16[224,128]{1,0:T(8,128)(2,1)S(1)}, u32[]{:S(2)}, u32[]{:S(2)}) collective-permute-start(bf16[224,128]{1,0:T(8,128)(2,1)S(1)} %get-tuple-element.61), channel_id=1, source_target_pairs={{0,12},{4,8},{8,4},{12,0},{1,13},{5,9},{9,5},{13,1},{2,14},{6,10},... | collective-permute-start | bytes 172040 | tf_op jit(solution)/shard_map/ppermute | solution.py:55
  15.5 5.9 %collective-permute-start.5 = (bf16[224,128]{1,0:T(8,128)(2,1)S(1)}, bf16[224,128]{1,0:T(8,128)(2,1)S(1)}, u32[]{:S(2)}, u32[]{:S(2)}) collective-permute-start(bf16[224,128]{1,0:T(8,128)(2,1)S(1)} %get-tuple-element.61), channel_id=1, source_target_pairs={{0,8},{4,12},{8,0},{12,4},{1,9},{5,13},{9,1},{13,5},{2,10},{6,14},... | collective-permute-start | bytes 172040 | tf_op jit(solution)/shard_map/ppermute | solution.py:55
  16.7 4.6 %collective-permute-start.4 = (bf16[224,128]{1,0:T(8,128)(2,1)S(1)}, bf16[224,128]{1,0:T(8,128)(2,1)S(1)}, u32[]{:S(2)}, u32[]{:S(2)}) collective-permute-start(bf16[224,128]{1,0:T(8,128)(2,1)S(1)} %get-tuple-element.61), channel_id=1, source_target_pairs={{0,4},{4,0},{8,12},{12,8},{1,5},{5,1},{9,13},{13,9},{2,6},{6,2},{1... | collective-permute-start | bytes 172040 | tf_op jit(solution)/shard_map/ppermute | solution.py:55
  18.4 11.2 %collective-permute-start.11 = (bf16[10,64,128]{2,1,0:T(8,128)(2,1)S(1)}, bf16[10,64,128]{2,1,0:T(8,128)(2,1)S(1)}, u32[]{:S(2)}, u32[]{:S(2)}) collective-permute-start(bf16[10,64,128]{2,1,0:T(8,128)(2,1)S(1)} %get-tuple-element.65), channel_id=1, source_target_pairs={{0,12},{4,8},{8,4},{12,0},{1,13},{5,9},{9,5},{13,1},{2,14},{6,10},... | collective-permute-start | bytes 491528 | tf_op jit(solution)/shard_map/ppermute | solution.py:37
  19.6 8.4 %collective-permute-start.7 = (bf16[10,64,128]{2,1,0:T(8,128)(2,1)S(1)}, bf16[10,64,128]{2,1,0:T(8,128)(2,1)S(1)}, u32[]{:S(2)}, u32[]{:S(2)}) collective-permute-start(bf16[10,64,128]{2,1,0:T(8,128)(2,1)S(1)} %get-tuple-element.66), channel_id=1, source_target_pairs={{0,4},{4,0},{8,12},{12,8},{1,5},{5,1},{9,13},{13,9},{2,6},{6,2},{1... | collective-permute-start | bytes 491528 | tf_op jit(solution)/shard_map/ppermute | solution.py:33
  21.4 9.4 %collective-permute-start.10 = (bf16[224,128]{1,0:T(8,128)(2,1)S(1)}, bf16[224,128]{1,0:T(8,128)(2,1)S(1)}, u32[]{:S(2)}, u32[]{:S(2)}) collective-permute-start(bf16[224,128]{1,0:T(8,128)(2,1)S(1)} %fusion.1), channel_id=1, source_target_pairs={{0,3},{1,2},{2,1},{3,0},{4,7},{5,6},{6,5},{7,4},{8,11},{9,10},{10,... | collective-permute-start | bytes 172040 | tf_op jit(solution)/shard_map/ppermute | solution.py:55
  25.1 5.8 %collective-permute-start.9 = (bf16[224,128]{1,0:T(8,128)(2,1)S(1)}, bf16[224,128]{1,0:T(8,128)(2,1)S(1)}, u32[]{:S(2)}, u32[]{:S(2)}) collective-permute-start(bf16[224,128]{1,0:T(8,128)(2,1)S(1)} %fusion.1), channel_id=1, source_target_pairs={{0,2},{1,3},{2,0},{3,1},{4,6},{5,7},{6,4},{7,5},{8,10},{9,11},{10,... | collective-permute-start | bytes 172040 | tf_op jit(solution)/shard_map/ppermute | solution.py:55
  28.0 4.2 %collective-permute-start.8 = (bf16[224,128]{1,0:T(8,128)(2,1)S(1)}, bf16[224,128]{1,0:T(8,128)(2,1)S(1)}, u32[]{:S(2)}, u32[]{:S(2)}) collective-permute-start(bf16[224,128]{1,0:T(8,128)(2,1)S(1)} %fusion.1), channel_id=1, source_target_pairs={{0,1},{1,0},{2,3},{3,2},{4,5},{5,4},{6,7},{7,6},{8,9},{9,8},{10,11... | collective-permute-start | bytes 172040 | tf_op jit(solution)/shard_map/ppermute | solution.py:55
  32.2 1.4 %collective-permute-start.12 = (f32[224,128]{1,0:T(8,128)S(1)}, f32[224,128]{1,0:T(8,128)S(1)}, u32[]{:S(2)}, u32[]{:S(2)}) collective-permute-start(f32[224,128]{1,0:T(8,128)S(1)} %add_add_fusion), channel_id=1, source_target_pairs={{0,16},{16,0},{1,17},{17,1},{2,18},{18,2},{3,19},{19,3},{4,20},{20... | collective-permute-start | bytes 344072 | tf_op jit(solution)/shard_map/ppermute | solution.py:55

commit v13 on v10

--- a/solution.py
+++ b/solution.py
@@ -332,9 +332,12 @@
         below, above, taps = lax.optimization_barrier((below, above, taps))
         first_row = jnp.concatenate([ends[:1], sides[: depth - 2], ends[height : height + 1]], axis=0)
         last_row = jnp.concatenate([ends[height - 1 : height], sides[depth - 2 :], ends[-1:]], axis=0)
+        w2 = jnp.flip(taps, (0, 1)).transpose(2, 3, 0, 1, 4).reshape(3 * ci, 9 * co)
+        first_row, last_row, below, above, w2 = lax.optimization_barrier(
+            (first_row, last_row, below, above, w2)
+        )
         around = exchange(*columns(first_row, last_row, below, above), "height")
         fields.append((inner, sides, ends, below, above, *around))
-    w2 = jnp.flip(taps, (0, 1)).transpose(2, 3, 0, 1, 4).reshape(3 * ci, 9 * co)
 
     def input_gradients(fields):
         grads = []

time: 33 us -> 33.2 us (level)
    ppermute x8, waiting for transfers between devices: 3.28 us -> 3.63 us  [swap(): lax.ppermute(array, axis, [(i, i ^ mask) for i in range(lax.axis_size(axi...]
    unnamed x6 -> x2, local copies, waits for them, and re-layouts: 1.95 us -> 1.89 us
  transfers between devices with their start and end apart: 14 -> 14, of which waited for: 10 -> 9; matrix products, arithmetic and copies ran while one was open for 7% -> 7% of each run, Pallas kernels for 14% -> 14%
where the time goes in v13:
time: 33.2 us; the launch traced here: 33 us
  starting transfers between devices  15.4 us (46%)
  waiting for transfers between devices  6.65 us (20%)
  Pallas kernels  6.62 us (20%)
  local copies, waits for them, and re-layouts  3.06 us (9%)
  between operations  0.89 us (3%)
  other arithmetic  0.34 us (1%)
    ppermute x8, starting transfers between devices, swap(): lax.ppermute(array, axis, [(i, i ^ mask) for i in range(lax.axis_size(axi...  8.23 us
    pallas_call x5, Pallas kernels, call(): pl.pallas_call(kernel, out_shape=outs, scratch_shapes=scratch, compiler_p...  5.41 us
    ppermute x2, starting transfers between devices, meet(): second = lax.ppermute(jnp.where(even, low_edge, high_edge), axis, outer)  5.2 us
    ppermute x8, waiting for transfers between devices, swap(): lax.ppermute(array, axis, [(i, i ^ mask) for i in range(lax.axis_size(axi...  3.63 us
    ppermute x4, waiting for transfers between devices, meet(): first = lax.ppermute(jnp.where(even, high_edge, low_edge), axis, inner)  3.01 us
    ppermute x4, starting transfers between devices, meet(): first = lax.ppermute(jnp.where(even, high_edge, low_edge), axis, inner)  1.98 us
    unnamed x2, local copies, waits for them, and re-layouts  1.89 us
    pallas_call x1, Pallas kernels, loaded(): pl.pallas_call(load_kernel, out_shape=[jax.ShapeDtypeStruct(a.shape, a.dt...  1.21 us
  transfers between devices with their start and end apart: 14, of which 9 were waited for; matrix products, arithmetic and copies ran while one was open for 7% of the time, Pallas kernels for 14%

profile of v13, /device:TPU:0, one launch (start us, length us, event | category | flops | bytes accessed | tf_op | source)
XLA Modules:
  0.0 33.0 jit_solution(255242708641387549)
XLA Ops:
  0.6 1.1 %copy.29 = bf16[1,32,8,4,128]{4,1,2,3,0:T(8,128)(2,1)S(1)} copy(bf16[1,32,8,4,128]{4,3,2,1,0:T(4,128)(2,1)} %param.4) | data formatting | bytes 524288 | tf_op args[0]
  1.7 4.0 %collective-permute-start = (bf16[8,32,128]{2,1,0:T(8,128)(2,1)S(1)}, bf16[8,32,128]{2,1,0:T(8,128)(2,1)S(1)}, u32[]{:S(2)}, u32[]{:S(2)}) collective-permute-start(bf16[8,32,128]{2,1,0:T(8,128)(2,1)S(1)} %get-tuple-element.89), channel_id=1, source_target_pairs={{0,12},{4,8},{8,4},{12,0},{1,13},{5,9},{9,5},{13,1},{2,14},{6,10},... | collective-permute-start | bytes 196616 | tf_op jit(solution)/shard_map/ppermute | solution.py:36
  5.7 0.5 %collective-permute-start.1 = (bf16[8,32,128]{2,1,0:T(8,128)(2,1)S(1)}, bf16[8,32,128]{2,1,0:T(8,128)(2,1)S(1)}, u32[]{:S(2)}, u32[]{:S(2)}) collective-permute-start(bf16[8,32,128]{2,1,0:T(8,128)(2,1)S(1)} %get-tuple-element.90), channel_id=1, source_target_pairs={{0,4},{4,0},{8,12},{12,8},{1,5},{5,1},{9,13},{13,9},{2,6},{6,2},{1... | collective-permute-start | bytes 196616 | tf_op jit(solution)/shard_map/ppermute | solution.py:32
  6.3 1.2 %shard_map.67 = (bf16[3,3,3,32,64]{4,3,2,1,0:T(8,128)(2,1)S(1)}, f32[1,64]{1,0:T(1,128)S(1)}, bf16[1,64,8,4,128]{4,3,2,1,0:T(4,128)(2,1)S(1)}) custom-call(bf16[3,3,3,32,64]{4,3,2,1,0:T(8,128)(2,1)} %bitcast.40, f32[1,64]{1,0:T(1,128)} %bitcast.41, bf16[1,64,8,4,128]{4,3,2,1,0:T(4,128)(2,1)} %refs_2_), custom_call_target="tpu_custom_call" | custom-call | tf_op jit(solution)/shard_map/pallas_call | solution.py:231
  8.2 1.1 %shard_map.68 = (bf16[12,64,128]{2,1,0:T(8,128)(2,1)S(1)}, f32[448,128]{1,0:T(8,128)S(1)}) custom-call(bf16[8,4,32,128]{3,2,1,0:T(8,128)(2,1)S(1)} %copy.22.x, bf16[192,288]{1,0:T(8,128)(2,1)S(1)} %copy.19.refs_0_.refs_2_.refs_4_, f32[1,64]{1,0:T(1,128)S(1)} %get-tuple-element.38.refs_1_.refs_3_.refs_5_, bf16[8,4,64,128]{3,2,1,0:T(8,128)(2,1)S(1)} %bitcast.32), custom_call_target="tpu_custom_call" | custom-call | flops 339738624 | bytes 1323264 | tf_op jit(solution)/shard_map/pallas_call | solution.py:243
  9.3 0.6 %collective-permute-done.1 = bf16[8,32,128]{2,1,0:T(8,128)(2,1)S(1)} collective-permute-done((bf16[8,32,128]{2,1,0:T(8,128)(2,1)S(1)}, bf16[8,32,128]{2,1,0:T(8,128)(2,1)S(1)}, u32[]{:S(2)}, u32[]{:S(2)}) %collective-permute-start.1) | collective-permute-done | bytes 65568 | tf_op jit(solution)/shard_map/ppermute | solution.py:32
  10.1 1.1 %shard_map.69 = (bf16[12,64,128]{2,1,0:T(8,128)(2,1)S(1)}, f32[448,128]{1,0:T(8,128)S(1)}) custom-call(bf16[8,4,32,128]{3,2,1,0:T(8,128)(2,1)S(1)} %copy.22.x, bf16[8,32,128]{2,1,0:T(8,128)(2,1)S(1)} %get-tuple-element.43.refs_0_, bf16[8,32,128]{2,1,0:T(8,128)(2,1)S(1)} %get-tuple-element.44.refs_1_, bf16[192,288]{1,0:T(8,128)(2,1)S(1)} %copy.19.refs_0_.refs_2_.refs_4_, ...), custom_call_target="tpu_custom_call" | custom-call | flops 339738624 | bytes 1683712 | tf_op jit(solution)/shard_map/pallas_call | solution.py:243
  11.3 1.1 %shard_map.70 = (bf16[8,64,128]{2,1,0:T(8,128)(2,1)S(1)}, f32[448,128]{1,0:T(8,128)S(1)}) custom-call(bf16[8,4,32,128]{3,2,1,0:T(8,128)(2,1)S(1)} %copy.22.x, bf16[8,32,128]{2,1,0:T(8,128)(2,1)S(1)} %get-tuple-element.43.refs_0_, bf16[8,32,128]{2,1,0:T(8,128)(2,1)S(1)} %get-tuple-element.44.refs_1_, bf16[6,32,128]{2,1,0:T(8,128)(2,1)S(1)} %get-tuple-element.102.refs_2_, ...), custom_call_target="tpu_custom_call" | custom-call | flops 226492416 | bytes 1716480 | tf_op jit(solution)/shard_map/pallas_call | solution.py:243
  12.5 0.5 %collective-permute-start.10 = (bf16[4,64,128]{2,1,0:T(8,128)(2,1)S(1)}, bf16[4,64,128]{2,1,0:T(8,128)(2,1)S(1)}, u32[]{:S(2)}, u32[]{:S(2)}) collective-permute-start(bf16[4,64,128]{2,1,0:T(8,128)(2,1)S(1)} %slice_select_fusion.1), channel_id=1, source_target_pairs={{0,16},{16,0},{1,17},{17,1},{2,18},{18,2},{3,19},{19,3},{4,20},{20... | collective-permute-start | bytes 196616 | tf_op jit(solution)/shard_map/ppermute | solution.py:32
  13.2 0.7 %collective-permute-done.10 = bf16[4,64,128]{2,1,0:T(8,128)(2,1)S(1)} collective-permute-done((bf16[4,64,128]{2,1,0:T(8,128)(2,1)S(1)}, bf16[4,64,128]{2,1,0:T(8,128)(2,1)S(1)}, u32[]{:S(2)}, u32[]{:S(2)}) %collective-permute-start.10) | collective-permute-done | bytes 65568 | tf_op jit(solution)/shard_map/ppermute | solution.py:32
  14.4 1.2 %collective-permute-start.6 = (bf16[224,128]{1,0:T(8,128)(2,1)S(1)}, bf16[224,128]{1,0:T(8,128)(2,1)S(1)}, u32[]{:S(2)}, u32[]{:S(2)}) collective-permute-start(bf16[224,128]{1,0:T(8,128)(2,1)S(1)} %get-tuple-element.69), channel_id=1, source_target_pairs={{0,12},{4,8},{8,4},{12,0},{1,13},{5,9},{9,5},{13,1},{2,14},{6,10},... | collective-permute-start | bytes 172040 | tf_op jit(solution)/shard_map/ppermute | solution.py:54
  15.7 1.3 %collective-permute-start.5 = (bf16[224,128]{1,0:T(8,128)(2,1)S(1)}, bf16[224,128]{1,0:T(8,128)(2,1)S(1)}, u32[]{:S(2)}, u32[]{:S(2)}) collective-permute-start(bf16[224,128]{1,0:T(8,128)(2,1)S(1)} %get-tuple-element.69), channel_id=1, source_target_pairs={{0,8},{4,12},{8,0},{12,4},{1,9},{5,13},{9,1},{13,5},{2,10},{6,14},... | collective-permute-start | bytes 172040 | tf_op jit(solution)/shard_map/ppermute | solution.py:54
  16.9 1.1 %collective-permute-start.4 = (bf16[224,128]{1,0:T(8,128)(2,1)S(1)}, bf16[224,128]{1,0:T(8,128)(2,1)S(1)}, u32[]{:S(2)}, u32[]{:S(2)}) collective-permute-start(bf16[224,128]{1,0:T(8,128)(2,1)S(1)} %get-tuple-element.69), channel_id=1, source_target_pairs={{0,4},{4,0},{8,12},{12,8},{1,5},{5,1},{9,13},{13,9},{2,6},{6,2},{1... | collective-permute-start | bytes 172040 | tf_op jit(solution)/shard_map/ppermute | solution.py:54
  18.0 1.2 %collective-permute-start.11 = (bf16[10,64,128]{2,1,0:T(8,128)(2,1)S(1)}, bf16[10,64,128]{2,1,0:T(8,128)(2,1)S(1)}, u32[]{:S(2)}, u32[]{:S(2)}) collective-permute-start(bf16[10,64,128]{2,1,0:T(8,128)(2,1)S(1)} %get-tuple-element.73), channel_id=1, source_target_pairs={{0,12},{4,8},{8,4},{12,0},{1,13},{5,9},{9,5},{13,1},{2,14},{6,10},... | collective-permute-start | bytes 491528 | tf_op jit(solution)/shard_map/ppermute | solution.py:36
  19.3 0.9 %collective-permute-start.12 = (bf16[10,64,128]{2,1,0:T(8,128)(2,1)S(1)}, bf16[10,64,128]{2,1,0:T(8,128)(2,1)S(1)}, u32[]{:S(2)}, u32[]{:S(2)}) collective-permute-start(bf16[10,64,128]{2,1,0:T(8,128)(2,1)S(1)} %get-tuple-element.74), channel_id=1, source_target_pairs={{0,4},{4,0},{8,12},{12,8},{1,5},{5,1},{9,13},{13,9},{2,6},{6,2},{1... | collective-permute-start | bytes 491528 | tf_op jit(solution)/shard_map/ppermute | solution.py:32
  20.2 0.6 %collective-permute-done.5 = bf16[224,128]{1,0:T(8,128)(2,1)S(1)} collective-permute-done((bf16[224,128]{1,0:T(8,128)(2,1)S(1)}, bf16[224,128]{1,0:T(8,128)(2,1)S(1)}, u32[]{:S(2)}, u32[]{:S(2)}) %collective-permute-start.5) | collective-permute-done | bytes 57376 | tf_op jit(solution)/shard_map/ppermute | solution.py:54
  20.8 1.0 %collective-permute-done.4 = bf16[224,128]{1,0:T(8,128)(2,1)S(1)} collective-permute-done((bf16[224,128]{1,0:T(8,128)(2,1)S(1)}, bf16[224,128]{1,0:T(8,128)(2,1)S(1)}, u32[]{:S(2)}, u32[]{:S(2)}) %collective-permute-start.4) | collective-permute-done | bytes 57376 | tf_op jit(solution)/shard_map/ppermute | solution.py:54
  21.8 3.7 %collective-permute-start.9 = (bf16[224,128]{1,0:T(8,128)(2,1)S(1)}, bf16[224,128]{1,0:T(8,128)(2,1)S(1)}, u32[]{:S(2)}, u32[]{:S(2)}) collective-permute-start(bf16[224,128]{1,0:T(8,128)(2,1)S(1)} %fusion), channel_id=1, source_target_pairs={{0,3},{1,2},{2,1},{3,0},{4,7},{5,6},{6,5},{7,4},{8,11},{9,10},{10,... | collective-permute-start | bytes 172040 | tf_op jit(solution)/shard_map/ppermute | solution.py:54
  25.4 0.8 %collective-permute-start.7 = (bf16[224,128]{1,0:T(8,128)(2,1)S(1)}, bf16[224,128]{1,0:T(8,128)(2,1)S(1)}, u32[]{:S(2)}, u32[]{:S(2)}) collective-permute-start(bf16[224,128]{1,0:T(8,128)(2,1)S(1)} %fusion), channel_id=1, source_target_pairs={{0,1},{1,0},{2,3},{3,2},{4,5},{5,4},{6,7},{7,6},{8,9},{9,8},{10,11... | collective-permute-start | bytes 172040 | tf_op jit(solution)/shard_map/ppermute | solution.py:54
  26.2 1.6 %collective-permute-done.12 = bf16[10,64,128]{2,1,0:T(8,128)(2,1)S(1)} collective-permute-done((bf16[10,64,128]{2,1,0:T(8,128)(2,1)S(1)}, bf16[10,64,128]{2,1,0:T(8,128)(2,1)S(1)}, u32[]{:S(2)}, u32[]{:S(2)}) %collective-permute-start.12) | collective-permute-done | bytes 163872 | tf_op jit(solution)/shard_map/ppermute | solution.py:32
  27.9 1.2 %shard_map.71 = bf16[8,4,32,128]{3,2,1,0:T(8,128)(2,1)S(1)} custom-call(bf16[12,64,128]{2,1,0:T(8,128)(2,1)S(1)} %get-tuple-element.48.inner, bf16[12,64,128]{2,1,0:T(8,128)(2,1)S(1)} %get-tuple-element.49.sides, bf16[8,64,128]{2,1,0:T(8,128)(2,1)S(1)} %get-tuple-element.50.ends, bf16[4,64,128]{2,1,0:T(8,128)(2,1)S(1)} %get-tuple-element.54.below, ...), custom_call_target="tpu_custom_call" | custom-call | flops 452984832 | bytes 1355776 | tf_op jit(solution)/shard_map/pallas_call | solution.py:243
  29.1 1.5 %collective-permute-done.8 = bf16[224,128]{1,0:T(8,128)(2,1)S(1)} collective-permute-done((bf16[224,128]{1,0:T(8,128)(2,1)S(1)}, bf16[224,128]{1,0:T(8,128)(2,1)S(1)}, u32[]{:S(2)}, u32[]{:S(2)}) %collective-permute-start.8) | collective-permute-done | bytes 57376 | tf_op jit(solution)/shard_map/ppermute | solution.py:54
  30.8 0.8 %copy.25 = bf16[1,32,8,4,128]{4,3,2,1,0:T(4,128)(2,1)} copy(bf16[1,32,8,4,128]{4,1,3,2,0:T(8,128)(2,1)S(1)} %bitcast.36) | data formatting | bytes 524288
  32.1 0.9 %shard_map.72 = (f32[864,64]{1,0:T(8,128)}, f32[1,64]{1,0:T(1,128)}) custom-call(f32[224,128]{1,0:T(8,128)S(1)} %get-tuple-element.80.refs_0_, f32[224,128]{1,0:T(8,128)S(1)} %get-tuple-element.79.refs_1_), custom_call_target="tpu_custom_call" | custom-call | flops 57344 | bytes 450816 | tf_op jit(solution)/shard_map/pallas_call | solution.py:243
  (42 shorter events, 2.4 us)
Async XLA Ops:
  1.7 7.6 %collective-permute-start = (bf16[8,32,128]{2,1,0:T(8,128)(2,1)S(1)}, bf16[8,32,128]{2,1,0:T(8,128)(2,1)S(1)}, u32[]{:S(2)}, u32[]{:S(2)}) collective-permute-start(bf16[8,32,128]{2,1,0:T(8,128)(2,1)S(1)} %get-tuple-element.89), channel_id=1, source_target_pairs={{0,12},{4,8},{8,4},{12,0},{1,13},{5,9},{9,5},{13,1},{2,14},{6,10},... | collective-permute-start | bytes 196616 | tf_op jit(solution)/shard_map/ppermute | solution.py:36
  5.7 4.3 %collective-permute-start.1 = (bf16[8,32,128]{2,1,0:T(8,128)(2,1)S(1)}, bf16[8,32,128]{2,1,0:T(8,128)(2,1)S(1)}, u32[]{:S(2)}, u32[]{:S(2)}) collective-permute-start(bf16[8,32,128]{2,1,0:T(8,128)(2,1)S(1)} %get-tuple-element.90), channel_id=1, source_target_pairs={{0,4},{4,0},{8,12},{12,8},{1,5},{5,1},{9,13},{13,9},{2,6},{6,2},{1... | collective-permute-start | bytes 196616 | tf_op jit(solution)/shard_map/ppermute | solution.py:32
  10.0 1.3 %collective-permute-start.2 = (bf16[6,32,128]{2,1,0:T(8,128)(2,1)S(1)}, bf16[6,32,128]{2,1,0:T(8,128)(2,1)S(1)}, u32[]{:S(2)}, u32[]{:S(2)}) collective-permute-start(bf16[6,32,128]{2,1,0:T(8,128)(2,1)S(1)} %maximum_select_fusion), channel_id=1, source_target_pairs={{0,16},{16,0},{1,17},{17,1},{2,18},{18,2},{3,19},{19,3},{4,20},{20... | collective-permute-start | bytes 147464 | tf_op jit(solution)/shard_map/ppermute | solution.py:32
  12.5 1.4 %collective-permute-start.10 = (bf16[4,64,128]{2,1,0:T(8,128)(2,1)S(1)}, bf16[4,64,128]{2,1,0:T(8,128)(2,1)S(1)}, u32[]{:S(2)}, u32[]{:S(2)}) collective-permute-start(bf16[4,64,128]{2,1,0:T(8,128)(2,1)S(1)} %slice_select_fusion.1), channel_id=1, source_target_pairs={{0,16},{16,0},{1,17},{17,1},{2,18},{18,2},{3,19},{19,3},{4,20},{20... | collective-permute-start | bytes 196616 | tf_op jit(solution)/shard_map/ppermute | solution.py:32
  13.0 1.4 %collective-permute-start.3 = (f32[224,128]{1,0:T(8,128)S(1)}, f32[224,128]{1,0:T(8,128)S(1)}, u32[]{:S(2)}, u32[]{:S(2)}) collective-permute-start(f32[224,128]{1,0:T(8,128)S(1)} %slice_select_fusion), channel_id=1, source_target_pairs={{0,16},{16,0},{1,17},{17,1},{2,18},{18,2},{3,19},{19,3},{4,20},{20... | collective-permute-start | bytes 344072 | tf_op jit(solution)/shard_map/ppermute | solution.py:54
  14.4 5.7 %collective-permute-start.6 = (bf16[224,128]{1,0:T(8,128)(2,1)S(1)}, bf16[224,128]{1,0:T(8,128)(2,1)S(1)}, u32[]{:S(2)}, u32[]{:S(2)}) collective-permute-start(bf16[224,128]{1,0:T(8,128)(2,1)S(1)} %get-tuple-element.69), channel_id=1, source_target_pairs={{0,12},{4,8},{8,4},{12,0},{1,13},{5,9},{9,5},{13,1},{2,14},{6,10},... | collective-permute-start | bytes 172040 | tf_op jit(solution)/shard_map/ppermute | solution.py:54
  15.7 5.1 %collective-permute-start.5 = (bf16[224,128]{1,0:T(8,128)(2,1)S(1)}, bf16[224,128]{1,0:T(8,128)(2,1)S(1)}, u32[]{:S(2)}, u32[]{:S(2)}) collective-permute-start(bf16[224,128]{1,0:T(8,128)(2,1)S(1)} %get-tuple-element.69), channel_id=1, source_target_pairs={{0,8},{4,12},{8,0},{12,4},{1,9},{5,13},{9,1},{13,5},{2,10},{6,14},... | collective-permute-start | bytes 172040 | tf_op jit(solution)/shard_map/ppermute | solution.py:54
  16.9 4.8 %collective-permute-start.4 = (bf16[224,128]{1,0:T(8,128)(2,1)S(1)}, bf16[224,128]{1,0:T(8,128)(2,1)S(1)}, u32[]{:S(2)}, u32[]{:S(2)}) collective-permute-start(bf16[224,128]{1,0:T(8,128)(2,1)S(1)} %get-tuple-element.69), channel_id=1, source_target_pairs={{0,4},{4,0},{8,12},{12,8},{1,5},{5,1},{9,13},{13,9},{2,6},{6,2},{1... | collective-permute-start | bytes 172040 | tf_op jit(solution)/shard_map/ppermute | solution.py:54
  18.0 8.2 %collective-permute-start.11 = (bf16[10,64,128]{2,1,0:T(8,128)(2,1)S(1)}, bf16[10,64,128]{2,1,0:T(8,128)(2,1)S(1)}, u32[]{:S(2)}, u32[]{:S(2)}) collective-permute-start(bf16[10,64,128]{2,1,0:T(8,128)(2,1)S(1)} %get-tuple-element.73), channel_id=1, source_target_pairs={{0,12},{4,8},{8,4},{12,0},{1,13},{5,9},{9,5},{13,1},{2,14},{6,10},... | collective-permute-start | bytes 491528 | tf_op jit(solution)/shard_map/ppermute | solution.py:36
  19.3 8.6 %collective-permute-start.12 = (bf16[10,64,128]{2,1,0:T(8,128)(2,1)S(1)}, bf16[10,64,128]{2,1,0:T(8,128)(2,1)S(1)}, u32[]{:S(2)}, u32[]{:S(2)}) collective-permute-start(bf16[10,64,128]{2,1,0:T(8,128)(2,1)S(1)} %get-tuple-element.74), channel_id=1, source_target_pairs={{0,4},{4,0},{8,12},{12,8},{1,5},{5,1},{9,13},{13,9},{2,6},{6,2},{1... | collective-permute-start | bytes 491528 | tf_op jit(solution)/shard_map/ppermute | solution.py:32
  21.8 7.3 %collective-permute-start.9 = (bf16[224,128]{1,0:T(8,128)(2,1)S(1)}, bf16[224,128]{1,0:T(8,128)(2,1)S(1)}, u32[]{:S(2)}, u32[]{:S(2)}) collective-permute-start(bf16[224,128]{1,0:T(8,128)(2,1)S(1)} %fusion), channel_id=1, source_target_pairs={{0,3},{1,2},{2,1},{3,0},{4,7},{5,6},{6,5},{7,4},{8,11},{9,10},{10,... | collective-permute-start | bytes 172040 | tf_op jit(solution)/shard_map/ppermute | solution.py:54
  25.4 5.2 %collective-permute-start.8 = (bf16[224,128]{1,0:T(8,128)(2,1)S(1)}, bf16[224,128]{1,0:T(8,128)(2,1)S(1)}, u32[]{:S(2)}, u32[]{:S(2)}) collective-permute-start(bf16[224,128]{1,0:T(8,128)(2,1)S(1)} %fusion), channel_id=1, source_target_pairs={{0,2},{1,3},{2,0},{3,1},{4,6},{5,7},{6,4},{7,5},{8,10},{9,11},{10,... | collective-permute-start | bytes 172040 | tf_op jit(solution)/shard_map/ppermute | solution.py:54
  25.4 5.2 %collective-permute-start.7 = (bf16[224,128]{1,0:T(8,128)(2,1)S(1)}, bf16[224,128]{1,0:T(8,128)(2,1)S(1)}, u32[]{:S(2)}, u32[]{:S(2)}) collective-permute-start(bf16[224,128]{1,0:T(8,128)(2,1)S(1)} %fusion), channel_id=1, source_target_pairs={{0,1},{1,0},{2,3},{3,2},{4,5},{5,4},{6,7},{7,6},{8,9},{9,8},{10,11... | collective-permute-start | bytes 172040 | tf_op jit(solution)/shard_map/ppermute | solution.py:54
  30.7 1.4 %collective-permute-start.13 = (f32[224,128]{1,0:T(8,128)S(1)}, f32[224,128]{1,0:T(8,128)S(1)}, u32[]{:S(2)}, u32[]{:S(2)}) collective-permute-start(f32[224,128]{1,0:T(8,128)S(1)} %add_add_fusion), channel_id=1, source_target_pairs={{0,16},{16,0},{1,17},{17,1},{2,18},{18,2},{3,19},{19,3},{4,20},{20... | collective-permute-start | bytes 344072 | tf_op jit(solution)/shard_map/ppermute | solution.py:54

commit v14 on v10

--- a/solution.py
+++ b/solution.py
@@ -11,7 +11,7 @@
 BF16 = jnp.bfloat16
 GROUP = 4
 AXES = ("depth", "height", "dp")
-WAYS = {"depth": (1, 2, 3), "height": (1, 2, 3), "dp": (1, 2, 3)}
+WAYS = {"depth": (1, 2, 3), "height": (1, 2, 3), "dp": (2, 1, 3)}
 
 
 def paired(axis):

time: 33 us -> 33 us (level)
  transfers between devices with their start and end apart: 14 -> 14, of which waited for: 10 -> 11; matrix products, arithmetic and copies ran while one was open for 7% -> 7% of each run, Pallas kernels for 14% -> 14%
where the time goes in v14:
time: 33 us; the launch traced here: 32.8 us
  starting transfers between devices  15.4 us (47%)
  Pallas kernels  6.62 us (20%)
  waiting for transfers between devices  6.54 us (20%)
  local copies, waits for them, and re-layouts  3.1 us (9%)
  between operations  0.87 us (3%)
    ppermute x8, starting transfers between devices, swap(): lax.ppermute(array, axis, [(i, i ^ mask) for i in range(lax.axis_size(axi...  8.26 us
    pallas_call x5, Pallas kernels, call(): pl.pallas_call(kernel, out_shape=outs, scratch_shapes=scratch, compiler_p...  5.42 us
    ppermute x2, starting transfers between devices, meet(): second = lax.ppermute(jnp.where(even, low_edge, high_edge), axis, outer)  5.2 us
    ppermute x8, waiting for transfers between devices, swap(): lax.ppermute(array, axis, [(i, i ^ mask) for i in range(lax.axis_size(axi...  3.28 us
    ppermute x4, waiting for transfers between devices, meet(): first = lax.ppermute(jnp.where(even, high_edge, low_edge), axis, inner)  2.98 us
    ppermute x4, starting transfers between devices, meet(): first = lax.ppermute(jnp.where(even, high_edge, low_edge), axis, inner)  1.96 us
    unnamed x6, local copies, waits for them, and re-layouts  1.95 us
    pallas_call x1, Pallas kernels, loaded(): pl.pallas_call(load_kernel, out_shape=[jax.ShapeDtypeStruct(a.shape, a.dt...  1.21 us
  transfers between devices with their start and end apart: 14, of which 11 were waited for; matrix products, arithmetic and copies ran while one was open for 7% of the time, Pallas kernels for 14%

profile of v14, /device:TPU:0, one launch (start us, length us, event | category | flops | bytes accessed | tf_op | source)
XLA Modules:
  0.0 32.8 jit_solution(13681562201871143856)
XLA Ops:
  0.6 1.1 %copy.29 = bf16[1,32,8,4,128]{4,1,2,3,0:T(8,128)(2,1)S(1)} copy(bf16[1,32,8,4,128]{4,3,2,1,0:T(4,128)(2,1)} %param.4) | data formatting | bytes 524288 | tf_op args[0]
  1.7 4.0 %collective-permute-start = (bf16[8,32,128]{2,1,0:T(8,128)(2,1)S(1)}, bf16[8,32,128]{2,1,0:T(8,128)(2,1)S(1)}, u32[]{:S(2)}, u32[]{:S(2)}) collective-permute-start(bf16[8,32,128]{2,1,0:T(8,128)(2,1)S(1)} %get-tuple-element.79), channel_id=1, source_target_pairs={{0,12},{4,8},{8,4},{12,0},{1,13},{5,9},{9,5},{13,1},{2,14},{6,10},... | collective-permute-start | bytes 196616 | tf_op jit(solution)/shard_map/ppermute | solution.py:36
  5.7 0.5 %collective-permute-start.1 = (bf16[8,32,128]{2,1,0:T(8,128)(2,1)S(1)}, bf16[8,32,128]{2,1,0:T(8,128)(2,1)S(1)}, u32[]{:S(2)}, u32[]{:S(2)}) collective-permute-start(bf16[8,32,128]{2,1,0:T(8,128)(2,1)S(1)} %get-tuple-element.80), channel_id=1, source_target_pairs={{0,4},{4,0},{8,12},{12,8},{1,5},{5,1},{9,13},{13,9},{2,6},{6,2},{1... | collective-permute-start | bytes 196616 | tf_op jit(solution)/shard_map/ppermute | solution.py:32
  6.3 1.2 %shard_map.67 = (bf16[3,3,3,32,64]{4,3,2,1,0:T(8,128)(2,1)S(1)}, f32[1,64]{1,0:T(1,128)S(1)}, bf16[1,64,8,4,128]{4,3,2,1,0:T(4,128)(2,1)S(1)}) custom-call(bf16[3,3,3,32,64]{4,3,2,1,0:T(8,128)(2,1)} %bitcast.40, f32[1,64]{1,0:T(1,128)} %bitcast.41, bf16[1,64,8,4,128]{4,3,2,1,0:T(4,128)(2,1)} %refs_2_), custom_call_target="tpu_custom_call" | custom-call | tf_op jit(solution)/shard_map/pallas_call | solution.py:231
  8.2 1.1 %shard_map.68 = (bf16[12,64,128]{2,1,0:T(8,128)(2,1)S(1)}, f32[448,128]{1,0:T(8,128)S(1)}) custom-call(bf16[8,4,32,128]{3,2,1,0:T(8,128)(2,1)S(1)} %copy.22.x, bf16[192,288]{1,0:T(8,128)(2,1)S(1)} %copy.19.refs_0_.refs_2_.refs_4_, f32[1,64]{1,0:T(1,128)S(1)} %get-tuple-element.33.refs_1_.refs_3_.refs_5_, bf16[8,4,64,128]{3,2,1,0:T(8,128)(2,1)S(1)} %bitcast.32), custom_call_target="tpu_custom_call" | custom-call | flops 339738624 | bytes 1323264 | tf_op jit(solution)/shard_map/pallas_call | solution.py:243
  9.3 0.6 %collective-permute-done.1 = bf16[8,32,128]{2,1,0:T(8,128)(2,1)S(1)} collective-permute-done((bf16[8,32,128]{2,1,0:T(8,128)(2,1)S(1)}, bf16[8,32,128]{2,1,0:T(8,128)(2,1)S(1)}, u32[]{:S(2)}, u32[]{:S(2)}) %collective-permute-start.1) | collective-permute-done | bytes 65568 | tf_op jit(solution)/shard_map/ppermute | solution.py:32
  10.1 1.1 %shard_map.69 = (bf16[12,64,128]{2,1,0:T(8,128)(2,1)S(1)}, f32[448,128]{1,0:T(8,128)S(1)}) custom-call(bf16[8,4,32,128]{3,2,1,0:T(8,128)(2,1)S(1)} %copy.22.x, bf16[8,32,128]{2,1,0:T(8,128)(2,1)S(1)} %get-tuple-element.38.refs_0_, bf16[8,32,128]{2,1,0:T(8,128)(2,1)S(1)} %get-tuple-element.39.refs_1_, bf16[192,288]{1,0:T(8,128)(2,1)S(1)} %copy.19.refs_0_.refs_2_.refs_4_, ...), custom_call_target="tpu_custom_call" | custom-call | flops 339738624 | bytes 1683712 | tf_op jit(solution)/shard_map/pallas_call | solution.py:243
  11.3 1.1 %shard_map.70 = (bf16[8,64,128]{2,1,0:T(8,128)(2,1)S(1)}, f32[448,128]{1,0:T(8,128)S(1)}) custom-call(bf16[8,4,32,128]{3,2,1,0:T(8,128)(2,1)S(1)} %copy.22.x, bf16[8,32,128]{2,1,0:T(8,128)(2,1)S(1)} %get-tuple-element.38.refs_0_, bf16[8,32,128]{2,1,0:T(8,128)(2,1)S(1)} %get-tuple-element.39.refs_1_, bf16[6,32,128]{2,1,0:T(8,128)(2,1)S(1)} %get-tuple-element.92.refs_2_, ...), custom_call_target="tpu_custom_call" | custom-call | flops 226492416 | bytes 1716480 | tf_op jit(solution)/shard_map/pallas_call | solution.py:243
  12.5 0.5 %collective-permute-start.10 = (bf16[4,64,128]{2,1,0:T(8,128)(2,1)S(1)}, bf16[4,64,128]{2,1,0:T(8,128)(2,1)S(1)}, u32[]{:S(2)}, u32[]{:S(2)}) collective-permute-start(bf16[4,64,128]{2,1,0:T(8,128)(2,1)S(1)} %slice_select_fusion.1), channel_id=1, source_target_pairs={{0,16},{16,0},{1,17},{17,1},{2,18},{18,2},{3,19},{19,3},{4,20},{20... | collective-permute-start | bytes 196616 | tf_op jit(solution)/shard_map/ppermute | solution.py:32
  13.2 0.7 %collective-permute-done.10 = bf16[4,64,128]{2,1,0:T(8,128)(2,1)S(1)} collective-permute-done((bf16[4,64,128]{2,1,0:T(8,128)(2,1)S(1)}, bf16[4,64,128]{2,1,0:T(8,128)(2,1)S(1)}, u32[]{:S(2)}, u32[]{:S(2)}) %collective-permute-start.10) | collective-permute-done | bytes 65568 | tf_op jit(solution)/shard_map/ppermute | solution.py:32
  14.4 1.2 %collective-permute-start.6 = (bf16[224,128]{1,0:T(8,128)(2,1)S(1)}, bf16[224,128]{1,0:T(8,128)(2,1)S(1)}, u32[]{:S(2)}, u32[]{:S(2)}) collective-permute-start(bf16[224,128]{1,0:T(8,128)(2,1)S(1)} %get-tuple-element.59), channel_id=1, source_target_pairs={{0,12},{4,8},{8,4},{12,0},{1,13},{5,9},{9,5},{13,1},{2,14},{6,10},... | collective-permute-start | bytes 172040 | tf_op jit(solution)/shard_map/ppermute | solution.py:54
  15.6 1.3 %collective-permute-start.5 = (bf16[224,128]{1,0:T(8,128)(2,1)S(1)}, bf16[224,128]{1,0:T(8,128)(2,1)S(1)}, u32[]{:S(2)}, u32[]{:S(2)}) collective-permute-start(bf16[224,128]{1,0:T(8,128)(2,1)S(1)} %get-tuple-element.59), channel_id=1, source_target_pairs={{0,8},{4,12},{8,0},{12,4},{1,9},{5,13},{9,1},{13,5},{2,10},{6,14},... | collective-permute-start | bytes 172040 | tf_op jit(solution)/shard_map/ppermute | solution.py:54
  16.9 1.1 %collective-permute-start.4 = (bf16[224,128]{1,0:T(8,128)(2,1)S(1)}, bf16[224,128]{1,0:T(8,128)(2,1)S(1)}, u32[]{:S(2)}, u32[]{:S(2)}) collective-permute-start(bf16[224,128]{1,0:T(8,128)(2,1)S(1)} %get-tuple-element.59), channel_id=1, source_target_pairs={{0,4},{4,0},{8,12},{12,8},{1,5},{5,1},{9,13},{13,9},{2,6},{6,2},{1... | collective-permute-start | bytes 172040 | tf_op jit(solution)/shard_map/ppermute | solution.py:54
  18.4 1.2 %collective-permute-start.11 = (bf16[10,64,128]{2,1,0:T(8,128)(2,1)S(1)}, bf16[10,64,128]{2,1,0:T(8,128)(2,1)S(1)}, u32[]{:S(2)}, u32[]{:S(2)}) collective-permute-start(bf16[10,64,128]{2,1,0:T(8,128)(2,1)S(1)} %get-tuple-element.63), channel_id=1, source_target_pairs={{0,12},{4,8},{8,4},{12,0},{1,13},{5,9},{9,5},{13,1},{2,14},{6,10},... | collective-permute-start | bytes 491528 | tf_op jit(solution)/shard_map/ppermute | solution.py:36
  19.6 0.9 %collective-permute-start.12 = (bf16[10,64,128]{2,1,0:T(8,128)(2,1)S(1)}, bf16[10,64,128]{2,1,0:T(8,128)(2,1)S(1)}, u32[]{:S(2)}, u32[]{:S(2)}) collective-permute-start(bf16[10,64,128]{2,1,0:T(8,128)(2,1)S(1)} %get-tuple-element.64), channel_id=1, source_target_pairs={{0,4},{4,0},{8,12},{12,8},{1,5},{5,1},{9,13},{13,9},{2,6},{6,2},{1... | collective-permute-start | bytes 491528 | tf_op jit(solution)/shard_map/ppermute | solution.py:32
  20.6 1.1 %collective-permute-done.4 = bf16[224,128]{1,0:T(8,128)(2,1)S(1)} collective-permute-done((bf16[224,128]{1,0:T(8,128)(2,1)S(1)}, bf16[224,128]{1,0:T(8,128)(2,1)S(1)}, u32[]{:S(2)}, u32[]{:S(2)}) %collective-permute-start.4) | collective-permute-done | bytes 57376 | tf_op jit(solution)/shard_map/ppermute | solution.py:54
  21.7 3.7 %collective-permute-start.9 = (bf16[224,128]{1,0:T(8,128)(2,1)S(1)}, bf16[224,128]{1,0:T(8,128)(2,1)S(1)}, u32[]{:S(2)}, u32[]{:S(2)}) collective-permute-start(bf16[224,128]{1,0:T(8,128)(2,1)S(1)} %fusion), channel_id=1, source_target_pairs={{0,3},{1,2},{2,1},{3,0},{4,7},{5,6},{6,5},{7,4},{8,11},{9,10},{10,... | collective-permute-start | bytes 172040 | tf_op jit(solution)/shard_map/ppermute | solution.py:54
  25.4 0.8 %collective-permute-start.7 = (bf16[224,128]{1,0:T(8,128)(2,1)S(1)}, bf16[224,128]{1,0:T(8,128)(2,1)S(1)}, u32[]{:S(2)}, u32[]{:S(2)}) collective-permute-start(bf16[224,128]{1,0:T(8,128)(2,1)S(1)} %fusion), channel_id=1, source_target_pairs={{0,2},{1,3},{2,0},{3,1},{4,6},{5,7},{6,4},{7,5},{8,10},{9,11},{10,... | collective-permute-start | bytes 172040 | tf_op jit(solution)/shard_map/ppermute | solution.py:54
  26.5 1.5 %collective-permute-done.12 = bf16[10,64,128]{2,1,0:T(8,128)(2,1)S(1)} collective-permute-done((bf16[10,64,128]{2,1,0:T(8,128)(2,1)S(1)}, bf16[10,64,128]{2,1,0:T(8,128)(2,1)S(1)}, u32[]{:S(2)}, u32[]{:S(2)}) %collective-permute-start.12) | collective-permute-done | bytes 163872 | tf_op jit(solution)/shard_map/ppermute | solution.py:32
  28.0 1.2 %shard_map.71 = bf16[8,4,32,128]{3,2,1,0:T(8,128)(2,1)S(1)} custom-call(bf16[12,64,128]{2,1,0:T(8,128)(2,1)S(1)} %get-tuple-element.43.inner, bf16[12,64,128]{2,1,0:T(8,128)(2,1)S(1)} %get-tuple-element.44.sides, bf16[8,64,128]{2,1,0:T(8,128)(2,1)S(1)} %get-tuple-element.45.ends, bf16[4,64,128]{2,1,0:T(8,128)(2,1)S(1)} %get-tuple-element.46.below, ...), custom_call_target="tpu_custom_call" | custom-call | flops 452984832 | bytes 1355776 | tf_op jit(solution)/shard_map/pallas_call | solution.py:243
  29.6 0.9 %collective-permute-done.7 = bf16[224,128]{1,0:T(8,128)(2,1)S(1)} collective-permute-done((bf16[224,128]{1,0:T(8,128)(2,1)S(1)}, bf16[224,128]{1,0:T(8,128)(2,1)S(1)}, u32[]{:S(2)}, u32[]{:S(2)}) %collective-permute-start.7) | collective-permute-done | bytes 57376 | tf_op jit(solution)/shard_map/ppermute | solution.py:54
  30.6 0.8 %copy.25 = bf16[1,32,8,4,128]{4,3,2,1,0:T(4,128)(2,1)} copy(bf16[1,32,8,4,128]{4,1,3,2,0:T(8,128)(2,1)S(1)} %bitcast.36) | data formatting | bytes 524288
  31.5 0.5 %collective-permute-done.13 = f32[224,128]{1,0:T(8,128)S(1)} collective-permute-done((f32[224,128]{1,0:T(8,128)S(1)}, f32[224,128]{1,0:T(8,128)S(1)}, u32[]{:S(2)}, u32[]{:S(2)}) %collective-permute-start.13) | collective-permute-done | bytes 114720 | tf_op jit(solution)/shard_map/ppermute | solution.py:54
  32.0 0.9 %shard_map.72 = (f32[864,64]{1,0:T(8,128)}, f32[1,64]{1,0:T(1,128)}) custom-call(f32[224,128]{1,0:T(8,128)S(1)} %get-tuple-element.70.refs_0_, f32[224,128]{1,0:T(8,128)S(1)} %get-tuple-element.69.refs_1_), custom_call_target="tpu_custom_call" | custom-call | flops 57344 | bytes 450816 | tf_op jit(solution)/shard_map/pallas_call | solution.py:243
  (41 shorter events, 3.0 us)
Async XLA Ops:
  1.7 7.6 %collective-permute-start = (bf16[8,32,128]{2,1,0:T(8,128)(2,1)S(1)}, bf16[8,32,128]{2,1,0:T(8,128)(2,1)S(1)}, u32[]{:S(2)}, u32[]{:S(2)}) collective-permute-start(bf16[8,32,128]{2,1,0:T(8,128)(2,1)S(1)} %get-tuple-element.79), channel_id=1, source_target_pairs={{0,12},{4,8},{8,4},{12,0},{1,13},{5,9},{9,5},{13,1},{2,14},{6,10},... | collective-permute-start | bytes 196616 | tf_op jit(solution)/shard_map/ppermute | solution.py:36
  5.7 4.3 %collective-permute-start.1 = (bf16[8,32,128]{2,1,0:T(8,128)(2,1)S(1)}, bf16[8,32,128]{2,1,0:T(8,128)(2,1)S(1)}, u32[]{:S(2)}, u32[]{:S(2)}) collective-permute-start(bf16[8,32,128]{2,1,0:T(8,128)(2,1)S(1)} %get-tuple-element.80), channel_id=1, source_target_pairs={{0,4},{4,0},{8,12},{12,8},{1,5},{5,1},{9,13},{13,9},{2,6},{6,2},{1... | collective-permute-start | bytes 196616 | tf_op jit(solution)/shard_map/ppermute | solution.py:32
  10.0 1.3 %collective-permute-start.2 = (bf16[6,32,128]{2,1,0:T(8,128)(2,1)S(1)}, bf16[6,32,128]{2,1,0:T(8,128)(2,1)S(1)}, u32[]{:S(2)}, u32[]{:S(2)}) collective-permute-start(bf16[6,32,128]{2,1,0:T(8,128)(2,1)S(1)} %maximum_select_fusion), channel_id=1, source_target_pairs={{0,16},{16,0},{1,17},{17,1},{2,18},{18,2},{3,19},{19,3},{4,20},{20... | collective-permute-start | bytes 147464 | tf_op jit(solution)/shard_map/ppermute | solution.py:32
  12.5 1.4 %collective-permute-start.10 = (bf16[4,64,128]{2,1,0:T(8,128)(2,1)S(1)}, bf16[4,64,128]{2,1,0:T(8,128)(2,1)S(1)}, u32[]{:S(2)}, u32[]{:S(2)}) collective-permute-start(bf16[4,64,128]{2,1,0:T(8,128)(2,1)S(1)} %slice_select_fusion.1), channel_id=1, source_target_pairs={{0,16},{16,0},{1,17},{17,1},{2,18},{18,2},{3,19},{19,3},{4,20},{20... | collective-permute-start | bytes 196616 | tf_op jit(solution)/shard_map/ppermute | solution.py:32
  13.0 1.4 %collective-permute-start.3 = (f32[224,128]{1,0:T(8,128)S(1)}, f32[224,128]{1,0:T(8,128)S(1)}, u32[]{:S(2)}, u32[]{:S(2)}) collective-permute-start(f32[224,128]{1,0:T(8,128)S(1)} %slice_select_fusion), channel_id=1, source_target_pairs={{0,16},{16,0},{1,17},{17,1},{2,18},{18,2},{3,19},{19,3},{4,20},{20... | collective-permute-start | bytes 344072 | tf_op jit(solution)/shard_map/ppermute | solution.py:54
  14.4 6.1 %collective-permute-start.6 = (bf16[224,128]{1,0:T(8,128)(2,1)S(1)}, bf16[224,128]{1,0:T(8,128)(2,1)S(1)}, u32[]{:S(2)}, u32[]{:S(2)}) collective-permute-start(bf16[224,128]{1,0:T(8,128)(2,1)S(1)} %get-tuple-element.59), channel_id=1, source_target_pairs={{0,12},{4,8},{8,4},{12,0},{1,13},{5,9},{9,5},{13,1},{2,14},{6,10},... | collective-permute-start | bytes 172040 | tf_op jit(solution)/shard_map/ppermute | solution.py:54
  15.6 4.9 %collective-permute-start.5 = (bf16[224,128]{1,0:T(8,128)(2,1)S(1)}, bf16[224,128]{1,0:T(8,128)(2,1)S(1)}, u32[]{:S(2)}, u32[]{:S(2)}) collective-permute-start(bf16[224,128]{1,0:T(8,128)(2,1)S(1)} %get-tuple-element.59), channel_id=1, source_target_pairs={{0,8},{4,12},{8,0},{12,4},{1,9},{5,13},{9,1},{13,5},{2,10},{6,14},... | collective-permute-start | bytes 172040 | tf_op jit(solution)/shard_map/ppermute | solution.py:54
  16.9 4.8 %collective-permute-start.4 = (bf16[224,128]{1,0:T(8,128)(2,1)S(1)}, bf16[224,128]{1,0:T(8,128)(2,1)S(1)}, u32[]{:S(2)}, u32[]{:S(2)}) collective-permute-start(bf16[224,128]{1,0:T(8,128)(2,1)S(1)} %get-tuple-element.59), channel_id=1, source_target_pairs={{0,4},{4,0},{8,12},{12,8},{1,5},{5,1},{9,13},{13,9},{2,6},{6,2},{1... | collective-permute-start | bytes 172040 | tf_op jit(solution)/shard_map/ppermute | solution.py:54
  18.4 8.1 %collective-permute-start.11 = (bf16[10,64,128]{2,1,0:T(8,128)(2,1)S(1)}, bf16[10,64,128]{2,1,0:T(8,128)(2,1)S(1)}, u32[]{:S(2)}, u32[]{:S(2)}) collective-permute-start(bf16[10,64,128]{2,1,0:T(8,128)(2,1)S(1)} %get-tuple-element.63), channel_id=1, source_target_pairs={{0,12},{4,8},{8,4},{12,0},{1,13},{5,9},{9,5},{13,1},{2,14},{6,10},... | collective-permute-start | bytes 491528 | tf_op jit(solution)/shard_map/ppermute | solution.py:36
  19.6 8.4 %collective-permute-start.12 = (bf16[10,64,128]{2,1,0:T(8,128)(2,1)S(1)}, bf16[10,64,128]{2,1,0:T(8,128)(2,1)S(1)}, u32[]{:S(2)}, u32[]{:S(2)}) collective-permute-start(bf16[10,64,128]{2,1,0:T(8,128)(2,1)S(1)} %get-tuple-element.64), channel_id=1, source_target_pairs={{0,4},{4,0},{8,12},{12,8},{1,5},{5,1},{9,13},{13,9},{2,6},{6,2},{1... | collective-permute-start | bytes 491528 | tf_op jit(solution)/shard_map/ppermute | solution.py:32
  21.7 7.5 %collective-permute-start.9 = (bf16[224,128]{1,0:T(8,128)(2,1)S(1)}, bf16[224,128]{1,0:T(8,128)(2,1)S(1)}, u32[]{:S(2)}, u32[]{:S(2)}) collective-permute-start(bf16[224,128]{1,0:T(8,128)(2,1)S(1)} %fusion), channel_id=1, source_target_pairs={{0,3},{1,2},{2,1},{3,0},{4,7},{5,6},{6,5},{7,4},{8,11},{9,10},{10,... | collective-permute-start | bytes 172040 | tf_op jit(solution)/shard_map/ppermute | solution.py:54
  25.4 4.2 %collective-permute-start.8 = (bf16[224,128]{1,0:T(8,128)(2,1)S(1)}, bf16[224,128]{1,0:T(8,128)(2,1)S(1)}, u32[]{:S(2)}, u32[]{:S(2)}) collective-permute-start(bf16[224,128]{1,0:T(8,128)(2,1)S(1)} %fusion), channel_id=1, source_target_pairs={{0,1},{1,0},{2,3},{3,2},{4,5},{5,4},{6,7},{7,6},{8,9},{9,8},{10,11... | collective-permute-start | bytes 172040 | tf_op jit(solution)/shard_map/ppermute | solution.py:54
  25.4 5.1 %collective-permute-start.7 = (bf16[224,128]{1,0:T(8,128)(2,1)S(1)}, bf16[224,128]{1,0:T(8,128)(2,1)S(1)}, u32[]{:S(2)}, u32[]{:S(2)}) collective-permute-start(bf16[224,128]{1,0:T(8,128)(2,1)S(1)} %fusion), channel_id=1, source_target_pairs={{0,2},{1,3},{2,0},{3,1},{4,6},{5,7},{6,4},{7,5},{8,10},{9,11},{10,... | collective-permute-start | bytes 172040 | tf_op jit(solution)/shard_map/ppermute | solution.py:54
  30.5 1.4 %collective-permute-start.13 = (f32[224,128]{1,0:T(8,128)S(1)}, f32[224,128]{1,0:T(8,128)S(1)}, u32[]{:S(2)}, u32[]{:S(2)}) collective-permute-start(f32[224,128]{1,0:T(8,128)S(1)} %add_add_fusion), channel_id=1, source_target_pairs={{0,16},{16,0},{1,17},{17,1},{2,18},{18,2},{3,19},{19,3},{4,20},{20... | collective-permute-start | bytes 344072 | tf_op jit(solution)/shard_map/ppermute | solution.py:54

commit v15 on v10

--- a/solution.py
+++ b/solution.py
@@ -9,7 +9,7 @@
 
 F32 = jnp.float32
 BF16 = jnp.bfloat16
-GROUP = 4
+GROUP = 6
 AXES = ("depth", "height", "dp")
 WAYS = {"depth": (1, 2, 3), "height": (1, 2, 3), "dp": (1, 2, 3)}
 

time: 33 us -> 33.2 us (level)
  transfers between devices with their start and end apart: 14 -> 14, of which waited for: 10 -> 9; matrix products, arithmetic and copies ran while one was open for 7% -> 7% of each run, Pallas kernels for 14% -> 15%
where the time goes in v15:
time: 33.2 us; the launch traced here: 33 us
  starting transfers between devices  15.4 us (46%)
  Pallas kernels  6.89 us (21%)
  waiting for transfers between devices  6.44 us (19%)
  local copies, waits for them, and re-layouts  3.1 us (9%)
  between operations  0.88 us (3%)
    ppermute x8, starting transfers between devices, swap(): lax.ppermute(array, axis, [(i, i ^ mask) for i in range(lax.axis_size(axi...  8.16 us
    pallas_call x5, Pallas kernels, call(): pl.pallas_call(kernel, out_shape=outs, scratch_shapes=scratch, compiler_p...  5.69 us
    ppermute x2, starting transfers between devices, meet(): second = lax.ppermute(jnp.where(even, low_edge, high_edge), axis, outer)  5.2 us
    ppermute x8, waiting for transfers between devices, swap(): lax.ppermute(array, axis, [(i, i ^ mask) for i in range(lax.axis_size(axi...  3.37 us
    ppermute x4, waiting for transfers between devices, meet(): first = lax.ppermute(jnp.where(even, high_edge, low_edge), axis, inner)  2.84 us
    ppermute x4, starting transfers between devices, meet(): first = lax.ppermute(jnp.where(even, high_edge, low_edge), axis, inner)  2.05 us
    unnamed x6, local copies, waits for them, and re-layouts  1.95 us
    pallas_call x1, Pallas kernels, loaded(): pl.pallas_call(load_kernel, out_shape=[jax.ShapeDtypeStruct(a.shape, a.dt...  1.21 us
  transfers between devices with their start and end apart: 14, of which 9 were waited for; matrix products, arithmetic and copies ran while one was open for 7% of the time, Pallas kernels for 15%

profile of v15, /device:TPU:0, one launch (start us, length us, event | category | flops | bytes accessed | tf_op | source)
XLA Modules:
  0.0 33.0 jit_solution(782976702158984944)
XLA Ops:
  0.6 1.1 %copy.29 = bf16[1,32,8,4,128]{4,1,2,3,0:T(8,128)(2,1)S(1)} copy(bf16[1,32,8,4,128]{4,3,2,1,0:T(4,128)(2,1)} %param.4) | data formatting | bytes 524288 | tf_op args[0]
  1.7 4.0 %collective-permute-start = (bf16[8,32,128]{2,1,0:T(8,128)(2,1)S(1)}, bf16[8,32,128]{2,1,0:T(8,128)(2,1)S(1)}, u32[]{:S(2)}, u32[]{:S(2)}) collective-permute-start(bf16[8,32,128]{2,1,0:T(8,128)(2,1)S(1)} %get-tuple-element.79), channel_id=1, source_target_pairs={{0,12},{4,8},{8,4},{12,0},{1,13},{5,9},{9,5},{13,1},{2,14},{6,10},... | collective-permute-start | bytes 196616 | tf_op jit(solution)/shard_map/ppermute | solution.py:36
  5.7 0.5 %collective-permute-start.1 = (bf16[8,32,128]{2,1,0:T(8,128)(2,1)S(1)}, bf16[8,32,128]{2,1,0:T(8,128)(2,1)S(1)}, u32[]{:S(2)}, u32[]{:S(2)}) collective-permute-start(bf16[8,32,128]{2,1,0:T(8,128)(2,1)S(1)} %get-tuple-element.80), channel_id=1, source_target_pairs={{0,4},{4,0},{8,12},{12,8},{1,5},{5,1},{9,13},{13,9},{2,6},{6,2},{1... | collective-permute-start | bytes 196616 | tf_op jit(solution)/shard_map/ppermute | solution.py:32
  6.3 1.2 %shard_map.67 = (bf16[3,3,3,32,64]{4,3,2,1,0:T(8,128)(2,1)S(1)}, f32[1,64]{1,0:T(1,128)S(1)}, bf16[1,64,8,4,128]{4,3,2,1,0:T(4,128)(2,1)S(1)}) custom-call(bf16[3,3,3,32,64]{4,3,2,1,0:T(8,128)(2,1)} %bitcast.40, f32[1,64]{1,0:T(1,128)} %bitcast.41, bf16[1,64,8,4,128]{4,3,2,1,0:T(4,128)(2,1)} %refs_2_), custom_call_target="tpu_custom_call" | custom-call | tf_op jit(solution)/shard_map/pallas_call | solution.py:231
  8.2 1.2 %shard_map.68 = (bf16[12,64,128]{2,1,0:T(8,128)(2,1)S(1)}, f32[448,128]{1,0:T(8,128)S(1)}) custom-call(bf16[8,4,32,128]{3,2,1,0:T(8,128)(2,1)S(1)} %copy.22.x, bf16[192,288]{1,0:T(8,128)(2,1)S(1)} %copy.19.refs_0_.refs_2_.refs_4_, f32[1,64]{1,0:T(1,128)S(1)} %get-tuple-element.33.refs_1_.refs_3_.refs_5_, bf16[8,4,64,128]{3,2,1,0:T(8,128)(2,1)S(1)} %bitcast.32), custom_call_target="tpu_custom_call" | custom-call | flops 339738624 | bytes 1323264 | tf_op jit(solution)/shard_map/pallas_call | solution.py:243
  9.5 0.5 %collective-permute-done.1 = bf16[8,32,128]{2,1,0:T(8,128)(2,1)S(1)} collective-permute-done((bf16[8,32,128]{2,1,0:T(8,128)(2,1)S(1)}, bf16[8,32,128]{2,1,0:T(8,128)(2,1)S(1)}, u32[]{:S(2)}, u32[]{:S(2)}) %collective-permute-start.1) | collective-permute-done | bytes 65568 | tf_op jit(solution)/shard_map/ppermute | solution.py:32
  10.1 1.2 %shard_map.69 = (bf16[12,64,128]{2,1,0:T(8,128)(2,1)S(1)}, f32[448,128]{1,0:T(8,128)S(1)}) custom-call(bf16[8,4,32,128]{3,2,1,0:T(8,128)(2,1)S(1)} %copy.22.x, bf16[8,32,128]{2,1,0:T(8,128)(2,1)S(1)} %get-tuple-element.38.refs_0_, bf16[8,32,128]{2,1,0:T(8,128)(2,1)S(1)} %get-tuple-element.39.refs_1_, bf16[192,288]{1,0:T(8,128)(2,1)S(1)} %copy.19.refs_0_.refs_2_.refs_4_, ...), custom_call_target="tpu_custom_call" | custom-call | flops 339738624 | bytes 1683712 | tf_op jit(solution)/shard_map/pallas_call | solution.py:243
  11.4 1.1 %shard_map.70 = (bf16[8,64,128]{2,1,0:T(8,128)(2,1)S(1)}, f32[448,128]{1,0:T(8,128)S(1)}) custom-call(bf16[8,4,32,128]{3,2,1,0:T(8,128)(2,1)S(1)} %copy.22.x, bf16[8,32,128]{2,1,0:T(8,128)(2,1)S(1)} %get-tuple-element.38.refs_0_, bf16[8,32,128]{2,1,0:T(8,128)(2,1)S(1)} %get-tuple-element.39.refs_1_, bf16[6,32,128]{2,1,0:T(8,128)(2,1)S(1)} %get-tuple-element.92.refs_2_, ...), custom_call_target="tpu_custom_call" | custom-call | flops 226492416 | bytes 1716480 | tf_op jit(solution)/shard_map/pallas_call | solution.py:243
  12.5 0.6 %collective-permute-start.10 = (bf16[4,64,128]{2,1,0:T(8,128)(2,1)S(1)}, bf16[4,64,128]{2,1,0:T(8,128)(2,1)S(1)}, u32[]{:S(2)}, u32[]{:S(2)}) collective-permute-start(bf16[4,64,128]{2,1,0:T(8,128)(2,1)S(1)} %slice_select_fusion.1), channel_id=1, source_target_pairs={{0,16},{16,0},{1,17},{17,1},{2,18},{18,2},{3,19},{19,3},{4,20},{20... | collective-permute-start | bytes 196616 | tf_op jit(solution)/shard_map/ppermute | solution.py:32
  13.2 0.8 %collective-permute-done.10 = bf16[4,64,128]{2,1,0:T(8,128)(2,1)S(1)} collective-permute-done((bf16[4,64,128]{2,1,0:T(8,128)(2,1)S(1)}, bf16[4,64,128]{2,1,0:T(8,128)(2,1)S(1)}, u32[]{:S(2)}, u32[]{:S(2)}) %collective-permute-start.10) | collective-permute-done | bytes 65568 | tf_op jit(solution)/shard_map/ppermute | solution.py:32
  14.5 1.2 %collective-permute-start.6 = (bf16[224,128]{1,0:T(8,128)(2,1)S(1)}, bf16[224,128]{1,0:T(8,128)(2,1)S(1)}, u32[]{:S(2)}, u32[]{:S(2)}) collective-permute-start(bf16[224,128]{1,0:T(8,128)(2,1)S(1)} %get-tuple-element.59), channel_id=1, source_target_pairs={{0,12},{4,8},{8,4},{12,0},{1,13},{5,9},{9,5},{13,1},{2,14},{6,10},... | collective-permute-start | bytes 172040 | tf_op jit(solution)/shard_map/ppermute | solution.py:54
  15.8 1.3 %collective-permute-start.5 = (bf16[224,128]{1,0:T(8,128)(2,1)S(1)}, bf16[224,128]{1,0:T(8,128)(2,1)S(1)}, u32[]{:S(2)}, u32[]{:S(2)}) collective-permute-start(bf16[224,128]{1,0:T(8,128)(2,1)S(1)} %get-tuple-element.59), channel_id=1, source_target_pairs={{0,8},{4,12},{8,0},{12,4},{1,9},{5,13},{9,1},{13,5},{2,10},{6,14},... | collective-permute-start | bytes 172040 | tf_op jit(solution)/shard_map/ppermute | solution.py:54
  17.1 1.0 %collective-permute-start.4 = (bf16[224,128]{1,0:T(8,128)(2,1)S(1)}, bf16[224,128]{1,0:T(8,128)(2,1)S(1)}, u32[]{:S(2)}, u32[]{:S(2)}) collective-permute-start(bf16[224,128]{1,0:T(8,128)(2,1)S(1)} %get-tuple-element.59), channel_id=1, source_target_pairs={{0,4},{4,0},{8,12},{12,8},{1,5},{5,1},{9,13},{13,9},{2,6},{6,2},{1... | collective-permute-start | bytes 172040 | tf_op jit(solution)/shard_map/ppermute | solution.py:54
  18.5 1.2 %collective-permute-start.11 = (bf16[10,64,128]{2,1,0:T(8,128)(2,1)S(1)}, bf16[10,64,128]{2,1,0:T(8,128)(2,1)S(1)}, u32[]{:S(2)}, u32[]{:S(2)}) collective-permute-start(bf16[10,64,128]{2,1,0:T(8,128)(2,1)S(1)} %get-tuple-element.63), channel_id=1, source_target_pairs={{0,12},{4,8},{8,4},{12,0},{1,13},{5,9},{9,5},{13,1},{2,14},{6,10},... | collective-permute-start | bytes 491528 | tf_op jit(solution)/shard_map/ppermute | solution.py:36
  19.7 0.9 %collective-permute-start.12 = (bf16[10,64,128]{2,1,0:T(8,128)(2,1)S(1)}, bf16[10,64,128]{2,1,0:T(8,128)(2,1)S(1)}, u32[]{:S(2)}, u32[]{:S(2)}) collective-permute-start(bf16[10,64,128]{2,1,0:T(8,128)(2,1)S(1)} %get-tuple-element.64), channel_id=1, source_target_pairs={{0,4},{4,0},{8,12},{12,8},{1,5},{5,1},{9,13},{13,9},{2,6},{6,2},{1... | collective-permute-start | bytes 491528 | tf_op jit(solution)/shard_map/ppermute | solution.py:32
  20.7 1.2 %collective-permute-done.4 = bf16[224,128]{1,0:T(8,128)(2,1)S(1)} collective-permute-done((bf16[224,128]{1,0:T(8,128)(2,1)S(1)}, bf16[224,128]{1,0:T(8,128)(2,1)S(1)}, u32[]{:S(2)}, u32[]{:S(2)}) %collective-permute-start.4) | collective-permute-done | bytes 57376 | tf_op jit(solution)/shard_map/ppermute | solution.py:54
  21.9 3.7 %collective-permute-start.9 = (bf16[224,128]{1,0:T(8,128)(2,1)S(1)}, bf16[224,128]{1,0:T(8,128)(2,1)S(1)}, u32[]{:S(2)}, u32[]{:S(2)}) collective-permute-start(bf16[224,128]{1,0:T(8,128)(2,1)S(1)} %fusion), channel_id=1, source_target_pairs={{0,3},{1,2},{2,1},{3,0},{4,7},{5,6},{6,5},{7,4},{8,11},{9,10},{10,... | collective-permute-start | bytes 172040 | tf_op jit(solution)/shard_map/ppermute | solution.py:54
  25.6 0.8 %collective-permute-start.7 = (bf16[224,128]{1,0:T(8,128)(2,1)S(1)}, bf16[224,128]{1,0:T(8,128)(2,1)S(1)}, u32[]{:S(2)}, u32[]{:S(2)}) collective-permute-start(bf16[224,128]{1,0:T(8,128)(2,1)S(1)} %fusion), channel_id=1, source_target_pairs={{0,1},{1,0},{2,3},{3,2},{4,5},{5,4},{6,7},{7,6},{8,9},{9,8},{10,11... | collective-permute-start | bytes 172040 | tf_op jit(solution)/shard_map/ppermute | solution.py:54
  26.6 1.5 %collective-permute-done.12 = bf16[10,64,128]{2,1,0:T(8,128)(2,1)S(1)} collective-permute-done((bf16[10,64,128]{2,1,0:T(8,128)(2,1)S(1)}, bf16[10,64,128]{2,1,0:T(8,128)(2,1)S(1)}, u32[]{:S(2)}, u32[]{:S(2)}) %collective-permute-start.12) | collective-permute-done | bytes 163872 | tf_op jit(solution)/shard_map/ppermute | solution.py:32
  28.2 1.2 %shard_map.71 = bf16[8,4,32,128]{3,2,1,0:T(8,128)(2,1)S(1)} custom-call(bf16[12,64,128]{2,1,0:T(8,128)(2,1)S(1)} %get-tuple-element.43.inner, bf16[12,64,128]{2,1,0:T(8,128)(2,1)S(1)} %get-tuple-element.44.sides, bf16[8,64,128]{2,1,0:T(8,128)(2,1)S(1)} %get-tuple-element.45.ends, bf16[4,64,128]{2,1,0:T(8,128)(2,1)S(1)} %get-tuple-element.46.below, ...), custom_call_target="tpu_custom_call" | custom-call | flops 452984832 | bytes 1355776 | tf_op jit(solution)/shard_map/pallas_call | solution.py:243
  29.4 1.3 %collective-permute-done.8 = bf16[224,128]{1,0:T(8,128)(2,1)S(1)} collective-permute-done((bf16[224,128]{1,0:T(8,128)(2,1)S(1)}, bf16[224,128]{1,0:T(8,128)(2,1)S(1)}, u32[]{:S(2)}, u32[]{:S(2)}) %collective-permute-start.8) | collective-permute-done | bytes 57376 | tf_op jit(solution)/shard_map/ppermute | solution.py:54
  30.8 0.8 %copy.25 = bf16[1,32,8,4,128]{4,3,2,1,0:T(4,128)(2,1)} copy(bf16[1,32,8,4,128]{4,1,3,2,0:T(8,128)(2,1)S(1)} %bitcast.36) | data formatting | bytes 524288
  31.6 0.5 %collective-permute-done.13 = f32[224,128]{1,0:T(8,128)S(1)} collective-permute-done((f32[224,128]{1,0:T(8,128)S(1)}, f32[224,128]{1,0:T(8,128)S(1)}, u32[]{:S(2)}, u32[]{:S(2)}) %collective-permute-start.13) | collective-permute-done | bytes 114720 | tf_op jit(solution)/shard_map/ppermute | solution.py:54
  32.1 0.9 %shard_map.72 = (f32[864,64]{1,0:T(8,128)}, f32[1,64]{1,0:T(1,128)}) custom-call(f32[224,128]{1,0:T(8,128)S(1)} %get-tuple-element.70.refs_0_, f32[224,128]{1,0:T(8,128)S(1)} %get-tuple-element.69.refs_1_), custom_call_target="tpu_custom_call" | custom-call | flops 57344 | bytes 450816 | tf_op jit(solution)/shard_map/pallas_call | solution.py:243
  (41 shorter events, 2.4 us)
Async XLA Ops:
  1.7 7.7 %collective-permute-start = (bf16[8,32,128]{2,1,0:T(8,128)(2,1)S(1)}, bf16[8,32,128]{2,1,0:T(8,128)(2,1)S(1)}, u32[]{:S(2)}, u32[]{:S(2)}) collective-permute-start(bf16[8,32,128]{2,1,0:T(8,128)(2,1)S(1)} %get-tuple-element.79), channel_id=1, source_target_pairs={{0,12},{4,8},{8,4},{12,0},{1,13},{5,9},{9,5},{13,1},{2,14},{6,10},... | collective-permute-start | bytes 196616 | tf_op jit(solution)/shard_map/ppermute | solution.py:36
  5.7 4.3 %collective-permute-start.1 = (bf16[8,32,128]{2,1,0:T(8,128)(2,1)S(1)}, bf16[8,32,128]{2,1,0:T(8,128)(2,1)S(1)}, u32[]{:S(2)}, u32[]{:S(2)}) collective-permute-start(bf16[8,32,128]{2,1,0:T(8,128)(2,1)S(1)} %get-tuple-element.80), channel_id=1, source_target_pairs={{0,4},{4,0},{8,12},{12,8},{1,5},{5,1},{9,13},{13,9},{2,6},{6,2},{1... | collective-permute-start | bytes 196616 | tf_op jit(solution)/shard_map/ppermute | solution.py:32
  10.0 1.3 %collective-permute-start.2 = (bf16[6,32,128]{2,1,0:T(8,128)(2,1)S(1)}, bf16[6,32,128]{2,1,0:T(8,128)(2,1)S(1)}, u32[]{:S(2)}, u32[]{:S(2)}) collective-permute-start(bf16[6,32,128]{2,1,0:T(8,128)(2,1)S(1)} %maximum_select_fusion), channel_id=1, source_target_pairs={{0,16},{16,0},{1,17},{17,1},{2,18},{18,2},{3,19},{19,3},{4,20},{20... | collective-permute-start | bytes 147464 | tf_op jit(solution)/shard_map/ppermute | solution.py:32
  12.5 1.5 %collective-permute-start.10 = (bf16[4,64,128]{2,1,0:T(8,128)(2,1)S(1)}, bf16[4,64,128]{2,1,0:T(8,128)(2,1)S(1)}, u32[]{:S(2)}, u32[]{:S(2)}) collective-permute-start(bf16[4,64,128]{2,1,0:T(8,128)(2,1)S(1)} %slice_select_fusion.1), channel_id=1, source_target_pairs={{0,16},{16,0},{1,17},{17,1},{2,18},{18,2},{3,19},{19,3},{4,20},{20... | collective-permute-start | bytes 196616 | tf_op jit(solution)/shard_map/ppermute | solution.py:32
  13.1 1.4 %collective-permute-start.3 = (f32[224,128]{1,0:T(8,128)S(1)}, f32[224,128]{1,0:T(8,128)S(1)}, u32[]{:S(2)}, u32[]{:S(2)}) collective-permute-start(f32[224,128]{1,0:T(8,128)S(1)} %slice_select_fusion), channel_id=1, source_target_pairs={{0,16},{16,0},{1,17},{17,1},{2,18},{18,2},{3,19},{19,3},{4,20},{20... | collective-permute-start | bytes 344072 | tf_op jit(solution)/shard_map/ppermute | solution.py:54
  14.5 6.1 %collective-permute-start.6 = (bf16[224,128]{1,0:T(8,128)(2,1)S(1)}, bf16[224,128]{1,0:T(8,128)(2,1)S(1)}, u32[]{:S(2)}, u32[]{:S(2)}) collective-permute-start(bf16[224,128]{1,0:T(8,128)(2,1)S(1)} %get-tuple-element.59), channel_id=1, source_target_pairs={{0,12},{4,8},{8,4},{12,0},{1,13},{5,9},{9,5},{13,1},{2,14},{6,10},... | collective-permute-start | bytes 172040 | tf_op jit(solution)/shard_map/ppermute | solution.py:54
  15.8 4.9 %collective-permute-start.5 = (bf16[224,128]{1,0:T(8,128)(2,1)S(1)}, bf16[224,128]{1,0:T(8,128)(2,1)S(1)}, u32[]{:S(2)}, u32[]{:S(2)}) collective-permute-start(bf16[224,128]{1,0:T(8,128)(2,1)S(1)} %get-tuple-element.59), channel_id=1, source_target_pairs={{0,8},{4,12},{8,0},{12,4},{1,9},{5,13},{9,1},{13,5},{2,10},{6,14},... | collective-permute-start | bytes 172040 | tf_op jit(solution)/shard_map/ppermute | solution.py:54
  17.1 4.8 %collective-permute-start.4 = (bf16[224,128]{1,0:T(8,128)(2,1)S(1)}, bf16[224,128]{1,0:T(8,128)(2,1)S(1)}, u32[]{:S(2)}, u32[]{:S(2)}) collective-permute-start(bf16[224,128]{1,0:T(8,128)(2,1)S(1)} %get-tuple-element.59), channel_id=1, source_target_pairs={{0,4},{4,0},{8,12},{12,8},{1,5},{5,1},{9,13},{13,9},{2,6},{6,2},{1... | collective-permute-start | bytes 172040 | tf_op jit(solution)/shard_map/ppermute | solution.py:54
  18.5 8.1 %collective-permute-start.11 = (bf16[10,64,128]{2,1,0:T(8,128)(2,1)S(1)}, bf16[10,64,128]{2,1,0:T(8,128)(2,1)S(1)}, u32[]{:S(2)}, u32[]{:S(2)}) collective-permute-start(bf16[10,64,128]{2,1,0:T(8,128)(2,1)S(1)} %get-tuple-element.63), channel_id=1, source_target_pairs={{0,12},{4,8},{8,4},{12,0},{1,13},{5,9},{9,5},{13,1},{2,14},{6,10},... | collective-permute-start | bytes 491528 | tf_op jit(solution)/shard_map/ppermute | solution.py:36
  19.7 8.4 %collective-permute-start.12 = (bf16[10,64,128]{2,1,0:T(8,128)(2,1)S(1)}, bf16[10,64,128]{2,1,0:T(8,128)(2,1)S(1)}, u32[]{:S(2)}, u32[]{:S(2)}) collective-permute-start(bf16[10,64,128]{2,1,0:T(8,128)(2,1)S(1)} %get-tuple-element.64), channel_id=1, source_target_pairs={{0,4},{4,0},{8,12},{12,8},{1,5},{5,1},{9,13},{13,9},{2,6},{6,2},{1... | collective-permute-start | bytes 491528 | tf_op jit(solution)/shard_map/ppermute | solution.py:32
  21.9 7.4 %collective-permute-start.9 = (bf16[224,128]{1,0:T(8,128)(2,1)S(1)}, bf16[224,128]{1,0:T(8,128)(2,1)S(1)}, u32[]{:S(2)}, u32[]{:S(2)}) collective-permute-start(bf16[224,128]{1,0:T(8,128)(2,1)S(1)} %fusion), channel_id=1, source_target_pairs={{0,3},{1,2},{2,1},{3,0},{4,7},{5,6},{6,5},{7,4},{8,11},{9,10},{10,... | collective-permute-start | bytes 172040 | tf_op jit(solution)/shard_map/ppermute | solution.py:54
  25.6 5.1 %collective-permute-start.8 = (bf16[224,128]{1,0:T(8,128)(2,1)S(1)}, bf16[224,128]{1,0:T(8,128)(2,1)S(1)}, u32[]{:S(2)}, u32[]{:S(2)}) collective-permute-start(bf16[224,128]{1,0:T(8,128)(2,1)S(1)} %fusion), channel_id=1, source_target_pairs={{0,2},{1,3},{2,0},{3,1},{4,6},{5,7},{6,4},{7,5},{8,10},{9,11},{10,... | collective-permute-start | bytes 172040 | tf_op jit(solution)/shard_map/ppermute | solution.py:54
  25.6 5.1 %collective-permute-start.7 = (bf16[224,128]{1,0:T(8,128)(2,1)S(1)}, bf16[224,128]{1,0:T(8,128)(2,1)S(1)}, u32[]{:S(2)}, u32[]{:S(2)}) collective-permute-start(bf16[224,128]{1,0:T(8,128)(2,1)S(1)} %fusion), channel_id=1, source_target_pairs={{0,1},{1,0},{2,3},{3,2},{4,5},{5,4},{6,7},{7,6},{8,9},{9,8},{10,11... | collective-permute-start | bytes 172040 | tf_op jit(solution)/shard_map/ppermute | solution.py:54
  30.7 1.4 %collective-permute-start.13 = (f32[224,128]{1,0:T(8,128)S(1)}, f32[224,128]{1,0:T(8,128)S(1)}, u32[]{:S(2)}, u32[]{:S(2)}) collective-permute-start(f32[224,128]{1,0:T(8,128)S(1)} %add_add_fusion), channel_id=1, source_target_pairs={{0,16},{16,0},{1,17},{17,1},{2,18},{18,2},{3,19},{19,3},{4,20},{20... | collective-permute-start | bytes 344072 | tf_op jit(solution)/shard_map/ppermute | solution.py:54
